TPU v7x, 32 devices: a whole 2x2x4 slice. The times are simulated.
32 devices in a mesh: patch: 8 (over z, y), var: 4 (over x, core).
Axes of the slice: x: 2, y: 2, z: 4, core: 2. Of those that a mesh axis runs over, the one named last changes fastest.
Arguments:
- input_field: bfloat16 [4, 1024, 48, 16], P(None, 'patch', 'var'), may hold values from -6 to 6
- counts: int32 [4], replicated, may hold values from 256 to 1024, as said below
- var_ids: int32 [4, 48], replicated, may hold values from 0 to 47, each once within a row
- patch_weight: bfloat16 [48, 16, 1024], replicated, may hold values from -1.5 to 1.5
- var_embed: bfloat16 [48, 1024], replicated, may hold values from -6 to 6
- agg_query: bfloat16 [1024], replicated, may hold values from -6 to 6
- query_proj: bfloat16 [1024, 1024], replicated, may hold values from -0.1875 to 0.1875
- key_proj: bfloat16 [1024, 1024], replicated, may hold values from -0.1875 to 0.1875
- value_proj: bfloat16 [1024, 1024], replicated, may hold values from -0.1875 to 0.1875
- agg_out: bfloat16 [1024, 1024], replicated, may hold values from -0.375 to 0.375
- norm_one: bfloat16 [1024], replicated, may hold values from 0.099609375 to 1.8984375
- trunk_qkv: bfloat16 [1024, 3072], replicated, may hold values from -0.1875 to 0.1875
- trunk_out: bfloat16 [1024, 1024], replicated, may hold values from -1.5 to 1.5
- norm_two: bfloat16 [1024], replicated, may hold values from 0.099609375 to 1.8984375
- mlp_in: bfloat16 [1024, 4096], replicated, may hold values from -0.1875 to 0.1875
- mlp_out: bfloat16 [4096, 1024], replicated, may hold values from -0.09375 to 0.09375
- cotangent: bfloat16 [4, 1024, 1024], P('var', 'patch'), may hold values from -6 to 6
Outputs:
- block_out: bfloat16 [4, 1024, 1024], P('var', 'patch')
- field_grad: bfloat16 [4, 1024, 48, 16], P(None, 'patch', 'var')
- patch_weight_grad: float32 [48, 16, 1024], P(None, None, 'patch')
- var_embed_grad: float32 [48, 1024], P(None, 'patch')
- agg_query_grad: float32 [1024], P('patch')
- query_proj_grad: float32 [1024, 1024], P('patch')
- key_proj_grad: float32 [1024, 1024], P('patch')
- value_proj_grad: float32 [1024, 1024], P('patch')
- agg_out_grad: float32 [1024, 1024], P('patch')
- norm_one_grad: float32 [1024], P('patch')
- trunk_qkv_grad: float32 [1024, 3072], P('patch')
- trunk_out_grad: float32 [1024, 1024], P('patch')
- norm_two_grad: float32 [1024], P('patch')
- mlp_in_grad: float32 [1024, 4096], P('patch')
- mlp_out_grad: float32 [4096, 1024], P('patch')
Inputs may be any that keep to these rules, and one draw needn't show every extreme that they name: Each sample fills its first counts slots; every count is 256 or 1024; some sample has 1024 and some other sample has 256. `var_ids`: each row is a permutation of the 48 variables.
All inputs are finite; a program needn't handle non-finite values.
Results may differ from a plain program's by a relative error of at most 0.04.
Values may be sent and summed in bfloat16 or wider, within the bound.
No kernel may reach another device: no remote copies, remote signals or barrier semaphores. Data moves between devices by JAX's collectives and lax.ppermute only.
A program may use at most 384 MiB of HBM per device.

v0:
```python
import functools
import math

import jax
import jax.numpy as jnp
from jax import lax
from jax.experimental import pallas as pl
from jax.experimental.pallas import tpu as pltpu
from jax.sharding import PartitionSpec as P

HEADS = 16
VARS = 48
EPSILON = 1e-05
MASKED = -1e30
HIGHEST = lax.Precision.HIGHEST
BF16 = jnp.bfloat16
F32 = jnp.float32
NN = (((1,), (0,)), ((), ()))
NT = (((1,), (1,)), ((), ()))
TN = (((0,), (0,)), ((), ()))


def cost(flops):
    return pl.CostEstimate(flops=flops, bytes_accessed=1 << 20, transcendentals=0)


def mm(a, b, dims=NN, precision=None):
    return lax.dot_general(a, b, dims, precision=precision, preferred_element_type=F32)


def layer_norm(values, gain_vec):
    average = jnp.mean(values, axis=-1, keepdims=True)
    center = values - average
    spread = jnp.mean(center * center, axis=-1, keepdims=True)
    return center * lax.rsqrt(spread + EPSILON) * gain_vec


def gelu_exact(values):
    return jax.nn.gelu(values, approximate=False)


def split_high_low(values):
    high = values.astype(BF16)
    return high, (values - high.astype(F32)).astype(BF16)


def front_forward_kernel(
    pixels, ids_ref, field_ref, spread_ref, bias_ref, vwt_ref, vet_ref, x_ref, p_ref, mixed_ref, mt_ref
):
    seg = field_ref.shape[1]
    head_dim = mixed_ref.shape[1] // HEADS
    for slot in range(VARS):
        start = pl.multiple_of(ids_ref[0, slot] * pixels, pixels)
        x_ref[pl.ds(start, pixels), :] = field_ref[slot * pixels : (slot + 1) * pixels, :]
    scores = mm(spread_ref[...], x_ref[...]) + bias_ref[...]
    scores = scores.reshape(HEADS, VARS, seg)
    top = jnp.max(scores, axis=1, keepdims=True)
    exponent = jnp.exp(scores - top)
    total = jnp.sum(exponent, axis=1, keepdims=True)
    p_ref[...] = (exponent * (1.0 / total)).reshape(HEADS * VARS, seg)

    def head(h, carry):
        shares = p_ref[pl.ds(pl.multiple_of(h * VARS, VARS), VARS), :]
        pix = x_ref[...].astype(F32).reshape(VARS, pixels, seg)
        scaled = (pix * shares[:, None, :]).astype(BF16).reshape(VARS * pixels, seg)
        rows = pl.ds(pl.multiple_of(h * head_dim, head_dim), head_dim)
        mt_ref[rows, :] = mm(vwt_ref[rows, :], scaled) + mm(vet_ref[rows, :], shares.astype(BF16))
        return carry

    lax.fori_loop(0, HEADS, head, 0)
    mixed_ref[...] = mt_ref[...].T.astype(BF16)


def front_forward(own_ids, own_field, spread, bias, vwt, vet):
    rows, seg = own_field.shape
    width = vwt.shape[0]
    vmem = pl.BlockSpec(memory_space=pltpu.VMEM)
    return pl.pallas_call(
        functools.partial(front_forward_kernel, rows // VARS),
        out_shape=(
            jax.ShapeDtypeStruct((rows, seg), BF16),
            jax.ShapeDtypeStruct((HEADS * VARS, seg), F32),
            jax.ShapeDtypeStruct((seg, width), BF16),
        ),
        in_specs=[pl.BlockSpec(memory_space=pltpu.SMEM)] + [vmem] * 5,
        out_specs=(vmem,) * 3,
        scratch_shapes=[pltpu.VMEM((width, seg), F32)],
        cost_estimate=cost(6 * 10**9),
        name="front_forward",
    )(own_ids, own_field, spread, bias, vwt, vet)


def front_backward_kernel(
    pixels,
    fast,
    place_ref,
    ids_ref,
    x_ref,
    p_ref,
    mg_ref,
    vw_ref,
    ve_ref,
    spread_ref,
    norm_one_ref,
    norm_two_ref,
    field_ref,
    *rest,
):
    rows, seg = x_ref.shape
    m_refs, (fs_ref, dx_ref, s_ref) = rest[:-3], rest[-3:]
    size = m_refs[0].shape[-1]

    def quarter_of(quarter, store):
        if not fast:
            store(m_refs[0].at[quarter])
            return
        mine = quarter // 2 == place_ref[CORE]
        pl.when(mine)(lambda: store(m_refs[0].at[quarter % 2]))
        pl.when(jnp.logical_not(mine))(lambda: store(m_refs[1].at[quarter % 2]))
    width = mg_ref.shape[1]
    head_dim = width // HEADS
    pair_dim = 2 * head_dim
    lane = lax.broadcasted_iota(jnp.int32, (seg, pair_dim), 1)
    dx_ref[...] = jnp.zeros_like(dx_ref)
    pairs = size // pair_dim

    def pair(q, carry):
        cols = pl.ds(pl.multiple_of(q * pair_dim, pair_dim), pair_dim)
        grad = mg_ref[:, cols]
        none = jnp.zeros_like(grad)
        both = jnp.concatenate(
            [jnp.where(lane < head_dim, grad, none), jnp.where(lane >= head_dim, grad, none)], axis=0
        )
        inner = mm(vw_ref[:, cols], both, NT)
        inner_e = mm(ve_ref[:, cols], both, NT)
        pix = x_ref[...].astype(F32).reshape(VARS, pixels, seg)
        scaled, weights = [], []
        for k in range(2):
            hrows = pl.ds(pl.multiple_of((2 * q + k) * VARS, VARS), VARS)
            shares = p_ref[hrows, :]
            part = inner[:, k * seg : (k + 1) * seg].reshape(VARS, pixels, seg)
            share_grad = jnp.sum(pix * part, axis=1) + inner_e[:, k * seg : (k + 1) * seg]
            delta = jnp.sum(shares * share_grad, axis=0, keepdims=True)
            fs_ref[hrows, :] = shares * (share_grad - delta)
            wide = shares[:, None, :]
            dx_ref[...] += (part * wide).reshape(rows, seg)
            scaled.append((pix * wide).astype(BF16).reshape(rows, seg))
            weights.append(shares.astype(BF16))
        quarter, within = q // pairs, pl.ds(pl.multiple_of(q % pairs * pair_dim, pair_dim), pair_dim)
        m_part = mm(jnp.concatenate(scaled, axis=1), both).astype(BF16)
        me_part = mm(jnp.concatenate(weights, axis=1), both).astype(BF16)

        def store(ref):
            ref[0:rows, within] = m_part
            ref[rows : rows + VARS, within] = me_part

        quarter_of(quarter, store)
        return carry

    lax.fori_loop(0, HEADS // 2, pair, 0)
    score_grad = fs_ref[...]
    low = score_grad.astype(BF16)
    dx = dx_ref[...] + mm(spread_ref[...], low, TN)
    dx_ref[...] = dx
    for slot in range(VARS):
        start = pl.multiple_of(ids_ref[0, slot] * pixels, pixels)
        field_ref[slot * pixels : (slot + 1) * pixels, :] = dx_ref[pl.ds(start, pixels), :].astype(BF16)
    ones = jnp.ones((8, seg), F32)
    s_ref[...] = jnp.zeros_like(s_ref)
    var_row = lax.broadcasted_iota(jnp.int32, (VARS, rows), 0)
    var_col = lax.broadcasted_iota(jnp.int32, (VARS, rows), 1) // pixels
    keep = var_row == var_col
    for h in range(HEADS):
        outer = mm(low[h * VARS : (h + 1) * VARS, :], x_ref[...], NT)
        s_ref[h : h + 1, 0:rows] = jnp.sum(jnp.where(keep, outer, 0.0), axis=0, keepdims=True)
        sums = mm(ones, score_grad[h * VARS : (h + 1) * VARS, :], NT, precision=HIGHEST)
        s_ref[h : h + 1, rows : rows + VARS] = sums[0:1, :]
    for h in range(HEADS):
        for ref, first in ((norm_one_ref, width - pair_dim), (norm_two_ref, width - head_dim)):
            s_ref[h : h + 1, first : first + head_dim] = ref[:, h * head_dim : (h + 1) * head_dim]
    for quarter in range(4):
        part = s_ref[:, quarter * size : (quarter + 1) * size].astype(BF16)

        def store_sums(ref, part=part):
            ref[rows + VARS :, :] = part

        quarter_of(quarter, store_sums)


def front_backward(fast, place, own_ids, x_own, shares, mixed_grad, vw, ve, spread, norm_one, norm_two):
    rows, seg = x_own.shape
    width = mixed_grad.shape[1]
    vmem = pl.BlockSpec(memory_space=pltpu.VMEM)
    smem = pl.BlockSpec(memory_space=pltpu.SMEM)
    tall = rows + VARS + HEADS
    if fast:
        sums = (jax.ShapeDtypeStruct((2, tall, width // 4), BF16),) * 2
    else:
        sums = (jax.ShapeDtypeStruct((4, tall, width // 4), BF16),)
    return pl.pallas_call(
        functools.partial(front_backward_kernel, rows // VARS, fast),
        out_shape=(jax.ShapeDtypeStruct((rows, seg), BF16), *sums),
        in_specs=[smem, smem] + [vmem] * 8,
        out_specs=(vmem,) * (1 + len(sums)),
        scratch_shapes=[
            pltpu.VMEM((HEADS * VARS, seg), F32),
            pltpu.VMEM((rows, seg), F32),
            pltpu.VMEM((HEADS, width), F32),
        ],
        cost_estimate=cost(10**8),
        name="front_backward",
    )(place, own_ids, x_own, shares, mixed_grad, vw, ve, spread, norm_one, norm_two)


def load_parts(ref, part, seg, out_ref):
    for source in range(ref.shape[0]):
        out_ref[source * seg : (source + 1) * seg, :] = ref[source, part * seg : (part + 1) * seg, :]


def attend_forward_kernel(head_dim, block, count_ref, qkv_ref, out_ref, lse_ref, q_ref, k_ref, vt_ref):
    full, width = q_ref.shape
    seg = full // qkv_ref.shape[0]
    scaling = 1.0 / math.sqrt(head_dim)
    load_parts(qkv_ref, 2, seg, q_ref)
    vt_ref[...] = q_ref[...].T
    load_parts(qkv_ref, 0, seg, q_ref)
    load_parts(qkv_ref, 1, seg, k_ref)
    count = count_ref[0, 0]
    lane = lax.broadcasted_iota(jnp.int32, (block, width), 1) // head_dim
    row = lax.broadcasted_iota(jnp.int32, (width, block), 0) // head_dim
    valid = lax.broadcasted_iota(jnp.int32, (full, block), 0) < count

    def step(i, carry):
        part = pl.ds(pl.multiple_of(i * block, block), block)
        query = q_ref[part, :]
        total = jnp.zeros((width, block), F32)
        for h in range(width // head_dim):
            own = jnp.where(lane == h, query, jnp.zeros_like(query))
            scores = jnp.where(valid, mm(k_ref[...], own, NT) * scaling, MASKED)
            top = jnp.max(scores, axis=0, keepdims=True)
            exponent = jnp.exp(scores - top)
            denominator = jnp.sum(exponent, axis=0, keepdims=True)
            shares = (exponent * (1.0 / denominator)).astype(BF16)
            lse_ref[h : h + 1, part] = top + jnp.log(denominator)
            total = jnp.where(row == h, mm(vt_ref[...], shares), total)
        out_ref[part, :] = total.T.astype(BF16)
        return carry

    lax.fori_loop(0, full // block, step, 0)


def attend_forward(count, qkv, head_dim):
    parts, triple_rows, width = qkv.shape
    full = parts * triple_rows // 3
    vmem = pl.BlockSpec(memory_space=pltpu.VMEM)
    block = min(256, full)
    return pl.pallas_call(
        functools.partial(attend_forward_kernel, head_dim, block),
        out_shape=(
            jax.ShapeDtypeStruct((full, width), BF16),
            jax.ShapeDtypeStruct((width // head_dim, full), F32),
        ),
        in_specs=[pl.BlockSpec(memory_space=pltpu.SMEM), vmem],
        out_specs=(vmem, vmem),
        scratch_shapes=[
            pltpu.VMEM((full, width), BF16),
            pltpu.VMEM((full, width), BF16),
            pltpu.VMEM((width, full), BF16),
        ],
        cost_estimate=cost(10 * 10**9),
        name="attend_forward",
    )(count, qkv)


def attend_backward_kernel(
    head_dim, block, count_ref, qkv_ref, grad_ref, lse_ref, out_ref, q_ref, k_ref, v_ref, kt_ref, dk_ref, dv_ref
):
    full, width = q_ref.shape
    seg = full // qkv_ref.shape[0]
    scaling = 1.0 / math.sqrt(head_dim)
    load_parts(qkv_ref, 0, seg, q_ref)
    load_parts(qkv_ref, 1, seg, k_ref)
    load_parts(qkv_ref, 2, seg, v_ref)
    kt_ref[...] = k_ref[...].T
    dk_ref[...] = jnp.zeros_like(dk_ref)
    dv_ref[...] = jnp.zeros_like(dv_ref)
    count = count_ref[0, 0]
    lane = lax.broadcasted_iota(jnp.int32, (block, width), 1) // head_dim
    row = lax.broadcasted_iota(jnp.int32, (width, block), 0) // head_dim
    valid = lax.broadcasted_iota(jnp.int32, (full, block), 0) < count

    def step(i, carry):
        part = pl.ds(pl.multiple_of(i * block, block), block)
        query = q_ref[part, :]
        grad = grad_ref[part, :]
        total = jnp.zeros((width, block), F32)
        for h in range(width // head_dim):
            own = jnp.where(lane == h, query, jnp.zeros_like(query))
            own_grad = jnp.where(lane == h, grad, jnp.zeros_like(grad))
            scores = jnp.where(valid, mm(k_ref[...], own, NT) * scaling, MASKED)
            shares = jnp.exp(scores - lse_ref[h : h + 1, part])
            share_grad = mm(v_ref[...], own_grad, NT)
            dot = jnp.sum(shares * share_grad, axis=0, keepdims=True)
            score_grad = (shares * (share_grad - dot)).astype(BF16)
            dv_ref[...] += mm(shares.astype(BF16), own_grad)
            dk_ref[...] += mm(score_grad, own)
            total = jnp.where(row == h, mm(kt_ref[...], score_grad), total)
        turned = (total * scaling).T.astype(BF16)
        for piece in range(block // seg):
            out_ref[i * (block // seg) + piece, 0:seg, :] = turned[piece * seg : (piece + 1) * seg, :]
        return carry

    lax.fori_loop(0, full // block, step, 0)
    for source in range(full // seg):
        rows = slice(source * seg, (source + 1) * seg)
        out_ref[source, seg : 2 * seg, :] = (dk_ref[rows, :] * scaling).astype(BF16)
        out_ref[source, 2 * seg : 3 * seg, :] = dv_ref[rows, :].astype(BF16)


def attend_backward(count, qkv, grad, lse, head_dim):
    parts, triple_rows, width = qkv.shape
    full = parts * triple_rows // 3
    vmem = pl.BlockSpec(memory_space=pltpu.VMEM)
    block = min(256, full)
    return pl.pallas_call(
        functools.partial(attend_backward_kernel, head_dim, block),
        out_shape=jax.ShapeDtypeStruct(qkv.shape, BF16),
        in_specs=[pl.BlockSpec(memory_space=pltpu.SMEM), vmem, vmem, vmem],
        out_specs=vmem,
        scratch_shapes=[pltpu.VMEM((full, width), BF16)] * 3
        + [pltpu.VMEM((width, full), BF16)]
        + [pltpu.VMEM((full, width), F32)] * 2,
        cost_estimate=cost(50 * 10**9),
        name="attend_backward",
    )(count, qkv, grad, lse)


def gathered_attention(triple, count, head_dim):
    seg, triple_width = triple.shape
    width = triple_width // 3
    scaling = 1.0 / math.sqrt(head_dim)
    full = seg * lax.axis_size("patch")
    query = triple[:, :width].reshape(seg, HEADS, head_dim)
    key = lax.all_gather(triple[:, width : 2 * width], "patch", axis=0, tiled=True)
    value = lax.all_gather(triple[:, 2 * width :], "patch", axis=0, tiled=True)
    key = key.reshape(full, HEADS, head_dim)
    value = value.reshape(full, HEADS, head_dim)
    valid = (jnp.arange(full, dtype=jnp.int32) < count)[None, None, :]

    def score():
        raw = jnp.einsum("qhd,khd->hqk", query, key, preferred_element_type=F32) * scaling
        return jnp.where(valid, raw, MASKED)

    masked = score()
    top = jnp.max(masked, axis=-1, keepdims=True)
    exponent = jnp.exp(masked - top)
    denominator = jnp.sum(exponent, axis=-1, keepdims=True)
    shares_low = (exponent / denominator).astype(BF16)
    lse = top + jnp.log(denominator)
    attended = jnp.einsum("hqk,khd->qhd", shares_low, value, preferred_element_type=F32)

    def backward(grad):
        grad = grad.reshape(seg, HEADS, head_dim)
        shares = jnp.exp(score() - lse)
        share_grad = jnp.einsum("qhd,khd->hqk", grad, value, preferred_element_type=F32)
        dot = jnp.sum(shares * share_grad, axis=-1, keepdims=True)
        score_grad = (shares * (share_grad - dot)).astype(BF16)
        q_grad = jnp.einsum("hqk,khd->qhd", score_grad, key, preferred_element_type=F32) * scaling
        v_all = jnp.einsum("hqk,qhd->khd", shares.astype(BF16), grad, preferred_element_type=F32)
        k_all = jnp.einsum("hqk,qhd->khd", score_grad, query, preferred_element_type=F32) * scaling
        k_grad, v_grad = (
            lax.psum_scatter(
                part.reshape(full, width).astype(BF16), "patch", scatter_dimension=0, tiled=True
            )
            for part in (k_all, v_all)
        )
        return jnp.concatenate([q_grad.reshape(seg, width).astype(BF16), k_grad, v_grad], axis=1)

    return attended.reshape(seg, width).astype(BF16), backward


def to_heads(values):
    return lax.all_to_all(values, "patch", split_axis=0, concat_axis=0, tiled=True)


def queries_to_heads(triple):
    seg, triple_width = triple.shape
    parts = lax.axis_size("patch")
    own = triple_width // (3 * parts)
    moved = triple.reshape(seg, 3, parts, own).transpose(2, 1, 0, 3).reshape(parts, 3 * seg, own)
    return to_heads(moved)


def weight_grad_kernel(jobs, near, away, place_ref, *refs):
    split = len(refs) - len(near) - len(away)
    arrays, outs = refs[:split], refs[split:]
    rows = outs[0].shape[1]
    sides = (1 - place_ref[Y],) * len(away) + (place_ref[Y],) * len(near)
    start = 0
    for left, left_start, right, right_start, cols in jobs:
        values = [arrays[4 * right + s][:, pl.ds(right_start, cols)] for s in range(4)]
        values = jnp.concatenate(values, axis=0)
        for out, side, blocks in zip(outs, sides, away + near):
            for slot, k in enumerate(blocks):
                source = 2 * (place_ref[Z] ^ k) + side
                group = arrays[4 * left : 4 * left + 4]
                if len(group[0].shape) == 3:
                    factor = [ref[source] for ref in group]
                else:
                    block = pl.ds(pl.multiple_of(left_start + source * rows, rows), rows)
                    factor = [ref[:, block] for ref in group]
                factor = jnp.concatenate(factor, axis=0)
                out[slot, :, start : start + cols] = mm(factor, values, TN).astype(BF16)
        start += cols


def weight_grads(place, jobs, groups, rows, near, away):
    arrays = [array for group in groups for array in group]
    total = sum(job[-1] for job in jobs)
    shapes = [((len(blocks), rows, total), BF16) for blocks in away + near]
    kernel = functools.partial(weight_grad_kernel, jobs, near, away)
    outs = small_call(kernel, place, arrays, shapes, effort=40, name="weight_grads")
    return outs[len(away) :], outs[: len(away)]


def swap(values, axis, bit):
    return lax.ppermute(values, axis, [(i, i ^ bit) for i in range(lax.axis_size(axis))])


def together(*values):
    return lax.optimization_barrier(values)


def after(value, *others):
    return lax.optimization_barrier((value, *others))[0]


def small_call(kernel, place, arrays, shapes, scratch=(), effort=20, name="small"):
    vmem = pl.BlockSpec(memory_space=pltpu.VMEM)
    return pl.pallas_call(
        kernel,
        out_shape=tuple(jax.ShapeDtypeStruct(dims, dtype) for dims, dtype in shapes),
        in_specs=[pl.BlockSpec(memory_space=pltpu.SMEM)] + [vmem] * len(arrays),
        out_specs=(vmem,) * len(shapes),
        scratch_shapes=list(scratch),
        cost_estimate=cost(effort * 10**9),
        name=name,
    )(place, *arrays)


ME, CORE, X, Y, Z = range(5)


def tokens_of_group(values):
    across = swap(values, "var", 2)
    return values, swap(values, "var", 1), across, swap(across, "var", 1)


def copies_of_group(values):
    return (values,) + tuple(swap(values, "var", bit) for bit in (1, 2, 3))


def slices_of_group(pieces):
    return (pieces[0],) + tuple(swap(pieces[bit], "var", bit) for bit in (1, 2, 3))


def z_pieces(place, near, got):
    _, rows, cols = near.shape

    def kernel(place_ref, near_ref, got_ref, *outs):
        for bit in range(4):
            block = place_ref[Z] ^ bit
            outs[bit][...] = (near_ref[block].astype(F32) + got_ref[block].astype(F32)).astype(BF16)

    return small_call(kernel, place, (near, got), [((rows, cols), BF16)] * 4, name="z_pieces")


def z_exchange(pieces):
    return (pieces[0],) + tuple(swap(pieces[bit], "patch", 2 * bit) for bit in (1, 2, 3))


def z_sum(place, arrays):

    def kernel(place_ref, first, second, third, fourth, out):
        total = first[...].astype(F32) + second[...].astype(F32) + third[...].astype(F32) + fourth[...].astype(F32)
        out[...] = total.astype(BF16)

    return small_call(kernel, place, arrays, [(arrays[0].shape, BF16)], name="z_sum")[0]


def pair_sum(place, near, gots):
    def kernel(place_ref, near_ref, *refs):
        for k in range(2):
            got = refs[0][k] if len(refs) == 2 else refs[k][0]
            refs[-1][k] = (near_ref[k].astype(F32) + got.astype(F32)).astype(BF16)

    return small_call(kernel, place, (near, *gots), [(near.shape, BF16)], name="pair_sum")[0]


def z_first_sum(place, near, gots, far):
    def kernel(place_ref, near_ref, *refs):
        gots, (far_ref, stay, away) = refs[:-3], refs[-3:]
        for out, k in ((away, 1), (stay, 0)):
            got = gots[0][k] if len(gots) == 1 else gots[k][0]
            out[...] = (near_ref[k].astype(F32) + got.astype(F32) + far_ref[k].astype(F32)).astype(BF16)

    return small_call(kernel, place, (near, *gots, far), [(near.shape[1:], BF16)] * 2, name="z_first_sum")


def z_last_sum(place, near, got):
    def kernel(place_ref, near_ref, got_ref, out):
        out[...] = (near_ref[...].astype(F32) + got_ref[...].astype(F32)).astype(BF16)

    return small_call(kernel, place, (near, got), [(near.shape, BF16)], name="z_last_sum")[0]


def gather_over_var(own):
    across = swap(own, "var", 2)
    return own, swap(own, "var", 1), across, swap(across, "var", 1)


def join(place, pieces, widths, stacked):
    rows = pieces[0].shape[0]

    def kernel(place_ref, *refs):
        start = 0
        for k, (out, size) in enumerate(zip(refs[4:], widths)):
            for s in range(4):
                v = place_ref[ME] ^ s
                values = refs[s][:, start : start + size].astype(F32)
                if k < stacked:
                    out[v] = values
                else:
                    out[:, pl.ds(pl.multiple_of(v * size, size), size)] = values
            start += size

    shapes = [((4, rows, size) if k < stacked else (rows, 4 * size), F32) for k, size in enumerate(widths)]
    return small_call(kernel, place, pieces, shapes, name="join")


def sum_over_all(place, stay, away, hooks):
    _, rows, cols = stay.shape
    half = rows // 2
    size = half // 4
    hooks = iter(hooks)

    def core_kernel(place_ref, stay_ref, got_ref, stay_out, away_out):
        for out, which in ((away_out, 1 - place_ref[X]), (stay_out, place_ref[X])):
            out[...] = (stay_ref[which].astype(F32) + got_ref[which].astype(F32)).astype(BF16)

    got = next(hooks)(swap(away, "var", 1))
    stay, away = small_call(core_kernel, place, (stay, got), [((rows, cols), BF16)] * 2, name="core_sum")

    def x_kernel(place_ref, stay_ref, got_ref, stay_out, away_out):
        for out, which in ((away_out, 1 - place_ref[Y]), (stay_out, place_ref[Y])):
            out[...] = (stay_ref[which].astype(F32) + got_ref[which].astype(F32)).astype(BF16)

    got = next(hooks)(swap(away, "var", 2))
    halves = (2, half, cols)
    stay, away = small_call(
        x_kernel, place, (stay.reshape(halves), got.reshape(halves)), [((half, cols), BF16)] * 2, name="x_sum"
    )
    got = next(hooks)(swap(away, "patch", 1))
    pieces = z_exchange(z_pieces(place, stay.reshape(4, size, cols), got.reshape(4, size, cols)))
    kept = z_sum(place, next(hooks)(pieces))

    def z_kernel(place_ref, *refs):
        for s in range(4):
            refs[4][place_ref[Z] ^ s] = refs[s][...]

    arrays = (kept,) + tuple(swap(kept, "patch", 2 * bit) for bit in (1, 2, 3))
    own = small_call(z_kernel, place, next(hooks)(arrays), [((4, size, cols), BF16)], name="z_join")[0]

    def y_kernel(place_ref, own_ref, other_ref, out):
        out[place_ref[Y]] = own_ref[...]
        out[1 - place_ref[Y]] = other_ref[...]

    own = own.reshape(half, cols)
    arrays = (own, next(hooks)(swap(own, "patch", 1)))
    full = small_call(y_kernel, place, arrays, [(halves, BF16)], name="y_join")[0].reshape(rows, cols)

    return gather_over_var(full)


def middle_kernel(
    place_ref,
    att_ref,
    front_ref,
    valid_ref,
    og_ref,
    tout_ref,
    gain_ref,
    win_ref,
    wout_ref,
    block_ref,
    late_ref,
    *refs,
):
    actives, middles = refs[0:4], refs[4:8]
    grad_ref, after_ref, gain_grad_ref, residual_ref, unit_ref, rate_ref, acc_ref, back_ref, wide_ref, branch_ref = refs[8:]
    step = pl.program_id(0)
    seg, width = front_ref.shape
    parts = att_ref.shape[0]
    own = width // parts
    me = place_ref[0]
    slot = actives[0].shape[1] // pl.num_programs(0)

    @pl.when(step == 0)
    def _():
        for p in range(parts):
            branch_ref[:, p * own : (p + 1) * own] = att_ref[p]
        after = front_ref[...] + mm(branch_ref[...], tout_ref[...])
        residual_ref[...] = after
        center = after - jnp.mean(after, axis=1, keepdims=True)
        rate = lax.rsqrt(jnp.mean(center * center, axis=1, keepdims=True) + EPSILON)
        unit = center * rate
        unit_ref[...] = unit
        rate_ref[...] = rate
        late_ref[...] = (unit * gain_ref[...]).astype(BF16)
        acc_ref[...] = jnp.zeros_like(acc_ref)
        back_ref[...] = jnp.zeros_like(back_ref)

    inner = mm(late_ref[...], win_ref[...])
    cumulative = 0.5 * (1.0 + lax.erf(inner * math.sqrt(0.5)))
    active = (inner * cumulative).astype(BF16)
    acc_ref[...] += mm(active, wout_ref[...])
    slope = cumulative + inner * (jnp.exp(-0.5 * inner * inner) * (1.0 / math.sqrt(2.0 * math.pi)))
    inner_grad = (mm(og_ref[...], wout_ref[...], NT) * slope).astype(BF16)
    back_ref[...] += mm(inner_grad, win_ref[...], NT)
    wide_ref[...] = active
    cols = pl.ds(pl.multiple_of(step * slot, slot), slot)
    for s in range(4):
        actives[s][:, cols] = wide_ref[:, pl.ds(pl.multiple_of((me ^ s) * slot, slot), slot)]
    block = inner_grad.shape[1]
    owner = step * block // width
    place = pl.ds(pl.multiple_of(step * block - owner * width, block), block)
    for s in range(4):

        @pl.when((me ^ s) == owner)
        def _(s=s):
            middles[s][:, place] = inner_grad

    @pl.when(step == pl.num_programs(0) - 1)
    def _():
        valid = valid_ref[...]
        block_ref[...] = ((residual_ref[...] + acc_ref[...]) * valid).astype(BF16)
        unit = unit_ref[...]
        back = back_ref[...]
        gain_grad_ref[...] = jnp.sum(back * unit, axis=0, keepdims=True)
        scaled = back * gain_ref[...]
        inside = jnp.mean(scaled * unit, axis=1, keepdims=True)
        total = rate_ref[...] * (scaled - jnp.mean(scaled, axis=1, keepdims=True) - unit * inside)
        total = og_ref[...].astype(F32) + total
        after_ref[...] = total
        branch_ref[...] = total.astype(BF16)
        quarter = width // 4
        for s in range(4):
            start = pl.multiple_of((me ^ s) * quarter, quarter)
            middles[s][:, width : width + quarter] = branch_ref[:, pl.ds(start, quarter)]
        turned = mm(branch_ref[...], tout_ref[...], NT).astype(BF16)
        for p in range(parts):
            grad_ref[p] = turned[:, p * own : (p + 1) * own]


def middle(place, attended, front_out, valid, out_grad, trunk_out, gain, mlp_in, mlp_out):
    seg, width = front_out.shape
    hidden = mlp_in.shape[1]
    parts = attended.shape[0]
    block = hidden // parts
    shape = jax.ShapeDtypeStruct

    def still(*dims):
        return pl.BlockSpec(dims, lambda i: (0,) * len(dims))

    piece, wider = shape((seg, hidden // 4), BF16), shape((seg, width + width // 4), BF16)
    return pl.pallas_call(
        middle_kernel,
        grid=(parts,),
        out_shape=(
            shape((seg, width), BF16),
            shape((seg, width), BF16),
            *((piece,) * 4),
            *((wider,) * 4),
            shape(attended.shape, BF16),
            shape((seg, width), F32),
            shape((1, width), F32),
        ),
        in_specs=[
            pl.BlockSpec(memory_space=pltpu.SMEM),
            still(*attended.shape),
            still(seg, width),
            still(seg, 1),
            still(seg, width),
            still(width, width),
            still(1, width),
            pl.BlockSpec((width, block), lambda i: (0, i)),
            pl.BlockSpec((block, width), lambda i: (i, 0)),
        ],
        out_specs=(
            still(seg, width),
            still(seg, width),
            *((still(*piece.shape),) * 4),
            *((still(*wider.shape),) * 4),
            still(*attended.shape),
            still(seg, width),
            still(1, width),
        ),
        scratch_shapes=[
            pltpu.VMEM((seg, width), F32),
            pltpu.VMEM((seg, width), F32),
            pltpu.VMEM((seg, 1), F32),
            pltpu.VMEM((seg, width), F32),
            pltpu.VMEM((seg, width), F32),
            pltpu.VMEM((seg, block), BF16),
            pltpu.VMEM((seg, width), BF16),
        ],
        compiler_params=pltpu.CompilerParams(dimension_semantics=("arbitrary",)),
        cost_estimate=cost(60 * 10**9),
        name="trunk_middle",
    )(place, attended, front_out, valid, out_grad, trunk_out, gain, mlp_in, mlp_out)


def trunk_back_kernel(
    place_ref, grads_ref, front_ref, gain_ref, after_ref, valid_ref, aout_ref, wqkv_ref, mixed_ref, gain_grad_ref, *rest
):
    pieces, triple_ref, back_ref, wide_ref = rest[:4], rest[4], rest[5], rest[6]
    step = pl.program_id(0)
    parts = grads_ref.shape[0]
    seg, width = front_ref.shape
    own = width // parts
    me = place_ref[ME]

    @pl.when(step == 0)
    def _():
        for c in range(3):
            for p in range(parts):
                triple_ref[c, :, p * own : (p + 1) * own] = grads_ref[p, c * seg : (c + 1) * seg, :]
        back_ref[...] = jnp.zeros_like(back_ref)

    back_ref[...] += mm(triple_ref[step], wqkv_ref[...], NT)

    @pl.when(step == pl.num_programs(0) - 1)
    def _():
        front = front_ref[...]
        center = front - jnp.mean(front, axis=1, keepdims=True)
        rate = lax.rsqrt(jnp.mean(center * center, axis=1, keepdims=True) + EPSILON)
        unit = center * rate
        back = back_ref[...]
        gain_grad_ref[...] = jnp.sum(back * unit, axis=0, keepdims=True)
        scaled = back * gain_ref[...]
        inside = jnp.mean(scaled * unit, axis=1, keepdims=True)
        total = rate * (scaled - jnp.mean(scaled, axis=1, keepdims=True) - unit * inside)
        total = ((after_ref[...] + total) * valid_ref[...]).astype(BF16)
        mixed_ref[...] = mm(total, aout_ref[...], NT).astype(BF16)
        wide_ref[...] = total
        part = width // 4
        for s in range(4):
            v = me ^ s
            pieces[s][:, 3 * part :] = wide_ref[:, pl.ds(pl.multiple_of(v * part, part), part)]
            for k in range(3):
                block = 3 * v + k
                cols = pl.ds(pl.multiple_of(block % 4 * part, part), part)
                pieces[s][:, k * part : (k + 1) * part] = triple_ref[block // 4, :, cols]


def trunk_back(place, grads, front_out, gain, after_grad, valid, agg_out, trunk_qkv):
    seg, width = front_out.shape
    shape = jax.ShapeDtypeStruct

    def still(*dims):
        return pl.BlockSpec(dims, lambda i: (0,) * len(dims))

    piece = shape((seg, width), BF16)
    return pl.pallas_call(
        trunk_back_kernel,
        grid=(3,),
        out_shape=(piece, shape((1, width), F32), *((piece,) * 4)),
        in_specs=[
            pl.BlockSpec(memory_space=pltpu.SMEM),
            still(*grads.shape),
            still(seg, width),
            still(1, width),
            still(seg, width),
            still(seg, 1),
            still(width, width),
            pl.BlockSpec((width, width), lambda i: (0, i)),
        ],
        out_specs=(still(seg, width), still(1, width), *((still(seg, width),) * 4)),
        scratch_shapes=[
            pltpu.VMEM((3, seg, width), BF16),
            pltpu.VMEM((seg, width), F32),
            pltpu.VMEM((seg, width), BF16),
        ],
        compiler_params=pltpu.CompilerParams(dimension_semantics=("arbitrary",)),
        cost_estimate=cost(80 * 10**9),
        name="trunk_back",
    )(place, grads, front_out, gain, after_grad, valid, agg_out, trunk_qkv)


def front_last_kernel(
    pixels,
    place_ref,
    m0,
    m1,
    m2,
    m3,
    weight_ref,
    embed_ref,
    weight_own_ref,
    embed_own_ref,
    value_rows_ref,
    key_query_ref,
    key_ref,
    aggq_ref,
    query_rows_ref,
    query_own_ref,
    value_out,
    patch_out,
    embed_out,
    key_out,
    query_out,
    agg_query_out,
    norm_one_out,
    norm_two_out,
    m_ref,
    sum_ref,
):
    rows, width = weight_ref.shape
    own = weight_own_ref.shape[1]
    size = m0.shape[1]
    head_dim = width // HEADS
    scaling = 1.0 / math.sqrt(head_dim)
    for s, ref in enumerate((m0, m1, m2, m3)):
        v = place_ref[ME] ^ s
        m_ref[:, pl.ds(pl.multiple_of((v % 2 * 2 + v // 2) * size, size), size)] = ref[...]
    m_sum, me_sum = m_ref[0:rows, :], m_ref[rows : rows + VARS, :]
    value_out[...] = mm(weight_own_ref[...], m_sum, TN) + mm(embed_own_ref[...], me_sum, TN)
    s_all = m_ref[rows + VARS : rows + VARS + HEADS, :]
    twice = jnp.concatenate([s_all, s_all], axis=0)
    patch_out[...] = mm(m_sum, value_rows_ref[...], NT) + mm(twice[:, 0:rows], key_query_ref[...], TN)
    embed_out[...] = mm(me_sum, value_rows_ref[...], NT) + mm(
        twice[:, rows : rows + VARS], key_query_ref[...], TN
    )
    key_sum = (mm(s_all[:, 0:rows], weight_ref[...]) + mm(s_all[:, rows : rows + VARS], embed_ref[...])) * scaling
    sum_ref[...] = key_sum
    lane = lax.broadcasted_iota(jnp.int32, (HEADS, width), 1) // head_dim
    mine = lane == lax.broadcasted_iota(jnp.int32, (HEADS, width), 0)
    start = pl.multiple_of((place_ref[Z] * 2 + place_ref[Y]) * own, own)
    head_rows = jnp.where(mine, aggq_ref[...], 0.0)
    key_out[...] = mm(sum_ref[:, pl.ds(start, own)], head_rows, TN, precision=HIGHEST)
    crossed = mm(jnp.concatenate(split_high_low(key_sum), axis=0), key_ref[...])
    crossed = crossed[0:HEADS, :] + crossed[HEADS:, :]
    aggq_grad = jnp.sum(jnp.where(mine, crossed, 0.0), axis=0, keepdims=True)
    query_out[...] = query_own_ref[...] * aggq_grad
    high, low = split_high_low(aggq_grad)
    agg_query_out[...] = mm(high, query_rows_ref[...], NT) + mm(low, query_rows_ref[...], NT)
    row = lax.broadcasted_iota(jnp.int32, (HEADS, own), 0)
    tail = s_all[:, width - own :].astype(F32)
    for k in range(own // head_dim):
        line = jnp.sum(jnp.where(row == start // head_dim + k, tail, 0.0), axis=0, keepdims=True)
        norm_one_out[:, k * head_dim : (k + 1) * head_dim] = line[:, 0:head_dim]
        norm_two_out[:, k * head_dim : (k + 1) * head_dim] = line[:, head_dim:own]


def front_last(place, pieces, arrays):
    weight_rows, own_weight, value_rows = arrays[0], arrays[2], arrays[4]
    rows, width = weight_rows.shape
    own = own_weight.shape[1]
    tall = pieces[0].shape[0]
    shapes = [((own, width), F32), ((rows, own), F32), ((VARS, own), F32)] + [((own, width), F32)] * 2
    shapes += [((1, own), F32)] * 3
    return small_call(
        functools.partial(front_last_kernel, rows // VARS),
        place,
        (*pieces, *arrays),
        shapes,
        scratch=[pltpu.VMEM((tall, width), BF16), pltpu.VMEM((HEADS, width), F32)],
        name="front_last",
    )


def local(
    input_field,
    counts,
    var_ids,
    patch_weight,
    var_embed,
    agg_query,
    query_proj,
    key_proj,
    value_proj,
    agg_out,
    norm_one,
    trunk_qkv,
    trunk_out,
    norm_two,
    mlp_in,
    mlp_out,
    cotangent,
):
    patches, group = lax.axis_size("patch"), lax.axis_size("var")
    fast = (patches, group) == (8, 4)
    me, spot = lax.axis_index("var"), lax.axis_index("patch")
    place = jnp.stack([me, me % 2, me // 2, spot % 2, spot // 2]).astype(jnp.int32)
    var_index = lax.axis_index("var")
    patch_index = lax.axis_index("patch")
    all_rows, seg, var_local, pixels = input_field.shape
    width = agg_out.shape[0]
    head_dim = width // HEADS
    hidden = mlp_in.shape[1]
    scaling = 1.0 / math.sqrt(head_dim)

    turned = input_field.transpose(0, 2, 3, 1).reshape(all_rows, var_local * pixels, seg)
    own_field = lax.all_to_all(turned, "var", split_axis=0, concat_axis=1, tiled=True)
    own_field = own_field.reshape(VARS * pixels, seg)
    own_ids = lax.dynamic_slice_in_dim(var_ids, var_index, 1, 0)
    own_count = lax.dynamic_slice_in_dim(counts, var_index, 1, 0)
    positions = patch_index * seg + jnp.arange(seg, dtype=jnp.int32)
    valid_rows = (positions < own_count).astype(F32)[:, None]
    out_grad = cotangent.reshape(seg, width).astype(F32) * valid_rows
    out_grad_low = out_grad.astype(BF16)

    weight_rows = patch_weight.reshape(VARS * pixels, width)
    agg_q = mm(agg_query[None], query_proj)[0]
    in_head = jnp.arange(width, dtype=jnp.int32)[:, None] // head_dim == jnp.arange(HEADS)[None, :]
    head_query = jnp.where(in_head, agg_q[:, None] * scaling, 0.0)
    key_query = mm(key_proj, jnp.concatenate(split_high_low(head_query), axis=1))
    key_query = key_query[:, :HEADS] + key_query[:, HEADS:]
    key_query_parts = jnp.concatenate(split_high_low(key_query), axis=1)
    score_weight = mm(key_query_parts, weight_rows, (((0,), (1,)), ((), ())))
    score_weight = score_weight[:HEADS] + score_weight[HEADS:]
    score_embed = mm(key_query_parts, var_embed, (((0,), (1,)), ((), ())))
    score_embed = (score_embed[:HEADS] + score_embed[HEADS:]).reshape(HEADS * VARS, 1)
    same_var = (jnp.arange(VARS)[:, None] == jnp.arange(VARS * pixels)[None, :] // pixels)[None]
    spread = jnp.where(same_var, score_weight[:, None, :], 0.0).astype(BF16)
    spread = spread.reshape(HEADS * VARS, VARS * pixels)
    vw = mm(weight_rows, value_proj).astype(BF16)
    ve = mm(var_embed, value_proj).astype(BF16)
    vwt = mm(value_proj, weight_rows, (((0,), (1,)), ((), ()))).astype(BF16)
    vet = mm(value_proj, var_embed, (((0,), (1,)), ((), ()))).astype(BF16)

    own_width = width // patches
    start = patch_index * own_width

    def own_cols(values):
        return lax.dynamic_slice_in_dim(values, start, own_width, 1)

    def own_rows(values):
        return lax.dynamic_slice_in_dim(values, start, own_width, 0)

    value_rows = own_rows(value_proj)
    key_query_rows = own_rows(key_query)
    own_query = lax.dynamic_slice_in_dim(agg_query, start, own_width, 0).astype(F32)[:, None]
    if fast:
        arrays = (
            weight_rows,
            var_embed,
            own_cols(weight_rows),
            own_cols(var_embed),
            value_rows,
            jnp.concatenate(split_high_low(key_query_rows), axis=1).T,
            key_proj,
            agg_q[None],
            own_rows(query_proj),
            own_query,
        )

    x_own, shares, mixed_low = front_forward(own_ids, own_field, spread, score_embed, vwt, vet)

    front_out = mm(mixed_low, agg_out) * valid_rows
    normed_one, norm_one_pull = jax.vjp(layer_norm, front_out, norm_one.astype(F32))
    normed_one_low = normed_one.astype(BF16)
    triple = mm(normed_one_low, trunk_qkv).astype(BF16)
    part = width // group
    quarter = hidden // group
    zs = patches // 2
    if fast:
        early = tokens_of_group(jnp.concatenate([out_grad_low, mixed_low, normed_one_low], axis=1))
        qkv, vw, ve, *arrays = together(queries_to_heads(triple), vw, ve, *arrays)
        count = own_count.reshape(1, 1)
        heads, lse = attend_forward(count, qkv, head_dim)
        attended = to_heads(heads.reshape(patches, seg, own_width))
        results = middle(
            place,
            attended,
            front_out,
            valid_rows,
            out_grad_low,
            trunk_out,
            norm_two.astype(F32)[None],
            mlp_in,
            mlp_out,
        )
        attended_group = copies_of_group(attended)
        results = together(*results, *attended_group, *early)
        attended_group, early = results[13:17], results[17:]
        block_out, normed_two_low, grads, after_grad, norm_two_grad = (results[k] for k in (0, 1, 10, 11, 12))
        block_out = block_out[None]
        grads = to_heads(grads)
        active_group, middle_group = slices_of_group(results[2:6]), results[6:10]
        across = swap(normed_two_low, "var", 2)
        result = attend_backward(count, qkv, grads.reshape(patches * seg, own_width), lse, head_dim)
        result, across, *rest = together(result, across, *active_group, *middle_group)
        active_group, middle_group = rest[:4], slices_of_group(rest[4:])
        normed_group = (normed_two_low, swap(normed_two_low, "var", 1), across, swap(across, "var", 1))
        result = to_heads(result)
        pairs = ((1, 3), (0, 2))
        jobs = ((0, 0, 1, 0, width), (2, 0, 4, 0, quarter), (3, 0, 4, quarter, part))
        groups = (active_group, early, normed_group, attended_group, middle_group)
        near, away = weight_grads(place, jobs, groups, own_width, pairs, pairs)
        result = after(result, *near)
        mlp = {"near": near, "away": away}
        mixed_grad, norm_one_grad, *pieces = trunk_back(
            place, result, front_out, norm_one.astype(F32)[None], after_grad, valid_rows, agg_out, trunk_qkv
        )
        mixed_grad, *pieces = together(mixed_grad, *pieces)
        last_group = slices_of_group(pieces)
    else:
        attended, attention_pull = gathered_attention(triple, own_count, head_dim)
        after_attn = front_out + mm(attended, trunk_out)
        normed_two, norm_two_pull = jax.vjp(layer_norm, after_attn, norm_two.astype(F32))
        normed_two_low = normed_two.astype(BF16)
        inner = mm(normed_two_low, mlp_in)
        active, gelu_pull = jax.vjp(gelu_exact, inner)
        active_low = active.astype(BF16)
        result = after_attn + mm(active_low, mlp_out)
        block_out = (result * valid_rows).astype(BF16)[None]
        inner_grad = gelu_pull(mm(out_grad_low, mlp_out, NT))[0].astype(BF16)
        normed_two_grad = mm(inner_grad, mlp_in, NT)
        after_ln_grad, norm_two_grad = norm_two_pull(normed_two_grad)
        after_grad = out_grad + after_ln_grad
        branch_low = after_grad.astype(BF16)
        triple_grad = attention_pull(mm(branch_low, trunk_out, NT).astype(BF16))
        normed_one_grad = mm(triple_grad, trunk_qkv, NT)
        front_ln_grad, norm_one_grad = norm_one_pull(normed_one_grad)
        agg_grad = ((after_grad + front_ln_grad) * valid_rows).astype(BF16)
        mixed_grad = mm(agg_grad, agg_out, NT).astype(BF16)
        norm_one_grad, norm_two_grad = norm_one_grad[None], norm_two_grad[None]

    field_low, *m_parts = front_backward(
        fast, place, own_ids, x_own, shares, mixed_grad, vw, ve, spread, norm_one_grad, norm_two_grad
    )

    field_low = field_low.reshape(group, var_local * pixels, seg)
    field_grad = lax.all_to_all(field_low, "var", split_axis=0, concat_axis=0, tiled=True)

    if fast:
        got = swap(mlp["away"][0], "patch", 1)
        m_stay, m_away, got = together(*m_parts, got)
        m_parts = (m_stay, m_away)
        mlp["far"] = pair_sum(place, mlp["near"][0], (got,))
        last = {}

        def core_done(values):
            return after(values, mlp["far"], *last_group)

        def x_done(values):
            jobs = ((0, 2 * width, 1, 0, 3 * part), (0, width, 1, 3 * part, part))
            last["near"], last["away"] = weight_grads(place, jobs, (early, last_group), own_width, pairs, pairs)
            values, mlp["got"], *_ = together(values, swap(mlp["away"][1], "patch", 1), *last["near"])
            return values

        def y_done(values):
            got, far = swap(last["away"][0], "patch", 1), swap(mlp["far"], "patch", 2)
            values, got, far, _ = together(values, got, far, field_grad)
            mlp["pair"] = z_first_sum(place, mlp["near"][1], (mlp["got"],), far)
            last["far"] = pair_sum(place, last["near"][0], (got,))
            return values

        def z_done(values):
            got = swap(last["away"][1], "patch", 1)
            rest = together(*values, got, last["far"], *mlp["pair"])
            last["got"] = rest[4]
            return rest[:4]

        def b_done(values):
            near, away = mlp["pair"]
            *values, got, far = together(*values, swap(away, "patch", 4), swap(last["far"], "patch", 2))
            mlp["own"] = z_last_sum(place, near, got)
            last["pair"] = z_first_sum(place, last["near"][1], (last["got"],), far)
            return values

        def y_back(values):
            near, away = last["pair"]
            values, got, mlp["across"] = together(values, swap(away, "patch", 4), swap(mlp["own"], "var", 2))
            last["own"] = z_last_sum(place, near, got)
            return values

        m_pieces = sum_over_all(place, *m_parts, (core_done, x_done, y_done, z_done, b_done, y_back))
        own, across = mlp["own"], mlp["across"]
        parts = (own, swap(own, "var", 1), across, swap(across, "var", 1))
        mlp_out_grad, mlp_in_grad, trunk_out_grad = join(place, parts, (width, quarter, part), 1)
        mlp_out_grad = mlp_out_grad.reshape(hidden // patches, width)
        trunk_qkv_grad, agg_out_grad = join(place, gather_over_var(last["own"]), (3 * part, part), 0)
    else:

        def slices(values):
            values = values.reshape(seg, group, values.shape[1] // group).transpose(1, 0, 2)
            return lax.all_to_all(values, "var", split_axis=0, concat_axis=0, tiled=True)

        def everyone(values):
            return lax.all_gather(values, "var", axis=0, tiled=True)

        def total(left, right):
            value = mm(left.reshape(-1, left.shape[-1]), right.reshape(-1, right.shape[-1]), TN).astype(BF16)
            value = lax.psum_scatter(value, "patch", scatter_dimension=0, tiled=True)
            return lax.all_gather(value, "var", axis=0)

        def joined(value):
            return value.transpose(1, 0, 2).reshape(value.shape[1], -1).astype(F32)

        size = hidden // (patches * group)
        active_rows = active_low.reshape(seg, patches, group, size).transpose(0, 2, 1, 3).reshape(seg, hidden)
        mlp_out_grad = total(slices(active_rows), everyone(out_grad_low)).reshape(hidden // patches, width).astype(F32)
        mlp_in_grad = joined(total(everyone(normed_two_low), slices(inner_grad)))
        trunk_out_grad = joined(total(everyone(attended), slices(branch_low)))
        trunk_qkv_grad = joined(total(everyone(normed_one_low), slices(triple_grad)))
        agg_out_grad = joined(total(everyone(mixed_low), slices(agg_grad)))
        m_all = lax.psum(m_parts[0], ("patch", "var")).transpose(1, 0, 2).reshape(-1, width)
    if fast:
        value_proj_grad, patch_grad, embed_grad, key_proj_grad, query_proj_grad, *lines = front_last(
            place, m_pieces, arrays
        )
        agg_query_grad, norm_one_grad, norm_two_grad = (line[0] for line in lines)
    else:
        m_sum, me_sum = m_all[: VARS * pixels], m_all[VARS * pixels : VARS * pixels + VARS]
        s_rows = m_all[VARS * pixels + VARS :].astype(F32)
        s_all = s_rows[:, : VARS * pixels]
        se_all = s_rows[:, VARS * pixels : VARS * pixels + VARS]
        norm_sums = s_rows[:, width - 2 * head_dim :]
        value_proj_grad = mm(own_cols(weight_rows), m_sum, TN) + mm(own_cols(var_embed), me_sum, TN)
        patch_grad = mm(m_sum, value_rows, NT) + mm(
            s_all, key_query_rows, (((0,), (1,)), ((), ())), precision=HIGHEST
        )
        embed_grad = mm(me_sum, value_rows, NT) + mm(
            se_all, key_query_rows, (((0,), (1,)), ((), ())), precision=HIGHEST
        )
        key_sum = (mm(s_all.astype(BF16), weight_rows) + mm(se_all.astype(BF16), var_embed)) * scaling
        head_rows = jnp.where(in_head.T, agg_q[None, :], 0.0)
        key_proj_grad = mm(own_cols(key_sum), head_rows, TN, precision=HIGHEST)
        crossed = mm(jnp.concatenate(split_high_low(key_sum), axis=0), key_proj)
        crossed = crossed[:HEADS] + crossed[HEADS:]
        aggq_grad = jnp.sum(jnp.where(in_head.T, crossed, 0.0), axis=0)
        query_proj_grad = own_query * aggq_grad[None, :]
        agg_query_grad = jnp.sum(own_rows(query_proj).astype(F32) * aggq_grad[None, :], axis=1)
        norm_one_grad = lax.dynamic_slice_in_dim(norm_sums[:, :head_dim].reshape(width), start, own_width, 0)
        norm_two_grad = lax.dynamic_slice_in_dim(norm_sums[:, head_dim:].reshape(width), start, own_width, 0)
    patch_grad = patch_grad.reshape(VARS, pixels, own_width)
    field_grad = field_grad.reshape(all_rows, var_local, pixels, seg).transpose(0, 3, 1, 2)
    return (
        block_out,
        field_grad,
        patch_grad,
        embed_grad,
        agg_query_grad,
        query_proj_grad,
        key_proj_grad,
        value_proj_grad,
        agg_out_grad,
        norm_one_grad,
        trunk_qkv_grad,
        trunk_out_grad,
        norm_two_grad,
        mlp_in_grad,
        mlp_out_grad,
    )


def solution(mesh):
    whole = P()
    placed = (P(None, "patch", "var", None),) + (whole,) * 15 + (P("var", "patch", None),)
    rows = P("patch", None)
    return jax.shard_map(
        local,
        mesh=mesh,
        in_specs=placed,
        out_specs=(
            P("var", "patch", None),
            P(None, "patch", "var", None),
            P(None, None, "patch"),
            P(None, "patch"),
            P("patch"),
            rows,
            rows,
            rows,
            rows,
            P("patch"),
            rows,
            rows,
            P("patch"),
            rows,
            rows,
        ),
        check_vma=False,
    )
```

profile of v0, /device:TPU:1, one launch (start us, length us, event | category | flops | bytes accessed | tf_op | source)
XLA Modules:
  0.0 330.9 jit_solution(2937684107079047952)
XLA Ops:
  0.7 4.4 %all-to-all-start = ((bf16[4,192,128]{2,1,0:T(8,128)(2,1)}), bf16[4,192,128]{2,1,0:T(8,128)(2,1)S(1)}, u32[]{:S(2)}, u32[]{:S(2)}) async-start(bf16[4,192,128]{2,1,0:T(8,128)(2,1)} %bitcast.79), calls=%async_computation | async-start | bytes 393216 | tf_op jit(solution)/shard_map/all_to_all | solution.py:914
  5.9 2.1 fusion.20.aggq_ref
  10.1 3.1 convolution_convert_fusion.2.vwt_ref
  13.7 1.6 constant_dynamic-slice_fusion.3.weight_own_ref
  22.8 1.7 constant_dynamic-slice_fusion.query_rows_ref
  25.2 6.5 %front_forward.1 = (bf16[768,128]{1,0:T(8,128)(2,1)}, f32[768,128]{1,0:T(8,128)}, bf16[128,1024]{1,0:T(8,128)(2,1)}) custom-call(s32[1,48]{1,0:T(1,128)} %constant_dynamic-slice_fusion.4.ids_ref, bf16[768,128]{1,0:T(8,128)(2,1)} %bitcast.80, bf16[768,768]{1,0:T(8,128)(2,1)} %bitcast.68, f32[768,1]{1,0:T(8,128)} %reshape.252.bias_ref, ...), custom_call_target="tpu_custom_call" | custom-call | flops 6000000000 | bytes 1048576 | tf_op jit(solution)/shard_map/front_forward/pallas_call | solution.py:78
  31.7 2.2 fusion.19
  34.3 3.8 %fusion = bf16[16,8,24,128]{3,1,2,0:T(8,128)(2,1)S(1)} fusion(bf16[128,1024]{1,0:T(8,128)(2,1)S(1)} %multiply_convert_fusion, bf16[1024,3072]{1,0:T(8,128)(2,1)} %wqkv_ref.1), kind=kOutput, calls=%fused_computation.4 | convolution fusion | flops 805699584 | bytes 7340032 | tf_op jit(solution)/shard_map/dot_general | solution.py:28
  39.3 6.1 %all-to-all-start.1 = ((bf16[8,384,128]{2,1,0:T(8,128)(2,1)}), bf16[8,384,128]{2,1,0:T(8,128)(2,1)S(1)}, u32[]{:S(2)}, u32[]{:S(2)}) async-start(bf16[8,384,128]{2,1,0:T(8,128)(2,1)} %bitcast.15), calls=%async_computation.1 | async-start | bytes 1572864 | tf_op jit(solution)/shard_map/all_to_all | solution.py:383
  45.4 1.4 bitcast_convert_fusion
  49.1 3.0 convolution_convert_fusion.1.vw_ref
  52.1 1.5 collective-permute-start.4
  53.6 11.8 %all-to-all-done.1.qkv_ref = bf16[8,384,128]{2,1,0:T(8,128)(2,1)S(1)} async-done(((bf16[8,384,128]{2,1,0:T(8,128)(2,1)}), bf16[8,384,128]{2,1,0:T(8,128)(2,1)S(1)}, u32[]{:S(2)}, u32[]{:S(2)}) %all-to-all-start.1) | async-done | bytes 786464 | tf_op jit(solution)/shard_map/all_to_all | solution.py:383
  66.3 10.3 %attend_forward.1 = (bf16[1024,128]{1,0:T(8,128)(2,1)}, f32[2,1024]{1,0:T(2,128)}) custom-call(s32[1,1]{1,0:T(1,128)} %bitcast.5.count_ref, bf16[8,384,128]{2,1,0:T(8,128)(2,1)} %copy-done.9), custom_call_target="tpu_custom_call" | custom-call | flops 10000000000 | bytes 1048576 | tf_op jit(solution)/shard_map/attend_forward/pallas_call | solution.py:257
  76.5 4.0 %all-to-all-start.2 = ((bf16[8,128,128]{2,1,0:T(8,128)(2,1)}), bf16[8,128,128]{2,1,0:T(8,128)(2,1)S(1)}, u32[]{:S(2)}, u32[]{:S(2)}) async-start(bf16[8,128,128]{2,1,0:T(8,128)(2,1)} %bitcast.77), calls=%async_computation.2 | async-start | bytes 524288 | tf_op jit(solution)/shard_map/all_to_all | solution.py:383
  83.9 4.2 %all-to-all-done.2.att_ref.refs_12_ = bf16[8,128,128]{2,1,0:T(8,128)(2,1)S(1)} async-done(((bf16[8,128,128]{2,1,0:T(8,128)(2,1)}), bf16[8,128,128]{2,1,0:T(8,128)(2,1)S(1)}, u32[]{:S(2)}, u32[]{:S(2)}) %all-to-all-start.2) | async-done | bytes 262176 | tf_op jit(solution)/shard_map/all_to_all | solution.py:383
  88.2 2.3 collective-permute-start
  92.1 18.1 %trunk_middle.1 = (bf16[128,1024]{1,0:T(8,128)(2,1)}, bf16[128,1024]{1,0:T(8,128)(2,1)}, bf16[128,1024]{1,0:T(8,128)(2,1)}, bf16[128,1024]{1,0:T(8,128)(2,1)}, b...) custom-call(s32[5]{0:T(128)} %stack.23.place_ref, ...), custom_call_target="tpu_custom_call" | custom-call | flops 60000002048 | bytes 1048576 | tf_op jit(solution)/shard_map/trunk_middle/pallas_call | solution.py:676
  110.3 3.4 %all-to-all-start.3 = ((bf16[8,128,128]{2,1,0:T(8,128)(2,1)}), bf16[8,128,128]{2,1,0:T(8,128)(2,1)S(1)}, u32[]{:S(2)}, u32[]{:S(2)}) async-start(bf16[8,128,128]{2,1,0:T(8,128)(2,1)} %get-tuple-element.167), calls=%async_computation.3 | async-start | bytes 524288 | tf_op jit(solution)/shard_map/all_to_all | solution.py:383
  115.8 1.5 collective-permute-start.9
  117.3 4.3 %all-to-all-done.3 = bf16[8,128,128]{2,1,0:T(8,128)(2,1)S(1)} async-done(((bf16[8,128,128]{2,1,0:T(8,128)(2,1)}), bf16[8,128,128]{2,1,0:T(8,128)(2,1)S(1)}, u32[]{:S(2)}, u32[]{:S(2)}) %all-to-all-start.3) | async-done | bytes 262176 | tf_op jit(solution)/shard_map/all_to_all | solution.py:383
  122.3 11.0 %attend_backward.1 = bf16[8,384,128]{2,1,0:T(8,128)(2,1)} custom-call(s32[1,1]{1,0:T(1,128)} %bitcast.5.count_ref, bf16[8,384,128]{2,1,0:T(8,128)(2,1)} %copy-done.9, bf16[1024,128]{1,0:T(8,128)(2,1)} %bitcast.78, f32[2,1024]{1,0:T(2,128)} %get-tuple-element.168.lse_ref), custom_call_target="tpu_custom_call" | custom-call | flops 49999998976 | bytes 1048576 | tf_op jit(solution)/shard_map/attend_backward/pallas_call | solution.py:325
  133.4 2.0 collective-permute-start.12
  137.6 3.7 %all-to-all-start.4 = ((bf16[8,384,128]{2,1,0:T(8,128)(2,1)}), bf16[8,384,128]{2,1,0:T(8,128)(2,1)S(1)}, u32[]{:S(2)}, u32[]{:S(2)}) async-start(bf16[8,384,128]{2,1,0:T(8,128)(2,1)} %attend_backward.1), calls=%async_computation.4 | async-start | bytes 1572864 | tf_op jit(solution)/shard_map/all_to_all | solution.py:383
  141.4 3.3 collective-permute-done.13.refs_18_
  144.6 7.5 %collective-permute-done.14.refs_19_ = bf16[128,1280]{1,0:T(8,128)(2,1)S(1)} collective-permute-done((bf16[128,1280]{1,0:T(8,128)(2,1)S(1)}, bf16[128,1280]{1,0:T(8,128)(2,1)S(1)}, u32[]{:S(2)}, u32[]{:S(2)}) %collective-permute-start.14) | collective-permute-done | bytes 327712 | tf_op jit(solution)/shard_map/ppermute | solution.py:427
  152.9 7.9 %weight_grads.2 = (bf16[2,128,2304]{2,1,0:T(8,128)(2,1)}, bf16[2,128,2304]{2,1,0:T(8,128)(2,1)}, bf16[2,128,2304]{2,1,0:T(8,128)(2,1)}, bf16[2,128,2304]{2,1,0:T(8,128)(2,1)}) custom-call(s32[5]{0:T(128)} %stack.23.place_ref, bf16[128,1024]{1,0:T(8,128)(2,1)} %get-tuple-element.179.refs_0_, bf16[128,1024]{1,0:T(8,128)(2,1)} %copy-done.49, ...), custom_call_target="tpu_custom_call" | custom-call | flops 40000000000 | bytes 1048576 | tf_op jit(solution)/shard_map/weight_grads/pallas_call | solution.py:440
  163.1 8.7 %trunk_back.1 = (bf16[128,1024]{1,0:T(8,128)(2,1)}, f32[1,1024]{1,0:T(1,128)}, bf16[128,1024]{1,0:T(8,128)(2,1)}, bf16[128,1024]{1,0:T(8,128)(2,1)}, bf16[128,10...) custom-call(s32[5]{0:T(128)} %stack.23.place_ref, bf16[8,384,128]{2,1,0:T(8,128)(2,1)} %copy-done.10, f32[128,1024]{1,0:T(8,128)} %copy-done.2, ...), custom_call_target="tpu_custom_call" | custom-call | flops 80000000000 | bytes 1048576 | tf_op jit(solution)/shard_map/trunk_back/pallas_call | solution.py:774
  174.0 8.9 %front_backward.1 = (bf16[768,128]{1,0:T(8,128)(2,1)}, bf16[2,832,256]{2,1,0:T(8,128)(2,1)}, bf16[2,832,256]{2,1,0:T(8,128)(2,1)}) custom-call(s32[5]{0:T(128)} %stack.23.place_ref, s32[1,48]{1,0:T(1,128)} %constant_dynamic-slice_fusion.4.ids_ref, bf16[768,128]{1,0:T(8,128)(2,1)} %get-tuple-element.165.x_ref, f32[768,128]{1,0:T(8,128)} %get-tuple-element.166.p_ref, ...), custom_call_target="tpu_custom_call" | custom-call | flops 100000000 | bytes 1048576 | tf_op jit(solution)/shard_map/front_backward/pallas_call | solution.py:200
  182.9 5.8 %collective-permute-done.15.refs_0_ = bf16[2,128,2304]{2,1,0:T(8,128)(2,1)S(1)} collective-permute-done((bf16[2,128,2304]{2,1,0:T(8,128)(2,1)}, bf16[2,128,2304]{2,1,0:T(8,128)(2,1)S(1)}, u32[]{:S(2)}, u32[]{:S(2)}) %collective-permute-start.15) | collective-permute-done | bytes 1179680 | tf_op jit(solution)/shard_map/ppermute | solution.py:427
  189.6 2.9 pair_sum.2
  194.3 2.4 core_sum.1
  198.1 4.6 %weight_grads.3 = (bf16[2,128,1024]{2,1,0:T(8,128)(2,1)}, bf16[2,128,1024]{2,1,0:T(8,128)(2,1)}, bf16[2,128,1024]{2,1,0:T(8,128)(2,1)}, bf16[2,128,1024]{2,1,0:T(8,128)(2,1)}) custom-call(s32[5]{0:T(128)} %stack.23.place_ref, bf16[128,3072]{1,0:T(8,128)(2,1)} %copy-done.8, bf16[128,3072]{1,0:T(8,128)(2,1)} %copy-done.26, bf16[128,3072]{1,0:T(8,128)(2,1)} %copy-done.25, ...), custom_call_target="tpu_custom_call" | custom-call | flops 40000000000 | bytes 1048576 | tf_op jit(solution)/shard_map/weight_grads/pallas_call | solution.py:440
  203.2 10.9 %collective-permute-done.21.refs_0_ = bf16[2,128,2304]{2,1,0:T(8,128)(2,1)} collective-permute-done((bf16[2,128,2304]{2,1,0:T(8,128)(2,1)}, bf16[2,128,2304]{2,1,0:T(8,128)(2,1)}, u32[]{:S(2)}, u32[]{:S(2)}) %collective-permute-start.21) | collective-permute-done | bytes 1179680 | tf_op jit(solution)/shard_map/ppermute | solution.py:427
  214.8 2.0 x_sum.1
  217.9 4.6 %all-to-all-start.5 = ((bf16[4,192,128]{2,1,0:T(8,128)(2,1)}), bf16[4,192,128]{2,1,0:T(8,128)(2,1)S(1)}, u32[]{:S(2)}, u32[]{:S(2)}) async-start(bf16[4,192,128]{2,1,0:T(8,128)(2,1)} %bitcast.24), calls=%async_computation.5 | async-start | bytes 393216 | tf_op jit(solution)/shard_map/all_to_all | solution.py:1045
  222.9 4.1 %all-to-all-done.5 = bf16[4,192,128]{2,1,0:T(8,128)(2,1)S(1)} async-done(((bf16[4,192,128]{2,1,0:T(8,128)(2,1)}), bf16[4,192,128]{2,1,0:T(8,128)(2,1)S(1)}, u32[]{:S(2)}, u32[]{:S(2)}) %all-to-all-start.5) | async-done | bytes 196640 | tf_op jit(solution)/shard_map/all_to_all | solution.py:1045
  227.0 2.7 collective-permute-done.22
  230.4 1.7 z_pieces.1
  233.9 1.8 collective-permute-start.27
  235.7 2.1 pair_sum.3
  237.9 3.3 z_first_sum.2
  241.2 1.8 collective-permute-start.33
  243.6 1.5 z_sum.1.refs_0_
  245.3 2.0 collective-permute-start.30
  247.3 1.5 collective-permute-start.31
  248.7 16.2 %collective-permute-done.29.refs_1_ = bf16[104,256]{1,0:T(8,128)(2,1)S(1)} collective-permute-done((bf16[104,256]{1,0:T(8,128)(2,1)}, bf16[104,256]{1,0:T(8,128)(2,1)S(1)}, u32[]{:S(2)}, u32[]{:S(2)}) %collective-permute-start.29) | collective-permute-done | bytes 53280 | tf_op jit(solution)/shard_map/ppermute | solution.py:427
  265.0 8.2 %collective-permute-done.30.refs_2_ = bf16[104,256]{1,0:T(8,128)(2,1)S(1)} collective-permute-done((bf16[104,256]{1,0:T(8,128)(2,1)}, bf16[104,256]{1,0:T(8,128)(2,1)S(1)}, u32[]{:S(2)}, u32[]{:S(2)}) %collective-permute-start.30) | collective-permute-done | bytes 53280 | tf_op jit(solution)/shard_map/ppermute | solution.py:427
  274.0 2.5 z_first_sum.3
  276.5 1.6 collective-permute-start.35
  278.1 2.2 z_last_sum.2.refs_0_
  281.6 1.6 z_join.1
  284.3 4.8 %collective-permute-done.34.other_ref = bf16[416,256]{1,0:T(8,128)(2,1)S(1)} collective-permute-done((bf16[416,256]{1,0:T(8,128)(2,1)}, bf16[416,256]{1,0:T(8,128)(2,1)S(1)}, u32[]{:S(2)}, u32[]{:S(2)}) %collective-permute-start.34) | collective-permute-done | bytes 213024 | tf_op jit(solution)/shard_map/ppermute | solution.py:427
  289.1 1.4 collective-permute-done.35.got_ref
  290.6 4.1 %collective-permute-done.36.refs_2_ = bf16[128,2304]{1,0:T(8,128)(2,1)S(1)} collective-permute-done((bf16[128,2304]{1,0:T(8,128)(2,1)}, bf16[128,2304]{1,0:T(8,128)(2,1)S(1)}, u32[]{:S(2)}, u32[]{:S(2)}) %collective-permute-start.36) | collective-permute-done | bytes 589856 | tf_op jit(solution)/shard_map/ppermute | solution.py:427
  294.6 2.0 z_last_sum.3.refs_0_
  298.0 1.8 y_join.1
  300.1 2.2 collective-permute-start.40
  303.2 4.8 %collective-permute-start.42 = (bf16[128,1024]{1,0:T(8,128)(2,1)}, bf16[128,1024]{1,0:T(8,128)(2,1)}, u32[]{:S(2)}, u32[]{:S(2)}) collective-permute-start(bf16[128,1024]{1,0:T(8,128)(2,1)} %collective-permute-done.41.refs_2_), channel_id=1, source_target_pairs={{0,1},{1,0},{2,3},{3,2},{4,5},{5,4},{6,7},{7,6},{8,9},{9,8},{10,11... | collective-permute-start | bytes 786440 | tf_op jit(solution)/shard_map/ppermute | solution.py:427
  309.3 2.9 collective-permute-done.38.m2
  312.2 2.6 collective-permute-start.39
  314.8 2.6 join.2
  319.1 4.0 %join.3 = (f32[4,128,1024]{2,1,0:T(8,128)}, f32[128,4096]{1,0:T(8,128)}, f32[128,1024]{1,0:T(8,128)}) custom-call(s32[5]{0:T(128)} %stack.23.place_ref, bf16[128,2304]{1,0:T(8,128)(2,1)} %z_last_sum.2.refs_0_, bf16[128,2304]{1,0:T(8,128)(2,1)} %copy-done.30, bf16[128,2304]{1,0:T(8,128)(2,1)} %copy-done.28, bf16[128,2304]{1,0:T(8,128)(2,1)} %copy-done.31), custom_call_target="tpu_custom_call" | custom-call | flops 20000000000 | bytes 1048576 | tf_op jit(solution)/shard_map/join/pallas_call | solution.py:440
  323.9 6.3 %front_last.1 = (f32[128,1024]{1,0:T(8,128)}, f32[768,128]{1,0:T(8,128)}, f32[48,128]{1,0:T(8,128)}, f32[128,1024]{1,0:T(8,128)}, f32[128,1024]{1,0:T(8,128)}, /...) custom-call(s32[5]{0:T(128)} %stack.23.place_ref, bf16[832,256]{1,0:T(8,128)(2,1)} %bitcast.86, ...), custom_call_target="tpu_custom_call" | custom-call | flops 20000000000 | bytes 1048576 | tf_op jit(solution)/shard_map/front_last/pallas_call | solution.py:440
  (241 shorter events, 51.9 us)
Async XLA Ops:
  0.7 23.8 %all-to-all-start = ((bf16[4,192,128]{2,1,0:T(8,128)(2,1)}), bf16[4,192,128]{2,1,0:T(8,128)(2,1)S(1)}, u32[]{:S(2)}, u32[]{:S(2)}) async-start(bf16[4,192,128]{2,1,0:T(8,128)(2,1)} %bitcast.79), calls=%async_computation | async-start | bytes 393216 | tf_op jit(solution)/shard_map/all_to_all | solution.py:914
  39.3 26.1 %all-to-all-start.1 = ((bf16[8,384,128]{2,1,0:T(8,128)(2,1)}), bf16[8,384,128]{2,1,0:T(8,128)(2,1)S(1)}, u32[]{:S(2)}, u32[]{:S(2)}) async-start(bf16[8,384,128]{2,1,0:T(8,128)(2,1)} %bitcast.15), calls=%async_computation.1 | async-start | bytes 1572864 | tf_op jit(solution)/shard_map/all_to_all | solution.py:383
  52.1 31.0 %copy-start.8 = (bf16[128,3072]{1,0:T(8,128)(2,1)}, bf16[128,3072]{1,0:T(8,128)(2,1)S(1)}, u32[]{:S(2)}) copy-start(bf16[128,3072]{1,0:T(8,128)(2,1)S(1)} %pad_maximum_fusion.refs_4_.refs_0_) | copy-start | bytes 2359300
  52.1 31.8 %collective-permute-start.4 = (bf16[128,3072]{1,0:T(8,128)(2,1)S(1)}, bf16[128,3072]{1,0:T(8,128)(2,1)S(1)}, u32[]{:S(2)}, u32[]{:S(2)}) collective-permute-start(bf16[128,3072]{1,0:T(8,128)(2,1)S(1)} %pad_maximum_fusion.refs_4_.refs_0_), channel_id=1, source_target_pairs={{0,2},{1,3},{2,0},{3,1},{4,6},{5,7},{6,4},{7,5},{8,10},{9,11},{10,... | collective-permute-start | bytes 2359304 | tf_op jit(solution)/shard_map/ppermute | solution.py:427
  66.3 14.3 %copy-start.20 = (bf16[1024]{0:T(1024)(128)(2,1)S(1)}, bf16[1024]{0:T(1024)(128)(2,1)}, u32[]{:S(2)}) copy-start(bf16[1024]{0:T(1024)(128)(2,1)} %param.30) | copy-start | bytes 6148
  76.5 11.6 %all-to-all-start.2 = ((bf16[8,128,128]{2,1,0:T(8,128)(2,1)}), bf16[8,128,128]{2,1,0:T(8,128)(2,1)S(1)}, u32[]{:S(2)}, u32[]{:S(2)}) async-start(bf16[8,128,128]{2,1,0:T(8,128)(2,1)} %bitcast.77), calls=%async_computation.2 | async-start | bytes 524288 | tf_op jit(solution)/shard_map/all_to_all | solution.py:383
  83.1 27.1 %collective-permute-start.3 = (bf16[128,3072]{1,0:T(8,128)(2,1)S(1)}, bf16[128,3072]{1,0:T(8,128)(2,1)S(1)}, u32[]{:S(2)}, u32[]{:S(2)}) collective-permute-start(bf16[128,3072]{1,0:T(8,128)(2,1)S(1)} %pad_maximum_fusion.refs_4_.refs_0_), channel_id=1, source_target_pairs={{0,1},{1,0},{2,3},{3,2},{4,5},{5,4},{6,7},{7,6},{8,9},{9,8},{10,11... | collective-permute-start | bytes 2359304 | tf_op jit(solution)/shard_map/ppermute | solution.py:427
  83.9 26.3 %copy-start.25 = (bf16[128,3072]{1,0:T(8,128)(2,1)}, bf16[128,3072]{1,0:T(8,128)(2,1)S(1)}, u32[]{:S(2)}) copy-start(bf16[128,3072]{1,0:T(8,128)(2,1)S(1)} %collective-permute-done.4.refs_6_.refs_2_) | copy-start | bytes 2359300
  83.9 26.3 %collective-permute-start.5 = (bf16[128,3072]{1,0:T(8,128)(2,1)S(1)}, bf16[128,3072]{1,0:T(8,128)(2,1)}, u32[]{:S(2)}, u32[]{:S(2)}) collective-permute-start(bf16[128,3072]{1,0:T(8,128)(2,1)S(1)} %collective-permute-done.4.refs_6_.refs_2_), channel_id=1, source_target_pairs={{0,1},{1,0},{2,3},{3,2},{4,5},{5,4},{6,7},{7,6},{8,9},{9,8},{10,11... | collective-permute-start | bytes 2359304 | tf_op jit(solution)/shard_map/ppermute | solution.py:427
  88.2 22.0 %collective-permute-start = (bf16[8,128,128]{2,1,0:T(8,128)(2,1)S(1)}, bf16[8,128,128]{2,1,0:T(8,128)(2,1)S(1)}, u32[]{:S(2)}, u32[]{:S(2)}) collective-permute-start(bf16[8,128,128]{2,1,0:T(8,128)(2,1)S(1)} %all-to-all-done.2.att_ref.refs_12_), channel_id=1, source_target_pairs={{0,1},{1,0},{2,3},{3,2},{4,5},{5,4},{6,7},{7,6},{8,9},{9,8},{10,11... | collective-permute-start | bytes 786440 | tf_op jit(solution)/shard_map/ppermute | solution.py:427
  90.4 19.8 %collective-permute-start.1 = (bf16[8,128,128]{2,1,0:T(8,128)(2,1)S(1)}, bf16[8,128,128]{2,1,0:T(8,128)(2,1)S(1)}, u32[]{:S(2)}, u32[]{:S(2)}) collective-permute-start(bf16[8,128,128]{2,1,0:T(8,128)(2,1)S(1)} %all-to-all-done.2.att_ref.refs_12_), channel_id=1, source_target_pairs={{0,2},{1,3},{2,0},{3,1},{4,6},{5,7},{6,4},{7,5},{8,10},{9,11},{10,... | collective-permute-start | bytes 786440 | tf_op jit(solution)/shard_map/ppermute | solution.py:427
  91.8 18.5 %collective-permute-start.2 = (bf16[8,128,128]{2,1,0:T(8,128)(2,1)S(1)}, bf16[8,128,128]{2,1,0:T(8,128)(2,1)S(1)}, u32[]{:S(2)}, u32[]{:S(2)}) collective-permute-start(bf16[8,128,128]{2,1,0:T(8,128)(2,1)S(1)} %all-to-all-done.2.att_ref.refs_12_), channel_id=1, source_target_pairs={{0,3},{1,2},{2,1},{3,0},{4,7},{5,6},{6,5},{7,4},{8,11},{9,10},{10,... | collective-permute-start | bytes 786440 | tf_op jit(solution)/shard_map/ppermute | solution.py:427
  110.2 23.1 %copy-start.26 = (bf16[128,3072]{1,0:T(8,128)(2,1)}, bf16[128,3072]{1,0:T(8,128)(2,1)S(1)}, u32[]{:S(2)}) copy-start(bf16[128,3072]{1,0:T(8,128)(2,1)S(1)} %collective-permute-done.3.refs_5_.refs_1_) | copy-start | bytes 2359300
  110.2 23.1 %copy-start.46 = (bf16[8,128,128]{2,1,0:T(8,128)(2,1)}, bf16[8,128,128]{2,1,0:T(8,128)(2,1)S(1)}, u32[]{:S(2)}) copy-start(bf16[8,128,128]{2,1,0:T(8,128)(2,1)S(1)} %collective-permute-done.refs_13_) | copy-start | bytes 786436
  110.2 23.1 %copy-start.47 = (bf16[8,128,128]{2,1,0:T(8,128)(2,1)}, bf16[8,128,128]{2,1,0:T(8,128)(2,1)S(1)}, u32[]{:S(2)}) copy-start(bf16[8,128,128]{2,1,0:T(8,128)(2,1)S(1)} %collective-permute-done.1.refs_14_) | copy-start | bytes 786436
  110.2 23.1 %copy-start.48 = (bf16[8,128,128]{2,1,0:T(8,128)(2,1)}, bf16[8,128,128]{2,1,0:T(8,128)(2,1)S(1)}, u32[]{:S(2)}) copy-start(bf16[8,128,128]{2,1,0:T(8,128)(2,1)S(1)} %collective-permute-done.2.refs_15_) | copy-start | bytes 786436
  110.3 11.3 %all-to-all-start.3 = ((bf16[8,128,128]{2,1,0:T(8,128)(2,1)}), bf16[8,128,128]{2,1,0:T(8,128)(2,1)S(1)}, u32[]{:S(2)}, u32[]{:S(2)}) async-start(bf16[8,128,128]{2,1,0:T(8,128)(2,1)} %get-tuple-element.167), calls=%async_computation.3 | async-start | bytes 524288 | tf_op jit(solution)/shard_map/all_to_all | solution.py:383
  113.7 19.6 %collective-permute-start.6 = (bf16[128,1024]{1,0:T(8,128)(2,1)}, bf16[128,1024]{1,0:T(8,128)(2,1)}, u32[]{:S(2)}, u32[]{:S(2)}) collective-permute-start(bf16[128,1024]{1,0:T(8,128)(2,1)} %get-tuple-element.169.refs_8_), channel_id=1, source_target_pairs={{0,2},{1,3},{2,0},{3,1},{4,6},{5,7},{6,4},{7,5},{8,10},{9,11},{10,... | collective-permute-start | bytes 786440 | tf_op jit(solution)/shard_map/ppermute | solution.py:427
  115.1 18.3 %collective-permute-start.7 = (bf16[128,1024]{1,0:T(8,128)(2,1)}, bf16[128,1024]{1,0:T(8,128)(2,1)S(1)}, u32[]{:S(2)}, u32[]{:S(2)}) collective-permute-start(bf16[128,1024]{1,0:T(8,128)(2,1)} %get-tuple-element.171), channel_id=1, source_target_pairs={{0,1},{1,0},{2,3},{3,2},{4,5},{5,4},{6,7},{7,6},{8,9},{9,8},{10,11... | collective-permute-start | bytes 786440 | tf_op jit(solution)/shard_map/ppermute | solution.py:427
  115.7 17.7 %collective-permute-start.8 = (bf16[128,1024]{1,0:T(8,128)(2,1)}, bf16[128,1024]{1,0:T(8,128)(2,1)S(1)}, u32[]{:S(2)}, u32[]{:S(2)}) collective-permute-start(bf16[128,1024]{1,0:T(8,128)(2,1)} %get-tuple-element.172), channel_id=1, source_target_pairs={{0,2},{1,3},{2,0},{3,1},{4,6},{5,7},{6,4},{7,5},{8,10},{9,11},{10,... | collective-permute-start | bytes 786440 | tf_op jit(solution)/shard_map/ppermute | solution.py:427
  115.8 17.6 %collective-permute-start.9 = (bf16[128,1024]{1,0:T(8,128)(2,1)}, bf16[128,1024]{1,0:T(8,128)(2,1)}, u32[]{:S(2)}, u32[]{:S(2)}) collective-permute-start(bf16[128,1024]{1,0:T(8,128)(2,1)} %get-tuple-element.173), channel_id=1, source_target_pairs={{0,3},{1,2},{2,1},{3,0},{4,7},{5,6},{6,5},{7,4},{8,11},{9,10},{10,... | collective-permute-start | bytes 786440 | tf_op jit(solution)/shard_map/ppermute | solution.py:427
  122.3 13.1 %copy-start.41 = (bf16[128,1280]{1,0:T(8,128)(2,1)S(1)}, bf16[128,1280]{1,0:T(8,128)(2,1)}, u32[]{:S(2)}) copy-start(bf16[128,1280]{1,0:T(8,128)(2,1)} %get-tuple-element.194) | copy-start | bytes 983044
  122.3 14.4 %copy-start.40 = (bf16[128,1280]{1,0:T(8,128)(2,1)S(1)}, bf16[128,1280]{1,0:T(8,128)(2,1)}, u32[]{:S(2)}) copy-start(bf16[128,1280]{1,0:T(8,128)(2,1)} %get-tuple-element.195) | copy-start | bytes 983044
  133.4 8.0 %collective-permute-start.12 = (bf16[128,1280]{1,0:T(8,128)(2,1)S(1)}, bf16[128,1280]{1,0:T(8,128)(2,1)S(1)}, u32[]{:S(2)}, u32[]{:S(2)}) collective-permute-start(bf16[128,1280]{1,0:T(8,128)(2,1)S(1)} %copy-done.42), channel_id=1, source_target_pairs={{0,1},{1,0},{2,3},{3,2},{4,5},{5,4},{6,7},{7,6},{8,9},{9,8},{10,11... | collective-permute-start | bytes 983048 | tf_op jit(solution)/shard_map/ppermute | solution.py:427
  135.4 9.3 %collective-permute-start.13 = (bf16[128,1280]{1,0:T(8,128)(2,1)S(1)}, bf16[128,1280]{1,0:T(8,128)(2,1)S(1)}, u32[]{:S(2)}, u32[]{:S(2)}) collective-permute-start(bf16[128,1280]{1,0:T(8,128)(2,1)S(1)} %copy-done.41), channel_id=1, source_target_pairs={{0,2},{1,3},{2,0},{3,1},{4,6},{5,7},{6,4},{7,5},{8,10},{9,11},{10,... | collective-permute-start | bytes 983048 | tf_op jit(solution)/shard_map/ppermute | solution.py:427
  136.7 15.4 %collective-permute-start.14 = (bf16[128,1280]{1,0:T(8,128)(2,1)S(1)}, bf16[128,1280]{1,0:T(8,128)(2,1)S(1)}, u32[]{:S(2)}, u32[]{:S(2)}) collective-permute-start(bf16[128,1280]{1,0:T(8,128)(2,1)S(1)} %copy-done.40), channel_id=1, source_target_pairs={{0,3},{1,2},{2,1},{3,0},{4,7},{5,6},{6,5},{7,4},{8,11},{9,10},{10,... | collective-permute-start | bytes 983048 | tf_op jit(solution)/shard_map/ppermute | solution.py:427
  137.1 4.2 %collective-permute-start.10 = (bf16[128,1024]{1,0:T(8,128)(2,1)}, bf16[128,1024]{1,0:T(8,128)(2,1)S(1)}, u32[]{:S(2)}, u32[]{:S(2)}) collective-permute-start(bf16[128,1024]{1,0:T(8,128)(2,1)} %get-tuple-element.169.refs_8_), channel_id=1, source_target_pairs={{0,1},{1,0},{2,3},{3,2},{4,5},{5,4},{6,7},{7,6},{8,9},{9,8},{10,11... | collective-permute-start | bytes 786440 | tf_op jit(solution)/shard_map/ppermute | solution.py:427
  137.2 4.1 %collective-permute-start.11 = (bf16[128,1024]{1,0:T(8,128)(2,1)}, bf16[128,1024]{1,0:T(8,128)(2,1)S(1)}, u32[]{:S(2)}, u32[]{:S(2)}) collective-permute-start(bf16[128,1024]{1,0:T(8,128)(2,1)} %collective-permute-done.6.refs_10_), channel_id=1, source_target_pairs={{0,1},{1,0},{2,3},{3,2},{4,5},{5,4},{6,7},{7,6},{8,9},{9,8},{10,11... | collective-permute-start | bytes 786440 | tf_op jit(solution)/shard_map/ppermute | solution.py:427
  137.6 24.6 %all-to-all-start.4 = ((bf16[8,384,128]{2,1,0:T(8,128)(2,1)}), bf16[8,384,128]{2,1,0:T(8,128)(2,1)S(1)}, u32[]{:S(2)}, u32[]{:S(2)}) async-start(bf16[8,384,128]{2,1,0:T(8,128)(2,1)} %attend_backward.1), calls=%async_computation.4 | async-start | bytes 1572864 | tf_op jit(solution)/shard_map/all_to_all | solution.py:383
  160.7 27.9 %collective-permute-start.15 = (bf16[2,128,2304]{2,1,0:T(8,128)(2,1)}, bf16[2,128,2304]{2,1,0:T(8,128)(2,1)S(1)}, u32[]{:S(2)}, u32[]{:S(2)}) collective-permute-start(bf16[2,128,2304]{2,1,0:T(8,128)(2,1)} %get-tuple-element.213), channel_id=1, source_target_pairs={{0,4},{4,0},{8,12},{12,8},{16,20},{20,16},{24,28},{28,24},{1,5},{5... | collective-permute-start | bytes 3538952 | tf_op jit(solution)/shard_map/ppermute | solution.py:427
  161.9 52.2 %collective-permute-start.21 = (bf16[2,128,2304]{2,1,0:T(8,128)(2,1)}, bf16[2,128,2304]{2,1,0:T(8,128)(2,1)}, u32[]{:S(2)}, u32[]{:S(2)}) collective-permute-start(bf16[2,128,2304]{2,1,0:T(8,128)(2,1)} %get-tuple-element.224), channel_id=1, source_target_pairs={{0,4},{4,0},{8,12},{12,8},{16,20},{20,16},{24,28},{28,24},{1,5},{5... | collective-permute-start | bytes 3538952 | tf_op jit(solution)/shard_map/ppermute | solution.py:427
  171.8 20.8 %collective-permute-start.17 = (bf16[128,1024]{1,0:T(8,128)(2,1)}, bf16[128,1024]{1,0:T(8,128)(2,1)S(1)}, u32[]{:S(2)}, u32[]{:S(2)}) collective-permute-start(bf16[128,1024]{1,0:T(8,128)(2,1)} %get-tuple-element.218), channel_id=1, source_target_pairs={{0,1},{1,0},{2,3},{3,2},{4,5},{5,4},{6,7},{7,6},{8,9},{9,8},{10,11... | collective-permute-start | bytes 786440 | tf_op jit(solution)/shard_map/ppermute | solution.py:427
  172.3 21.1 %collective-permute-start.18 = (bf16[128,1024]{1,0:T(8,128)(2,1)}, bf16[128,1024]{1,0:T(8,128)(2,1)S(1)}, u32[]{:S(2)}, u32[]{:S(2)}) collective-permute-start(bf16[128,1024]{1,0:T(8,128)(2,1)} %get-tuple-element.219), channel_id=1, source_target_pairs={{0,2},{1,3},{2,0},{3,1},{4,6},{5,7},{6,4},{7,5},{8,10},{9,11},{10,... | collective-permute-start | bytes 786440 | tf_op jit(solution)/shard_map/ppermute | solution.py:427
  173.6 19.8 %collective-permute-start.19 = (bf16[128,1024]{1,0:T(8,128)(2,1)}, bf16[128,1024]{1,0:T(8,128)(2,1)}, u32[]{:S(2)}, u32[]{:S(2)}) collective-permute-start(bf16[128,1024]{1,0:T(8,128)(2,1)} %get-tuple-element.220), channel_id=1, source_target_pairs={{0,3},{1,2},{2,1},{3,0},{4,7},{5,6},{6,5},{7,4},{8,11},{9,10},{10,... | collective-permute-start | bytes 786440 | tf_op jit(solution)/shard_map/ppermute | solution.py:427
  188.6 4.7 %collective-permute-start.16 = (bf16[2,832,256]{2,1,0:T(8,128)(2,1)}, bf16[2,832,256]{2,1,0:T(8,128)(2,1)S(1)}, u32[]{:S(2)}, u32[]{:S(2)}) collective-permute-start(bf16[2,832,256]{2,1,0:T(8,128)(2,1)} %get-tuple-element.215), channel_id=1, source_target_pairs={{0,1},{1,0},{2,3},{3,2},{4,5},{5,4},{6,7},{7,6},{8,9},{9,8},{10,11... | collective-permute-start | bytes 2555912 | tf_op jit(solution)/shard_map/ppermute | solution.py:427
  192.6 34.4 %collective-permute-start.24 = (bf16[2,128,2304]{2,1,0:T(8,128)(2,1)}, bf16[2,128,2304]{2,1,0:T(8,128)(2,1)S(1)}, u32[]{:S(2)}, u32[]{:S(2)}) collective-permute-start(bf16[2,128,2304]{2,1,0:T(8,128)(2,1)} %pair_sum.2), channel_id=1, source_target_pairs={{0,8},{4,12},{8,0},{12,4},{16,24},{20,28},{24,16},{28,20},{1,9},{5... | collective-permute-start | bytes 3538952 | tf_op jit(solution)/shard_map/ppermute | solution.py:427
  196.7 17.3 %collective-permute-start.20 = (bf16[832,256]{1,0:T(8,128)(2,1)}, bf16[832,256]{1,0:T(8,128)(2,1)S(1)}, u32[]{:S(2)}, u32[]{:S(2)}) collective-permute-start(bf16[832,256]{1,0:T(8,128)(2,1)} %get-tuple-element.223), channel_id=1, source_target_pairs={{0,2},{1,3},{2,0},{3,1},{4,6},{5,7},{6,4},{7,5},{8,10},{9,11},{10,... | collective-permute-start | bytes 1277960 | tf_op jit(solution)/shard_map/ppermute | solution.py:427
  202.8 24.2 %collective-permute-start.23 = (bf16[2,128,1024]{2,1,0:T(8,128)(2,1)}, bf16[2,128,1024]{2,1,0:T(8,128)(2,1)S(1)}, u32[]{:S(2)}, u32[]{:S(2)}) collective-permute-start(bf16[2,128,1024]{2,1,0:T(8,128)(2,1)} %get-tuple-element.230), channel_id=1, source_target_pairs={{0,4},{4,0},{8,12},{12,8},{16,20},{20,16},{24,28},{28,24},{1,5},{5... | collective-permute-start | bytes 1572872 | tf_op jit(solution)/shard_map/ppermute | solution.py:427
  216.8 12.9 %collective-permute-start.22 = (bf16[416,256]{1,0:T(8,128)(2,1)}, bf16[416,256]{1,0:T(8,128)(2,1)S(1)}, u32[]{:S(2)}, u32[]{:S(2)}) collective-permute-start(bf16[416,256]{1,0:T(8,128)(2,1)} %get-tuple-element.229), channel_id=1, source_target_pairs={{0,4},{4,0},{8,12},{12,8},{16,20},{20,16},{24,28},{28,24},{1,5},{5... | collective-permute-start | bytes 638984 | tf_op jit(solution)/shard_map/ppermute | solution.py:427
  217.9 9.1 %all-to-all-start.5 = ((bf16[4,192,128]{2,1,0:T(8,128)(2,1)}), bf16[4,192,128]{2,1,0:T(8,128)(2,1)S(1)}, u32[]{:S(2)}, u32[]{:S(2)}) async-start(bf16[4,192,128]{2,1,0:T(8,128)(2,1)} %bitcast.24), calls=%async_computation.5 | async-start | bytes 393216 | tf_op jit(solution)/shard_map/all_to_all | solution.py:1045
  222.5 18.6 %collective-permute-start.28 = (bf16[2,128,1024]{2,1,0:T(8,128)(2,1)S(1)}, bf16[2,128,1024]{2,1,0:T(8,128)(2,1)S(1)}, u32[]{:S(2)}, u32[]{:S(2)}) collective-permute-start(bf16[2,128,1024]{2,1,0:T(8,128)(2,1)S(1)} %copy-done.33), channel_id=1, source_target_pairs={{0,4},{4,0},{8,12},{12,8},{16,20},{20,16},{24,28},{28,24},{1,5},{5... | collective-permute-start | bytes 1572872 | tf_op jit(solution)/shard_map/ppermute | solution.py:427
  232.1 10.8 %collective-permute-start.25 = (bf16[104,256]{1,0:T(8,128)(2,1)}, bf16[104,256]{1,0:T(8,128)(2,1)S(1)}, u32[]{:S(2)}, u32[]{:S(2)}) collective-permute-start(bf16[104,256]{1,0:T(8,128)(2,1)} %get-tuple-element.233), channel_id=1, source_target_pairs={{0,8},{4,12},{8,0},{12,4},{16,24},{20,28},{24,16},{28,20},{1,9},{5... | collective-permute-start | bytes 159752 | tf_op jit(solution)/shard_map/ppermute | solution.py:427
  233.0 10.0 %collective-permute-start.26 = (bf16[104,256]{1,0:T(8,128)(2,1)}, bf16[104,256]{1,0:T(8,128)(2,1)S(1)}, u32[]{:S(2)}, u32[]{:S(2)}) collective-permute-start(bf16[104,256]{1,0:T(8,128)(2,1)} %get-tuple-element.234), channel_id=1, source_target_pairs={{0,16},{4,20},{8,24},{12,28},{16,0},{20,4},{24,8},{28,12},{1,17},{... | collective-permute-start | bytes 159752 | tf_op jit(solution)/shard_map/ppermute | solution.py:427
  233.9 9.1 %collective-permute-start.27 = (bf16[104,256]{1,0:T(8,128)(2,1)}, bf16[104,256]{1,0:T(8,128)(2,1)S(1)}, u32[]{:S(2)}, u32[]{:S(2)}) collective-permute-start(bf16[104,256]{1,0:T(8,128)(2,1)} %get-tuple-element.235), channel_id=1, source_target_pairs={{0,24},{4,28},{8,16},{12,20},{16,8},{20,12},{24,0},{28,4},{1,25},{... | collective-permute-start | bytes 159752 | tf_op jit(solution)/shard_map/ppermute | solution.py:427
  241.2 32.0 %collective-permute-start.32 = (bf16[128,2304]{1,0:T(8,128)(2,1)}, bf16[128,2304]{1,0:T(8,128)(2,1)S(1)}, u32[]{:S(2)}, u32[]{:S(2)}) collective-permute-start(bf16[128,2304]{1,0:T(8,128)(2,1)} %get-tuple-element.241), channel_id=1, source_target_pairs={{0,16},{4,20},{8,24},{12,28},{16,0},{20,4},{24,8},{28,12},{1,17},{... | collective-permute-start | bytes 1769480 | tf_op jit(solution)/shard_map/ppermute | solution.py:427
  241.2 32.0 %collective-permute-start.33 = (bf16[2,128,1024]{2,1,0:T(8,128)(2,1)S(1)}, bf16[2,128,1024]{2,1,0:T(8,128)(2,1)S(1)}, u32[]{:S(2)}, u32[]{:S(2)}) collective-permute-start(bf16[2,128,1024]{2,1,0:T(8,128)(2,1)S(1)} %copy-done.35), channel_id=1, source_target_pairs={{0,8},{4,12},{8,0},{12,4},{16,24},{20,28},{24,16},{28,20},{1,9},{5... | collective-permute-start | bytes 1572872 | tf_op jit(solution)/shard_map/ppermute | solution.py:427
  245.2 19.8 %collective-permute-start.29 = (bf16[104,256]{1,0:T(8,128)(2,1)}, bf16[104,256]{1,0:T(8,128)(2,1)S(1)}, u32[]{:S(2)}, u32[]{:S(2)}) collective-permute-start(bf16[104,256]{1,0:T(8,128)(2,1)} %z_sum.1.refs_0_), channel_id=1, source_target_pairs={{0,8},{4,12},{8,0},{12,4},{16,24},{20,28},{24,16},{28,20},{1,9},{5... | collective-permute-start | bytes 159752 | tf_op jit(solution)/shard_map/ppermute | solution.py:427
  245.3 27.9 %collective-permute-start.30 = (bf16[104,256]{1,0:T(8,128)(2,1)}, bf16[104,256]{1,0:T(8,128)(2,1)S(1)}, u32[]{:S(2)}, u32[]{:S(2)}) collective-permute-start(bf16[104,256]{1,0:T(8,128)(2,1)} %z_sum.1.refs_0_), channel_id=1, source_target_pairs={{0,16},{4,20},{8,24},{12,28},{16,0},{20,4},{24,8},{28,12},{1,17},{... | collective-permute-start | bytes 159752 | tf_op jit(solution)/shard_map/ppermute | solution.py:427
  247.3 25.9 %collective-permute-start.31 = (bf16[104,256]{1,0:T(8,128)(2,1)}, bf16[104,256]{1,0:T(8,128)(2,1)S(1)}, u32[]{:S(2)}, u32[]{:S(2)}) collective-permute-start(bf16[104,256]{1,0:T(8,128)(2,1)} %z_sum.1.refs_0_), channel_id=1, source_target_pairs={{0,24},{4,28},{8,16},{12,20},{16,8},{20,12},{24,0},{28,4},{1,25},{... | collective-permute-start | bytes 159752 | tf_op jit(solution)/shard_map/ppermute | solution.py:427
  265.0 11.5 %copy-start.60 = (bf16[104,256]{1,0:T(8,128)(2,1)}, bf16[104,256]{1,0:T(8,128)(2,1)S(1)}, u32[]{:S(2)}) copy-start(bf16[104,256]{1,0:T(8,128)(2,1)S(1)} %collective-permute-done.29.refs_1_) | copy-start | bytes 159748
  276.5 14.1 %collective-permute-start.35 = (bf16[128,1024]{1,0:T(8,128)(2,1)}, bf16[128,1024]{1,0:T(8,128)(2,1)S(1)}, u32[]{:S(2)}, u32[]{:S(2)}) collective-permute-start(bf16[128,1024]{1,0:T(8,128)(2,1)} %get-tuple-element.252), channel_id=1, source_target_pairs={{0,16},{4,20},{8,24},{12,28},{16,0},{20,4},{24,8},{28,12},{1,17},{... | collective-permute-start | bytes 786440 | tf_op jit(solution)/shard_map/ppermute | solution.py:427
  280.3 14.3 %collective-permute-start.36 = (bf16[128,2304]{1,0:T(8,128)(2,1)}, bf16[128,2304]{1,0:T(8,128)(2,1)S(1)}, u32[]{:S(2)}, u32[]{:S(2)}) collective-permute-start(bf16[128,2304]{1,0:T(8,128)(2,1)} %z_last_sum.2.refs_0_), channel_id=1, source_target_pairs={{0,2},{1,3},{2,0},{3,1},{4,6},{5,7},{6,4},{7,5},{8,10},{9,11},{10,... | collective-permute-start | bytes 1769480 | tf_op jit(solution)/shard_map/ppermute | solution.py:427
  283.2 5.9 %collective-permute-start.34 = (bf16[416,256]{1,0:T(8,128)(2,1)}, bf16[416,256]{1,0:T(8,128)(2,1)S(1)}, u32[]{:S(2)}, u32[]{:S(2)}) collective-permute-start(bf16[416,256]{1,0:T(8,128)(2,1)} %bitcast.89), channel_id=1, source_target_pairs={{0,4},{4,0},{8,12},{12,8},{16,20},{20,16},{24,28},{28,24},{1,5},{5... | collective-permute-start | bytes 638984 | tf_op jit(solution)/shard_map/ppermute | solution.py:427
  294.6 14.6 %copy-start.28 = (bf16[128,2304]{1,0:T(8,128)(2,1)}, bf16[128,2304]{1,0:T(8,128)(2,1)S(1)}, u32[]{:S(2)}) copy-start(bf16[128,2304]{1,0:T(8,128)(2,1)S(1)} %collective-permute-done.36.refs_2_) | copy-start | bytes 1769476
  296.6 11.3 %copy-start.21 = (f32[128,1]{0,1:T(1,128)S(1)}, f32[128,1]{0,1:T(1,128)}, u32[]{:S(2)}) copy-start(f32[128,1]{0,1:T(1,128)} %bitcast_convert_fusion) | copy-start | bytes 1540
  296.6 12.0 %copy-start.27 = (bf16[128,2304]{1,0:T(8,128)(2,1)S(1)}, bf16[128,2304]{1,0:T(8,128)(2,1)}, u32[]{:S(2)}) copy-start(bf16[128,2304]{1,0:T(8,128)(2,1)} %z_last_sum.2.refs_0_) | copy-start | bytes 1769476
  296.6 6.5 %collective-permute-start.41 = (bf16[128,1024]{1,0:T(8,128)(2,1)}, bf16[128,1024]{1,0:T(8,128)(2,1)}, u32[]{:S(2)}, u32[]{:S(2)}) collective-permute-start(bf16[128,1024]{1,0:T(8,128)(2,1)} %z_last_sum.3.refs_0_), channel_id=1, source_target_pairs={{0,2},{1,3},{2,0},{3,1},{4,6},{5,7},{6,4},{7,5},{8,10},{9,11},{10,... | collective-permute-start | bytes 786440 | tf_op jit(solution)/shard_map/ppermute | solution.py:427
  299.9 12.3 %collective-permute-start.38 = (bf16[832,256]{1,0:T(8,128)(2,1)}, bf16[832,256]{1,0:T(8,128)(2,1)S(1)}, u32[]{:S(2)}, u32[]{:S(2)}) collective-permute-start(bf16[832,256]{1,0:T(8,128)(2,1)} %bitcast.84), channel_id=1, source_target_pairs={{0,2},{1,3},{2,0},{3,1},{4,6},{5,7},{6,4},{7,5},{8,10},{9,11},{10,... | collective-permute-start | bytes 1277960 | tf_op jit(solution)/shard_map/ppermute | solution.py:427
  300.1 9.1 %collective-permute-start.40 = (bf16[128,1024]{1,0:T(8,128)(2,1)S(1)}, bf16[128,1024]{1,0:T(8,128)(2,1)}, u32[]{:S(2)}, u32[]{:S(2)}) collective-permute-start(bf16[128,1024]{1,0:T(8,128)(2,1)S(1)} %copy-done.53), channel_id=1, source_target_pairs={{0,1},{1,0},{2,3},{3,2},{4,5},{5,4},{6,7},{7,6},{8,9},{9,8},{10,11... | collective-permute-start | bytes 786440 | tf_op jit(solution)/shard_map/ppermute | solution.py:427
  303.2 11.6 %collective-permute-start.42 = (bf16[128,1024]{1,0:T(8,128)(2,1)}, bf16[128,1024]{1,0:T(8,128)(2,1)}, u32[]{:S(2)}, u32[]{:S(2)}) collective-permute-start(bf16[128,1024]{1,0:T(8,128)(2,1)} %collective-permute-done.41.refs_2_), channel_id=1, source_target_pairs={{0,1},{1,0},{2,3},{3,2},{4,5},{5,4},{6,7},{7,6},{8,9},{9,8},{10,11... | collective-permute-start | bytes 786440 | tf_op jit(solution)/shard_map/ppermute | solution.py:427
  308.7 8.7 %collective-permute-start.43 = (bf16[128,2304]{1,0:T(8,128)(2,1)S(1)}, bf16[128,2304]{1,0:T(8,128)(2,1)S(1)}, u32[]{:S(2)}, u32[]{:S(2)}) collective-permute-start(bf16[128,2304]{1,0:T(8,128)(2,1)S(1)} %copy-done.27), channel_id=1, source_target_pairs={{0,1},{1,0},{2,3},{3,2},{4,5},{5,4},{6,7},{7,6},{8,9},{9,8},{10,11... | collective-permute-start | bytes 1769480 | tf_op jit(solution)/shard_map/ppermute | solution.py:427
  308.7 14.5 %collective-permute-start.37 = (bf16[832,256]{1,0:T(8,128)(2,1)}, bf16[832,256]{1,0:T(8,128)(2,1)S(1)}, u32[]{:S(2)}, u32[]{:S(2)}) collective-permute-start(bf16[832,256]{1,0:T(8,128)(2,1)} %bitcast.85), channel_id=1, source_target_pairs={{0,1},{1,0},{2,3},{3,2},{4,5},{5,4},{6,7},{7,6},{8,9},{9,8},{10,11... | collective-permute-start | bytes 1277960 | tf_op jit(solution)/shard_map/ppermute | solution.py:427
  309.2 8.2 %collective-permute-start.44 = (bf16[128,2304]{1,0:T(8,128)(2,1)S(1)}, bf16[128,2304]{1,0:T(8,128)(2,1)S(1)}, u32[]{:S(2)}, u32[]{:S(2)}) collective-permute-start(bf16[128,2304]{1,0:T(8,128)(2,1)S(1)} %collective-permute-done.36.refs_2_), channel_id=1, source_target_pairs={{0,1},{1,0},{2,3},{3,2},{4,5},{5,4},{6,7},{7,6},{8,9},{9,8},{10,11... | collective-permute-start | bytes 1769480 | tf_op jit(solution)/shard_map/ppermute | solution.py:427
  312.2 11.0 %collective-permute-start.39 = (bf16[832,256]{1,0:T(8,128)(2,1)S(1)}, bf16[832,256]{1,0:T(8,128)(2,1)}, u32[]{:S(2)}, u32[]{:S(2)}) collective-permute-start(bf16[832,256]{1,0:T(8,128)(2,1)S(1)} %collective-permute-done.38.m2), channel_id=1, source_target_pairs={{0,1},{1,0},{2,3},{3,2},{4,5},{5,4},{6,7},{7,6},{8,9},{9,8},{10,11... | collective-permute-start | bytes 1277960 | tf_op jit(solution)/shard_map/ppermute | solution.py:427
  (53 other events, 214.4 us)
where the time goes:
time: 333 us; the launch traced here: 331 us
  Pallas kernels  115 us (35%)
  waiting for transfers between devices  93.1 us (28%)
  starting transfers between devices  73.7 us (22%)
  local copies, waits for them, and re-layouts  23.2 us (7%)
  matrix products  17.1 us (5%)
  other arithmetic  7.38 us (2%)
    ppermute x45, waiting for transfers between devices, swap(): lax.ppermute(values, axis, [(i, i ^ bit) for i in range(lax.axis_size(axi...  68.7 us
    pallas_call x17, Pallas kernels, small_call(): pl.pallas_call(kernel, out_shape=tuple((jax.ShapeDtypeStruct(dims, dtype)...  51.7 us
    ppermute x45, starting transfers between devices, swap(): lax.ppermute(values, axis, [(i, i ^ bit) for i in range(lax.axis_size(axi...  47.3 us
    all_to_all x4, waiting for transfers between devices, to_heads(): lax.all_to_all(values, 'patch', split_axis=0, concat_axis=0, tiled=True)  20.3 us
    pallas_call x1, Pallas kernels, middle(): pl.pallas_call(middle_kernel, grid=(parts,), out_shape=(shape((seg, width...  18.1 us
    all_to_all x4, starting transfers between devices, to_heads(): lax.all_to_all(values, 'patch', split_axis=0, concat_axis=0, tiled=True)  17.3 us
    dot_general x10, matrix products, mm(): lax.dot_general(a, b, dims, precision=precision, preferred_element_type=F32)  17.1 us
    unnamed x135, local copies, waits for them, and re-layouts  12.5 us
  transfers between devices with their start and end apart: 51, of which 16 were waited for; matrix products, arithmetic and copies ran while one was open for 9% of the time, Pallas kernels for 30%

commit v1 on v0

--- a/solution.py
+++ b/solution.py
@@ -85,7 +85,7 @@
         in_specs=[pl.BlockSpec(memory_space=pltpu.SMEM)] + [vmem] * 5,
         out_specs=(vmem,) * 3,
         scratch_shapes=[pltpu.VMEM((width, seg), F32)],
-        cost_estimate=cost(6 * 10**9),
+        cost_estimate=cost(60000000000),
         name="front_forward",
     )(own_ids, own_field, spread, bias, vwt, vet)
 
@@ -207,7 +207,7 @@
             pltpu.VMEM((rows, seg), F32),
             pltpu.VMEM((HEADS, width), F32),
         ],
-        cost_estimate=cost(10**8),
+        cost_estimate=cost(100000000),
         name="front_backward",
     )(place, own_ids, x_own, shares, mixed_grad, vw, ve, spread, norm_one, norm_two)
 
@@ -220,7 +220,7 @@
 def attend_forward_kernel(head_dim, block, count_ref, qkv_ref, out_ref, lse_ref, q_ref, k_ref, vt_ref):
     full, width = q_ref.shape
     seg = full // qkv_ref.shape[0]
-    scaling = 1.0 / math.sqrt(head_dim)
+    scaling = jnp.asarray(1.0 / math.sqrt(head_dim), BF16)
     load_parts(qkv_ref, 2, seg, q_ref)
     vt_ref[...] = q_ref[...].T
     load_parts(qkv_ref, 0, seg, q_ref)
@@ -235,14 +235,14 @@
         query = q_ref[part, :]
         total = jnp.zeros((width, block), F32)
         for h in range(width // head_dim):
-            own = jnp.where(lane == h, query, jnp.zeros_like(query))
-            scores = jnp.where(valid, mm(k_ref[...], own, NT) * scaling, MASKED)
+            own = jnp.where(lane == h, query, jnp.zeros_like(query)) * scaling
+            scores = jnp.where(valid, mm(k_ref[...], own, NT), MASKED)
             top = jnp.max(scores, axis=0, keepdims=True)
             exponent = jnp.exp(scores - top)
             denominator = jnp.sum(exponent, axis=0, keepdims=True)
-            shares = (exponent * (1.0 / denominator)).astype(BF16)
             lse_ref[h : h + 1, part] = top + jnp.log(denominator)
-            total = jnp.where(row == h, mm(vt_ref[...], shares), total)
+            mixed = mm(vt_ref[...], exponent.astype(BF16)) * (1.0 / denominator)
+            total = jnp.where(row == h, mixed, total)
         out_ref[part, :] = total.T.astype(BF16)
         return carry
 
@@ -267,7 +267,7 @@
             pltpu.VMEM((full, width), BF16),
             pltpu.VMEM((width, full), BF16),
         ],
-        cost_estimate=cost(10 * 10**9),
+        cost_estimate=cost(60000000000),
         name="attend_forward",
     )(count, qkv)
 
@@ -295,9 +295,9 @@
         grad = grad_ref[part, :]
         total = jnp.zeros((width, block), F32)
         for h in range(width // head_dim):
-            own = jnp.where(lane == h, query, jnp.zeros_like(query))
+            own = jnp.where(lane == h, query, jnp.zeros_like(query)) * jnp.asarray(scaling, BF16)
             own_grad = jnp.where(lane == h, grad, jnp.zeros_like(grad))
-            scores = jnp.where(valid, mm(k_ref[...], own, NT) * scaling, MASKED)
+            scores = jnp.where(valid, mm(k_ref[...], own, NT), MASKED)
             shares = jnp.exp(scores - lse_ref[h : h + 1, part])
             share_grad = mm(v_ref[...], own_grad, NT)
             dot = jnp.sum(shares * share_grad, axis=0, keepdims=True)
@@ -313,7 +313,7 @@
     lax.fori_loop(0, full // block, step, 0)
     for source in range(full // seg):
         rows = slice(source * seg, (source + 1) * seg)
-        out_ref[source, seg : 2 * seg, :] = (dk_ref[rows, :] * scaling).astype(BF16)
+        out_ref[source, seg : 2 * seg, :] = dk_ref[rows, :].astype(BF16)
         out_ref[source, 2 * seg : 3 * seg, :] = dv_ref[rows, :].astype(BF16)
 
 
@@ -330,7 +330,7 @@
         scratch_shapes=[pltpu.VMEM((full, width), BF16)] * 3
         + [pltpu.VMEM((width, full), BF16)]
         + [pltpu.VMEM((full, width), F32)] * 2,
-        cost_estimate=cost(50 * 10**9),
+        cost_estimate=cost(100000000000),
         name="attend_backward",
     )(count, qkv, grad, lse)
 
@@ -419,7 +419,7 @@
     total = sum(job[-1] for job in jobs)
     shapes = [((len(blocks), rows, total), BF16) for blocks in away + near]
     kernel = functools.partial(weight_grad_kernel, jobs, near, away)
-    outs = small_call(kernel, place, arrays, shapes, effort=40, name="weight_grads")
+    outs = small_call(kernel, place, arrays, shapes, effort=2000, name="weight_grads")
     return outs[len(away) :], outs[: len(away)]
 
 
@@ -435,7 +435,7 @@
     return lax.optimization_barrier((value, *others))[0]
 
 
-def small_call(kernel, place, arrays, shapes, scratch=(), effort=20, name="small"):
+def small_call(kernel, place, arrays, shapes, scratch=(), effort=200, name="small"):
     vmem = pl.BlockSpec(memory_space=pltpu.VMEM)
     return pl.pallas_call(
         kernel,
@@ -443,7 +443,7 @@
         in_specs=[pl.BlockSpec(memory_space=pltpu.SMEM)] + [vmem] * len(arrays),
         out_specs=(vmem,) * len(shapes),
         scratch_shapes=list(scratch),
-        cost_estimate=cost(effort * 10**9),
+        cost_estimate=cost(int(effort * 10**9)),
         name=name,
     )(place, *arrays)
 
@@ -488,23 +488,23 @@
     return small_call(kernel, place, arrays, [(arrays[0].shape, BF16)], name="z_sum")[0]
 
 
-def pair_sum(place, near, gots):
-    def kernel(place_ref, near_ref, *refs):
+def pair_sum(place, near, got):
+    def kernel(place_ref, near_ref, got_ref, out):
         for k in range(2):
-            got = refs[0][k] if len(refs) == 2 else refs[k][0]
-            refs[-1][k] = (near_ref[k].astype(F32) + got.astype(F32)).astype(BF16)
-
-    return small_call(kernel, place, (near, *gots), [(near.shape, BF16)], name="pair_sum")[0]
-
-
-def z_first_sum(place, near, gots, far):
-    def kernel(place_ref, near_ref, *refs):
-        gots, (far_ref, stay, away) = refs[:-3], refs[-3:]
+            out[k] = (near_ref[k].astype(F32) + got_ref[k].astype(F32)).astype(BF16)
+
+    return small_call(kernel, place, (near, got), [(near.shape, BF16)], name="pair_sum")[0]
+
+
+def z_first_sum(place, near, got, far):
+    first = got.shape[0] - 2
+
+    def kernel(place_ref, near_ref, got_ref, far_ref, stay, away):
         for out, k in ((away, 1), (stay, 0)):
-            got = gots[0][k] if len(gots) == 1 else gots[k][0]
-            out[...] = (near_ref[k].astype(F32) + got.astype(F32) + far_ref[k].astype(F32)).astype(BF16)
-
-    return small_call(kernel, place, (near, *gots, far), [(near.shape[1:], BF16)] * 2, name="z_first_sum")
+            total = near_ref[k].astype(F32) + got_ref[first + k].astype(F32) + far_ref[k].astype(F32)
+            out[...] = total.astype(BF16)
+
+    return small_call(kernel, place, (near, got, far), [(near.shape[1:], BF16)] * 2, name="z_first_sum")
 
 
 def z_last_sum(place, near, got):
@@ -579,7 +579,8 @@
     arrays = (own, next(hooks)(swap(own, "patch", 1)))
     full = small_call(y_kernel, place, arrays, [(halves, BF16)], name="y_join")[0].reshape(rows, cols)
 
-    return gather_over_var(full)
+    across = next(hooks)(swap(full, "var", 2))
+    return full, swap(full, "var", 1), across, swap(across, "var", 1)
 
 
 def middle_kernel(
@@ -596,14 +597,17 @@
     late_ref,
     *refs,
 ):
-    actives, middles = refs[0:4], refs[4:8]
-    grad_ref, after_ref, gain_grad_ref, residual_ref, unit_ref, rate_ref, acc_ref, back_ref, wide_ref, branch_ref = refs[8:]
+    slices = refs[0:4]
+    grad_ref, after_ref, gain_grad_ref, residual_ref, unit_ref, rate_ref, acc_ref, back_ref, wide_ref, branch_ref = refs[4:]
     step = pl.program_id(0)
     seg, width = front_ref.shape
     parts = att_ref.shape[0]
     own = width // parts
     me = place_ref[0]
-    slot = actives[0].shape[1] // pl.num_programs(0)
+    block = win_ref.shape[1]
+    slot = block // 4
+    quarter = width // 4
+    hidden = slot * pl.num_programs(0)
 
     @pl.when(step == 0)
     def _():
@@ -630,15 +634,14 @@
     wide_ref[...] = active
     cols = pl.ds(pl.multiple_of(step * slot, slot), slot)
     for s in range(4):
-        actives[s][:, cols] = wide_ref[:, pl.ds(pl.multiple_of((me ^ s) * slot, slot), slot)]
-    block = inner_grad.shape[1]
-    owner = step * block // width
-    place = pl.ds(pl.multiple_of(step * block - owner * width, block), block)
+        slices[s][:, cols] = wide_ref[:, pl.ds(pl.multiple_of((me ^ s) * slot, slot), slot)]
+    owner = step * block // hidden
+    place = pl.ds(pl.multiple_of(hidden + step * block - owner * hidden, block), block)
     for s in range(4):
 
         @pl.when((me ^ s) == owner)
         def _(s=s):
-            middles[s][:, place] = inner_grad
+            slices[s][:, place] = inner_grad
 
     @pl.when(step == pl.num_programs(0) - 1)
     def _():
@@ -653,10 +656,9 @@
         total = og_ref[...].astype(F32) + total
         after_ref[...] = total
         branch_ref[...] = total.astype(BF16)
-        quarter = width // 4
         for s in range(4):
             start = pl.multiple_of((me ^ s) * quarter, quarter)
-            middles[s][:, width : width + quarter] = branch_ref[:, pl.ds(start, quarter)]
+            slices[s][:, 2 * hidden :] = branch_ref[:, pl.ds(start, quarter)]
         turned = mm(branch_ref[...], tout_ref[...], NT).astype(BF16)
         for p in range(parts):
             grad_ref[p] = turned[:, p * own : (p + 1) * own]
@@ -672,7 +674,7 @@
     def still(*dims):
         return pl.BlockSpec(dims, lambda i: (0,) * len(dims))
 
-    piece, wider = shape((seg, hidden // 4), BF16), shape((seg, width + width // 4), BF16)
+    piece = shape((seg, hidden // 2 + width // 4), BF16)
     return pl.pallas_call(
         middle_kernel,
         grid=(parts,),
@@ -680,7 +682,6 @@
             shape((seg, width), BF16),
             shape((seg, width), BF16),
             *((piece,) * 4),
-            *((wider,) * 4),
             shape(attended.shape, BF16),
             shape((seg, width), F32),
             shape((1, width), F32),
@@ -700,7 +701,6 @@
             still(seg, width),
             still(seg, width),
             *((still(*piece.shape),) * 4),
-            *((still(*wider.shape),) * 4),
             still(*attended.shape),
             still(seg, width),
             still(1, width),
@@ -715,7 +715,7 @@
             pltpu.VMEM((seg, width), BF16),
         ],
         compiler_params=pltpu.CompilerParams(dimension_semantics=("arbitrary",)),
-        cost_estimate=cost(60 * 10**9),
+        cost_estimate=cost(100000000000),
         name="trunk_middle",
     )(place, attended, front_out, valid, out_grad, trunk_out, gain, mlp_in, mlp_out)
 
@@ -792,7 +792,7 @@
             pltpu.VMEM((seg, width), BF16),
         ],
         compiler_params=pltpu.CompilerParams(dimension_semantics=("arbitrary",)),
-        cost_estimate=cost(80 * 10**9),
+        cost_estimate=cost(100000000000),
         name="trunk_back",
     )(place, grads, front_out, gain, after_grad, valid, agg_out, trunk_qkv)
 
@@ -934,8 +934,6 @@
     same_var = (jnp.arange(VARS)[:, None] == jnp.arange(VARS * pixels)[None, :] // pixels)[None]
     spread = jnp.where(same_var, score_weight[:, None, :], 0.0).astype(BF16)
     spread = spread.reshape(HEADS * VARS, VARS * pixels)
-    vw = mm(weight_rows, value_proj).astype(BF16)
-    ve = mm(var_embed, value_proj).astype(BF16)
     vwt = mm(value_proj, weight_rows, (((0,), (1,)), ((), ()))).astype(BF16)
     vet = mm(value_proj, var_embed, (((0,), (1,)), ((), ()))).astype(BF16)
 
@@ -948,21 +946,24 @@
     def own_rows(values):
         return lax.dynamic_slice_in_dim(values, start, own_width, 0)
 
-    value_rows = own_rows(value_proj)
-    key_query_rows = own_rows(key_query)
-    own_query = lax.dynamic_slice_in_dim(agg_query, start, own_width, 0).astype(F32)[:, None]
-    if fast:
-        arrays = (
-            weight_rows,
-            var_embed,
-            own_cols(weight_rows),
-            own_cols(var_embed),
-            value_rows,
-            jnp.concatenate(split_high_low(key_query_rows), axis=1).T,
+    def own_query(values):
+        return lax.dynamic_slice_in_dim(values, start, own_width, 0).astype(F32)[:, None]
+
+    def last_operands(ready):
+        weights, embeds, values, queries, line, key_queries, _ = together(
+            weight_rows, var_embed, value_proj, query_proj, agg_query, key_query, ready
+        )
+        return (
+            weights,
+            embeds,
+            own_cols(weights),
+            own_cols(embeds),
+            own_rows(values),
+            jnp.concatenate(split_high_low(own_rows(key_queries)), axis=1).T,
             key_proj,
             agg_q[None],
-            own_rows(query_proj),
-            own_query,
+            own_rows(queries),
+            own_query(line),
         )
 
     x_own, shares, mixed_low = front_forward(own_ids, own_field, spread, score_embed, vwt, vet)
@@ -974,9 +975,12 @@
     part = width // group
     quarter = hidden // group
     zs = patches // 2
+    ready = after(value_proj, triple)
+    vw = mm(weight_rows, ready).astype(BF16)
+    ve = mm(var_embed, ready).astype(BF16)
     if fast:
         early = tokens_of_group(jnp.concatenate([out_grad_low, mixed_low, normed_one_low], axis=1))
-        qkv, vw, ve, *arrays = together(queries_to_heads(triple), vw, ve, *arrays)
+        qkv, vw, ve, *arrays = together(queries_to_heads(triple), vw, ve, *last_operands(triple))
         count = own_count.reshape(1, 1)
         heads, lse = attend_forward(count, qkv, head_dim)
         attended = to_heads(heads.reshape(patches, seg, own_width))
@@ -993,21 +997,23 @@
         )
         attended_group = copies_of_group(attended)
         results = together(*results, *attended_group, *early)
-        attended_group, early = results[13:17], results[17:]
-        block_out, normed_two_low, grads, after_grad, norm_two_grad = (results[k] for k in (0, 1, 10, 11, 12))
+        attended_group, early = results[9:13], results[13:]
+        block_out, normed_two_low, grads, after_grad, norm_two_grad = (results[k] for k in (0, 1, 6, 7, 8))
         block_out = block_out[None]
         grads = to_heads(grads)
-        active_group, middle_group = slices_of_group(results[2:6]), results[6:10]
+        mlp_group = slices_of_group(results[2:6])
         across = swap(normed_two_low, "var", 2)
         result = attend_backward(count, qkv, grads.reshape(patches * seg, own_width), lse, head_dim)
-        result, across, *rest = together(result, across, *active_group, *middle_group)
-        active_group, middle_group = rest[:4], slices_of_group(rest[4:])
+        result, across = together(result, across)
         normed_group = (normed_two_low, swap(normed_two_low, "var", 1), across, swap(across, "var", 1))
         result = to_heads(result)
         pairs = ((1, 3), (0, 2))
-        jobs = ((0, 0, 1, 0, width), (2, 0, 4, 0, quarter), (3, 0, 4, quarter, part))
-        groups = (active_group, early, normed_group, attended_group, middle_group)
-        near, away = weight_grads(place, jobs, groups, own_width, pairs, pairs)
+        jobs = ((0, 0, 1, 0, width), (2, 0, 0, quarter, quarter), (3, 0, 0, 2 * quarter, part))
+        groups = (mlp_group, early, normed_group, attended_group)
+        _, away = weight_grads(place, jobs, groups, own_width, (), pairs[:1])
+        held = together(away[0], *groups[0])
+        near, more = weight_grads(place, jobs, (held[1:], *groups[1:]), own_width, pairs, pairs[1:])
+        away = (*away, *more)
         result = after(result, *near)
         mlp = {"near": near, "away": away}
         mixed_grad, norm_one_grad, *pieces = trunk_back(
@@ -1048,48 +1054,49 @@
         got = swap(mlp["away"][0], "patch", 1)
         m_stay, m_away, got = together(*m_parts, got)
         m_parts = (m_stay, m_away)
-        mlp["far"] = pair_sum(place, mlp["near"][0], (got,))
+        mlp["first"] = got
+        mlp["far"] = pair_sum(place, mlp["near"][0], got)
         last = {}
 
         def core_done(values):
-            return after(values, mlp["far"], *last_group)
+            return values
 
         def x_done(values):
             jobs = ((0, 2 * width, 1, 0, 3 * part), (0, width, 1, 3 * part, part))
-            last["near"], last["away"] = weight_grads(place, jobs, (early, last_group), own_width, pairs, pairs)
-            values, mlp["got"], *_ = together(values, swap(mlp["away"][1], "patch", 1), *last["near"])
-            return values
+            groups = (early, last_group)
+            last["near"], last["away"] = weight_grads(place, jobs, groups, own_width, pairs, ((1, 3, 0, 2),))
+            return after(values, mlp["far"], field_grad, *last["near"])
 
         def y_done(values):
-            got, far = swap(last["away"][0], "patch", 1), swap(mlp["far"], "patch", 2)
-            values, got, far, _ = together(values, got, far, field_grad)
-            mlp["pair"] = z_first_sum(place, mlp["near"][1], (mlp["got"],), far)
-            last["far"] = pair_sum(place, last["near"][0], (got,))
-            return values
+            got = swap(after(mlp["away"][1], mlp["first"]), "patch", 1)
+            values, got, far = together(values, got, swap(mlp["far"], "patch", 2))
+            mlp["pair"] = z_first_sum(place, mlp["near"][1], got, far)
+            return after(values, mlp["pair"][0])
 
         def z_done(values):
-            got = swap(last["away"][1], "patch", 1)
-            rest = together(*values, got, last["far"], *mlp["pair"])
-            last["got"] = rest[4]
-            return rest[:4]
+            *values, last["got"] = together(*values, swap(last["away"][0], "patch", 1))
+            last["far"] = pair_sum(place, last["near"][0], last["got"])
+            return [after(values[0], last["far"]), *values[1:]]
 
         def b_done(values):
             near, away = mlp["pair"]
-            *values, got, far = together(*values, swap(away, "patch", 4), swap(last["far"], "patch", 2))
+            *values, got = together(*values, swap(away, "patch", 4))
             mlp["own"] = z_last_sum(place, near, got)
-            last["pair"] = z_first_sum(place, last["near"][1], (last["got"],), far)
             return values
 
         def y_back(values):
-            near, away = last["pair"]
-            values, got, mlp["across"] = together(values, swap(away, "patch", 4), swap(mlp["own"], "var", 2))
+            return values
+
+        def var_done(values):
+            far, across = swap(last["far"], "patch", 2), swap(mlp["own"], "var", 2)
+            near, away = z_first_sum(place, last["near"][1], last["got"], far)
+            values, got, across = together(values, swap(away, "patch", 4), across)
+            mlp["parts"] = (mlp["own"], swap(mlp["own"], "var", 1), across, swap(across, "var", 1))
             last["own"] = z_last_sum(place, near, got)
             return values
 
-        m_pieces = sum_over_all(place, *m_parts, (core_done, x_done, y_done, z_done, b_done, y_back))
-        own, across = mlp["own"], mlp["across"]
-        parts = (own, swap(own, "var", 1), across, swap(across, "var", 1))
-        mlp_out_grad, mlp_in_grad, trunk_out_grad = join(place, parts, (width, quarter, part), 1)
+        m_pieces = sum_over_all(place, *m_parts, (core_done, x_done, y_done, z_done, b_done, y_back, var_done))
+        mlp_out_grad, mlp_in_grad, trunk_out_grad = join(place, mlp["parts"], (width, quarter, part), 1)
         mlp_out_grad = mlp_out_grad.reshape(hidden // patches, width)
         trunk_qkv_grad, agg_out_grad = join(place, gather_over_var(last["own"]), (3 * part, part), 0)
     else:
@@ -1123,6 +1130,7 @@
         )
         agg_query_grad, norm_one_grad, norm_two_grad = (line[0] for line in lines)
     else:
+        value_rows, key_query_rows = own_rows(value_proj), own_rows(key_query)
         m_sum, me_sum = m_all[: VARS * pixels], m_all[VARS * pixels : VARS * pixels + VARS]
         s_rows = m_all[VARS * pixels + VARS :].astype(F32)
         s_all = s_rows[:, : VARS * pixels]
@@ -1141,7 +1149,7 @@
         crossed = mm(jnp.concatenate(split_high_low(key_sum), axis=0), key_proj)
         crossed = crossed[:HEADS] + crossed[HEADS:]
         aggq_grad = jnp.sum(jnp.where(in_head.T, crossed, 0.0), axis=0)
-        query_proj_grad = own_query * aggq_grad[None, :]
+        query_proj_grad = own_query(agg_query) * aggq_grad[None, :]
         agg_query_grad = jnp.sum(own_rows(query_proj).astype(F32) * aggq_grad[None, :], axis=1)
         norm_one_grad = lax.dynamic_slice_in_dim(norm_sums[:, :head_dim].reshape(width), start, own_width, 0)
         norm_two_grad = lax.dynamic_slice_in_dim(norm_sums[:, head_dim:].reshape(width), start, own_width, 0)

time: 333 us -> 312 us (0.937)
  waiting for transfers between devices: 93.1 us -> 84.2 us
  local copies, waits for them, and re-layouts: 23.2 us -> 15.6 us
  starting transfers between devices: 73.7 us -> 67.3 us
    ppermute x45 -> x41, starting transfers between devices: 47.3 us -> 40.8 us  [swap(): lax.ppermute(values, axis, [(i, i ^ bit) for i in range(lax.axis_size(axi...]
    unnamed x135 -> x67, local copies, waits for them, and re-layouts: 12.5 us -> 6.23 us
    all_to_all x4, waiting for transfers between devices: 20.3 us -> 15.7 us  [to_heads(): lax.all_to_all(values, 'patch', split_axis=0, concat_axis=0, tiled=True)]
    all_to_all x1, waiting for transfers between devices: 4.12 us -> 0.01 us  [local(): lax.all_to_all(field_low, 'var', split_axis=0, concat_axis=0, tiled=True)]
    pallas_call x17 -> x18, Pallas kernels: 51.7 us -> 55.5 us  [small_call(): pl.pallas_call(kernel, out_shape=tuple((jax.ShapeDtypeStruct(dims, dtype)...]
    ppermute x45 -> x41, waiting for transfers between devices: 68.7 us -> 68.5 us  [swap(): lax.ppermute(values, axis, [(i, i ^ bit) for i in range(lax.axis_size(axi...]
  transfers between devices with their start and end apart: 51 -> 47, of which waited for: 16 -> 16; matrix products, arithmetic and copies ran while one was open for 9% -> 9% of each run, Pallas kernels for 30% -> 35%
where the time goes in v1:
time: 312 us; the launch traced here: 310 us
  Pallas kernels  118 us (38%)
  waiting for transfers between devices  84.2 us (27%)
  starting transfers between devices  67.3 us (22%)
  matrix products  17.1 us (5%)
  local copies, waits for them, and re-layouts  15.6 us (5%)
  other arithmetic  7.13 us (2%)
    ppermute x41, waiting for transfers between devices, swap(): lax.ppermute(values, axis, [(i, i ^ bit) for i in range(lax.axis_size(axi...  68.5 us
    pallas_call x18, Pallas kernels, small_call(): pl.pallas_call(kernel, out_shape=tuple((jax.ShapeDtypeStruct(dims, dtype)...  55.5 us
    ppermute x41, starting transfers between devices, swap(): lax.ppermute(values, axis, [(i, i ^ bit) for i in range(lax.axis_size(axi...  40.8 us
    all_to_all x4, starting transfers between devices, to_heads(): lax.all_to_all(values, 'patch', split_axis=0, concat_axis=0, tiled=True)  18 us
    pallas_call x1, Pallas kernels, middle(): pl.pallas_call(middle_kernel, grid=(parts,), out_shape=(shape((seg, width...  17.9 us
    dot_general x10, matrix products, mm(): lax.dot_general(a, b, dims, precision=precision, preferred_element_type=F32)  17.1 us
    all_to_all x4, waiting for transfers between devices, to_heads(): lax.all_to_all(values, 'patch', split_axis=0, concat_axis=0, tiled=True)  15.7 us
    pallas_call x1, Pallas kernels, attend_backward(): pl.pallas_call(functools.partial(attend_backward_kernel, head_dim, block)...  11 us
  transfers between devices with their start and end apart: 47, of which 16 were waited for; matrix products, arithmetic and copies ran while one was open for 9% of the time, Pallas kernels for 35%

profile of v1, /device:TPU:1, one launch (start us, length us, event | category | flops | bytes accessed | tf_op | source)
XLA Modules:
  0.0 310.2 jit_solution(1006625168135793653)
XLA Ops:
  0.7 4.3 %all-to-all-start = ((bf16[4,192,128]{2,1,0:T(8,128)(2,1)}), bf16[4,192,128]{2,1,0:T(8,128)(2,1)S(1)}, u32[]{:S(2)}, u32[]{:S(2)}) async-start(bf16[4,192,128]{2,1,0:T(8,128)(2,1)} %bitcast.82), calls=%async_computation | async-start | bytes 393216 | tf_op jit(solution)/shard_map/all_to_all | solution.py:914
  5.8 2.1 fusion.21.aggq_ref
  10.1 3.0 convolution_convert_fusion.2.vwt_ref
  19.3 6.5 %front_forward.1 = (bf16[768,128]{1,0:T(8,128)(2,1)}, f32[768,128]{1,0:T(8,128)}, bf16[128,1024]{1,0:T(8,128)(2,1)}) custom-call(s32[1,48]{1,0:T(1,128)} %constant_dynamic-slice_fusion.4.ids_ref, bf16[768,128]{1,0:T(8,128)(2,1)} %bitcast.84, bf16[768,768]{1,0:T(8,128)(2,1)} %bitcast.71, f32[768,1]{1,0:T(8,128)} %reshape.252.bias_ref, ...), custom_call_target="tpu_custom_call" | custom-call | flops 60000002048 | bytes 1048576 | tf_op jit(solution)/shard_map/front_forward/pallas_call | solution.py:78
  25.8 2.2 fusion.20
  28.4 3.8 %convolution_convert_fusion = bf16[128,3072]{1,0:T(8,128)(2,1)S(1)} fusion(bf16[128,1024]{1,0:T(8,128)(2,1)S(1)} %multiply_convert_fusion, bf16[1024,3072]{1,0:T(8,128)(2,1)} %wqkv_ref.1), kind=kOutput, calls=%fused_computation | convolution fusion | flops 805699584 | bytes 7340032 | tf_op jit(solution)/shard_map/dot_general | solution.py:28
  33.5 6.1 %all-to-all-start.1 = ((bf16[8,384,128]{2,1,0:T(8,128)(2,1)}), bf16[8,384,128]{2,1,0:T(8,128)(2,1)}, u32[]{:S(2)}, u32[]{:S(2)}) async-start(bf16[8,384,128]{2,1,0:T(8,128)(2,1)} %bitcast.15), calls=%async_computation.1 | async-start | bytes 1572864 | tf_op jit(solution)/shard_map/all_to_all | solution.py:383
  40.7 1.4 collective-permute-start.4
  44.5 1.6 constant_dynamic-slice_fusion.3.weight_own_ref
  46.2 1.8 constant_dynamic-slice_fusion
  49.1 3.0 fusion.vw_ref
  52.1 7.6 %all-to-all-done.1.qkv_ref = bf16[8,384,128]{2,1,0:T(8,128)(2,1)} async-done(((bf16[8,384,128]{2,1,0:T(8,128)(2,1)}), bf16[8,384,128]{2,1,0:T(8,128)(2,1)}, u32[]{:S(2)}, u32[]{:S(2)}) %all-to-all-start.1) | async-done | bytes 786464 | tf_op jit(solution)/shard_map/all_to_all | solution.py:383
  59.7 9.3 %attend_forward.1 = (bf16[1024,128]{1,0:T(8,128)(2,1)}, f32[2,1024]{1,0:T(2,128)}) custom-call(s32[1,1]{1,0:T(1,128)} %bitcast.5.count_ref, bf16[8,384,128]{2,1,0:T(8,128)(2,1)} %all-to-all-done.1.qkv_ref), custom_call_target="tpu_custom_call" | custom-call | flops 60000002048 | bytes 1048576 | tf_op jit(solution)/shard_map/attend_forward/pallas_call | solution.py:257
  68.9 4.0 %all-to-all-start.2 = ((bf16[8,128,128]{2,1,0:T(8,128)(2,1)}), bf16[8,128,128]{2,1,0:T(8,128)(2,1)S(1)}, u32[]{:S(2)}, u32[]{:S(2)}) async-start(bf16[8,128,128]{2,1,0:T(8,128)(2,1)} %bitcast.80), calls=%async_computation.2 | async-start | bytes 524288 | tf_op jit(solution)/shard_map/all_to_all | solution.py:383
  76.2 4.3 %all-to-all-done.2.att_ref.refs_12_ = bf16[8,128,128]{2,1,0:T(8,128)(2,1)S(1)} async-done(((bf16[8,128,128]{2,1,0:T(8,128)(2,1)}), bf16[8,128,128]{2,1,0:T(8,128)(2,1)S(1)}, u32[]{:S(2)}, u32[]{:S(2)}) %all-to-all-start.2) | async-done | bytes 262176 | tf_op jit(solution)/shard_map/all_to_all | solution.py:383
  80.6 2.3 collective-permute-start
  84.5 17.9 %trunk_middle.1 = (bf16[128,1024]{1,0:T(8,128)(2,1)}, bf16[128,1024]{1,0:T(8,128)(2,1)}, bf16[128,2304]{1,0:T(8,128)(2,1)}, bf16[128,2304]{1,0:T(8,128)(2,1)}, b...) custom-call(s32[5]{0:T(128)} %stack.23.place_ref, ...), custom_call_target="tpu_custom_call" | custom-call | flops 99999997952 | bytes 1048576 | tf_op jit(solution)/shard_map/trunk_middle/pallas_call | solution.py:678
  102.5 3.4 %all-to-all-start.3 = ((bf16[8,128,128]{2,1,0:T(8,128)(2,1)}), bf16[8,128,128]{2,1,0:T(8,128)(2,1)S(1)}, u32[]{:S(2)}, u32[]{:S(2)}) async-start(bf16[8,128,128]{2,1,0:T(8,128)(2,1)} %get-tuple-element.163), calls=%async_computation.3 | async-start | bytes 524288 | tf_op jit(solution)/shard_map/all_to_all | solution.py:383
  105.9 1.4 collective-permute-start.6
  108.1 2.0 collective-permute-start.9
  110.1 3.8 %all-to-all-done.3 = bf16[8,128,128]{2,1,0:T(8,128)(2,1)S(1)} async-done(((bf16[8,128,128]{2,1,0:T(8,128)(2,1)}), bf16[8,128,128]{2,1,0:T(8,128)(2,1)S(1)}, u32[]{:S(2)}, u32[]{:S(2)}) %all-to-all-start.3) | async-done | bytes 262176 | tf_op jit(solution)/shard_map/all_to_all | solution.py:383
  114.5 11.0 %attend_backward.1 = bf16[8,384,128]{2,1,0:T(8,128)(2,1)} custom-call(s32[1,1]{1,0:T(1,128)} %bitcast.5.count_ref, bf16[8,384,128]{2,1,0:T(8,128)(2,1)} %all-to-all-done.1.qkv_ref, bf16[1024,128]{1,0:T(8,128)(2,1)} %bitcast.81, f32[2,1024]{1,0:T(2,128)} %get-tuple-element.164.lse_ref), custom_call_target="tpu_custom_call" | custom-call | flops 99999997952 | bytes 1048576 | tf_op jit(solution)/shard_map/attend_backward/pallas_call | solution.py:325
  125.6 2.0 collective-permute-start.11
  127.6 4.4 %all-to-all-start.4 = ((bf16[8,384,128]{2,1,0:T(8,128)(2,1)}), bf16[8,384,128]{2,1,0:T(8,128)(2,1)}, u32[]{:S(2)}, u32[]{:S(2)}) async-start(bf16[8,384,128]{2,1,0:T(8,128)(2,1)} %attend_backward.1), calls=%async_computation.4 | async-start | bytes 1572864 | tf_op jit(solution)/shard_map/all_to_all | solution.py:383
  132.1 7.9 %collective-permute-done.9.refs_3_ = bf16[128,2304]{1,0:T(8,128)(2,1)} collective-permute-done((bf16[128,2304]{1,0:T(8,128)(2,1)}, bf16[128,2304]{1,0:T(8,128)(2,1)}, u32[]{:S(2)}, u32[]{:S(2)}) %collective-permute-start.9) | collective-permute-done | bytes 589856 | tf_op jit(solution)/shard_map/ppermute | solution.py:427
  140.7 5.0 %weight_grads.3 = bf16[2,128,2304]{2,1,0:T(8,128)(2,1)} custom-call(s32[5]{0:T(128)} %stack.23.place_ref, bf16[128,2304]{1,0:T(8,128)(2,1)} %get-tuple-element.180.refs_0_, bf16[128,2304]{1,0:T(8,128)(2,1)} %copy-done.21, bf16[128,2304]{1,0:T(8,128)(2,1)} %copy-done.22, bf16[128,2304]{1,0:T(8,128)(2,1)} %collective-permute-done.9.refs_3_, ...), custom_call_target="tpu_custom_call" | custom-call | flops 1999999991808 | bytes 1048576 | tf_op jit(solution)/shard_map/weight_grads/pallas_call | solution.py:440
  147.0 6.9 %weight_grads.4 = (bf16[2,128,2304]{2,1,0:T(8,128)(2,1)}, bf16[2,128,2304]{2,1,0:T(8,128)(2,1)}, bf16[2,128,2304]{2,1,0:T(8,128)(2,1)}) custom-call(s32[5]{0:T(128)} %stack.23.place_ref, bf16[128,2304]{1,0:T(8,128)(2,1)} %get-tuple-element.180.refs_0_, bf16[128,2304]{1,0:T(8,128)(2,1)} %copy-done.21, bf16[128,2304]{1,0:T(8,128)(2,1)} %copy-done.22, ...), custom_call_target="tpu_custom_call" | custom-call | flops 1999999991808 | bytes 1048576 | tf_op jit(solution)/shard_map/weight_grads/pallas_call | solution.py:440
  153.9 8.7 %trunk_back.1 = (bf16[128,1024]{1,0:T(8,128)(2,1)}, f32[1,1024]{1,0:T(1,128)}, bf16[128,1024]{1,0:T(8,128)(2,1)}, bf16[128,1024]{1,0:T(8,128)(2,1)}, bf16[128,10...) custom-call(s32[5]{0:T(128)} %stack.23.place_ref, bf16[8,384,128]{2,1,0:T(8,128)(2,1)} %all-to-all-done.4.grads_ref, ...), custom_call_target="tpu_custom_call" | custom-call | flops 99999997952 | bytes 1048576 | tf_op jit(solution)/shard_map/trunk_back/pallas_call | solution.py:774
  162.6 8.9 %front_backward.1 = (bf16[768,128]{1,0:T(8,128)(2,1)}, bf16[2,832,256]{2,1,0:T(8,128)(2,1)}, bf16[2,832,256]{2,1,0:T(8,128)(2,1)}) custom-call(s32[5]{0:T(128)} %stack.23.place_ref, s32[1,48]{1,0:T(1,128)} %constant_dynamic-slice_fusion.4.ids_ref, bf16[768,128]{1,0:T(8,128)(2,1)} %get-tuple-element.161.x_ref, f32[768,128]{1,0:T(8,128)} %get-tuple-element.162.p_ref, ...), custom_call_target="tpu_custom_call" | custom-call | flops 100000000 | bytes 1048576 | tf_op jit(solution)/shard_map/front_backward/pallas_call | solution.py:200
  171.5 4.2 %all-to-all-start.5 = ((bf16[4,192,128]{2,1,0:T(8,128)(2,1)}), bf16[4,192,128]{2,1,0:T(8,128)(2,1)}, u32[]{:S(2)}, u32[]{:S(2)}) async-start(bf16[4,192,128]{2,1,0:T(8,128)(2,1)} %bitcast.83), calls=%async_computation.5 | async-start | bytes 393216 | tf_op jit(solution)/shard_map/all_to_all | solution.py:1051
  175.8 1.4 collective-permute-start.16
  177.9 2.9 pair_sum.2
  182.3 2.4 core_sum.1
  186.2 5.8 %collective-permute-done.17.refs_7_ = bf16[128,1024]{1,0:T(8,128)(2,1)} collective-permute-done((bf16[128,1024]{1,0:T(8,128)(2,1)}, bf16[128,1024]{1,0:T(8,128)(2,1)}, u32[]{:S(2)}, u32[]{:S(2)}) %collective-permute-start.17) | collective-permute-done | bytes 262176 | tf_op jit(solution)/shard_map/ppermute | solution.py:427
  192.0 4.7 %weight_grads.5 = (bf16[4,128,1024]{2,1,0:T(8,128)(2,1)}, bf16[2,128,1024]{2,1,0:T(8,128)(2,1)}, bf16[2,128,1024]{2,1,0:T(8,128)(2,1)}) custom-call(s32[5]{0:T(128)} %stack.23.place_ref, bf16[128,3072]{1,0:T(8,128)(2,1)} %pad_maximum_fusion.refs_4_.refs_0_, bf16[128,3072]{1,0:T(8,128)(2,1)} %copy-done.19, ...), custom_call_target="tpu_custom_call" | custom-call | flops 1999999991808 | bytes 1048576 | tf_op jit(solution)/shard_map/weight_grads/pallas_call | solution.py:440
  196.7 4.2 %collective-permute-done.14 = bf16[832,256]{1,0:T(8,128)(2,1)} collective-permute-done((bf16[832,256]{1,0:T(8,128)(2,1)}, bf16[832,256]{1,0:T(8,128)(2,1)}, u32[]{:S(2)}, u32[]{:S(2)}) %collective-permute-start.14) | collective-permute-done | bytes 426016 | tf_op jit(solution)/shard_map/ppermute | solution.py:427
  201.0 2.0 x_sum.1
  202.9 1.5 collective-permute-start.24
  204.4 3.8 %collective-permute-done.19.got_ref = bf16[2,128,2304]{2,1,0:T(8,128)(2,1)} collective-permute-done((bf16[2,128,2304]{2,1,0:T(8,128)(2,1)}, bf16[2,128,2304]{2,1,0:T(8,128)(2,1)}, u32[]{:S(2)}, u32[]{:S(2)}) %collective-permute-start.19) | collective-permute-done | bytes 1179680 | tf_op jit(solution)/shard_map/ppermute | solution.py:427
  208.2 4.6 %collective-permute-done.18 = bf16[416,256]{1,0:T(8,128)(2,1)} collective-permute-done((bf16[416,256]{1,0:T(8,128)(2,1)}, bf16[416,256]{1,0:T(8,128)(2,1)}, u32[]{:S(2)}, u32[]{:S(2)}) %collective-permute-start.18) | collective-permute-done | bytes 213024 | tf_op jit(solution)/shard_map/ppermute | solution.py:427
  212.8 3.2 %z_first_sum.2 = (bf16[128,2304]{1,0:T(8,128)(2,1)}, bf16[128,2304]{1,0:T(8,128)(2,1)}) custom-call(s32[5]{0:T(128)} %stack.23.place_ref, bf16[2,128,2304]{2,1,0:T(8,128)(2,1)} %get-tuple-element.185.near_ref, bf16[2,128,2304]{2,1,0:T(8,128)(2,1)} %collective-permute-done.19.got_ref, bf16[2,128,2304]{2,1,0:T(8,128)(2,1)} %collective-permute-done.20.far_ref), custom_call_target="tpu_custom_call" | custom-call | flops 199999995904 | bytes 1048576 | tf_op jit(solution)/shard_map/z_first_sum/pallas_call | solution.py:440
  216.0 1.7 z_pieces.1
  218.9 2.1 collective-permute-start.22
  222.5 12.7 %collective-permute-done.24.got_ref = bf16[4,128,1024]{2,1,0:T(8,128)(2,1)} collective-permute-done((bf16[4,128,1024]{2,1,0:T(8,128)(2,1)}, bf16[4,128,1024]{2,1,0:T(8,128)(2,1)}, u32[]{:S(2)}, u32[]{:S(2)}) %collective-permute-start.24) | collective-permute-done | bytes 1048608 | tf_op jit(solution)/shard_map/ppermute | solution.py:427
  235.2 2.3 pair_sum.3
  237.6 1.5 z_sum.1.refs_0_
  240.3 2.1 collective-permute-start.26
  242.9 2.0 collective-permute-done.25.refs_1_
  245.0 10.0 %collective-permute-done.26.refs_2_ = bf16[104,256]{1,0:T(8,128)(2,1)S(1)} collective-permute-done((bf16[104,256]{1,0:T(8,128)(2,1)}, bf16[104,256]{1,0:T(8,128)(2,1)S(1)}, u32[]{:S(2)}, u32[]{:S(2)}) %collective-permute-start.26) | collective-permute-done | bytes 53280 | tf_op jit(solution)/shard_map/ppermute | solution.py:427
  255.7 1.6 z_join.1
  257.5 2.2 z_last_sum.2.refs_0_
  260.9 1.7 collective-permute-done.29.other_ref
  262.6 1.8 y_join.1
  265.8 1.6 collective-permute-done.32.far_ref
  267.4 2.4 z_first_sum.3
  269.8 1.4 collective-permute-start.33
  271.2 2.9 collective-permute-start.30
  274.1 9.7 %collective-permute-done.33.got_ref = bf16[128,1024]{1,0:T(8,128)(2,1)S(1)} collective-permute-done((bf16[128,1024]{1,0:T(8,128)(2,1)}, bf16[128,1024]{1,0:T(8,128)(2,1)S(1)}, u32[]{:S(2)}, u32[]{:S(2)}) %collective-permute-start.33) | collective-permute-done | bytes 262176 | tf_op jit(solution)/shard_map/ppermute | solution.py:427
  284.9 1.8 z_last_sum.3.refs_0_
  290.0 4.3 %collective-permute-done.37.refs_2_ = bf16[128,1024]{1,0:T(8,128)(2,1)} collective-permute-done((bf16[128,1024]{1,0:T(8,128)(2,1)}, bf16[128,1024]{1,0:T(8,128)(2,1)}, u32[]{:S(2)}, u32[]{:S(2)}) %collective-permute-start.37) | collective-permute-done | bytes 262176 | tf_op jit(solution)/shard_map/ppermute | solution.py:427
  295.7 6.2 %front_last.1 = (f32[128,1024]{1,0:T(8,128)}, f32[768,128]{1,0:T(8,128)}, f32[48,128]{1,0:T(8,128)}, f32[128,1024]{1,0:T(8,128)}, f32[128,1024]{1,0:T(8,128)}, /...) custom-call(s32[5]{0:T(128)} %stack.23.place_ref, bf16[832,256]{1,0:T(8,128)(2,1)} %bitcast.34.m0, ...), custom_call_target="tpu_custom_call" | custom-call | flops 199999995904 | bytes 1048576 | tf_op jit(solution)/shard_map/front_last/pallas_call | solution.py:440
  301.9 2.6 join.2
  304.6 4.0 %join.3 = (f32[4,128,1024]{2,1,0:T(8,128)}, f32[128,4096]{1,0:T(8,128)}, f32[128,1024]{1,0:T(8,128)}) custom-call(s32[5]{0:T(128)} %stack.23.place_ref, bf16[128,2304]{1,0:T(8,128)(2,1)} %z_last_sum.2.refs_0_, bf16[128,2304]{1,0:T(8,128)(2,1)} %collective-permute-done.39.refs_1_, bf16[128,2304]{1,0:T(8,128)(2,1)} %collective-permute-done.34.refs_2_, ...), custom_call_target="tpu_custom_call" | custom-call | flops 199999995904 | bytes 1048576 | tf_op jit(solution)/shard_map/join/pallas_call | solution.py:440
  308.6 1.6 copy.54
  (165 shorter events, 41.1 us)
Async XLA Ops:
  0.6 17.5 %copy-start = (s32[4,48]{1,0:T(4,128)S(1)}, s32[4,48]{1,0:T(4,128)}, u32[]{:S(2)}) copy-start(s32[4,48]{1,0:T(4,128)} %param.19) | copy-start | bytes 2308
  0.7 18.0 %all-to-all-start = ((bf16[4,192,128]{2,1,0:T(8,128)(2,1)}), bf16[4,192,128]{2,1,0:T(8,128)(2,1)S(1)}, u32[]{:S(2)}, u32[]{:S(2)}) async-start(bf16[4,192,128]{2,1,0:T(8,128)(2,1)} %bitcast.82), calls=%async_computation | async-start | bytes 393216 | tf_op jit(solution)/shard_map/all_to_all | solution.py:914
  13.2 4.9 %copy-start.16 = (bf16[1024]{0:T(1024)(128)(2,1)S(1)}, bf16[1024]{0:T(1024)(128)(2,1)}, u32[]{:S(2)}) copy-start(bf16[1024]{0:T(1024)(128)(2,1)} %param.27) | copy-start | bytes 6148
  16.3 23.3 %copy-start.7 = (bf16[128,1024]{1,0:T(8,128)(2,1)}, bf16[128,1024]{1,0:T(8,128)(2,1)S(1)}, u32[]{:S(2)}) copy-start(bf16[128,1024]{1,0:T(8,128)(2,1)S(1)} %fusion.2.og_ref) | copy-start | bytes 786436
  18.1 10.1 %copy-start.15 = (f32[1024]{0:T(1024)}, f32[1024]{0:T(1024)S(1)}, u32[]{:S(2)}) copy-start(f32[1024]{0:T(1024)S(1)} %convert_element_type.97) | copy-start | bytes 12292
  28.0 4.2 %copy-start.3 = (f32[128,1024]{1,0:T(8,128)}, f32[128,1024]{1,0:T(8,128)S(1)}, u32[]{:S(2)}) copy-start(f32[128,1024]{1,0:T(8,128)S(1)} %get-tuple-element.272.front_ref) | copy-start | bytes 1572868
  32.2 7.4 %copy-start.8 = (bf16[128,1024]{1,0:T(8,128)(2,1)S(1)}, bf16[128,1024]{1,0:T(8,128)(2,1)}, u32[]{:S(2)}) copy-start(bf16[128,1024]{1,0:T(8,128)(2,1)} %get-tuple-element.141) | copy-start | bytes 786436
  33.5 26.2 %all-to-all-start.1 = ((bf16[8,384,128]{2,1,0:T(8,128)(2,1)}), bf16[8,384,128]{2,1,0:T(8,128)(2,1)}, u32[]{:S(2)}, u32[]{:S(2)}) async-start(bf16[8,384,128]{2,1,0:T(8,128)(2,1)} %bitcast.15), calls=%async_computation.1 | async-start | bytes 1572864 | tf_op jit(solution)/shard_map/all_to_all | solution.py:383
  40.7 8.4 %copy-start.6 = (bf16[48,16,1024]{2,1,0:T(8,128)(2,1)S(1)}, bf16[48,16,1024]{2,1,0:T(8,128)(2,1)}, u32[]{:S(2)}) copy-start(bf16[48,16,1024]{2,1,0:T(8,128)(2,1)} %param.20) | copy-start | bytes 4718596
  40.7 35.6 %collective-permute-start.4 = (bf16[128,3072]{1,0:T(8,128)(2,1)}, bf16[128,3072]{1,0:T(8,128)(2,1)}, u32[]{:S(2)}, u32[]{:S(2)}) collective-permute-start(bf16[128,3072]{1,0:T(8,128)(2,1)} %pad_maximum_fusion.refs_4_.refs_0_), channel_id=1, source_target_pairs={{0,2},{1,3},{2,0},{3,1},{4,6},{5,7},{6,4},{7,5},{8,10},{9,11},{10,... | collective-permute-start | bytes 2359304 | tf_op jit(solution)/shard_map/ppermute | solution.py:427
  59.7 13.3 %copy-start.17 = (bf16[1024]{0:T(1024)(128)(2,1)S(1)}, bf16[1024]{0:T(1024)(128)(2,1)}, u32[]{:S(2)}) copy-start(bf16[1024]{0:T(1024)(128)(2,1)} %param.30) | copy-start | bytes 6148
  68.9 11.6 %all-to-all-start.2 = ((bf16[8,128,128]{2,1,0:T(8,128)(2,1)}), bf16[8,128,128]{2,1,0:T(8,128)(2,1)S(1)}, u32[]{:S(2)}, u32[]{:S(2)}) async-start(bf16[8,128,128]{2,1,0:T(8,128)(2,1)} %bitcast.80), calls=%async_computation.2 | async-start | bytes 524288 | tf_op jit(solution)/shard_map/all_to_all | solution.py:383
  75.5 27.0 %collective-permute-start.3 = (bf16[128,3072]{1,0:T(8,128)(2,1)}, bf16[128,3072]{1,0:T(8,128)(2,1)S(1)}, u32[]{:S(2)}, u32[]{:S(2)}) collective-permute-start(bf16[128,3072]{1,0:T(8,128)(2,1)} %pad_maximum_fusion.refs_4_.refs_0_), channel_id=1, source_target_pairs={{0,1},{1,0},{2,3},{3,2},{4,5},{5,4},{6,7},{7,6},{8,9},{9,8},{10,11... | collective-permute-start | bytes 2359304 | tf_op jit(solution)/shard_map/ppermute | solution.py:427
  76.2 26.2 %collective-permute-start.5 = (bf16[128,3072]{1,0:T(8,128)(2,1)}, bf16[128,3072]{1,0:T(8,128)(2,1)S(1)}, u32[]{:S(2)}, u32[]{:S(2)}) collective-permute-start(bf16[128,3072]{1,0:T(8,128)(2,1)} %collective-permute-done.4.refs_6_.refs_2_), channel_id=1, source_target_pairs={{0,1},{1,0},{2,3},{3,2},{4,5},{5,4},{6,7},{7,6},{8,9},{9,8},{10,11... | collective-permute-start | bytes 2359304 | tf_op jit(solution)/shard_map/ppermute | solution.py:427
  80.6 21.9 %collective-permute-start = (bf16[8,128,128]{2,1,0:T(8,128)(2,1)S(1)}, bf16[8,128,128]{2,1,0:T(8,128)(2,1)S(1)}, u32[]{:S(2)}, u32[]{:S(2)}) collective-permute-start(bf16[8,128,128]{2,1,0:T(8,128)(2,1)S(1)} %all-to-all-done.2.att_ref.refs_12_), channel_id=1, source_target_pairs={{0,1},{1,0},{2,3},{3,2},{4,5},{5,4},{6,7},{7,6},{8,9},{9,8},{10,11... | collective-permute-start | bytes 786440 | tf_op jit(solution)/shard_map/ppermute | solution.py:427
  82.9 19.6 %collective-permute-start.1 = (bf16[8,128,128]{2,1,0:T(8,128)(2,1)S(1)}, bf16[8,128,128]{2,1,0:T(8,128)(2,1)S(1)}, u32[]{:S(2)}, u32[]{:S(2)}) collective-permute-start(bf16[8,128,128]{2,1,0:T(8,128)(2,1)S(1)} %all-to-all-done.2.att_ref.refs_12_), channel_id=1, source_target_pairs={{0,2},{1,3},{2,0},{3,1},{4,6},{5,7},{6,4},{7,5},{8,10},{9,11},{10,... | collective-permute-start | bytes 786440 | tf_op jit(solution)/shard_map/ppermute | solution.py:427
  84.2 18.3 %collective-permute-start.2 = (bf16[8,128,128]{2,1,0:T(8,128)(2,1)S(1)}, bf16[8,128,128]{2,1,0:T(8,128)(2,1)S(1)}, u32[]{:S(2)}, u32[]{:S(2)}) collective-permute-start(bf16[8,128,128]{2,1,0:T(8,128)(2,1)S(1)} %all-to-all-done.2.att_ref.refs_12_), channel_id=1, source_target_pairs={{0,3},{1,2},{2,1},{3,0},{4,7},{5,6},{6,5},{7,4},{8,11},{9,10},{10,... | collective-permute-start | bytes 786440 | tf_op jit(solution)/shard_map/ppermute | solution.py:427
  102.4 23.1 %copy-start.19 = (bf16[128,3072]{1,0:T(8,128)(2,1)}, bf16[128,3072]{1,0:T(8,128)(2,1)S(1)}, u32[]{:S(2)}) copy-start(bf16[128,3072]{1,0:T(8,128)(2,1)S(1)} %collective-permute-done.3.refs_5_.refs_1_) | copy-start | bytes 2359300
  102.4 23.1 %copy-start.20 = (bf16[128,3072]{1,0:T(8,128)(2,1)}, bf16[128,3072]{1,0:T(8,128)(2,1)S(1)}, u32[]{:S(2)}) copy-start(bf16[128,3072]{1,0:T(8,128)(2,1)S(1)} %collective-permute-done.5.refs_7_.refs_3_) | copy-start | bytes 2359300
  102.5 23.1 %copy-start.23 = (bf16[8,128,128]{2,1,0:T(8,128)(2,1)}, bf16[8,128,128]{2,1,0:T(8,128)(2,1)S(1)}, u32[]{:S(2)}) copy-start(bf16[8,128,128]{2,1,0:T(8,128)(2,1)S(1)} %collective-permute-done.refs_13_) | copy-start | bytes 786436
  102.5 23.0 %copy-start.24 = (bf16[8,128,128]{2,1,0:T(8,128)(2,1)}, bf16[8,128,128]{2,1,0:T(8,128)(2,1)S(1)}, u32[]{:S(2)}) copy-start(bf16[8,128,128]{2,1,0:T(8,128)(2,1)S(1)} %collective-permute-done.1.refs_14_) | copy-start | bytes 786436
  102.5 4.8 %copy-start.25 = (bf16[8,128,128]{2,1,0:T(8,128)(2,1)}, bf16[8,128,128]{2,1,0:T(8,128)(2,1)S(1)}, u32[]{:S(2)}) copy-start(bf16[8,128,128]{2,1,0:T(8,128)(2,1)S(1)} %collective-permute-done.2.refs_15_) | copy-start | bytes 786436
  102.5 11.3 %all-to-all-start.3 = ((bf16[8,128,128]{2,1,0:T(8,128)(2,1)}), bf16[8,128,128]{2,1,0:T(8,128)(2,1)S(1)}, u32[]{:S(2)}, u32[]{:S(2)}) async-start(bf16[8,128,128]{2,1,0:T(8,128)(2,1)} %get-tuple-element.163), calls=%async_computation.3 | async-start | bytes 524288 | tf_op jit(solution)/shard_map/all_to_all | solution.py:383
  105.9 19.6 %collective-permute-start.6 = (bf16[128,1024]{1,0:T(8,128)(2,1)}, bf16[128,1024]{1,0:T(8,128)(2,1)}, u32[]{:S(2)}, u32[]{:S(2)}) collective-permute-start(bf16[128,1024]{1,0:T(8,128)(2,1)} %get-tuple-element.165.refs_8_), channel_id=1, source_target_pairs={{0,2},{1,3},{2,0},{3,1},{4,6},{5,7},{6,4},{7,5},{8,10},{9,11},{10,... | collective-permute-start | bytes 786440 | tf_op jit(solution)/shard_map/ppermute | solution.py:427
  107.3 24.7 %collective-permute-start.10 = (bf16[128,1024]{1,0:T(8,128)(2,1)}, bf16[128,1024]{1,0:T(8,128)(2,1)}, u32[]{:S(2)}, u32[]{:S(2)}) collective-permute-start(bf16[128,1024]{1,0:T(8,128)(2,1)} %get-tuple-element.165.refs_8_), channel_id=1, source_target_pairs={{0,1},{1,0},{2,3},{3,2},{4,5},{5,4},{6,7},{7,6},{8,9},{9,8},{10,11... | collective-permute-start | bytes 786440 | tf_op jit(solution)/shard_map/ppermute | solution.py:427
  107.9 24.1 %collective-permute-start.7 = (bf16[128,2304]{1,0:T(8,128)(2,1)}, bf16[128,2304]{1,0:T(8,128)(2,1)S(1)}, u32[]{:S(2)}, u32[]{:S(2)}) collective-permute-start(bf16[128,2304]{1,0:T(8,128)(2,1)} %get-tuple-element.168), channel_id=1, source_target_pairs={{0,1},{1,0},{2,3},{3,2},{4,5},{5,4},{6,7},{7,6},{8,9},{9,8},{10,11... | collective-permute-start | bytes 1769480 | tf_op jit(solution)/shard_map/ppermute | solution.py:427
  107.9 24.1 %collective-permute-start.8 = (bf16[128,2304]{1,0:T(8,128)(2,1)}, bf16[128,2304]{1,0:T(8,128)(2,1)S(1)}, u32[]{:S(2)}, u32[]{:S(2)}) collective-permute-start(bf16[128,2304]{1,0:T(8,128)(2,1)} %get-tuple-element.169), channel_id=1, source_target_pairs={{0,2},{1,3},{2,0},{3,1},{4,6},{5,7},{6,4},{7,5},{8,10},{9,11},{10,... | collective-permute-start | bytes 1769480 | tf_op jit(solution)/shard_map/ppermute | solution.py:427
  108.1 31.8 %collective-permute-start.9 = (bf16[128,2304]{1,0:T(8,128)(2,1)}, bf16[128,2304]{1,0:T(8,128)(2,1)}, u32[]{:S(2)}, u32[]{:S(2)}) collective-permute-start(bf16[128,2304]{1,0:T(8,128)(2,1)} %get-tuple-element.170), channel_id=1, source_target_pairs={{0,3},{1,2},{2,1},{3,0},{4,7},{5,6},{6,5},{7,4},{8,11},{9,10},{10,... | collective-permute-start | bytes 1769480 | tf_op jit(solution)/shard_map/ppermute | solution.py:427
  125.6 14.4 %collective-permute-start.11 = (bf16[128,1024]{1,0:T(8,128)(2,1)}, bf16[128,1024]{1,0:T(8,128)(2,1)S(1)}, u32[]{:S(2)}, u32[]{:S(2)}) collective-permute-start(bf16[128,1024]{1,0:T(8,128)(2,1)} %collective-permute-done.6.refs_10_), channel_id=1, source_target_pairs={{0,1},{1,0},{2,3},{3,2},{4,5},{5,4},{6,7},{7,6},{8,9},{9,8},{10,11... | collective-permute-start | bytes 786440 | tf_op jit(solution)/shard_map/ppermute | solution.py:427
  127.6 26.3 %all-to-all-start.4 = ((bf16[8,384,128]{2,1,0:T(8,128)(2,1)}), bf16[8,384,128]{2,1,0:T(8,128)(2,1)}, u32[]{:S(2)}, u32[]{:S(2)}) async-start(bf16[8,384,128]{2,1,0:T(8,128)(2,1)} %attend_backward.1), calls=%async_computation.4 | async-start | bytes 1572864 | tf_op jit(solution)/shard_map/all_to_all | solution.py:383
  132.0 7.9 %copy-start.21 = (bf16[128,2304]{1,0:T(8,128)(2,1)}, bf16[128,2304]{1,0:T(8,128)(2,1)S(1)}, u32[]{:S(2)}) copy-start(bf16[128,2304]{1,0:T(8,128)(2,1)S(1)} %collective-permute-done.7.refs_1_) | copy-start | bytes 1769476
  132.0 7.9 %copy-start.22 = (bf16[128,2304]{1,0:T(8,128)(2,1)}, bf16[128,2304]{1,0:T(8,128)(2,1)S(1)}, u32[]{:S(2)}) copy-start(bf16[128,2304]{1,0:T(8,128)(2,1)S(1)} %collective-permute-done.8.refs_2_) | copy-start | bytes 1769476
  145.7 32.2 %collective-permute-start.12 = (bf16[2,128,2304]{2,1,0:T(8,128)(2,1)}, bf16[2,128,2304]{2,1,0:T(8,128)(2,1)}, u32[]{:S(2)}, u32[]{:S(2)}) collective-permute-start(bf16[2,128,2304]{2,1,0:T(8,128)(2,1)} %weight_grads.3), channel_id=1, source_target_pairs={{0,4},{4,0},{8,12},{12,8},{16,20},{20,16},{24,28},{28,24},{1,5},{5... | collective-permute-start | bytes 3538952 | tf_op jit(solution)/shard_map/ppermute | solution.py:427
  171.5 25.3 %all-to-all-start.5 = ((bf16[4,192,128]{2,1,0:T(8,128)(2,1)}), bf16[4,192,128]{2,1,0:T(8,128)(2,1)}, u32[]{:S(2)}, u32[]{:S(2)}) async-start(bf16[4,192,128]{2,1,0:T(8,128)(2,1)} %bitcast.83), calls=%async_computation.5 | async-start | bytes 393216 | tf_op jit(solution)/shard_map/all_to_all | solution.py:1051
  175.7 9.1 %collective-permute-start.15 = (bf16[128,1024]{1,0:T(8,128)(2,1)}, bf16[128,1024]{1,0:T(8,128)(2,1)}, u32[]{:S(2)}, u32[]{:S(2)}) collective-permute-start(bf16[128,1024]{1,0:T(8,128)(2,1)} %get-tuple-element.207), channel_id=1, source_target_pairs={{0,1},{1,0},{2,3},{3,2},{4,5},{5,4},{6,7},{7,6},{8,9},{9,8},{10,11... | collective-permute-start | bytes 786440 | tf_op jit(solution)/shard_map/ppermute | solution.py:427
  175.8 10.4 %collective-permute-start.16 = (bf16[128,1024]{1,0:T(8,128)(2,1)}, bf16[128,1024]{1,0:T(8,128)(2,1)}, u32[]{:S(2)}, u32[]{:S(2)}) collective-permute-start(bf16[128,1024]{1,0:T(8,128)(2,1)} %get-tuple-element.208), channel_id=1, source_target_pairs={{0,2},{1,3},{2,0},{3,1},{4,6},{5,7},{6,4},{7,5},{8,10},{9,11},{10,... | collective-permute-start | bytes 786440 | tf_op jit(solution)/shard_map/ppermute | solution.py:427
  177.2 14.8 %collective-permute-start.17 = (bf16[128,1024]{1,0:T(8,128)(2,1)}, bf16[128,1024]{1,0:T(8,128)(2,1)}, u32[]{:S(2)}, u32[]{:S(2)}) collective-permute-start(bf16[128,1024]{1,0:T(8,128)(2,1)} %get-tuple-element.209), channel_id=1, source_target_pairs={{0,3},{1,2},{2,1},{3,0},{4,7},{5,6},{6,5},{7,4},{8,11},{9,10},{10,... | collective-permute-start | bytes 786440 | tf_op jit(solution)/shard_map/ppermute | solution.py:427
  177.9 3.1 %collective-permute-start.13 = (bf16[2,832,256]{2,1,0:T(8,128)(2,1)}, bf16[2,832,256]{2,1,0:T(8,128)(2,1)}, u32[]{:S(2)}, u32[]{:S(2)}) collective-permute-start(bf16[2,832,256]{2,1,0:T(8,128)(2,1)} %get-tuple-element.202), channel_id=1, source_target_pairs={{0,1},{1,0},{2,3},{3,2},{4,5},{5,4},{6,7},{7,6},{8,9},{9,8},{10,11... | collective-permute-start | bytes 2555912 | tf_op jit(solution)/shard_map/ppermute | solution.py:427
  180.8 27.3 %collective-permute-start.19 = (bf16[2,128,2304]{2,1,0:T(8,128)(2,1)}, bf16[2,128,2304]{2,1,0:T(8,128)(2,1)}, u32[]{:S(2)}, u32[]{:S(2)}) collective-permute-start(bf16[2,128,2304]{2,1,0:T(8,128)(2,1)} %get-tuple-element.216), channel_id=1, source_target_pairs={{0,4},{4,0},{8,12},{12,8},{16,20},{20,16},{24,28},{28,24},{1,5},{5... | collective-permute-start | bytes 3538952 | tf_op jit(solution)/shard_map/ppermute | solution.py:427
  181.0 27.2 %collective-permute-start.20 = (bf16[2,128,2304]{2,1,0:T(8,128)(2,1)}, bf16[2,128,2304]{2,1,0:T(8,128)(2,1)}, u32[]{:S(2)}, u32[]{:S(2)}) collective-permute-start(bf16[2,128,2304]{2,1,0:T(8,128)(2,1)} %pair_sum.2), channel_id=1, source_target_pairs={{0,8},{4,12},{8,0},{12,4},{16,24},{20,28},{24,16},{28,20},{1,9},{5... | collective-permute-start | bytes 3538952 | tf_op jit(solution)/shard_map/ppermute | solution.py:427
  184.8 16.2 %collective-permute-start.14 = (bf16[832,256]{1,0:T(8,128)(2,1)}, bf16[832,256]{1,0:T(8,128)(2,1)}, u32[]{:S(2)}, u32[]{:S(2)}) collective-permute-start(bf16[832,256]{1,0:T(8,128)(2,1)} %get-tuple-element.204), channel_id=1, source_target_pairs={{0,2},{1,3},{2,0},{3,1},{4,6},{5,7},{6,4},{7,5},{8,10},{9,11},{10,... | collective-permute-start | bytes 1277960 | tf_op jit(solution)/shard_map/ppermute | solution.py:427
  202.9 9.8 %collective-permute-start.18 = (bf16[416,256]{1,0:T(8,128)(2,1)}, bf16[416,256]{1,0:T(8,128)(2,1)}, u32[]{:S(2)}, u32[]{:S(2)}) collective-permute-start(bf16[416,256]{1,0:T(8,128)(2,1)} %get-tuple-element.214), channel_id=1, source_target_pairs={{0,4},{4,0},{8,12},{12,8},{16,20},{20,16},{24,28},{28,24},{1,5},{5... | collective-permute-start | bytes 638984 | tf_op jit(solution)/shard_map/ppermute | solution.py:427
  202.9 32.3 %collective-permute-start.24 = (bf16[4,128,1024]{2,1,0:T(8,128)(2,1)}, bf16[4,128,1024]{2,1,0:T(8,128)(2,1)}, u32[]{:S(2)}, u32[]{:S(2)}) collective-permute-start(bf16[4,128,1024]{2,1,0:T(8,128)(2,1)} %get-tuple-element.226), channel_id=1, source_target_pairs={{0,4},{4,0},{8,12},{12,8},{16,20},{20,16},{24,28},{28,24},{1,5},{5... | collective-permute-start | bytes 3145736 | tf_op jit(solution)/shard_map/ppermute | solution.py:427
  217.7 17.5 %collective-permute-start.21 = (bf16[104,256]{1,0:T(8,128)(2,1)}, bf16[104,256]{1,0:T(8,128)(2,1)}, u32[]{:S(2)}, u32[]{:S(2)}) collective-permute-start(bf16[104,256]{1,0:T(8,128)(2,1)} %get-tuple-element.223), channel_id=1, source_target_pairs={{0,8},{4,12},{8,0},{12,4},{16,24},{20,28},{24,16},{28,20},{1,9},{5... | collective-permute-start | bytes 159752 | tf_op jit(solution)/shard_map/ppermute | solution.py:427
  218.9 16.3 %collective-permute-start.22 = (bf16[104,256]{1,0:T(8,128)(2,1)}, bf16[104,256]{1,0:T(8,128)(2,1)}, u32[]{:S(2)}, u32[]{:S(2)}) collective-permute-start(bf16[104,256]{1,0:T(8,128)(2,1)} %get-tuple-element.224), channel_id=1, source_target_pairs={{0,16},{4,20},{8,24},{12,28},{16,0},{20,4},{24,8},{28,12},{1,17},{... | collective-permute-start | bytes 159752 | tf_op jit(solution)/shard_map/ppermute | solution.py:427
  221.0 14.2 %collective-permute-start.23 = (bf16[104,256]{1,0:T(8,128)(2,1)}, bf16[104,256]{1,0:T(8,128)(2,1)}, u32[]{:S(2)}, u32[]{:S(2)}) collective-permute-start(bf16[104,256]{1,0:T(8,128)(2,1)} %get-tuple-element.225), channel_id=1, source_target_pairs={{0,24},{4,28},{8,16},{12,20},{16,8},{20,12},{24,0},{28,4},{1,25},{... | collective-permute-start | bytes 159752 | tf_op jit(solution)/shard_map/ppermute | solution.py:427
  221.3 33.8 %collective-permute-start.28 = (bf16[128,2304]{1,0:T(8,128)(2,1)}, bf16[128,2304]{1,0:T(8,128)(2,1)}, u32[]{:S(2)}, u32[]{:S(2)}) collective-permute-start(bf16[128,2304]{1,0:T(8,128)(2,1)} %get-tuple-element.233), channel_id=1, source_target_pairs={{0,16},{4,20},{8,24},{12,28},{16,0},{20,4},{24,8},{28,12},{1,17},{... | collective-permute-start | bytes 1769480 | tf_op jit(solution)/shard_map/ppermute | solution.py:427
  239.1 5.9 %collective-permute-start.25 = (bf16[104,256]{1,0:T(8,128)(2,1)}, bf16[104,256]{1,0:T(8,128)(2,1)S(1)}, u32[]{:S(2)}, u32[]{:S(2)}) collective-permute-start(bf16[104,256]{1,0:T(8,128)(2,1)} %z_sum.1.refs_0_), channel_id=1, source_target_pairs={{0,8},{4,12},{8,0},{12,4},{16,24},{20,28},{24,16},{28,20},{1,9},{5... | collective-permute-start | bytes 159752 | tf_op jit(solution)/shard_map/ppermute | solution.py:427
  240.3 14.7 %collective-permute-start.26 = (bf16[104,256]{1,0:T(8,128)(2,1)}, bf16[104,256]{1,0:T(8,128)(2,1)S(1)}, u32[]{:S(2)}, u32[]{:S(2)}) collective-permute-start(bf16[104,256]{1,0:T(8,128)(2,1)} %z_sum.1.refs_0_), channel_id=1, source_target_pairs={{0,16},{4,20},{8,24},{12,28},{16,0},{20,4},{24,8},{28,12},{1,17},{... | collective-permute-start | bytes 159752 | tf_op jit(solution)/shard_map/ppermute | solution.py:427
  242.4 12.6 %collective-permute-start.27 = (bf16[104,256]{1,0:T(8,128)(2,1)}, bf16[104,256]{1,0:T(8,128)(2,1)S(1)}, u32[]{:S(2)}, u32[]{:S(2)}) collective-permute-start(bf16[104,256]{1,0:T(8,128)(2,1)} %z_sum.1.refs_0_), channel_id=1, source_target_pairs={{0,24},{4,28},{8,16},{12,20},{16,8},{20,12},{24,0},{28,4},{1,25},{... | collective-permute-start | bytes 159752 | tf_op jit(solution)/shard_map/ppermute | solution.py:427
  242.6 24.7 %collective-permute-start.32 = (bf16[2,128,1024]{2,1,0:T(8,128)(2,1)}, bf16[2,128,1024]{2,1,0:T(8,128)(2,1)}, u32[]{:S(2)}, u32[]{:S(2)}) collective-permute-start(bf16[2,128,1024]{2,1,0:T(8,128)(2,1)} %pair_sum.3), channel_id=1, source_target_pairs={{0,8},{4,12},{8,0},{12,4},{16,24},{20,28},{24,16},{28,20},{1,9},{5... | collective-permute-start | bytes 1572872 | tf_op jit(solution)/shard_map/ppermute | solution.py:427
  245.0 10.1 %copy-start.28 = (bf16[104,256]{1,0:T(8,128)(2,1)}, bf16[104,256]{1,0:T(8,128)(2,1)S(1)}, u32[]{:S(2)}) copy-start(bf16[104,256]{1,0:T(8,128)(2,1)S(1)} %collective-permute-done.25.refs_1_) | copy-start | bytes 159748
  257.3 5.3 %collective-permute-start.29 = (bf16[416,256]{1,0:T(8,128)(2,1)}, bf16[416,256]{1,0:T(8,128)(2,1)}, u32[]{:S(2)}, u32[]{:S(2)}) collective-permute-start(bf16[416,256]{1,0:T(8,128)(2,1)} %bitcast.88), channel_id=1, source_target_pairs={{0,4},{4,0},{8,12},{12,8},{16,20},{20,16},{24,28},{28,24},{1,5},{5... | collective-permute-start | bytes 638984 | tf_op jit(solution)/shard_map/ppermute | solution.py:427
  259.7 24.1 %collective-permute-start.34 = (bf16[128,2304]{1,0:T(8,128)(2,1)}, bf16[128,2304]{1,0:T(8,128)(2,1)}, u32[]{:S(2)}, u32[]{:S(2)}) collective-permute-start(bf16[128,2304]{1,0:T(8,128)(2,1)} %z_last_sum.2.refs_0_), channel_id=1, source_target_pairs={{0,2},{1,3},{2,0},{3,1},{4,6},{5,7},{6,4},{7,5},{8,10},{9,11},{10,... | collective-permute-start | bytes 1769480 | tf_op jit(solution)/shard_map/ppermute | solution.py:427
  264.4 19.4 %collective-permute-start.31 = (bf16[832,256]{1,0:T(8,128)(2,1)}, bf16[832,256]{1,0:T(8,128)(2,1)}, u32[]{:S(2)}, u32[]{:S(2)}) collective-permute-start(bf16[832,256]{1,0:T(8,128)(2,1)} %bitcast.34.m0), channel_id=1, source_target_pairs={{0,2},{1,3},{2,0},{3,1},{4,6},{5,7},{6,4},{7,5},{8,10},{9,11},{10,... | collective-permute-start | bytes 1277960 | tf_op jit(solution)/shard_map/ppermute | solution.py:427
  269.8 14.0 %collective-permute-start.33 = (bf16[128,1024]{1,0:T(8,128)(2,1)}, bf16[128,1024]{1,0:T(8,128)(2,1)S(1)}, u32[]{:S(2)}, u32[]{:S(2)}) collective-permute-start(bf16[128,1024]{1,0:T(8,128)(2,1)} %get-tuple-element.238), channel_id=1, source_target_pairs={{0,16},{4,20},{8,24},{12,28},{16,0},{20,4},{24,8},{28,12},{1,17},{... | collective-permute-start | bytes 786440 | tf_op jit(solution)/shard_map/ppermute | solution.py:427
  271.2 18.4 %collective-permute-start.30 = (bf16[832,256]{1,0:T(8,128)(2,1)}, bf16[832,256]{1,0:T(8,128)(2,1)}, u32[]{:S(2)}, u32[]{:S(2)}) collective-permute-start(bf16[832,256]{1,0:T(8,128)(2,1)} %bitcast.34.m0), channel_id=1, source_target_pairs={{0,1},{1,0},{2,3},{3,2},{4,5},{5,4},{6,7},{7,6},{8,9},{9,8},{10,11... | collective-permute-start | bytes 1277960 | tf_op jit(solution)/shard_map/ppermute | solution.py:427
  283.8 11.9 %collective-permute-start.35 = (bf16[832,256]{1,0:T(8,128)(2,1)}, bf16[832,256]{1,0:T(8,128)(2,1)}, u32[]{:S(2)}, u32[]{:S(2)}) collective-permute-start(bf16[832,256]{1,0:T(8,128)(2,1)} %collective-permute-done.31.m2), channel_id=1, source_target_pairs={{0,1},{1,0},{2,3},{3,2},{4,5},{5,4},{6,7},{7,6},{8,9},{9,8},{10,11... | collective-permute-start | bytes 1277960 | tf_op jit(solution)/shard_map/ppermute | solution.py:427
  286.7 7.7 %collective-permute-start.37 = (bf16[128,1024]{1,0:T(8,128)(2,1)}, bf16[128,1024]{1,0:T(8,128)(2,1)}, u32[]{:S(2)}, u32[]{:S(2)}) collective-permute-start(bf16[128,1024]{1,0:T(8,128)(2,1)} %z_last_sum.3.refs_0_), channel_id=1, source_target_pairs={{0,2},{1,3},{2,0},{3,1},{4,6},{5,7},{6,4},{7,5},{8,10},{9,11},{10,... | collective-permute-start | bytes 786440 | tf_op jit(solution)/shard_map/ppermute | solution.py:427
  288.8 15.8 %collective-permute-start.39 = (bf16[128,2304]{1,0:T(8,128)(2,1)}, bf16[128,2304]{1,0:T(8,128)(2,1)}, u32[]{:S(2)}, u32[]{:S(2)}) collective-permute-start(bf16[128,2304]{1,0:T(8,128)(2,1)} %z_last_sum.2.refs_0_), channel_id=1, source_target_pairs={{0,1},{1,0},{2,3},{3,2},{4,5},{5,4},{6,7},{7,6},{8,9},{9,8},{10,11... | collective-permute-start | bytes 1769480 | tf_op jit(solution)/shard_map/ppermute | solution.py:427
  289.5 12.4 %collective-permute-start.36 = (bf16[128,1024]{1,0:T(8,128)(2,1)}, bf16[128,1024]{1,0:T(8,128)(2,1)}, u32[]{:S(2)}, u32[]{:S(2)}) collective-permute-start(bf16[128,1024]{1,0:T(8,128)(2,1)} %z_last_sum.3.refs_0_), channel_id=1, source_target_pairs={{0,1},{1,0},{2,3},{3,2},{4,5},{5,4},{6,7},{7,6},{8,9},{9,8},{10,11... | collective-permute-start | bytes 786440 | tf_op jit(solution)/shard_map/ppermute | solution.py:427
  289.5 15.0 %collective-permute-start.40 = (bf16[128,2304]{1,0:T(8,128)(2,1)}, bf16[128,2304]{1,0:T(8,128)(2,1)}, u32[]{:S(2)}, u32[]{:S(2)}) collective-permute-start(bf16[128,2304]{1,0:T(8,128)(2,1)} %collective-permute-done.34.refs_2_), channel_id=1, source_target_pairs={{0,1},{1,0},{2,3},{3,2},{4,5},{5,4},{6,7},{7,6},{8,9},{9,8},{10,11... | collective-permute-start | bytes 1769480 | tf_op jit(solution)/shard_map/ppermute | solution.py:427
  294.3 7.6 %collective-permute-start.38 = (bf16[128,1024]{1,0:T(8,128)(2,1)}, bf16[128,1024]{1,0:T(8,128)(2,1)}, u32[]{:S(2)}, u32[]{:S(2)}) collective-permute-start(bf16[128,1024]{1,0:T(8,128)(2,1)} %collective-permute-done.37.refs_2_), channel_id=1, source_target_pairs={{0,1},{1,0},{2,3},{3,2},{4,5},{5,4},{6,7},{7,6},{8,9},{9,8},{10,11... | collective-permute-start | bytes 786440 | tf_op jit(solution)/shard_map/ppermute | solution.py:427
  304.6 5.7 %copy-start.1 = (s32[4,48]{1,0:T(4,128)S(1)}, s32[4,48]{1,0:T(4,128)}, u32[]{:S(2)}) copy-start(s32[4,48]{1,0:T(4,128)} %param.19) | copy-start | bytes 2308
  (15 other events, 25.8 us)

commit v2 on v1

--- a/solution.py
+++ b/solution.py
@@ -391,19 +391,24 @@
     return to_heads(moved)
 
 
-def weight_grad_kernel(jobs, near, away, place_ref, *refs):
+def weight_grad_kernel(jobs, index, near, away, place_ref, *refs):
     split = len(refs) - len(near) - len(away)
     arrays, outs = refs[:split], refs[split:]
     rows = outs[0].shape[1]
+
+    def member(group, s):
+        first, stacked = index[group]
+        return arrays[first].at[place_ref[ME] ^ s] if stacked else arrays[first + s]
+
     sides = (1 - place_ref[Y],) * len(away) + (place_ref[Y],) * len(near)
     start = 0
     for left, left_start, right, right_start, cols in jobs:
-        values = [arrays[4 * right + s][:, pl.ds(right_start, cols)] for s in range(4)]
+        values = [member(right, s)[:, pl.ds(right_start, cols)] for s in range(4)]
         values = jnp.concatenate(values, axis=0)
         for out, side, blocks in zip(outs, sides, away + near):
             for slot, k in enumerate(blocks):
                 source = 2 * (place_ref[Z] ^ k) + side
-                group = arrays[4 * left : 4 * left + 4]
+                group = [member(left, s) for s in range(4)]
                 if len(group[0].shape) == 3:
                     factor = [ref[source] for ref in group]
                 else:
@@ -415,10 +420,14 @@
 
 
 def weight_grads(place, jobs, groups, rows, near, away):
-    arrays = [array for group in groups for array in group]
+    arrays, index = [], []
+    for group in groups:
+        stacked = not isinstance(group, (list, tuple))
+        index.append((len(arrays), stacked))
+        arrays += [group] if stacked else list(group)
     total = sum(job[-1] for job in jobs)
     shapes = [((len(blocks), rows, total), BF16) for blocks in away + near]
-    kernel = functools.partial(weight_grad_kernel, jobs, near, away)
+    kernel = functools.partial(weight_grad_kernel, jobs, index, near, away)
     outs = small_call(kernel, place, arrays, shapes, effort=2000, name="weight_grads")
     return outs[len(away) :], outs[: len(away)]
 
@@ -538,7 +547,7 @@
     return small_call(kernel, place, pieces, shapes, name="join")
 
 
-def sum_over_all(place, stay, away, hooks):
+def sum_over_all(place, stay, away, hooks, marks):
     _, rows, cols = stay.shape
     half = rows // 2
     size = half // 4
@@ -550,6 +559,7 @@
 
     got = next(hooks)(swap(away, "var", 1))
     stay, away = small_call(core_kernel, place, (stay, got), [((rows, cols), BF16)] * 2, name="core_sum")
+    marks.append(stay)
 
     def x_kernel(place_ref, stay_ref, got_ref, stay_out, away_out):
         for out, which in ((away_out, 1 - place_ref[Y]), (stay_out, place_ref[Y])):
@@ -560,6 +570,7 @@
     stay, away = small_call(
         x_kernel, place, (stay.reshape(halves), got.reshape(halves)), [((half, cols), BF16)] * 2, name="x_sum"
     )
+    marks.append(stay)
     got = next(hooks)(swap(away, "patch", 1))
     pieces = z_exchange(z_pieces(place, stay.reshape(4, size, cols), got.reshape(4, size, cols)))
     kept = z_sum(place, next(hooks)(pieces))
@@ -597,8 +608,8 @@
     late_ref,
     *refs,
 ):
-    slices = refs[0:4]
-    grad_ref, after_ref, gain_grad_ref, residual_ref, unit_ref, rate_ref, acc_ref, back_ref, wide_ref, branch_ref = refs[4:]
+    actives, middles = refs[0:4], refs[4:8]
+    grad_ref, after_ref, gain_grad_ref, residual_ref, unit_ref, rate_ref, acc_ref, back_ref, wide_ref, branch_ref = refs[8:]
     step = pl.program_id(0)
     seg, width = front_ref.shape
     parts = att_ref.shape[0]
@@ -634,14 +645,14 @@
     wide_ref[...] = active
     cols = pl.ds(pl.multiple_of(step * slot, slot), slot)
     for s in range(4):
-        slices[s][:, cols] = wide_ref[:, pl.ds(pl.multiple_of((me ^ s) * slot, slot), slot)]
+        actives[s][:, cols] = wide_ref[:, pl.ds(pl.multiple_of((me ^ s) * slot, slot), slot)]
     owner = step * block // hidden
-    place = pl.ds(pl.multiple_of(hidden + step * block - owner * hidden, block), block)
+    place = pl.ds(pl.multiple_of(step * block - owner * hidden, block), block)
     for s in range(4):
 
         @pl.when((me ^ s) == owner)
         def _(s=s):
-            slices[s][:, place] = inner_grad
+            middles[s][:, place] = inner_grad
 
     @pl.when(step == pl.num_programs(0) - 1)
     def _():
@@ -658,7 +669,7 @@
         branch_ref[...] = total.astype(BF16)
         for s in range(4):
             start = pl.multiple_of((me ^ s) * quarter, quarter)
-            slices[s][:, 2 * hidden :] = branch_ref[:, pl.ds(start, quarter)]
+            middles[s][:, hidden:] = branch_ref[:, pl.ds(start, quarter)]
         turned = mm(branch_ref[...], tout_ref[...], NT).astype(BF16)
         for p in range(parts):
             grad_ref[p] = turned[:, p * own : (p + 1) * own]
@@ -674,7 +685,7 @@
     def still(*dims):
         return pl.BlockSpec(dims, lambda i: (0,) * len(dims))
 
-    piece = shape((seg, hidden // 2 + width // 4), BF16)
+    piece, wider = shape((seg, hidden // 4), BF16), shape((seg, hidden // 4 + width // 4), BF16)
     return pl.pallas_call(
         middle_kernel,
         grid=(parts,),
@@ -682,6 +693,7 @@
             shape((seg, width), BF16),
             shape((seg, width), BF16),
             *((piece,) * 4),
+            *((wider,) * 4),
             shape(attended.shape, BF16),
             shape((seg, width), F32),
             shape((1, width), F32),
@@ -701,6 +713,7 @@
             still(seg, width),
             still(seg, width),
             *((still(*piece.shape),) * 4),
+            *((still(*wider.shape),) * 4),
             still(*attended.shape),
             still(seg, width),
             still(1, width),
@@ -723,7 +736,7 @@
 def trunk_back_kernel(
     place_ref, grads_ref, front_ref, gain_ref, after_ref, valid_ref, aout_ref, wqkv_ref, mixed_ref, gain_grad_ref, *rest
 ):
-    pieces, triple_ref, back_ref, wide_ref = rest[:4], rest[4], rest[5], rest[6]
+    stack_ref, triple_ref, back_ref = rest
     step = pl.program_id(0)
     parts = grads_ref.shape[0]
     seg, width = front_ref.shape
@@ -752,15 +765,13 @@
         total = rate * (scaled - jnp.mean(scaled, axis=1, keepdims=True) - unit * inside)
         total = ((after_ref[...] + total) * valid_ref[...]).astype(BF16)
         mixed_ref[...] = mm(total, aout_ref[...], NT).astype(BF16)
-        wide_ref[...] = total
         part = width // 4
-        for s in range(4):
-            v = me ^ s
-            pieces[s][:, 3 * part :] = wide_ref[:, pl.ds(pl.multiple_of(v * part, part), part)]
+        for v in range(4):
+            stack_ref[v, :, 3 * part :] = total[:, v * part : (v + 1) * part]
             for k in range(3):
                 block = 3 * v + k
-                cols = pl.ds(pl.multiple_of(block % 4 * part, part), part)
-                pieces[s][:, k * part : (k + 1) * part] = triple_ref[block // 4, :, cols]
+                source = triple_ref[block // 4, :, block % 4 * part : (block % 4 + 1) * part]
+                stack_ref[v, :, k * part : (k + 1) * part] = source
 
 
 def trunk_back(place, grads, front_out, gain, after_grad, valid, agg_out, trunk_qkv):
@@ -774,7 +785,7 @@
     return pl.pallas_call(
         trunk_back_kernel,
         grid=(3,),
-        out_shape=(piece, shape((1, width), F32), *((piece,) * 4)),
+        out_shape=(piece, shape((1, width), F32), shape((4, seg, width), BF16)),
         in_specs=[
             pl.BlockSpec(memory_space=pltpu.SMEM),
             still(*grads.shape),
@@ -785,11 +796,10 @@
             still(width, width),
             pl.BlockSpec((width, width), lambda i: (0, i)),
         ],
-        out_specs=(still(seg, width), still(1, width), *((still(seg, width),) * 4)),
+        out_specs=(still(seg, width), still(1, width), still(4, seg, width)),
         scratch_shapes=[
             pltpu.VMEM((3, seg, width), BF16),
             pltpu.VMEM((seg, width), F32),
-            pltpu.VMEM((seg, width), BF16),
         ],
         compiler_params=pltpu.CompilerParams(dimension_semantics=("arbitrary",)),
         cost_estimate=cost(100000000000),
@@ -997,30 +1007,32 @@
         )
         attended_group = copies_of_group(attended)
         results = together(*results, *attended_group, *early)
-        attended_group, early = results[9:13], results[13:]
-        block_out, normed_two_low, grads, after_grad, norm_two_grad = (results[k] for k in (0, 1, 6, 7, 8))
+        attended_group, early = results[13:17], results[17:]
+        block_out, normed_two_low, grads, after_grad, norm_two_grad = (results[k] for k in (0, 1, 10, 11, 12))
         block_out = block_out[None]
         grads = to_heads(grads)
-        mlp_group = slices_of_group(results[2:6])
+        active_group = slices_of_group(results[2:6])
         across = swap(normed_two_low, "var", 2)
         result = attend_backward(count, qkv, grads.reshape(patches * seg, own_width), lse, head_dim)
-        result, across = together(result, across)
+        result, across, *rest = together(result, across, *active_group, *results[6:10])
+        active_group, middle_group = rest[:4], slices_of_group(rest[4:])
         normed_group = (normed_two_low, swap(normed_two_low, "var", 1), across, swap(across, "var", 1))
         result = to_heads(result)
-        pairs = ((1, 3), (0, 2))
-        jobs = ((0, 0, 1, 0, width), (2, 0, 0, quarter, quarter), (3, 0, 0, 2 * quarter, part))
-        groups = (mlp_group, early, normed_group, attended_group)
-        _, away = weight_grads(place, jobs, groups, own_width, (), pairs[:1])
-        held = together(away[0], *groups[0])
-        near, more = weight_grads(place, jobs, (held[1:], *groups[1:]), own_width, pairs, pairs[1:])
-        away = (*away, *more)
-        result = after(result, *near)
-        mlp = {"near": near, "away": away}
-        mixed_grad, norm_one_grad, *pieces = trunk_back(
+        pairs, whole_order = ((1, 3), (0, 2)), ((1, 3, 0, 2),)
+        jobs = ((0, 0, 1, 0, width),)
+        near_one, away_one = weight_grads(place, jobs, (active_group, early), own_width, pairs, whole_order)
+        jobs = ((0, 0, 2, 0, quarter), (1, 0, 2, quarter, part))
+        groups = (together(normed_group[0], *near_one)[:1] + normed_group[1:], attended_group, middle_group)
+        near_two, away_two = weight_grads(place, jobs, groups, own_width, pairs, pairs)
+        result = after(result, *near_two)
+        one = {"near": near_one, "got": swap(away_one[0], "patch", 1)}
+        two = {"near": near_two, "away": away_two}
+        mixed_grad, norm_one_grad, stack = trunk_back(
             place, result, front_out, norm_one.astype(F32)[None], after_grad, valid_rows, agg_out, trunk_qkv
         )
-        mixed_grad, *pieces = together(mixed_grad, *pieces)
-        last_group = slices_of_group(pieces)
+        one["far"] = pair_sum(place, after(one["near"][0], mixed_grad), one["got"])
+        mixed_grad = after(mixed_grad, one["far"])
+        last_group = lax.all_to_all(stack, "var", split_axis=0, concat_axis=0, tiled=True)
     else:
         attended, attention_pull = gathered_attention(triple, own_count, head_dim)
         after_attn = front_out + mm(attended, trunk_out)
@@ -1048,55 +1060,65 @@
     )
 
     field_low = field_low.reshape(group, var_local * pixels, seg)
-    field_grad = lax.all_to_all(field_low, "var", split_axis=0, concat_axis=0, tiled=True)
+    field_grad = None if fast else lax.all_to_all(field_low, "var", split_axis=0, concat_axis=0, tiled=True)
 
     if fast:
-        got = swap(mlp["away"][0], "patch", 1)
-        m_stay, m_away, got = together(*m_parts, got)
+        m_stay, m_away, two["first"], last_group = together(*m_parts, swap(two["away"][0], "patch", 1), last_group)
         m_parts = (m_stay, m_away)
-        mlp["first"] = got
-        mlp["far"] = pair_sum(place, mlp["near"][0], got)
-        last = {}
+        two["far"] = pair_sum(place, two["near"][0], two["first"])
+        last, marks = {}, []
 
         def core_done(values):
             return values
 
         def x_done(values):
+            far = swap(one["far"], "patch", 2)
+            far, near, _ = together(far, one["near"][1], *marks)
+            one["pair"] = z_first_sum(place, near, one["got"], far)
+            return after(values, one["pair"][0])
+
+        def y_done(values):
             jobs = ((0, 2 * width, 1, 0, 3 * part), (0, width, 1, 3 * part, part))
-            groups = (early, last_group)
-            last["near"], last["away"] = weight_grads(place, jobs, groups, own_width, pairs, ((1, 3, 0, 2),))
-            return after(values, mlp["far"], field_grad, *last["near"])
-
-        def y_done(values):
-            got = swap(after(mlp["away"][1], mlp["first"]), "patch", 1)
-            values, got, far = together(values, got, swap(mlp["far"], "patch", 2))
-            mlp["pair"] = z_first_sum(place, mlp["near"][1], got, far)
-            return after(values, mlp["pair"][0])
+            groups = (early, after(last_group, marks[-1]))
+            last["near"], last["away"] = weight_grads(place, jobs, groups, own_width, pairs, whole_order)
+            got = swap(after(two["away"][1], two["first"]), "patch", 1)
+            values, got, far, *_ = together(values, got, swap(two["far"], "patch", 2), *last["near"])
+            two["pair"] = z_first_sum(place, two["near"][1], got, far)
+            return values
 
         def z_done(values):
-            *values, last["got"] = together(*values, swap(last["away"][0], "patch", 1))
+            near, away = one["pair"]
+            *values, got, _ = together(*values, swap(away, "patch", 4), two["pair"][0])
+            one["own"] = z_last_sum(place, near, got)
+            return values
+
+        def b_done(values):
+            near, away = two["pair"]
+            *values, last["got"], got = together(*values, swap(last["away"][0], "patch", 1), swap(away, "patch", 4))
+            late = after(field_low, last["got"])
+            last["field"] = lax.all_to_all(late, "var", split_axis=0, concat_axis=0, tiled=True)
             last["far"] = pair_sum(place, last["near"][0], last["got"])
+            two["own"] = z_last_sum(place, near, got)
             return [after(values[0], last["far"]), *values[1:]]
 
-        def b_done(values):
-            near, away = mlp["pair"]
-            *values, got = together(*values, swap(away, "patch", 4))
-            mlp["own"] = z_last_sum(place, near, got)
+        def y_back(values):
+            values, one["across"], last["field"] = together(values, swap(one["own"], "var", 2), last["field"])
             return values
 
-        def y_back(values):
+        def var_done(values):
+            far, across = swap(last["far"], "patch", 2), swap(two["own"], "var", 2)
+            near, away = z_first_sum(place, last["near"][1], last["got"], far)
+            two["parts"] = (two["own"], swap(two["own"], "var", 1), across, swap(across, "var", 1))
+            last["own"] = z_last_sum(place, near, swap(away, "patch", 4))
+            own, across = one["own"], one["across"]
+            values, inner, corner, _ = together(values, swap(own, "var", 1), swap(across, "var", 1), near)
+            one["parts"] = (own, inner, across, corner)
             return values
 
-        def var_done(values):
-            far, across = swap(last["far"], "patch", 2), swap(mlp["own"], "var", 2)
-            near, away = z_first_sum(place, last["near"][1], last["got"], far)
-            values, got, across = together(values, swap(away, "patch", 4), across)
-            mlp["parts"] = (mlp["own"], swap(mlp["own"], "var", 1), across, swap(across, "var", 1))
-            last["own"] = z_last_sum(place, near, got)
-            return values
-
-        m_pieces = sum_over_all(place, *m_parts, (core_done, x_done, y_done, z_done, b_done, y_back, var_done))
-        mlp_out_grad, mlp_in_grad, trunk_out_grad = join(place, mlp["parts"], (width, quarter, part), 1)
+        m_pieces = sum_over_all(place, *m_parts, (core_done, x_done, y_done, z_done, b_done, y_back, var_done), marks)
+        field_grad = last["field"]
+        (mlp_out_grad,) = join(place, one["parts"], (width,), 1)
+        mlp_in_grad, trunk_out_grad = join(place, two["parts"], (quarter, part), 0)
         mlp_out_grad = mlp_out_grad.reshape(hidden // patches, width)
         trunk_qkv_grad, agg_out_grad = join(place, gather_over_var(last["own"]), (3 * part, part), 0)
     else:

time: 312 us -> 301 us (0.965)
  waiting for transfers between devices: 84.2 us -> 61.8 us
  starting transfers between devices: 67.3 us -> 76.6 us
    ppermute x41 -> x47, waiting for transfers between devices: 68.5 us -> 44.3 us  [swap(): lax.ppermute(values, axis, [(i, i ^ bit) for i in range(lax.axis_size(axi...]
    all_to_all x1 -> x2, starting transfers between devices: 4.25 us -> 9.55 us  [the longest x1 5.08 us: b_done(): lax.all_to_all(late, 'var', split_axis=0, concat_axis=0, tiled=True)]
    pallas_call x18 -> x22, Pallas kernels: 55.5 us -> 59.1 us  [small_call(): pl.pallas_call(kernel, out_shape=tuple((jax.ShapeDtypeStruct(dims, dtype)...]
    ppermute x41 -> x47, starting transfers between devices: 40.8 us -> 43.8 us  [swap(): lax.ppermute(values, axis, [(i, i ^ bit) for i in range(lax.axis_size(axi...]
  transfers between devices with their start and end apart: 47 -> 54, of which waited for: 16 -> 15; matrix products, arithmetic and copies ran while one was open for 9% -> 9% of each run, Pallas kernels for 35% -> 38%
where the time goes in v2:
time: 301 us; the launch traced here: 299 us
  Pallas kernels  121 us (40%)
  starting transfers between devices  76.6 us (25%)
  waiting for transfers between devices  61.8 us (21%)
  matrix products  17.1 us (6%)
  local copies, waits for them, and re-layouts  14.2 us (5%)
  other arithmetic  7.02 us (2%)
    pallas_call x22, Pallas kernels, small_call(): pl.pallas_call(kernel, out_shape=tuple((jax.ShapeDtypeStruct(dims, dtype)...  59.1 us
    ppermute x47, waiting for transfers between devices, swap(): lax.ppermute(values, axis, [(i, i ^ bit) for i in range(lax.axis_size(axi...  44.3 us
    ppermute x47, starting transfers between devices, swap(): lax.ppermute(values, axis, [(i, i ^ bit) for i in range(lax.axis_size(axi...  43.8 us
    all_to_all x4, starting transfers between devices, to_heads(): lax.all_to_all(values, 'patch', split_axis=0, concat_axis=0, tiled=True)  19 us
    pallas_call x1, Pallas kernels, middle(): pl.pallas_call(middle_kernel, grid=(parts,), out_shape=(shape((seg, width...  18.1 us
    dot_general x10, matrix products, mm(): lax.dot_general(a, b, dims, precision=precision, preferred_element_type=F32)  17.1 us
    all_to_all x4, waiting for transfers between devices, to_heads(): lax.all_to_all(values, 'patch', split_axis=0, concat_axis=0, tiled=True)  15.1 us
    pallas_call x1, Pallas kernels, attend_backward(): pl.pallas_call(functools.partial(attend_backward_kernel, head_dim, block)...  11 us
  transfers between devices with their start and end apart: 54, of which 15 were waited for; matrix products, arithmetic and copies ran while one was open for 9% of the time, Pallas kernels for 38%

profile of v2, /device:TPU:1, one launch (start us, length us, event | category | flops | bytes accessed | tf_op | source)
XLA Modules:
  0.0 299.3 jit_solution(16959574999009849920)
XLA Ops:
  0.7 4.3 %all-to-all-start = ((bf16[4,192,128]{2,1,0:T(8,128)(2,1)}), bf16[4,192,128]{2,1,0:T(8,128)(2,1)S(1)}, u32[]{:S(2)}, u32[]{:S(2)}) async-start(bf16[4,192,128]{2,1,0:T(8,128)(2,1)} %bitcast.82), calls=%async_computation | async-start | bytes 393216 | tf_op jit(solution)/shard_map/all_to_all | solution.py:924
  5.8 2.1 fusion.21.aggq_ref
  10.1 3.0 %convolution_convert_fusion.2.vwt_ref = bf16[1024,768]{1,0:T(8,128)(2,1)} fusion(bf16[1024,1024]{1,0:T(8,128)(2,1)S(1)} %copy-done.2, bf16[768,1024]{1,0:T(8,128)(2,1)S(1)} %bitcast.78), kind=kOutput, calls=%fused_computation.3 | convolution fusion | flops 1611399168 | bytes 5242880 | tf_op jit(solution)/shard_map/dot_general | solution.py:28
  19.3 6.5 %front_forward.1 = (bf16[768,128]{1,0:T(8,128)(2,1)}, f32[768,128]{1,0:T(8,128)}, bf16[128,1024]{1,0:T(8,128)(2,1)}) custom-call(s32[1,48]{1,0:T(1,128)} %constant_dynamic-slice_fusion.4.ids_ref, bf16[768,128]{1,0:T(8,128)(2,1)} %bitcast.83, bf16[768,768]{1,0:T(8,128)(2,1)} %bitcast.71, f32[768,1]{1,0:T(8,128)} %reshape.252.bias_ref, ...), custom_call_target="tpu_custom_call" | custom-call | flops 60000002048 | bytes 1048576 | tf_op jit(solution)/shard_map/front_forward/pallas_call | solution.py:78
  25.8 2.2 fusion.20
  28.4 3.8 %convolution_convert_fusion = bf16[128,3072]{1,0:T(8,128)(2,1)S(1)} fusion(bf16[128,1024]{1,0:T(8,128)(2,1)S(1)} %multiply_convert_fusion, bf16[1024,3072]{1,0:T(8,128)(2,1)} %wqkv_ref.1), kind=kOutput, calls=%fused_computation | convolution fusion | flops 805699584 | bytes 7340032 | tf_op jit(solution)/shard_map/dot_general | solution.py:28
  33.4 6.1 %all-to-all-start.1 = ((bf16[8,384,128]{2,1,0:T(8,128)(2,1)}), bf16[8,384,128]{2,1,0:T(8,128)(2,1)}, u32[]{:S(2)}, u32[]{:S(2)}) async-start(bf16[8,384,128]{2,1,0:T(8,128)(2,1)} %bitcast.15), calls=%async_computation.1 | async-start | bytes 1572864 | tf_op jit(solution)/shard_map/all_to_all | solution.py:383
  44.4 1.6 constant_dynamic-slice_fusion.3.weight_own_ref
  46.0 1.8 constant_dynamic-slice_fusion
  49.0 3.0 fusion.vw_ref
  52.0 7.7 %all-to-all-done.1.qkv_ref = bf16[8,384,128]{2,1,0:T(8,128)(2,1)} async-done(((bf16[8,384,128]{2,1,0:T(8,128)(2,1)}), bf16[8,384,128]{2,1,0:T(8,128)(2,1)}, u32[]{:S(2)}, u32[]{:S(2)}) %all-to-all-start.1) | async-done | bytes 786464 | tf_op jit(solution)/shard_map/all_to_all | solution.py:383
  59.6 9.3 %attend_forward.1 = (bf16[1024,128]{1,0:T(8,128)(2,1)}, f32[2,1024]{1,0:T(2,128)}) custom-call(s32[1,1]{1,0:T(1,128)} %bitcast.5.count_ref, bf16[8,384,128]{2,1,0:T(8,128)(2,1)} %all-to-all-done.1.qkv_ref), custom_call_target="tpu_custom_call" | custom-call | flops 60000002048 | bytes 1048576 | tf_op jit(solution)/shard_map/attend_forward/pallas_call | solution.py:257
  68.9 4.0 %all-to-all-start.2 = ((bf16[8,128,128]{2,1,0:T(8,128)(2,1)}), bf16[8,128,128]{2,1,0:T(8,128)(2,1)S(1)}, u32[]{:S(2)}, u32[]{:S(2)}) async-start(bf16[8,128,128]{2,1,0:T(8,128)(2,1)} %bitcast.80), calls=%async_computation.2 | async-start | bytes 524288 | tf_op jit(solution)/shard_map/all_to_all | solution.py:383
  76.1 4.4 %all-to-all-done.2.att_ref.refs_4_ = bf16[8,128,128]{2,1,0:T(8,128)(2,1)S(1)} async-done(((bf16[8,128,128]{2,1,0:T(8,128)(2,1)}), bf16[8,128,128]{2,1,0:T(8,128)(2,1)S(1)}, u32[]{:S(2)}, u32[]{:S(2)}) %all-to-all-start.2) | async-done | bytes 262176 | tf_op jit(solution)/shard_map/all_to_all | solution.py:383
  80.5 2.3 collective-permute-start
  84.5 18.1 %trunk_middle.1 = (bf16[128,1024]{1,0:T(8,128)(2,1)}, bf16[128,1024]{1,0:T(8,128)(2,1)}, bf16[128,1024]{1,0:T(8,128)(2,1)}, bf16[128,1024]{1,0:T(8,128)(2,1)}, b...) custom-call(s32[5]{0:T(128)} %stack.23.place_ref, ...), custom_call_target="tpu_custom_call" | custom-call | flops 99999997952 | bytes 1048576 | tf_op jit(solution)/shard_map/trunk_middle/pallas_call | solution.py:689
  102.6 3.4 %all-to-all-start.3 = ((bf16[8,128,128]{2,1,0:T(8,128)(2,1)}), bf16[8,128,128]{2,1,0:T(8,128)(2,1)S(1)}, u32[]{:S(2)}, u32[]{:S(2)}) async-start(bf16[8,128,128]{2,1,0:T(8,128)(2,1)} %get-tuple-element.187), calls=%async_computation.3 | async-start | bytes 524288 | tf_op jit(solution)/shard_map/all_to_all | solution.py:383
  108.9 2.0 collective-permute-start.9
  110.9 3.1 %all-to-all-done.3 = bf16[8,128,128]{2,1,0:T(8,128)(2,1)S(1)} async-done(((bf16[8,128,128]{2,1,0:T(8,128)(2,1)}), bf16[8,128,128]{2,1,0:T(8,128)(2,1)S(1)}, u32[]{:S(2)}, u32[]{:S(2)}) %all-to-all-start.3) | async-done | bytes 262176 | tf_op jit(solution)/shard_map/all_to_all | solution.py:383
  114.7 11.0 %attend_backward.1 = bf16[8,384,128]{2,1,0:T(8,128)(2,1)} custom-call(s32[1,1]{1,0:T(1,128)} %bitcast.5.count_ref, bf16[8,384,128]{2,1,0:T(8,128)(2,1)} %all-to-all-done.1.qkv_ref, bf16[1024,128]{1,0:T(8,128)(2,1)} %bitcast.81, f32[2,1024]{1,0:T(2,128)} %get-tuple-element.188.lse_ref), custom_call_target="tpu_custom_call" | custom-call | flops 99999997952 | bytes 1048576 | tf_op jit(solution)/shard_map/attend_backward/pallas_call | solution.py:325
  126.3 5.4 %all-to-all-start.4 = ((bf16[8,384,128]{2,1,0:T(8,128)(2,1)}), bf16[8,384,128]{2,1,0:T(8,128)(2,1)}, u32[]{:S(2)}, u32[]{:S(2)}) async-start(bf16[8,384,128]{2,1,0:T(8,128)(2,1)} %attend_backward.1), calls=%async_computation.4 | async-start | bytes 1572864 | tf_op jit(solution)/shard_map/all_to_all | solution.py:383
  134.1 4.3 %weight_grads.3 = (bf16[4,128,1024]{2,1,0:T(8,128)(2,1)}, bf16[2,128,1024]{2,1,0:T(8,128)(2,1)}, bf16[2,128,1024]{2,1,0:T(8,128)(2,1)}) custom-call(s32[5]{0:T(128)} %stack.23.place_ref, bf16[128,1024]{1,0:T(8,128)(2,1)} %get-tuple-element.199.refs_0_, bf16[128,1024]{1,0:T(8,128)(2,1)} %copy-done.24, bf16[128,1024]{1,0:T(8,128)(2,1)} %copy-done.25, ...), custom_call_target="tpu_custom_call" | custom-call | flops 1999999991808 | bytes 1048576 | tf_op jit(solution)/shard_map/weight_grads/pallas_call | solution.py:449
  138.4 1.6 collective-permute-start.15
  140.1 1.4 collective-permute-done.13.refs_10_
  141.5 7.7 %collective-permute-done.14.refs_11_ = bf16[128,1280]{1,0:T(8,128)(2,1)} collective-permute-done((bf16[128,1280]{1,0:T(8,128)(2,1)}, bf16[128,1280]{1,0:T(8,128)(2,1)}, u32[]{:S(2)}, u32[]{:S(2)}) %collective-permute-start.14) | collective-permute-done | bytes 327712 | tf_op jit(solution)/shard_map/ppermute | solution.py:436
  149.2 4.8 %weight_grads.4 = (bf16[2,128,1280]{2,1,0:T(8,128)(2,1)}, bf16[2,128,1280]{2,1,0:T(8,128)(2,1)}, bf16[2,128,1280]{2,1,0:T(8,128)(2,1)}, bf16[2,128,1280]{2,1,0:T(8,128)(2,1)}) custom-call(s32[5]{0:T(128)} %stack.23.place_ref, bf16[128,1024]{1,0:T(8,128)(2,1)} %get-tuple-element.209.refs_0_, bf16[128,1024]{1,0:T(8,128)(2,1)} %collective-permute-done.10.refs_1_, ...), custom_call_target="tpu_custom_call" | custom-call | flops 1999999991808 | bytes 1048576 | tf_op jit(solution)/shard_map/weight_grads/pallas_call | solution.py:449
  154.1 1.5 collective-permute-start.16
  155.5 8.5 %trunk_back.1 = (bf16[128,1024]{1,0:T(8,128)(2,1)}, f32[1,1024]{1,0:T(1,128)}, bf16[4,128,1024]{2,1,0:T(8,128)(2,1)}) custom-call(s32[5]{0:T(128)} %stack.23.place_ref, bf16[8,384,128]{2,1,0:T(8,128)(2,1)} %all-to-all-done.4.grads_ref, f32[128,1024]{1,0:T(8,128)} %copy-done.3, f32[1,1024]{1,0:T(1,128)} %bitcast.85, ...), custom_call_target="tpu_custom_call" | custom-call | flops 99999997952 | bytes 1048576 | tf_op jit(solution)/shard_map/trunk_back/pallas_call | solution.py:785
  164.1 4.5 %all-to-all-start.5 = ((bf16[4,128,1024]{2,1,0:T(8,128)(2,1)}), bf16[4,128,1024]{2,1,0:T(8,128)(2,1)}, u32[]{:S(2)}, u32[]{:S(2)}) async-start(bf16[4,128,1024]{2,1,0:T(8,128)(2,1)} %get-tuple-element.234), calls=%async_computation.5 | async-start | bytes 2097152 | tf_op jit(solution)/shard_map/all_to_all | solution.py:1035
  168.6 2.3 pair_sum.3
  172.1 8.9 %front_backward.1 = (bf16[768,128]{1,0:T(8,128)(2,1)}, bf16[2,832,256]{2,1,0:T(8,128)(2,1)}, bf16[2,832,256]{2,1,0:T(8,128)(2,1)}) custom-call(s32[5]{0:T(128)} %stack.23.place_ref, s32[1,48]{1,0:T(1,128)} %constant_dynamic-slice_fusion.4.ids_ref, bf16[768,128]{1,0:T(8,128)(2,1)} %get-tuple-element.185.x_ref, f32[768,128]{1,0:T(8,128)} %get-tuple-element.186.p_ref, ...), custom_call_target="tpu_custom_call" | custom-call | flops 100000000 | bytes 1048576 | tf_op jit(solution)/shard_map/front_backward/pallas_call | solution.py:200
  181.0 1.5 all-to-all-done.5.refs_4_
  183.0 2.3 pair_sum.4
  185.3 1.4 collective-permute-start.22
  186.8 2.4 core_sum.1
  190.2 2.4 z_first_sum.3
  193.8 6.5 %collective-permute-done.18 = bf16[832,256]{1,0:T(8,128)(2,1)} collective-permute-done((bf16[832,256]{1,0:T(8,128)(2,1)}, bf16[832,256]{1,0:T(8,128)(2,1)}, u32[]{:S(2)}, u32[]{:S(2)}) %collective-permute-start.18) | collective-permute-done | bytes 426016 | tf_op jit(solution)/shard_map/ppermute | solution.py:436
  200.3 2.0 x_sum.1
  203.5 4.7 %weight_grads.5 = (bf16[4,128,1024]{2,1,0:T(8,128)(2,1)}, bf16[2,128,1024]{2,1,0:T(8,128)(2,1)}, bf16[2,128,1024]{2,1,0:T(8,128)(2,1)}) custom-call(s32[5]{0:T(128)} %stack.23.place_ref, bf16[128,3072]{1,0:T(8,128)(2,1)} %pad_maximum_fusion.refs_4_.refs_0_, bf16[128,3072]{1,0:T(8,128)(2,1)} %copy-done.19, ...), custom_call_target="tpu_custom_call" | custom-call | flops 1999999991808 | bytes 1048576 | tf_op jit(solution)/shard_map/weight_grads/pallas_call | solution.py:449
  208.5 1.8 z_pieces.1
  210.3 2.3 collective-permute-start.24
  213.8 2.5 z_first_sum.4
  218.2 1.5 z_sum.1.refs_0_
  220.9 2.4 collective-permute-start.29
  223.3 1.8 z_last_sum.3.refs_0_
  225.8 12.3 %collective-permute-done.28.refs_2_ = bf16[104,256]{1,0:T(8,128)(2,1)} collective-permute-done((bf16[104,256]{1,0:T(8,128)(2,1)}, bf16[104,256]{1,0:T(8,128)(2,1)}, u32[]{:S(2)}, u32[]{:S(2)}) %collective-permute-start.28) | collective-permute-done | bytes 53280 | tf_op jit(solution)/shard_map/ppermute | solution.py:436
  238.8 2.3 pair_sum.5
  241.8 1.6 z_join.1
  244.6 5.1 %all-to-all-start.6 = ((bf16[4,192,128]{2,1,0:T(8,128)(2,1)}), bf16[4,192,128]{2,1,0:T(8,128)(2,1)}, u32[]{:S(2)}, u32[]{:S(2)}) async-start(bf16[4,192,128]{2,1,0:T(8,128)(2,1)} %bitcast.31), calls=%async_computation.6 | async-start | bytes 393216 | tf_op jit(solution)/shard_map/all_to_all | solution.py:1099
  249.6 1.9 z_last_sum.5.refs_0_
  251.6 1.7 collective-permute-start.45
  254.2 1.8 y_join.1
  257.3 2.4 z_first_sum.5
  259.7 1.5 collective-permute-done.45.refs_2_
  261.2 1.7 collective-permute-start.46
  263.5 6.8 %collective-permute-done.35.m2 = bf16[832,256]{1,0:T(8,128)(2,1)} collective-permute-done((bf16[832,256]{1,0:T(8,128)(2,1)}, bf16[832,256]{1,0:T(8,128)(2,1)}, u32[]{:S(2)}, u32[]{:S(2)}) %collective-permute-start.35) | collective-permute-done | bytes 426016 | tf_op jit(solution)/shard_map/ppermute | solution.py:436
  271.4 2.7 join.5
  274.0 3.9 %collective-permute-done.40.got_ref = bf16[128,1024]{1,0:T(8,128)(2,1)} collective-permute-done((bf16[128,1024]{1,0:T(8,128)(2,1)}, bf16[128,1024]{1,0:T(8,128)(2,1)}, u32[]{:S(2)}, u32[]{:S(2)}) %collective-permute-start.40) | collective-permute-done | bytes 262176 | tf_op jit(solution)/shard_map/ppermute | solution.py:436
  278.0 1.8 z_last_sum.4.refs_0_
  281.2 2.9 join.4
  284.8 2.7 collective-permute-done.42.refs_2_
  288.8 6.2 %front_last.1 = (f32[128,1024]{1,0:T(8,128)}, f32[768,128]{1,0:T(8,128)}, f32[48,128]{1,0:T(8,128)}, f32[128,1024]{1,0:T(8,128)}, f32[128,1024]{1,0:T(8,128)}, /...) custom-call(s32[5]{0:T(128)} %stack.23.place_ref, bf16[832,256]{1,0:T(8,128)(2,1)} %bitcast.34.m0, ...), custom_call_target="tpu_custom_call" | custom-call | flops 199999995904 | bytes 1048576 | tf_op jit(solution)/shard_map/front_last/pallas_call | solution.py:449
  295.1 2.6 join.3
  297.7 1.6 copy.54
  (175 shorter events, 48.3 us)
Async XLA Ops:
  0.6 17.5 %copy-start = (s32[4,48]{1,0:T(4,128)S(1)}, s32[4,48]{1,0:T(4,128)}, u32[]{:S(2)}) copy-start(s32[4,48]{1,0:T(4,128)} %param.19) | copy-start | bytes 2308
  0.7 18.0 %all-to-all-start = ((bf16[4,192,128]{2,1,0:T(8,128)(2,1)}), bf16[4,192,128]{2,1,0:T(8,128)(2,1)S(1)}, u32[]{:S(2)}, u32[]{:S(2)}) async-start(bf16[4,192,128]{2,1,0:T(8,128)(2,1)} %bitcast.82), calls=%async_computation | async-start | bytes 393216 | tf_op jit(solution)/shard_map/all_to_all | solution.py:924
  16.3 23.3 %copy-start.7 = (bf16[128,1024]{1,0:T(8,128)(2,1)}, bf16[128,1024]{1,0:T(8,128)(2,1)S(1)}, u32[]{:S(2)}) copy-start(bf16[128,1024]{1,0:T(8,128)(2,1)S(1)} %fusion.2.og_ref) | copy-start | bytes 786436
  18.1 10.1 %copy-start.15 = (f32[1024]{0:T(1024)}, f32[1024]{0:T(1024)S(1)}, u32[]{:S(2)}) copy-start(f32[1024]{0:T(1024)S(1)} %convert_element_type.97) | copy-start | bytes 12292
  33.4 26.2 %all-to-all-start.1 = ((bf16[8,384,128]{2,1,0:T(8,128)(2,1)}), bf16[8,384,128]{2,1,0:T(8,128)(2,1)}, u32[]{:S(2)}, u32[]{:S(2)}) async-start(bf16[8,384,128]{2,1,0:T(8,128)(2,1)} %bitcast.15), calls=%async_computation.1 | async-start | bytes 1572864 | tf_op jit(solution)/shard_map/all_to_all | solution.py:383
  40.5 35.6 %collective-permute-start.4 = (bf16[128,3072]{1,0:T(8,128)(2,1)}, bf16[128,3072]{1,0:T(8,128)(2,1)}, u32[]{:S(2)}, u32[]{:S(2)}) collective-permute-start(bf16[128,3072]{1,0:T(8,128)(2,1)} %pad_maximum_fusion.refs_4_.refs_0_), channel_id=1, source_target_pairs={{0,2},{1,3},{2,0},{3,1},{4,6},{5,7},{6,4},{7,5},{8,10},{9,11},{10,... | collective-permute-start | bytes 2359304 | tf_op jit(solution)/shard_map/ppermute | solution.py:436
  59.6 13.3 %copy-start.17 = (bf16[1024]{0:T(1024)(128)(2,1)S(1)}, bf16[1024]{0:T(1024)(128)(2,1)}, u32[]{:S(2)}) copy-start(bf16[1024]{0:T(1024)(128)(2,1)} %param.30) | copy-start | bytes 6148
  68.9 11.6 %all-to-all-start.2 = ((bf16[8,128,128]{2,1,0:T(8,128)(2,1)}), bf16[8,128,128]{2,1,0:T(8,128)(2,1)S(1)}, u32[]{:S(2)}, u32[]{:S(2)}) async-start(bf16[8,128,128]{2,1,0:T(8,128)(2,1)} %bitcast.80), calls=%async_computation.2 | async-start | bytes 524288 | tf_op jit(solution)/shard_map/all_to_all | solution.py:383
  75.4 27.2 %collective-permute-start.3 = (bf16[128,3072]{1,0:T(8,128)(2,1)}, bf16[128,3072]{1,0:T(8,128)(2,1)S(1)}, u32[]{:S(2)}, u32[]{:S(2)}) collective-permute-start(bf16[128,3072]{1,0:T(8,128)(2,1)} %pad_maximum_fusion.refs_4_.refs_0_), channel_id=1, source_target_pairs={{0,1},{1,0},{2,3},{3,2},{4,5},{5,4},{6,7},{7,6},{8,9},{9,8},{10,11... | collective-permute-start | bytes 2359304 | tf_op jit(solution)/shard_map/ppermute | solution.py:436
  76.1 26.4 %collective-permute-start.5 = (bf16[128,3072]{1,0:T(8,128)(2,1)}, bf16[128,3072]{1,0:T(8,128)(2,1)S(1)}, u32[]{:S(2)}, u32[]{:S(2)}) collective-permute-start(bf16[128,3072]{1,0:T(8,128)(2,1)} %collective-permute-done.4.refs_6_.refs_2_), channel_id=1, source_target_pairs={{0,1},{1,0},{2,3},{3,2},{4,5},{5,4},{6,7},{7,6},{8,9},{9,8},{10,11... | collective-permute-start | bytes 2359304 | tf_op jit(solution)/shard_map/ppermute | solution.py:436
  80.5 22.0 %collective-permute-start = (bf16[8,128,128]{2,1,0:T(8,128)(2,1)S(1)}, bf16[8,128,128]{2,1,0:T(8,128)(2,1)S(1)}, u32[]{:S(2)}, u32[]{:S(2)}) collective-permute-start(bf16[8,128,128]{2,1,0:T(8,128)(2,1)S(1)} %all-to-all-done.2.att_ref.refs_4_), channel_id=1, source_target_pairs={{0,1},{1,0},{2,3},{3,2},{4,5},{5,4},{6,7},{7,6},{8,9},{9,8},{10,11... | collective-permute-start | bytes 786440 | tf_op jit(solution)/shard_map/ppermute | solution.py:436
  82.8 19.8 %collective-permute-start.1 = (bf16[8,128,128]{2,1,0:T(8,128)(2,1)S(1)}, bf16[8,128,128]{2,1,0:T(8,128)(2,1)S(1)}, u32[]{:S(2)}, u32[]{:S(2)}) collective-permute-start(bf16[8,128,128]{2,1,0:T(8,128)(2,1)S(1)} %all-to-all-done.2.att_ref.refs_4_), channel_id=1, source_target_pairs={{0,2},{1,3},{2,0},{3,1},{4,6},{5,7},{6,4},{7,5},{8,10},{9,11},{10,... | collective-permute-start | bytes 786440 | tf_op jit(solution)/shard_map/ppermute | solution.py:436
  84.1 18.5 %collective-permute-start.2 = (bf16[8,128,128]{2,1,0:T(8,128)(2,1)S(1)}, bf16[8,128,128]{2,1,0:T(8,128)(2,1)S(1)}, u32[]{:S(2)}, u32[]{:S(2)}) collective-permute-start(bf16[8,128,128]{2,1,0:T(8,128)(2,1)S(1)} %all-to-all-done.2.att_ref.refs_4_), channel_id=1, source_target_pairs={{0,3},{1,2},{2,1},{3,0},{4,7},{5,6},{6,5},{7,4},{8,11},{9,10},{10,... | collective-permute-start | bytes 786440 | tf_op jit(solution)/shard_map/ppermute | solution.py:436
  84.5 21.6 %copy-start.18 = (f32[128,1]{0,1:T(1,128)S(1)}, f32[128,1]{0,1:T(1,128)}, u32[]{:S(2)}) copy-start(f32[128,1]{0,1:T(1,128)} %bitcast_convert_fusion) | copy-start | bytes 1540
  102.5 23.1 %copy-start.19 = (bf16[128,3072]{1,0:T(8,128)(2,1)}, bf16[128,3072]{1,0:T(8,128)(2,1)S(1)}, u32[]{:S(2)}) copy-start(bf16[128,3072]{1,0:T(8,128)(2,1)S(1)} %collective-permute-done.3.refs_5_.refs_1_) | copy-start | bytes 2359300
  102.6 23.1 %copy-start.20 = (bf16[128,3072]{1,0:T(8,128)(2,1)}, bf16[128,3072]{1,0:T(8,128)(2,1)S(1)}, u32[]{:S(2)}) copy-start(bf16[128,3072]{1,0:T(8,128)(2,1)S(1)} %collective-permute-done.5.refs_7_.refs_3_) | copy-start | bytes 2359300
  102.6 23.1 %copy-start.21 = (bf16[8,128,128]{2,1,0:T(8,128)(2,1)}, bf16[8,128,128]{2,1,0:T(8,128)(2,1)S(1)}, u32[]{:S(2)}) copy-start(bf16[8,128,128]{2,1,0:T(8,128)(2,1)S(1)} %collective-permute-done.refs_5_) | copy-start | bytes 786436
  102.6 23.1 %copy-start.22 = (bf16[8,128,128]{2,1,0:T(8,128)(2,1)}, bf16[8,128,128]{2,1,0:T(8,128)(2,1)S(1)}, u32[]{:S(2)}) copy-start(bf16[8,128,128]{2,1,0:T(8,128)(2,1)S(1)} %collective-permute-done.1.refs_6_) | copy-start | bytes 786436
  102.6 23.1 %copy-start.23 = (bf16[8,128,128]{2,1,0:T(8,128)(2,1)}, bf16[8,128,128]{2,1,0:T(8,128)(2,1)S(1)}, u32[]{:S(2)}) copy-start(bf16[8,128,128]{2,1,0:T(8,128)(2,1)S(1)} %collective-permute-done.2.refs_7_) | copy-start | bytes 786436
  102.6 11.4 %all-to-all-start.3 = ((bf16[8,128,128]{2,1,0:T(8,128)(2,1)}), bf16[8,128,128]{2,1,0:T(8,128)(2,1)S(1)}, u32[]{:S(2)}, u32[]{:S(2)}) async-start(bf16[8,128,128]{2,1,0:T(8,128)(2,1)} %get-tuple-element.187), calls=%async_computation.3 | async-start | bytes 524288 | tf_op jit(solution)/shard_map/all_to_all | solution.py:383
  106.8 18.9 %collective-permute-start.6 = (bf16[128,1024]{1,0:T(8,128)(2,1)}, bf16[128,1024]{1,0:T(8,128)(2,1)}, u32[]{:S(2)}, u32[]{:S(2)}) collective-permute-start(bf16[128,1024]{1,0:T(8,128)(2,1)} %get-tuple-element.209.refs_0_), channel_id=1, source_target_pairs={{0,2},{1,3},{2,0},{3,1},{4,6},{5,7},{6,4},{7,5},{8,10},{9,11},{10,... | collective-permute-start | bytes 786440 | tf_op jit(solution)/shard_map/ppermute | solution.py:436
  108.1 30.3 %collective-permute-start.10 = (bf16[128,1024]{1,0:T(8,128)(2,1)}, bf16[128,1024]{1,0:T(8,128)(2,1)}, u32[]{:S(2)}, u32[]{:S(2)}) collective-permute-start(bf16[128,1024]{1,0:T(8,128)(2,1)} %get-tuple-element.209.refs_0_), channel_id=1, source_target_pairs={{0,1},{1,0},{2,3},{3,2},{4,5},{5,4},{6,7},{7,6},{8,9},{9,8},{10,11... | collective-permute-start | bytes 786440 | tf_op jit(solution)/shard_map/ppermute | solution.py:436
  108.8 16.9 %collective-permute-start.7 = (bf16[128,1024]{1,0:T(8,128)(2,1)}, bf16[128,1024]{1,0:T(8,128)(2,1)S(1)}, u32[]{:S(2)}, u32[]{:S(2)}) collective-permute-start(bf16[128,1024]{1,0:T(8,128)(2,1)} %get-tuple-element.191), channel_id=1, source_target_pairs={{0,1},{1,0},{2,3},{3,2},{4,5},{5,4},{6,7},{7,6},{8,9},{9,8},{10,11... | collective-permute-start | bytes 786440 | tf_op jit(solution)/shard_map/ppermute | solution.py:436
  108.8 17.0 %collective-permute-start.8 = (bf16[128,1024]{1,0:T(8,128)(2,1)}, bf16[128,1024]{1,0:T(8,128)(2,1)S(1)}, u32[]{:S(2)}, u32[]{:S(2)}) collective-permute-start(bf16[128,1024]{1,0:T(8,128)(2,1)} %get-tuple-element.192), channel_id=1, source_target_pairs={{0,2},{1,3},{2,0},{3,1},{4,6},{5,7},{6,4},{7,5},{8,10},{9,11},{10,... | collective-permute-start | bytes 786440 | tf_op jit(solution)/shard_map/ppermute | solution.py:436
  108.9 17.4 %collective-permute-start.9 = (bf16[128,1024]{1,0:T(8,128)(2,1)}, bf16[128,1024]{1,0:T(8,128)(2,1)S(1)}, u32[]{:S(2)}, u32[]{:S(2)}) collective-permute-start(bf16[128,1024]{1,0:T(8,128)(2,1)} %get-tuple-element.193), channel_id=1, source_target_pairs={{0,3},{1,2},{2,1},{3,0},{4,7},{5,6},{6,5},{7,4},{8,11},{9,10},{10,... | collective-permute-start | bytes 786440 | tf_op jit(solution)/shard_map/ppermute | solution.py:436
  126.3 29.2 %all-to-all-start.4 = ((bf16[8,384,128]{2,1,0:T(8,128)(2,1)}), bf16[8,384,128]{2,1,0:T(8,128)(2,1)}, u32[]{:S(2)}, u32[]{:S(2)}) async-start(bf16[8,384,128]{2,1,0:T(8,128)(2,1)} %attend_backward.1), calls=%async_computation.4 | async-start | bytes 1572864 | tf_op jit(solution)/shard_map/all_to_all | solution.py:383
  131.7 8.4 %collective-permute-start.11 = (bf16[128,1024]{1,0:T(8,128)(2,1)}, bf16[128,1024]{1,0:T(8,128)(2,1)}, u32[]{:S(2)}, u32[]{:S(2)}) collective-permute-start(bf16[128,1024]{1,0:T(8,128)(2,1)} %collective-permute-done.6.refs_2_), channel_id=1, source_target_pairs={{0,1},{1,0},{2,3},{3,2},{4,5},{5,4},{6,7},{7,6},{8,9},{9,8},{10,11... | collective-permute-start | bytes 786440 | tf_op jit(solution)/shard_map/ppermute | solution.py:436
  132.0 8.1 %collective-permute-start.12 = (bf16[128,1280]{1,0:T(8,128)(2,1)}, bf16[128,1280]{1,0:T(8,128)(2,1)}, u32[]{:S(2)}, u32[]{:S(2)}) collective-permute-start(bf16[128,1280]{1,0:T(8,128)(2,1)} %get-tuple-element.216), channel_id=1, source_target_pairs={{0,1},{1,0},{2,3},{3,2},{4,5},{5,4},{6,7},{7,6},{8,9},{9,8},{10,11... | collective-permute-start | bytes 983048 | tf_op jit(solution)/shard_map/ppermute | solution.py:436
  132.2 9.3 %collective-permute-start.13 = (bf16[128,1280]{1,0:T(8,128)(2,1)}, bf16[128,1280]{1,0:T(8,128)(2,1)}, u32[]{:S(2)}, u32[]{:S(2)}) collective-permute-start(bf16[128,1280]{1,0:T(8,128)(2,1)} %get-tuple-element.217), channel_id=1, source_target_pairs={{0,2},{1,3},{2,0},{3,1},{4,6},{5,7},{6,4},{7,5},{8,10},{9,11},{10,... | collective-permute-start | bytes 983048 | tf_op jit(solution)/shard_map/ppermute | solution.py:436
  133.5 15.8 %collective-permute-start.14 = (bf16[128,1280]{1,0:T(8,128)(2,1)}, bf16[128,1280]{1,0:T(8,128)(2,1)}, u32[]{:S(2)}, u32[]{:S(2)}) collective-permute-start(bf16[128,1280]{1,0:T(8,128)(2,1)} %get-tuple-element.218), channel_id=1, source_target_pairs={{0,3},{1,2},{2,1},{3,0},{4,7},{5,6},{6,5},{7,4},{8,11},{9,10},{10,... | collective-permute-start | bytes 983048 | tf_op jit(solution)/shard_map/ppermute | solution.py:436
  138.4 30.1 %collective-permute-start.15 = (bf16[4,128,1024]{2,1,0:T(8,128)(2,1)}, bf16[4,128,1024]{2,1,0:T(8,128)(2,1)}, u32[]{:S(2)}, u32[]{:S(2)}) collective-permute-start(bf16[4,128,1024]{2,1,0:T(8,128)(2,1)} %get-tuple-element.225), channel_id=1, source_target_pairs={{0,4},{4,0},{8,12},{12,8},{16,20},{20,16},{24,28},{28,24},{1,5},{5... | collective-permute-start | bytes 3145736 | tf_op jit(solution)/shard_map/ppermute | solution.py:436
  154.1 26.9 %collective-permute-start.16 = (bf16[2,128,1280]{2,1,0:T(8,128)(2,1)}, bf16[2,128,1280]{2,1,0:T(8,128)(2,1)}, u32[]{:S(2)}, u32[]{:S(2)}) collective-permute-start(bf16[2,128,1280]{2,1,0:T(8,128)(2,1)} %get-tuple-element.233), channel_id=1, source_target_pairs={{0,4},{4,0},{8,12},{12,8},{16,20},{20,16},{24,28},{28,24},{1,5},{5... | collective-permute-start | bytes 1966088 | tf_op jit(solution)/shard_map/ppermute | solution.py:436
  164.1 18.4 %all-to-all-start.5 = ((bf16[4,128,1024]{2,1,0:T(8,128)(2,1)}), bf16[4,128,1024]{2,1,0:T(8,128)(2,1)}, u32[]{:S(2)}, u32[]{:S(2)}) async-start(bf16[4,128,1024]{2,1,0:T(8,128)(2,1)} %get-tuple-element.234), calls=%async_computation.5 | async-start | bytes 2097152 | tf_op jit(solution)/shard_map/all_to_all | solution.py:1035
  170.9 19.3 %collective-permute-start.19 = (bf16[2,128,1024]{2,1,0:T(8,128)(2,1)}, bf16[2,128,1024]{2,1,0:T(8,128)(2,1)}, u32[]{:S(2)}, u32[]{:S(2)}) collective-permute-start(bf16[2,128,1024]{2,1,0:T(8,128)(2,1)} %pair_sum.3), channel_id=1, source_target_pairs={{0,8},{4,12},{8,0},{12,4},{16,24},{20,28},{24,16},{28,20},{1,9},{5... | collective-permute-start | bytes 1572872 | tf_op jit(solution)/shard_map/ppermute | solution.py:436
  182.5 4.3 %collective-permute-start.17 = (bf16[2,832,256]{2,1,0:T(8,128)(2,1)}, bf16[2,832,256]{2,1,0:T(8,128)(2,1)}, u32[]{:S(2)}, u32[]{:S(2)}) collective-permute-start(bf16[2,832,256]{2,1,0:T(8,128)(2,1)} %get-tuple-element.236), channel_id=1, source_target_pairs={{0,1},{1,0},{2,3},{3,2},{4,5},{5,4},{6,7},{7,6},{8,9},{9,8},{10,11... | collective-permute-start | bytes 2555912 | tf_op jit(solution)/shard_map/ppermute | solution.py:436
  185.3 23.2 %collective-permute-start.21 = (bf16[2,128,1280]{2,1,0:T(8,128)(2,1)}, bf16[2,128,1280]{2,1,0:T(8,128)(2,1)}, u32[]{:S(2)}, u32[]{:S(2)}) collective-permute-start(bf16[2,128,1280]{2,1,0:T(8,128)(2,1)} %get-tuple-element.247), channel_id=1, source_target_pairs={{0,4},{4,0},{8,12},{12,8},{16,20},{20,16},{24,28},{28,24},{1,5},{5... | collective-permute-start | bytes 1966088 | tf_op jit(solution)/shard_map/ppermute | solution.py:436
  185.3 23.2 %collective-permute-start.22 = (bf16[2,128,1280]{2,1,0:T(8,128)(2,1)}, bf16[2,128,1280]{2,1,0:T(8,128)(2,1)}, u32[]{:S(2)}, u32[]{:S(2)}) collective-permute-start(bf16[2,128,1280]{2,1,0:T(8,128)(2,1)} %pair_sum.4), channel_id=1, source_target_pairs={{0,8},{4,12},{8,0},{12,4},{16,24},{20,28},{24,16},{28,20},{1,9},{5... | collective-permute-start | bytes 1966088 | tf_op jit(solution)/shard_map/ppermute | solution.py:436
  189.2 11.1 %collective-permute-start.18 = (bf16[832,256]{1,0:T(8,128)(2,1)}, bf16[832,256]{1,0:T(8,128)(2,1)}, u32[]{:S(2)}, u32[]{:S(2)}) collective-permute-start(bf16[832,256]{1,0:T(8,128)(2,1)} %get-tuple-element.238), channel_id=1, source_target_pairs={{0,2},{1,3},{2,0},{3,1},{4,6},{5,7},{6,4},{7,5},{8,10},{9,11},{10,... | collective-permute-start | bytes 1277960 | tf_op jit(solution)/shard_map/ppermute | solution.py:436
  192.6 23.6 %collective-permute-start.26 = (bf16[128,1024]{1,0:T(8,128)(2,1)}, bf16[128,1024]{1,0:T(8,128)(2,1)}, u32[]{:S(2)}, u32[]{:S(2)}) collective-permute-start(bf16[128,1024]{1,0:T(8,128)(2,1)} %get-tuple-element.257), channel_id=1, source_target_pairs={{0,16},{4,20},{8,24},{12,28},{16,0},{20,4},{24,8},{28,12},{1,17},{... | collective-permute-start | bytes 786440 | tf_op jit(solution)/shard_map/ppermute | solution.py:436
  202.3 6.2 %collective-permute-start.20 = (bf16[416,256]{1,0:T(8,128)(2,1)}, bf16[416,256]{1,0:T(8,128)(2,1)}, u32[]{:S(2)}, u32[]{:S(2)}) collective-permute-start(bf16[416,256]{1,0:T(8,128)(2,1)} %get-tuple-element.244), channel_id=1, source_target_pairs={{0,4},{4,0},{8,12},{12,8},{16,20},{20,16},{24,28},{28,24},{1,5},{5... | collective-permute-start | bytes 638984 | tf_op jit(solution)/shard_map/ppermute | solution.py:436
  208.2 30.6 %collective-permute-start.30 = (bf16[4,128,1024]{2,1,0:T(8,128)(2,1)}, bf16[4,128,1024]{2,1,0:T(8,128)(2,1)}, u32[]{:S(2)}, u32[]{:S(2)}) collective-permute-start(bf16[4,128,1024]{2,1,0:T(8,128)(2,1)} %get-tuple-element.265), channel_id=1, source_target_pairs={{0,4},{4,0},{8,12},{12,8},{16,20},{20,16},{24,28},{28,24},{1,5},{5... | collective-permute-start | bytes 3145736 | tf_op jit(solution)/shard_map/ppermute | solution.py:436
  210.3 7.2 %collective-permute-start.23 = (bf16[104,256]{1,0:T(8,128)(2,1)}, bf16[104,256]{1,0:T(8,128)(2,1)}, u32[]{:S(2)}, u32[]{:S(2)}) collective-permute-start(bf16[104,256]{1,0:T(8,128)(2,1)} %get-tuple-element.254), channel_id=1, source_target_pairs={{0,8},{4,12},{8,0},{12,4},{16,24},{20,28},{24,16},{28,20},{1,9},{5... | collective-permute-start | bytes 159752 | tf_op jit(solution)/shard_map/ppermute | solution.py:436
  210.3 7.2 %collective-permute-start.24 = (bf16[104,256]{1,0:T(8,128)(2,1)}, bf16[104,256]{1,0:T(8,128)(2,1)}, u32[]{:S(2)}, u32[]{:S(2)}) collective-permute-start(bf16[104,256]{1,0:T(8,128)(2,1)} %get-tuple-element.255), channel_id=1, source_target_pairs={{0,16},{4,20},{8,24},{12,28},{16,0},{20,4},{24,8},{28,12},{1,17},{... | collective-permute-start | bytes 159752 | tf_op jit(solution)/shard_map/ppermute | solution.py:436
  212.6 5.6 %collective-permute-start.25 = (bf16[104,256]{1,0:T(8,128)(2,1)}, bf16[104,256]{1,0:T(8,128)(2,1)}, u32[]{:S(2)}, u32[]{:S(2)}) collective-permute-start(bf16[104,256]{1,0:T(8,128)(2,1)} %get-tuple-element.256), channel_id=1, source_target_pairs={{0,24},{4,28},{8,16},{12,20},{16,8},{20,12},{24,0},{28,4},{1,25},{... | collective-permute-start | bytes 159752 | tf_op jit(solution)/shard_map/ppermute | solution.py:436
  216.3 22.5 %collective-permute-start.31 = (bf16[128,1280]{1,0:T(8,128)(2,1)}, bf16[128,1280]{1,0:T(8,128)(2,1)}, u32[]{:S(2)}, u32[]{:S(2)}) collective-permute-start(bf16[128,1280]{1,0:T(8,128)(2,1)} %get-tuple-element.266), channel_id=1, source_target_pairs={{0,16},{4,20},{8,24},{12,28},{16,0},{20,4},{24,8},{28,12},{1,17},{... | collective-permute-start | bytes 983048 | tf_op jit(solution)/shard_map/ppermute | solution.py:436
  219.8 5.4 %collective-permute-start.27 = (bf16[104,256]{1,0:T(8,128)(2,1)}, bf16[104,256]{1,0:T(8,128)(2,1)}, u32[]{:S(2)}, u32[]{:S(2)}) collective-permute-start(bf16[104,256]{1,0:T(8,128)(2,1)} %z_sum.1.refs_0_), channel_id=1, source_target_pairs={{0,8},{4,12},{8,0},{12,4},{16,24},{20,28},{24,16},{28,20},{1,9},{5... | collective-permute-start | bytes 159752 | tf_op jit(solution)/shard_map/ppermute | solution.py:436
  220.2 17.8 %collective-permute-start.28 = (bf16[104,256]{1,0:T(8,128)(2,1)}, bf16[104,256]{1,0:T(8,128)(2,1)}, u32[]{:S(2)}, u32[]{:S(2)}) collective-permute-start(bf16[104,256]{1,0:T(8,128)(2,1)} %z_sum.1.refs_0_), channel_id=1, source_target_pairs={{0,16},{4,20},{8,24},{12,28},{16,0},{20,4},{24,8},{28,12},{1,17},{... | collective-permute-start | bytes 159752 | tf_op jit(solution)/shard_map/ppermute | solution.py:436
  220.9 17.9 %collective-permute-start.29 = (bf16[104,256]{1,0:T(8,128)(2,1)}, bf16[104,256]{1,0:T(8,128)(2,1)}, u32[]{:S(2)}, u32[]{:S(2)}) collective-permute-start(bf16[104,256]{1,0:T(8,128)(2,1)} %z_sum.1.refs_0_), channel_id=1, source_target_pairs={{0,24},{4,28},{8,16},{12,20},{16,8},{20,12},{24,0},{28,4},{1,25},{... | collective-permute-start | bytes 159752 | tf_op jit(solution)/shard_map/ppermute | solution.py:436
  225.1 26.5 %collective-permute-start.33 = (bf16[128,1024]{1,0:T(8,128)(2,1)}, bf16[128,1024]{1,0:T(8,128)(2,1)}, u32[]{:S(2)}, u32[]{:S(2)}) collective-permute-start(bf16[128,1024]{1,0:T(8,128)(2,1)} %z_last_sum.3.refs_0_), channel_id=1, source_target_pairs={{0,2},{1,3},{2,0},{3,1},{4,6},{5,7},{6,4},{7,5},{8,10},{9,11},{10,... | collective-permute-start | bytes 786440 | tf_op jit(solution)/shard_map/ppermute | solution.py:436
  238.0 21.7 %collective-permute-start.36 = (bf16[128,1024]{1,0:T(8,128)(2,1)}, bf16[128,1024]{1,0:T(8,128)(2,1)}, u32[]{:S(2)}, u32[]{:S(2)}) collective-permute-start(bf16[128,1024]{1,0:T(8,128)(2,1)} %z_last_sum.3.refs_0_), channel_id=1, source_target_pairs={{0,1},{1,0},{2,3},{3,2},{4,5},{5,4},{6,7},{7,6},{8,9},{9,8},{10,11... | collective-permute-start | bytes 786440 | tf_op jit(solution)/shard_map/ppermute | solution.py:436
  241.1 15.3 %collective-permute-start.38 = (bf16[2,128,1024]{2,1,0:T(8,128)(2,1)}, bf16[2,128,1024]{2,1,0:T(8,128)(2,1)}, u32[]{:S(2)}, u32[]{:S(2)}) collective-permute-start(bf16[2,128,1024]{2,1,0:T(8,128)(2,1)} %pair_sum.5), channel_id=1, source_target_pairs={{0,8},{4,12},{8,0},{12,4},{16,24},{20,28},{24,16},{28,20},{1,9},{5... | collective-permute-start | bytes 1572872 | tf_op jit(solution)/shard_map/ppermute | solution.py:436
  243.4 10.8 %collective-permute-start.32 = (bf16[416,256]{1,0:T(8,128)(2,1)}, bf16[416,256]{1,0:T(8,128)(2,1)}, u32[]{:S(2)}, u32[]{:S(2)}) collective-permute-start(bf16[416,256]{1,0:T(8,128)(2,1)} %bitcast.87), channel_id=1, source_target_pairs={{0,4},{4,0},{8,12},{12,8},{16,20},{20,16},{24,28},{28,24},{1,5},{5... | collective-permute-start | bytes 638984 | tf_op jit(solution)/shard_map/ppermute | solution.py:436
  244.6 9.7 %all-to-all-start.6 = ((bf16[4,192,128]{2,1,0:T(8,128)(2,1)}), bf16[4,192,128]{2,1,0:T(8,128)(2,1)}, u32[]{:S(2)}, u32[]{:S(2)}) async-start(bf16[4,192,128]{2,1,0:T(8,128)(2,1)} %bitcast.31), calls=%async_computation.6 | async-start | bytes 393216 | tf_op jit(solution)/shard_map/all_to_all | solution.py:1099
  251.5 29.7 %collective-permute-start.44 = (bf16[128,1280]{1,0:T(8,128)(2,1)}, bf16[128,1280]{1,0:T(8,128)(2,1)}, u32[]{:S(2)}, u32[]{:S(2)}) collective-permute-start(bf16[128,1280]{1,0:T(8,128)(2,1)} %z_last_sum.5.refs_0_), channel_id=1, source_target_pairs={{0,1},{1,0},{2,3},{3,2},{4,5},{5,4},{6,7},{7,6},{8,9},{9,8},{10,11... | collective-permute-start | bytes 983048 | tf_op jit(solution)/shard_map/ppermute | solution.py:436
  251.6 9.6 %collective-permute-start.45 = (bf16[128,1280]{1,0:T(8,128)(2,1)}, bf16[128,1280]{1,0:T(8,128)(2,1)}, u32[]{:S(2)}, u32[]{:S(2)}) collective-permute-start(bf16[128,1280]{1,0:T(8,128)(2,1)} %z_last_sum.5.refs_0_), channel_id=1, source_target_pairs={{0,2},{1,3},{2,0},{3,1},{4,6},{5,7},{6,4},{7,5},{8,10},{9,11},{10,... | collective-permute-start | bytes 983048 | tf_op jit(solution)/shard_map/ppermute | solution.py:436
  256.1 14.3 %collective-permute-start.35 = (bf16[832,256]{1,0:T(8,128)(2,1)}, bf16[832,256]{1,0:T(8,128)(2,1)}, u32[]{:S(2)}, u32[]{:S(2)}) collective-permute-start(bf16[832,256]{1,0:T(8,128)(2,1)} %bitcast.34.m0), channel_id=1, source_target_pairs={{0,2},{1,3},{2,0},{3,1},{4,6},{5,7},{6,4},{7,5},{8,10},{9,11},{10,... | collective-permute-start | bytes 1277960 | tf_op jit(solution)/shard_map/ppermute | solution.py:436
  256.4 6.5 %collective-permute-start.37 = (bf16[128,1024]{1,0:T(8,128)(2,1)}, bf16[128,1024]{1,0:T(8,128)(2,1)}, u32[]{:S(2)}, u32[]{:S(2)}) collective-permute-start(bf16[128,1024]{1,0:T(8,128)(2,1)} %collective-permute-done.33.refs_2_), channel_id=1, source_target_pairs={{0,1},{1,0},{2,3},{3,2},{4,5},{5,4},{6,7},{7,6},{8,9},{9,8},{10,11... | collective-permute-start | bytes 786440 | tf_op jit(solution)/shard_map/ppermute | solution.py:436
  259.7 29.1 %collective-permute-start.34 = (bf16[832,256]{1,0:T(8,128)(2,1)}, bf16[832,256]{1,0:T(8,128)(2,1)}, u32[]{:S(2)}, u32[]{:S(2)}) collective-permute-start(bf16[832,256]{1,0:T(8,128)(2,1)} %bitcast.34.m0), channel_id=1, source_target_pairs={{0,1},{1,0},{2,3},{3,2},{4,5},{5,4},{6,7},{7,6},{8,9},{9,8},{10,11... | collective-permute-start | bytes 1277960 | tf_op jit(solution)/shard_map/ppermute | solution.py:436
  261.2 20.0 %collective-permute-start.46 = (bf16[128,1280]{1,0:T(8,128)(2,1)}, bf16[128,1280]{1,0:T(8,128)(2,1)}, u32[]{:S(2)}, u32[]{:S(2)}) collective-permute-start(bf16[128,1280]{1,0:T(8,128)(2,1)} %collective-permute-done.45.refs_2_), channel_id=1, source_target_pairs={{0,1},{1,0},{2,3},{3,2},{4,5},{5,4},{6,7},{7,6},{8,9},{9,8},{10,11... | collective-permute-start | bytes 983048 | tf_op jit(solution)/shard_map/ppermute | solution.py:436
  262.9 15.1 %collective-permute-start.40 = (bf16[128,1024]{1,0:T(8,128)(2,1)}, bf16[128,1024]{1,0:T(8,128)(2,1)}, u32[]{:S(2)}, u32[]{:S(2)}) collective-permute-start(bf16[128,1024]{1,0:T(8,128)(2,1)} %get-tuple-element.297), channel_id=1, source_target_pairs={{0,16},{4,20},{8,24},{12,28},{16,0},{20,4},{24,8},{28,12},{1,17},{... | collective-permute-start | bytes 786440 | tf_op jit(solution)/shard_map/ppermute | solution.py:436
  270.3 18.5 %collective-permute-start.39 = (bf16[832,256]{1,0:T(8,128)(2,1)}, bf16[832,256]{1,0:T(8,128)(2,1)}, u32[]{:S(2)}, u32[]{:S(2)}) collective-permute-start(bf16[832,256]{1,0:T(8,128)(2,1)} %collective-permute-done.35.m2), channel_id=1, source_target_pairs={{0,1},{1,0},{2,3},{3,2},{4,5},{5,4},{6,7},{7,6},{8,9},{9,8},{10,11... | collective-permute-start | bytes 1277960 | tf_op jit(solution)/shard_map/ppermute | solution.py:436
  279.8 7.8 %collective-permute-start.42 = (bf16[128,1024]{1,0:T(8,128)(2,1)}, bf16[128,1024]{1,0:T(8,128)(2,1)}, u32[]{:S(2)}, u32[]{:S(2)}) collective-permute-start(bf16[128,1024]{1,0:T(8,128)(2,1)} %z_last_sum.4.refs_0_), channel_id=1, source_target_pairs={{0,2},{1,3},{2,0},{3,1},{4,6},{5,7},{6,4},{7,5},{8,10},{9,11},{10,... | collective-permute-start | bytes 786440 | tf_op jit(solution)/shard_map/ppermute | solution.py:436
  284.1 10.9 %collective-permute-start.41 = (bf16[128,1024]{1,0:T(8,128)(2,1)}, bf16[128,1024]{1,0:T(8,128)(2,1)}, u32[]{:S(2)}, u32[]{:S(2)}) collective-permute-start(bf16[128,1024]{1,0:T(8,128)(2,1)} %z_last_sum.4.refs_0_), channel_id=1, source_target_pairs={{0,1},{1,0},{2,3},{3,2},{4,5},{5,4},{6,7},{7,6},{8,9},{9,8},{10,11... | collective-permute-start | bytes 786440 | tf_op jit(solution)/shard_map/ppermute | solution.py:436
  287.5 7.5 %collective-permute-start.43 = (bf16[128,1024]{1,0:T(8,128)(2,1)}, bf16[128,1024]{1,0:T(8,128)(2,1)}, u32[]{:S(2)}, u32[]{:S(2)}) collective-permute-start(bf16[128,1024]{1,0:T(8,128)(2,1)} %collective-permute-done.42.refs_2_), channel_id=1, source_target_pairs={{0,1},{1,0},{2,3},{3,2},{4,5},{5,4},{6,7},{7,6},{8,9},{9,8},{10,11... | collective-permute-start | bytes 786440 | tf_op jit(solution)/shard_map/ppermute | solution.py:436
  (18 other events, 73.4 us)

commit v3 on v2

--- a/solution.py
+++ b/solution.py
@@ -45,15 +45,23 @@
 
 
 def front_forward_kernel(
-    pixels, ids_ref, field_ref, spread_ref, bias_ref, vwt_ref, vet_ref, x_ref, p_ref, mixed_ref, mt_ref
+    pixels, ids_ref, field_ref, weight_ref, bias_ref, vwt_ref, vet_ref, x_ref, p_ref, mixed_ref, spread_ref, mt_ref
 ):
     seg = field_ref.shape[1]
     head_dim = mixed_ref.shape[1] // HEADS
     for slot in range(VARS):
         start = pl.multiple_of(ids_ref[0, slot] * pixels, pixels)
         x_ref[pl.ds(start, pixels), :] = field_ref[slot * pixels : (slot + 1) * pixels, :]
-    scores = mm(spread_ref[...], x_ref[...]) + bias_ref[...]
-    scores = scores.reshape(HEADS, VARS, seg)
+    rows = VARS * pixels
+    mine = lax.broadcasted_iota(jnp.int32, (VARS, rows), 1) // pixels
+    mine = mine == lax.broadcasted_iota(jnp.int32, (VARS, rows), 0)
+    bias = bias_ref[...].T
+    parts = []
+    for h in range(HEADS):
+        spread = jnp.where(mine, weight_ref[h : h + 1, :], 0.0).astype(BF16)
+        spread_ref[h * VARS : (h + 1) * VARS, :] = spread
+        parts.append(mm(spread, x_ref[...]) + bias[:, h : h + 1])
+    scores = jnp.stack(parts)
     top = jnp.max(scores, axis=1, keepdims=True)
     exponent = jnp.exp(scores - top)
     total = jnp.sum(exponent, axis=1, keepdims=True)
@@ -67,11 +75,11 @@
         mt_ref[rows, :] = mm(vwt_ref[rows, :], scaled) + mm(vet_ref[rows, :], shares.astype(BF16))
         return carry
 
-    lax.fori_loop(0, HEADS, head, 0)
+    lax.fori_loop(0, HEADS, head, 0, unroll=4)
     mixed_ref[...] = mt_ref[...].T.astype(BF16)
 
 
-def front_forward(own_ids, own_field, spread, bias, vwt, vet):
+def front_forward(own_ids, own_field, score_weight, bias, vwt, vet):
     rows, seg = own_field.shape
     width = vwt.shape[0]
     vmem = pl.BlockSpec(memory_space=pltpu.VMEM)
@@ -81,13 +89,14 @@
             jax.ShapeDtypeStruct((rows, seg), BF16),
             jax.ShapeDtypeStruct((HEADS * VARS, seg), F32),
             jax.ShapeDtypeStruct((seg, width), BF16),
+            jax.ShapeDtypeStruct((HEADS * VARS, rows), BF16),
         ),
         in_specs=[pl.BlockSpec(memory_space=pltpu.SMEM)] + [vmem] * 5,
-        out_specs=(vmem,) * 3,
+        out_specs=(vmem,) * 4,
         scratch_shapes=[pltpu.VMEM((width, seg), F32)],
         cost_estimate=cost(60000000000),
         name="front_forward",
-    )(own_ids, own_field, spread, bias, vwt, vet)
+    )(own_ids, own_field, score_weight, bias, vwt, vet)
 
 
 def front_backward_kernel(
@@ -253,7 +262,7 @@
     parts, triple_rows, width = qkv.shape
     full = parts * triple_rows // 3
     vmem = pl.BlockSpec(memory_space=pltpu.VMEM)
-    block = min(256, full)
+    block = min(512, full)
     return pl.pallas_call(
         functools.partial(attend_forward_kernel, head_dim, block),
         out_shape=(
@@ -406,7 +415,11 @@
         values = [member(right, s)[:, pl.ds(right_start, cols)] for s in range(4)]
         values = jnp.concatenate(values, axis=0)
         for out, side, blocks in zip(outs, sides, away + near):
-            for slot, k in enumerate(blocks):
+
+            def step(slot, carry, out=out, side=side, blocks=blocks, start=start):
+                k = blocks[0] + 2 * slot
+                if len(blocks) == 4:
+                    k = jnp.where(slot < 2, k, 2 * slot - 4)
                 source = 2 * (place_ref[Z] ^ k) + side
                 group = [member(left, s) for s in range(4)]
                 if len(group[0].shape) == 3:
@@ -416,6 +429,9 @@
                     factor = [ref[:, block] for ref in group]
                 factor = jnp.concatenate(factor, axis=0)
                 out[slot, :, start : start + cols] = mm(factor, values, TN).astype(BF16)
+                return carry
+
+            lax.fori_loop(0, len(blocks), step, 0)
         start += cols
 
 
@@ -595,6 +611,7 @@
 
 
 def middle_kernel(
+    sub,
     place_ref,
     att_ref,
     front_ref,
@@ -616,9 +633,9 @@
     own = width // parts
     me = place_ref[0]
     block = win_ref.shape[1]
-    slot = block // 4
+    slot = block // (4 * sub)
     quarter = width // 4
-    hidden = slot * pl.num_programs(0)
+    hidden = slot * sub * pl.num_programs(0)
 
     @pl.when(step == 0)
     def _():
@@ -643,9 +660,10 @@
     inner_grad = (mm(og_ref[...], wout_ref[...], NT) * slope).astype(BF16)
     back_ref[...] += mm(inner_grad, win_ref[...], NT)
     wide_ref[...] = active
-    cols = pl.ds(pl.multiple_of(step * slot, slot), slot)
-    for s in range(4):
-        actives[s][:, cols] = wide_ref[:, pl.ds(pl.multiple_of((me ^ s) * slot, slot), slot)]
+    for q in range(sub):
+        cols = pl.ds(pl.multiple_of((step * sub + q) * slot, slot), slot)
+        for s in range(4):
+            actives[s][:, cols] = wide_ref[:, pl.ds(pl.multiple_of((4 * q + (me ^ s)) * slot, slot), slot)]
     owner = step * block // hidden
     place = pl.ds(pl.multiple_of(step * block - owner * hidden, block), block)
     for s in range(4):
@@ -679,7 +697,8 @@
     seg, width = front_out.shape
     hidden = mlp_in.shape[1]
     parts = attended.shape[0]
-    block = hidden // parts
+    sub = 2
+    block = hidden * sub // parts
     shape = jax.ShapeDtypeStruct
 
     def still(*dims):
@@ -687,8 +706,8 @@
 
     piece, wider = shape((seg, hidden // 4), BF16), shape((seg, hidden // 4 + width // 4), BF16)
     return pl.pallas_call(
-        middle_kernel,
-        grid=(parts,),
+        functools.partial(middle_kernel, sub),
+        grid=(parts // sub,),
         out_shape=(
             shape((seg, width), BF16),
             shape((seg, width), BF16),
@@ -940,10 +959,7 @@
     score_weight = mm(key_query_parts, weight_rows, (((0,), (1,)), ((), ())))
     score_weight = score_weight[:HEADS] + score_weight[HEADS:]
     score_embed = mm(key_query_parts, var_embed, (((0,), (1,)), ((), ())))
-    score_embed = (score_embed[:HEADS] + score_embed[HEADS:]).reshape(HEADS * VARS, 1)
-    same_var = (jnp.arange(VARS)[:, None] == jnp.arange(VARS * pixels)[None, :] // pixels)[None]
-    spread = jnp.where(same_var, score_weight[:, None, :], 0.0).astype(BF16)
-    spread = spread.reshape(HEADS * VARS, VARS * pixels)
+    score_embed = score_embed[:HEADS] + score_embed[HEADS:]
     vwt = mm(value_proj, weight_rows, (((0,), (1,)), ((), ()))).astype(BF16)
     vet = mm(value_proj, var_embed, (((0,), (1,)), ((), ()))).astype(BF16)
 
@@ -976,7 +992,7 @@
             own_query(line),
         )
 
-    x_own, shares, mixed_low = front_forward(own_ids, own_field, spread, score_embed, vwt, vet)
+    x_own, shares, mixed_low, spread = front_forward(own_ids, own_field, score_weight, score_embed, vwt, vet)
 
     front_out = mm(mixed_low, agg_out) * valid_rows
     normed_one, norm_one_pull = jax.vjp(layer_norm, front_out, norm_one.astype(F32))

time: 301 us -> 300 us (level)
    pallas_call x22, Pallas kernels: 59.1 us -> 67 us  [small_call(): pl.pallas_call(kernel, out_shape=tuple((jax.ShapeDtypeStruct(dims, dtype)...]
  transfers between devices with their start and end apart: 54 -> 54, of which waited for: 15 -> 14; matrix products, arithmetic and copies ran while one was open for 9% -> 9% of each run, Pallas kernels for 38% -> 39%
where the time goes in v3:
time: 300 us; the launch traced here: 299 us
  Pallas kernels  123 us (41%)
  starting transfers between devices  76 us (25%)
  waiting for transfers between devices  60.8 us (20%)
  matrix products  17.1 us (6%)
  local copies, waits for them, and re-layouts  13.2 us (4%)
  other arithmetic  7.1 us (2%)
    pallas_call x22, Pallas kernels, small_call(): pl.pallas_call(kernel, out_shape=tuple((jax.ShapeDtypeStruct(dims, dtype)...  67 us
    ppermute x47, waiting for transfers between devices, swap(): lax.ppermute(values, axis, [(i, i ^ bit) for i in range(lax.axis_size(axi...  43.4 us
    ppermute x47, starting transfers between devices, swap(): lax.ppermute(values, axis, [(i, i ^ bit) for i in range(lax.axis_size(axi...  43.2 us
    all_to_all x4, starting transfers between devices, to_heads(): lax.all_to_all(values, 'patch', split_axis=0, concat_axis=0, tiled=True)  19 us
    dot_general x10, matrix products, mm(): lax.dot_general(a, b, dims, precision=precision, preferred_element_type=F32)  17.1 us
    pallas_call x1, Pallas kernels, middle(): pl.pallas_call(functools.partial(middle_kernel, sub), grid=(parts // sub,...  16.3 us
    all_to_all x4, waiting for transfers between devices, to_heads(): lax.all_to_all(values, 'patch', split_axis=0, concat_axis=0, tiled=True)  15 us
    pallas_call x1, Pallas kernels, attend_backward(): pl.pallas_call(functools.partial(attend_backward_kernel, head_dim, block)...  11 us
  transfers between devices with their start and end apart: 54, of which 14 were waited for; matrix products, arithmetic and copies ran while one was open for 9% of the time, Pallas kernels for 39%

profile of v3, /device:TPU:1, one launch (start us, length us, event | category | flops | bytes accessed | tf_op | source)
XLA Modules:
  0.0 298.6 jit_solution(17498553411981709622)
XLA Ops:
  0.7 4.3 %all-to-all-start = ((bf16[4,192,128]{2,1,0:T(8,128)(2,1)}), bf16[4,192,128]{2,1,0:T(8,128)(2,1)S(1)}, u32[]{:S(2)}, u32[]{:S(2)}) async-start(bf16[4,192,128]{2,1,0:T(8,128)(2,1)} %bitcast.79), calls=%async_computation | async-start | bytes 393216 | tf_op jit(solution)/shard_map/all_to_all | solution.py:943
  5.8 2.1 fusion.18.aggq_ref
  10.1 3.0 %convolution_convert_fusion.2.vwt_ref = bf16[1024,768]{1,0:T(8,128)(2,1)} fusion(bf16[1024,1024]{1,0:T(8,128)(2,1)S(1)} %copy-done.2, bf16[768,1024]{1,0:T(8,128)(2,1)S(1)} %bitcast.75), kind=kOutput, calls=%fused_computation.2 | convolution fusion | flops 1611399168 | bytes 5242880 | tf_op jit(solution)/shard_map/dot_general | solution.py:28
  18.4 4.8 %front_forward.1 = (bf16[768,128]{1,0:T(8,128)(2,1)}, f32[768,128]{1,0:T(8,128)}, bf16[128,1024]{1,0:T(8,128)(2,1)}, bf16[768,768]{1,0:T(8,128)(2,1)}) custom-call(s32[1,48]{1,0:T(1,128)} %constant_dynamic-slice_fusion.4.ids_ref, bf16[768,128]{1,0:T(8,128)(2,1)} %bitcast.80, f32[16,768]{1,0:T(8,128)} %slice_add_fusion.1.weight_ref, ...), custom_call_target="tpu_custom_call" | custom-call | flops 60000002048 | bytes 1048576 | tf_op jit(solution)/shard_map/front_forward/pallas_call | solution.py:86
  23.1 2.2 fusion.17
  25.7 3.8 %convolution_convert_fusion = bf16[128,3072]{1,0:T(8,128)(2,1)S(1)} fusion(bf16[128,1024]{1,0:T(8,128)(2,1)S(1)} %multiply_convert_fusion, bf16[1024,3072]{1,0:T(8,128)(2,1)} %wqkv_ref.1), kind=kOutput, calls=%fused_computation | convolution fusion | flops 805699584 | bytes 7340032 | tf_op jit(solution)/shard_map/dot_general | solution.py:28
  30.8 6.1 %all-to-all-start.1 = ((bf16[8,384,128]{2,1,0:T(8,128)(2,1)}), bf16[8,384,128]{2,1,0:T(8,128)(2,1)}, u32[]{:S(2)}, u32[]{:S(2)}) async-start(bf16[8,384,128]{2,1,0:T(8,128)(2,1)} %bitcast.14), calls=%async_computation.1 | async-start | bytes 1572864 | tf_op jit(solution)/shard_map/all_to_all | solution.py:392
  41.8 1.6 constant_dynamic-slice_fusion.3.weight_own_ref
  43.4 1.8 constant_dynamic-slice_fusion
  46.3 3.0 fusion.vw_ref
  49.3 7.7 %all-to-all-done.1.qkv_ref = bf16[8,384,128]{2,1,0:T(8,128)(2,1)} async-done(((bf16[8,384,128]{2,1,0:T(8,128)(2,1)}), bf16[8,384,128]{2,1,0:T(8,128)(2,1)}, u32[]{:S(2)}, u32[]{:S(2)}) %all-to-all-start.1) | async-done | bytes 786464 | tf_op jit(solution)/shard_map/all_to_all | solution.py:392
  57.0 6.8 %attend_forward.1 = (bf16[1024,128]{1,0:T(8,128)(2,1)}, f32[2,1024]{1,0:T(2,128)}) custom-call(s32[1,1]{1,0:T(1,128)} %bitcast.5.count_ref, bf16[8,384,128]{2,1,0:T(8,128)(2,1)} %all-to-all-done.1.qkv_ref), custom_call_target="tpu_custom_call" | custom-call | flops 60000002048 | bytes 1048576 | tf_op jit(solution)/shard_map/attend_forward/pallas_call | solution.py:266
  63.8 4.0 %all-to-all-start.2 = ((bf16[8,128,128]{2,1,0:T(8,128)(2,1)}), bf16[8,128,128]{2,1,0:T(8,128)(2,1)S(1)}, u32[]{:S(2)}, u32[]{:S(2)}) async-start(bf16[8,128,128]{2,1,0:T(8,128)(2,1)} %bitcast.77), calls=%async_computation.2 | async-start | bytes 524288 | tf_op jit(solution)/shard_map/all_to_all | solution.py:392
  71.0 4.4 %all-to-all-done.2.att_ref.refs_4_ = bf16[8,128,128]{2,1,0:T(8,128)(2,1)S(1)} async-done(((bf16[8,128,128]{2,1,0:T(8,128)(2,1)}), bf16[8,128,128]{2,1,0:T(8,128)(2,1)S(1)}, u32[]{:S(2)}, u32[]{:S(2)}) %all-to-all-start.2) | async-done | bytes 262176 | tf_op jit(solution)/shard_map/all_to_all | solution.py:392
  75.4 2.3 collective-permute-start
  79.3 16.3 %trunk_middle.1 = (bf16[128,1024]{1,0:T(8,128)(2,1)}, bf16[128,1024]{1,0:T(8,128)(2,1)}, bf16[128,1024]{1,0:T(8,128)(2,1)}, bf16[128,1024]{1,0:T(8,128)(2,1)}, b...) custom-call(s32[5]{0:T(128)} %stack.23.place_ref, ...), custom_call_target="tpu_custom_call" | custom-call | flops 99999997952 | bytes 1048576 | tf_op jit(solution)/shard_map/trunk_middle/pallas_call | solution.py:708
  95.7 3.4 %all-to-all-start.3 = ((bf16[8,128,128]{2,1,0:T(8,128)(2,1)}), bf16[8,128,128]{2,1,0:T(8,128)(2,1)S(1)}, u32[]{:S(2)}, u32[]{:S(2)}) async-start(bf16[8,128,128]{2,1,0:T(8,128)(2,1)} %get-tuple-element.188), calls=%async_computation.3 | async-start | bytes 524288 | tf_op jit(solution)/shard_map/all_to_all | solution.py:392
  102.1 2.0 collective-permute-start.9
  104.0 3.0 all-to-all-done.3
  107.7 11.0 %attend_backward.1 = bf16[8,384,128]{2,1,0:T(8,128)(2,1)} custom-call(s32[1,1]{1,0:T(1,128)} %bitcast.5.count_ref, bf16[8,384,128]{2,1,0:T(8,128)(2,1)} %all-to-all-done.1.qkv_ref, bf16[1024,128]{1,0:T(8,128)(2,1)} %bitcast.78, f32[2,1024]{1,0:T(2,128)} %get-tuple-element.189.lse_ref), custom_call_target="tpu_custom_call" | custom-call | flops 99999997952 | bytes 1048576 | tf_op jit(solution)/shard_map/attend_backward/pallas_call | solution.py:334
  119.4 5.4 %all-to-all-start.4 = ((bf16[8,384,128]{2,1,0:T(8,128)(2,1)}), bf16[8,384,128]{2,1,0:T(8,128)(2,1)}, u32[]{:S(2)}, u32[]{:S(2)}) async-start(bf16[8,384,128]{2,1,0:T(8,128)(2,1)} %attend_backward.1), calls=%async_computation.4 | async-start | bytes 1572864 | tf_op jit(solution)/shard_map/all_to_all | solution.py:392
  127.2 5.9 %weight_grads.3 = (bf16[4,128,1024]{2,1,0:T(8,128)(2,1)}, bf16[2,128,1024]{2,1,0:T(8,128)(2,1)}, bf16[2,128,1024]{2,1,0:T(8,128)(2,1)}) custom-call(s32[5]{0:T(128)} %stack.23.place_ref, bf16[128,1024]{1,0:T(8,128)(2,1)} %get-tuple-element.200.refs_0_, bf16[128,1024]{1,0:T(8,128)(2,1)} %copy-done.24, bf16[128,1024]{1,0:T(8,128)(2,1)} %copy-done.25, ...), custom_call_target="tpu_custom_call" | custom-call | flops 1999999991808 | bytes 1048576 | tf_op jit(solution)/shard_map/weight_grads/pallas_call | solution.py:465
  133.2 1.6 collective-permute-start.15
  134.8 7.5 %collective-permute-done.14.refs_11_ = bf16[128,1280]{1,0:T(8,128)(2,1)} collective-permute-done((bf16[128,1280]{1,0:T(8,128)(2,1)}, bf16[128,1280]{1,0:T(8,128)(2,1)}, u32[]{:S(2)}, u32[]{:S(2)}) %collective-permute-start.14) | collective-permute-done | bytes 327712 | tf_op jit(solution)/shard_map/ppermute | solution.py:452
  142.3 7.9 %weight_grads.4 = (bf16[2,128,1280]{2,1,0:T(8,128)(2,1)}, bf16[2,128,1280]{2,1,0:T(8,128)(2,1)}, bf16[2,128,1280]{2,1,0:T(8,128)(2,1)}, bf16[2,128,1280]{2,1,0:T(8,128)(2,1)}) custom-call(s32[5]{0:T(128)} %stack.23.place_ref, bf16[128,1024]{1,0:T(8,128)(2,1)} %get-tuple-element.210.refs_0_, bf16[128,1024]{1,0:T(8,128)(2,1)} %collective-permute-done.10.refs_1_, ...), custom_call_target="tpu_custom_call" | custom-call | flops 1999999991808 | bytes 1048576 | tf_op jit(solution)/shard_map/weight_grads/pallas_call | solution.py:465
  150.2 1.5 collective-permute-start.16
  151.7 8.5 %trunk_back.1 = (bf16[128,1024]{1,0:T(8,128)(2,1)}, f32[1,1024]{1,0:T(1,128)}, bf16[4,128,1024]{2,1,0:T(8,128)(2,1)}) custom-call(s32[5]{0:T(128)} %stack.23.place_ref, bf16[8,384,128]{2,1,0:T(8,128)(2,1)} %all-to-all-done.4.grads_ref, f32[128,1024]{1,0:T(8,128)} %copy-done.3, f32[1,1024]{1,0:T(1,128)} %bitcast.82, ...), custom_call_target="tpu_custom_call" | custom-call | flops 99999997952 | bytes 1048576 | tf_op jit(solution)/shard_map/trunk_back/pallas_call | solution.py:804
  160.2 4.5 %all-to-all-start.5 = ((bf16[4,128,1024]{2,1,0:T(8,128)(2,1)}), bf16[4,128,1024]{2,1,0:T(8,128)(2,1)}, u32[]{:S(2)}, u32[]{:S(2)}) async-start(bf16[4,128,1024]{2,1,0:T(8,128)(2,1)} %get-tuple-element.236), calls=%async_computation.5 | async-start | bytes 2097152 | tf_op jit(solution)/shard_map/all_to_all | solution.py:1051
  164.7 2.3 pair_sum.3
  168.2 8.9 %front_backward.1 = (bf16[768,128]{1,0:T(8,128)(2,1)}, bf16[2,832,256]{2,1,0:T(8,128)(2,1)}, bf16[2,832,256]{2,1,0:T(8,128)(2,1)}) custom-call(s32[5]{0:T(128)} %stack.23.place_ref, s32[1,48]{1,0:T(1,128)} %constant_dynamic-slice_fusion.4.ids_ref, bf16[768,128]{1,0:T(8,128)(2,1)} %get-tuple-element.186.x_ref, f32[768,128]{1,0:T(8,128)} %get-tuple-element.187.p_ref, ...), custom_call_target="tpu_custom_call" | custom-call | flops 100000000 | bytes 1048576 | tf_op jit(solution)/shard_map/front_backward/pallas_call | solution.py:209
  177.2 1.5 all-to-all-done.5.refs_4_
  179.2 2.3 pair_sum.4
  181.5 1.4 collective-permute-start.22
  182.9 2.4 core_sum.1
  185.5 2.4 z_first_sum.3
  187.9 2.1 collective-permute-start.26
  190.0 6.5 %collective-permute-done.18 = bf16[832,256]{1,0:T(8,128)(2,1)} collective-permute-done((bf16[832,256]{1,0:T(8,128)(2,1)}, bf16[832,256]{1,0:T(8,128)(2,1)}, u32[]{:S(2)}, u32[]{:S(2)}) %collective-permute-start.18) | collective-permute-done | bytes 426016 | tf_op jit(solution)/shard_map/ppermute | solution.py:452
  196.5 2.0 x_sum.1
  199.7 7.9 %weight_grads.5 = (bf16[4,128,1024]{2,1,0:T(8,128)(2,1)}, bf16[2,128,1024]{2,1,0:T(8,128)(2,1)}, bf16[2,128,1024]{2,1,0:T(8,128)(2,1)}) custom-call(s32[5]{0:T(128)} %stack.23.place_ref, bf16[128,3072]{1,0:T(8,128)(2,1)} %pad_maximum_fusion.refs_4_.refs_0_, bf16[128,3072]{1,0:T(8,128)(2,1)} %copy-done.19, ...), custom_call_target="tpu_custom_call" | custom-call | flops 1999999991808 | bytes 1048576 | tf_op jit(solution)/shard_map/weight_grads/pallas_call | solution.py:465
  207.8 1.8 z_pieces.1
  209.6 2.3 collective-permute-start.24
  213.1 2.5 z_first_sum.4
  217.5 1.5 z_sum.1.refs_0_
  220.2 2.4 collective-permute-start.29
  222.6 1.8 z_last_sum.3.refs_0_
  224.4 13.0 %collective-permute-done.28.refs_2_ = bf16[104,256]{1,0:T(8,128)(2,1)} collective-permute-done((bf16[104,256]{1,0:T(8,128)(2,1)}, bf16[104,256]{1,0:T(8,128)(2,1)}, u32[]{:S(2)}, u32[]{:S(2)}) %collective-permute-start.28) | collective-permute-done | bytes 53280 | tf_op jit(solution)/shard_map/ppermute | solution.py:452
  238.1 2.3 pair_sum.5
  241.1 1.6 z_join.1
  243.9 5.1 %all-to-all-start.6 = ((bf16[4,192,128]{2,1,0:T(8,128)(2,1)}), bf16[4,192,128]{2,1,0:T(8,128)(2,1)}, u32[]{:S(2)}, u32[]{:S(2)}) async-start(bf16[4,192,128]{2,1,0:T(8,128)(2,1)} %bitcast.30), calls=%async_computation.6 | async-start | bytes 393216 | tf_op jit(solution)/shard_map/all_to_all | solution.py:1115
  249.0 1.9 z_last_sum.5.refs_0_
  250.9 1.7 collective-permute-start.45
  253.6 1.8 y_join.1
  256.6 2.4 z_first_sum.5
  259.1 1.5 collective-permute-done.45.refs_2_
  260.6 1.7 collective-permute-start.46
  262.9 6.8 %collective-permute-done.35.m2 = bf16[832,256]{1,0:T(8,128)(2,1)} collective-permute-done((bf16[832,256]{1,0:T(8,128)(2,1)}, bf16[832,256]{1,0:T(8,128)(2,1)}, u32[]{:S(2)}, u32[]{:S(2)}) %collective-permute-start.35) | collective-permute-done | bytes 426016 | tf_op jit(solution)/shard_map/ppermute | solution.py:452
  270.7 2.7 join.5
  273.4 3.9 %collective-permute-done.40.got_ref = bf16[128,1024]{1,0:T(8,128)(2,1)} collective-permute-done((bf16[128,1024]{1,0:T(8,128)(2,1)}, bf16[128,1024]{1,0:T(8,128)(2,1)}, u32[]{:S(2)}, u32[]{:S(2)}) %collective-permute-start.40) | collective-permute-done | bytes 262176 | tf_op jit(solution)/shard_map/ppermute | solution.py:452
  277.3 1.8 z_last_sum.4.refs_0_
  280.5 2.9 join.4
  284.2 2.7 collective-permute-done.42.refs_2_
  288.2 6.2 %front_last.1 = (f32[128,1024]{1,0:T(8,128)}, f32[768,128]{1,0:T(8,128)}, f32[48,128]{1,0:T(8,128)}, f32[128,1024]{1,0:T(8,128)}, f32[128,1024]{1,0:T(8,128)}, /...) custom-call(s32[5]{0:T(128)} %stack.23.place_ref, bf16[832,256]{1,0:T(8,128)(2,1)} %bitcast.33.m0, ...), custom_call_target="tpu_custom_call" | custom-call | flops 199999995904 | bytes 1048576 | tf_op jit(solution)/shard_map/front_last/pallas_call | solution.py:465
  294.4 2.6 join.3
  297.0 1.6 copy.47
  (171 shorter events, 44.9 us)
Async XLA Ops:
  0.6 16.5 %copy-start = (s32[4,48]{1,0:T(4,128)S(1)}, s32[4,48]{1,0:T(4,128)}, u32[]{:S(2)}) copy-start(s32[4,48]{1,0:T(4,128)} %param.19) | copy-start | bytes 2308
  0.7 17.0 %all-to-all-start = ((bf16[4,192,128]{2,1,0:T(8,128)(2,1)}), bf16[4,192,128]{2,1,0:T(8,128)(2,1)S(1)}, u32[]{:S(2)}, u32[]{:S(2)}) async-start(bf16[4,192,128]{2,1,0:T(8,128)(2,1)} %bitcast.79), calls=%async_computation | async-start | bytes 393216 | tf_op jit(solution)/shard_map/all_to_all | solution.py:943
  15.7 21.3 %copy-start.7 = (bf16[128,1024]{1,0:T(8,128)(2,1)}, bf16[128,1024]{1,0:T(8,128)(2,1)S(1)}, u32[]{:S(2)}) copy-start(bf16[128,1024]{1,0:T(8,128)(2,1)S(1)} %fusion.2.og_ref) | copy-start | bytes 786436
  30.8 26.2 %all-to-all-start.1 = ((bf16[8,384,128]{2,1,0:T(8,128)(2,1)}), bf16[8,384,128]{2,1,0:T(8,128)(2,1)}, u32[]{:S(2)}, u32[]{:S(2)}) async-start(bf16[8,384,128]{2,1,0:T(8,128)(2,1)} %bitcast.14), calls=%async_computation.1 | async-start | bytes 1572864 | tf_op jit(solution)/shard_map/all_to_all | solution.py:392
  37.9 33.2 %collective-permute-start.4 = (bf16[128,3072]{1,0:T(8,128)(2,1)}, bf16[128,3072]{1,0:T(8,128)(2,1)}, u32[]{:S(2)}, u32[]{:S(2)}) collective-permute-start(bf16[128,3072]{1,0:T(8,128)(2,1)} %pad_maximum_fusion.refs_4_.refs_0_), channel_id=1, source_target_pairs={{0,2},{1,3},{2,0},{3,1},{4,6},{5,7},{6,4},{7,5},{8,10},{9,11},{10,... | collective-permute-start | bytes 2359304 | tf_op jit(solution)/shard_map/ppermute | solution.py:452
  57.0 10.9 %copy-start.17 = (bf16[1024]{0:T(1024)(128)(2,1)S(1)}, bf16[1024]{0:T(1024)(128)(2,1)}, u32[]{:S(2)}) copy-start(bf16[1024]{0:T(1024)(128)(2,1)} %param.30) | copy-start | bytes 6148
  63.8 11.6 %all-to-all-start.2 = ((bf16[8,128,128]{2,1,0:T(8,128)(2,1)}), bf16[8,128,128]{2,1,0:T(8,128)(2,1)S(1)}, u32[]{:S(2)}, u32[]{:S(2)}) async-start(bf16[8,128,128]{2,1,0:T(8,128)(2,1)} %bitcast.77), calls=%async_computation.2 | async-start | bytes 524288 | tf_op jit(solution)/shard_map/all_to_all | solution.py:392
  70.3 25.3 %collective-permute-start.3 = (bf16[128,3072]{1,0:T(8,128)(2,1)}, bf16[128,3072]{1,0:T(8,128)(2,1)S(1)}, u32[]{:S(2)}, u32[]{:S(2)}) collective-permute-start(bf16[128,3072]{1,0:T(8,128)(2,1)} %pad_maximum_fusion.refs_4_.refs_0_), channel_id=1, source_target_pairs={{0,1},{1,0},{2,3},{3,2},{4,5},{5,4},{6,7},{7,6},{8,9},{9,8},{10,11... | collective-permute-start | bytes 2359304 | tf_op jit(solution)/shard_map/ppermute | solution.py:452
  71.0 24.6 %collective-permute-start.5 = (bf16[128,3072]{1,0:T(8,128)(2,1)}, bf16[128,3072]{1,0:T(8,128)(2,1)S(1)}, u32[]{:S(2)}, u32[]{:S(2)}) collective-permute-start(bf16[128,3072]{1,0:T(8,128)(2,1)} %collective-permute-done.4.refs_6_.refs_2_), channel_id=1, source_target_pairs={{0,1},{1,0},{2,3},{3,2},{4,5},{5,4},{6,7},{7,6},{8,9},{9,8},{10,11... | collective-permute-start | bytes 2359304 | tf_op jit(solution)/shard_map/ppermute | solution.py:452
  75.4 20.2 %collective-permute-start = (bf16[8,128,128]{2,1,0:T(8,128)(2,1)S(1)}, bf16[8,128,128]{2,1,0:T(8,128)(2,1)S(1)}, u32[]{:S(2)}, u32[]{:S(2)}) collective-permute-start(bf16[8,128,128]{2,1,0:T(8,128)(2,1)S(1)} %all-to-all-done.2.att_ref.refs_4_), channel_id=1, source_target_pairs={{0,1},{1,0},{2,3},{3,2},{4,5},{5,4},{6,7},{7,6},{8,9},{9,8},{10,11... | collective-permute-start | bytes 786440 | tf_op jit(solution)/shard_map/ppermute | solution.py:452
  77.7 18.0 %collective-permute-start.1 = (bf16[8,128,128]{2,1,0:T(8,128)(2,1)S(1)}, bf16[8,128,128]{2,1,0:T(8,128)(2,1)S(1)}, u32[]{:S(2)}, u32[]{:S(2)}) collective-permute-start(bf16[8,128,128]{2,1,0:T(8,128)(2,1)S(1)} %all-to-all-done.2.att_ref.refs_4_), channel_id=1, source_target_pairs={{0,2},{1,3},{2,0},{3,1},{4,6},{5,7},{6,4},{7,5},{8,10},{9,11},{10,... | collective-permute-start | bytes 786440 | tf_op jit(solution)/shard_map/ppermute | solution.py:452
  79.0 16.7 %collective-permute-start.2 = (bf16[8,128,128]{2,1,0:T(8,128)(2,1)S(1)}, bf16[8,128,128]{2,1,0:T(8,128)(2,1)S(1)}, u32[]{:S(2)}, u32[]{:S(2)}) collective-permute-start(bf16[8,128,128]{2,1,0:T(8,128)(2,1)S(1)} %all-to-all-done.2.att_ref.refs_4_), channel_id=1, source_target_pairs={{0,3},{1,2},{2,1},{3,0},{4,7},{5,6},{6,5},{7,4},{8,11},{9,10},{10,... | collective-permute-start | bytes 786440 | tf_op jit(solution)/shard_map/ppermute | solution.py:452
  79.3 19.8 %copy-start.18 = (f32[128,1]{0,1:T(1,128)S(1)}, f32[128,1]{0,1:T(1,128)}, u32[]{:S(2)}) copy-start(f32[128,1]{0,1:T(1,128)} %bitcast_convert_fusion) | copy-start | bytes 1540
  95.6 23.1 %copy-start.19 = (bf16[128,3072]{1,0:T(8,128)(2,1)}, bf16[128,3072]{1,0:T(8,128)(2,1)S(1)}, u32[]{:S(2)}) copy-start(bf16[128,3072]{1,0:T(8,128)(2,1)S(1)} %collective-permute-done.3.refs_5_.refs_1_) | copy-start | bytes 2359300
  95.6 23.0 %copy-start.20 = (bf16[128,3072]{1,0:T(8,128)(2,1)}, bf16[128,3072]{1,0:T(8,128)(2,1)S(1)}, u32[]{:S(2)}) copy-start(bf16[128,3072]{1,0:T(8,128)(2,1)S(1)} %collective-permute-done.5.refs_7_.refs_3_) | copy-start | bytes 2359300
  95.7 23.0 %copy-start.21 = (bf16[8,128,128]{2,1,0:T(8,128)(2,1)}, bf16[8,128,128]{2,1,0:T(8,128)(2,1)S(1)}, u32[]{:S(2)}) copy-start(bf16[8,128,128]{2,1,0:T(8,128)(2,1)S(1)} %collective-permute-done.refs_5_) | copy-start | bytes 786436
  95.7 23.0 %copy-start.22 = (bf16[8,128,128]{2,1,0:T(8,128)(2,1)}, bf16[8,128,128]{2,1,0:T(8,128)(2,1)S(1)}, u32[]{:S(2)}) copy-start(bf16[8,128,128]{2,1,0:T(8,128)(2,1)S(1)} %collective-permute-done.1.refs_6_) | copy-start | bytes 786436
  95.7 23.0 %copy-start.23 = (bf16[8,128,128]{2,1,0:T(8,128)(2,1)}, bf16[8,128,128]{2,1,0:T(8,128)(2,1)S(1)}, u32[]{:S(2)}) copy-start(bf16[8,128,128]{2,1,0:T(8,128)(2,1)S(1)} %collective-permute-done.2.refs_7_) | copy-start | bytes 786436
  95.7 11.3 %all-to-all-start.3 = ((bf16[8,128,128]{2,1,0:T(8,128)(2,1)}), bf16[8,128,128]{2,1,0:T(8,128)(2,1)S(1)}, u32[]{:S(2)}, u32[]{:S(2)}) async-start(bf16[8,128,128]{2,1,0:T(8,128)(2,1)} %get-tuple-element.188), calls=%async_computation.3 | async-start | bytes 524288 | tf_op jit(solution)/shard_map/all_to_all | solution.py:392
  99.9 18.8 %collective-permute-start.6 = (bf16[128,1024]{1,0:T(8,128)(2,1)}, bf16[128,1024]{1,0:T(8,128)(2,1)}, u32[]{:S(2)}, u32[]{:S(2)}) collective-permute-start(bf16[128,1024]{1,0:T(8,128)(2,1)} %get-tuple-element.210.refs_0_), channel_id=1, source_target_pairs={{0,2},{1,3},{2,0},{3,1},{4,6},{5,7},{6,4},{7,5},{8,10},{9,11},{10,... | collective-permute-start | bytes 786440 | tf_op jit(solution)/shard_map/ppermute | solution.py:452
  101.2 31.9 %collective-permute-start.10 = (bf16[128,1024]{1,0:T(8,128)(2,1)}, bf16[128,1024]{1,0:T(8,128)(2,1)}, u32[]{:S(2)}, u32[]{:S(2)}) collective-permute-start(bf16[128,1024]{1,0:T(8,128)(2,1)} %get-tuple-element.210.refs_0_), channel_id=1, source_target_pairs={{0,1},{1,0},{2,3},{3,2},{4,5},{5,4},{6,7},{7,6},{8,9},{9,8},{10,11... | collective-permute-start | bytes 786440 | tf_op jit(solution)/shard_map/ppermute | solution.py:452
  101.9 16.8 %collective-permute-start.7 = (bf16[128,1024]{1,0:T(8,128)(2,1)}, bf16[128,1024]{1,0:T(8,128)(2,1)S(1)}, u32[]{:S(2)}, u32[]{:S(2)}) collective-permute-start(bf16[128,1024]{1,0:T(8,128)(2,1)} %get-tuple-element.192), channel_id=1, source_target_pairs={{0,1},{1,0},{2,3},{3,2},{4,5},{5,4},{6,7},{7,6},{8,9},{9,8},{10,11... | collective-permute-start | bytes 786440 | tf_op jit(solution)/shard_map/ppermute | solution.py:452
  101.9 16.8 %collective-permute-start.8 = (bf16[128,1024]{1,0:T(8,128)(2,1)}, bf16[128,1024]{1,0:T(8,128)(2,1)S(1)}, u32[]{:S(2)}, u32[]{:S(2)}) collective-permute-start(bf16[128,1024]{1,0:T(8,128)(2,1)} %get-tuple-element.193), channel_id=1, source_target_pairs={{0,2},{1,3},{2,0},{3,1},{4,6},{5,7},{6,4},{7,5},{8,10},{9,11},{10,... | collective-permute-start | bytes 786440 | tf_op jit(solution)/shard_map/ppermute | solution.py:452
  102.1 17.3 %collective-permute-start.9 = (bf16[128,1024]{1,0:T(8,128)(2,1)}, bf16[128,1024]{1,0:T(8,128)(2,1)S(1)}, u32[]{:S(2)}, u32[]{:S(2)}) collective-permute-start(bf16[128,1024]{1,0:T(8,128)(2,1)} %get-tuple-element.194), channel_id=1, source_target_pairs={{0,3},{1,2},{2,1},{3,0},{4,7},{5,6},{6,5},{7,4},{8,11},{9,10},{10,... | collective-permute-start | bytes 786440 | tf_op jit(solution)/shard_map/ppermute | solution.py:452
  118.7 8.5 %copy-start.24 = (bf16[128,1024]{1,0:T(8,128)(2,1)}, bf16[128,1024]{1,0:T(8,128)(2,1)S(1)}, u32[]{:S(2)}) copy-start(bf16[128,1024]{1,0:T(8,128)(2,1)S(1)} %collective-permute-done.7.refs_1_) | copy-start | bytes 786436
  119.4 32.3 %all-to-all-start.4 = ((bf16[8,384,128]{2,1,0:T(8,128)(2,1)}), bf16[8,384,128]{2,1,0:T(8,128)(2,1)}, u32[]{:S(2)}, u32[]{:S(2)}) async-start(bf16[8,384,128]{2,1,0:T(8,128)(2,1)} %attend_backward.1), calls=%async_computation.4 | async-start | bytes 1572864 | tf_op jit(solution)/shard_map/all_to_all | solution.py:392
  124.7 10.0 %collective-permute-start.11 = (bf16[128,1024]{1,0:T(8,128)(2,1)}, bf16[128,1024]{1,0:T(8,128)(2,1)}, u32[]{:S(2)}, u32[]{:S(2)}) collective-permute-start(bf16[128,1024]{1,0:T(8,128)(2,1)} %collective-permute-done.6.refs_2_), channel_id=1, source_target_pairs={{0,1},{1,0},{2,3},{3,2},{4,5},{5,4},{6,7},{7,6},{8,9},{9,8},{10,11... | collective-permute-start | bytes 786440 | tf_op jit(solution)/shard_map/ppermute | solution.py:452
  125.1 9.7 %collective-permute-start.12 = (bf16[128,1280]{1,0:T(8,128)(2,1)}, bf16[128,1280]{1,0:T(8,128)(2,1)}, u32[]{:S(2)}, u32[]{:S(2)}) collective-permute-start(bf16[128,1280]{1,0:T(8,128)(2,1)} %get-tuple-element.217), channel_id=1, source_target_pairs={{0,1},{1,0},{2,3},{3,2},{4,5},{5,4},{6,7},{7,6},{8,9},{9,8},{10,11... | collective-permute-start | bytes 983048 | tf_op jit(solution)/shard_map/ppermute | solution.py:452
  125.3 9.5 %collective-permute-start.13 = (bf16[128,1280]{1,0:T(8,128)(2,1)}, bf16[128,1280]{1,0:T(8,128)(2,1)}, u32[]{:S(2)}, u32[]{:S(2)}) collective-permute-start(bf16[128,1280]{1,0:T(8,128)(2,1)} %get-tuple-element.218), channel_id=1, source_target_pairs={{0,2},{1,3},{2,0},{3,1},{4,6},{5,7},{6,4},{7,5},{8,10},{9,11},{10,... | collective-permute-start | bytes 983048 | tf_op jit(solution)/shard_map/ppermute | solution.py:452
  126.6 15.8 %collective-permute-start.14 = (bf16[128,1280]{1,0:T(8,128)(2,1)}, bf16[128,1280]{1,0:T(8,128)(2,1)}, u32[]{:S(2)}, u32[]{:S(2)}) collective-permute-start(bf16[128,1280]{1,0:T(8,128)(2,1)} %get-tuple-element.219), channel_id=1, source_target_pairs={{0,3},{1,2},{2,1},{3,0},{4,7},{5,6},{6,5},{7,4},{8,11},{9,10},{10,... | collective-permute-start | bytes 983048 | tf_op jit(solution)/shard_map/ppermute | solution.py:452
  133.2 31.6 %collective-permute-start.15 = (bf16[4,128,1024]{2,1,0:T(8,128)(2,1)}, bf16[4,128,1024]{2,1,0:T(8,128)(2,1)}, u32[]{:S(2)}, u32[]{:S(2)}) collective-permute-start(bf16[4,128,1024]{2,1,0:T(8,128)(2,1)} %get-tuple-element.226), channel_id=1, source_target_pairs={{0,4},{4,0},{8,12},{12,8},{16,20},{20,16},{24,28},{28,24},{1,5},{5... | collective-permute-start | bytes 3145736 | tf_op jit(solution)/shard_map/ppermute | solution.py:452
  150.2 26.9 %collective-permute-start.16 = (bf16[2,128,1280]{2,1,0:T(8,128)(2,1)}, bf16[2,128,1280]{2,1,0:T(8,128)(2,1)}, u32[]{:S(2)}, u32[]{:S(2)}) collective-permute-start(bf16[2,128,1280]{2,1,0:T(8,128)(2,1)} %get-tuple-element.235), channel_id=1, source_target_pairs={{0,4},{4,0},{8,12},{12,8},{16,20},{20,16},{24,28},{28,24},{1,5},{5... | collective-permute-start | bytes 1966088 | tf_op jit(solution)/shard_map/ppermute | solution.py:452
  160.2 18.4 %all-to-all-start.5 = ((bf16[4,128,1024]{2,1,0:T(8,128)(2,1)}), bf16[4,128,1024]{2,1,0:T(8,128)(2,1)}, u32[]{:S(2)}, u32[]{:S(2)}) async-start(bf16[4,128,1024]{2,1,0:T(8,128)(2,1)} %get-tuple-element.236), calls=%async_computation.5 | async-start | bytes 2097152 | tf_op jit(solution)/shard_map/all_to_all | solution.py:1051
  167.0 18.5 %collective-permute-start.19 = (bf16[2,128,1024]{2,1,0:T(8,128)(2,1)}, bf16[2,128,1024]{2,1,0:T(8,128)(2,1)}, u32[]{:S(2)}, u32[]{:S(2)}) collective-permute-start(bf16[2,128,1024]{2,1,0:T(8,128)(2,1)} %pair_sum.3), channel_id=1, source_target_pairs={{0,8},{4,12},{8,0},{12,4},{16,24},{20,28},{24,16},{28,20},{1,9},{5... | collective-permute-start | bytes 1572872 | tf_op jit(solution)/shard_map/ppermute | solution.py:452
  178.6 4.3 %collective-permute-start.17 = (bf16[2,832,256]{2,1,0:T(8,128)(2,1)}, bf16[2,832,256]{2,1,0:T(8,128)(2,1)}, u32[]{:S(2)}, u32[]{:S(2)}) collective-permute-start(bf16[2,832,256]{2,1,0:T(8,128)(2,1)} %get-tuple-element.238), channel_id=1, source_target_pairs={{0,1},{1,0},{2,3},{3,2},{4,5},{5,4},{6,7},{7,6},{8,9},{9,8},{10,11... | collective-permute-start | bytes 2555912 | tf_op jit(solution)/shard_map/ppermute | solution.py:452
  181.5 26.3 %collective-permute-start.21 = (bf16[2,128,1280]{2,1,0:T(8,128)(2,1)}, bf16[2,128,1280]{2,1,0:T(8,128)(2,1)}, u32[]{:S(2)}, u32[]{:S(2)}) collective-permute-start(bf16[2,128,1280]{2,1,0:T(8,128)(2,1)} %get-tuple-element.249), channel_id=1, source_target_pairs={{0,4},{4,0},{8,12},{12,8},{16,20},{20,16},{24,28},{28,24},{1,5},{5... | collective-permute-start | bytes 1966088 | tf_op jit(solution)/shard_map/ppermute | solution.py:452
  181.5 26.3 %collective-permute-start.22 = (bf16[2,128,1280]{2,1,0:T(8,128)(2,1)}, bf16[2,128,1280]{2,1,0:T(8,128)(2,1)}, u32[]{:S(2)}, u32[]{:S(2)}) collective-permute-start(bf16[2,128,1280]{2,1,0:T(8,128)(2,1)} %pair_sum.4), channel_id=1, source_target_pairs={{0,8},{4,12},{8,0},{12,4},{16,24},{20,28},{24,16},{28,20},{1,9},{5... | collective-permute-start | bytes 1966088 | tf_op jit(solution)/shard_map/ppermute | solution.py:452
  185.4 11.1 %collective-permute-start.18 = (bf16[832,256]{1,0:T(8,128)(2,1)}, bf16[832,256]{1,0:T(8,128)(2,1)}, u32[]{:S(2)}, u32[]{:S(2)}) collective-permute-start(bf16[832,256]{1,0:T(8,128)(2,1)} %get-tuple-element.240), channel_id=1, source_target_pairs={{0,2},{1,3},{2,0},{3,1},{4,6},{5,7},{6,4},{7,5},{8,10},{9,11},{10,... | collective-permute-start | bytes 1277960 | tf_op jit(solution)/shard_map/ppermute | solution.py:452
  187.9 27.7 %collective-permute-start.26 = (bf16[128,1024]{1,0:T(8,128)(2,1)}, bf16[128,1024]{1,0:T(8,128)(2,1)}, u32[]{:S(2)}, u32[]{:S(2)}) collective-permute-start(bf16[128,1024]{1,0:T(8,128)(2,1)} %get-tuple-element.259), channel_id=1, source_target_pairs={{0,16},{4,20},{8,24},{12,28},{16,0},{20,4},{24,8},{28,12},{1,17},{... | collective-permute-start | bytes 786440 | tf_op jit(solution)/shard_map/ppermute | solution.py:452
  198.5 9.4 %collective-permute-start.20 = (bf16[416,256]{1,0:T(8,128)(2,1)}, bf16[416,256]{1,0:T(8,128)(2,1)}, u32[]{:S(2)}, u32[]{:S(2)}) collective-permute-start(bf16[416,256]{1,0:T(8,128)(2,1)} %get-tuple-element.246), channel_id=1, source_target_pairs={{0,4},{4,0},{8,12},{12,8},{16,20},{20,16},{24,28},{28,24},{1,5},{5... | collective-permute-start | bytes 638984 | tf_op jit(solution)/shard_map/ppermute | solution.py:452
  207.6 30.6 %collective-permute-start.30 = (bf16[4,128,1024]{2,1,0:T(8,128)(2,1)}, bf16[4,128,1024]{2,1,0:T(8,128)(2,1)}, u32[]{:S(2)}, u32[]{:S(2)}) collective-permute-start(bf16[4,128,1024]{2,1,0:T(8,128)(2,1)} %get-tuple-element.267), channel_id=1, source_target_pairs={{0,4},{4,0},{8,12},{12,8},{16,20},{20,16},{24,28},{28,24},{1,5},{5... | collective-permute-start | bytes 3145736 | tf_op jit(solution)/shard_map/ppermute | solution.py:452
  209.6 7.2 %collective-permute-start.23 = (bf16[104,256]{1,0:T(8,128)(2,1)}, bf16[104,256]{1,0:T(8,128)(2,1)}, u32[]{:S(2)}, u32[]{:S(2)}) collective-permute-start(bf16[104,256]{1,0:T(8,128)(2,1)} %get-tuple-element.256), channel_id=1, source_target_pairs={{0,8},{4,12},{8,0},{12,4},{16,24},{20,28},{24,16},{28,20},{1,9},{5... | collective-permute-start | bytes 159752 | tf_op jit(solution)/shard_map/ppermute | solution.py:452
  209.6 7.2 %collective-permute-start.24 = (bf16[104,256]{1,0:T(8,128)(2,1)}, bf16[104,256]{1,0:T(8,128)(2,1)}, u32[]{:S(2)}, u32[]{:S(2)}) collective-permute-start(bf16[104,256]{1,0:T(8,128)(2,1)} %get-tuple-element.257), channel_id=1, source_target_pairs={{0,16},{4,20},{8,24},{12,28},{16,0},{20,4},{24,8},{28,12},{1,17},{... | collective-permute-start | bytes 159752 | tf_op jit(solution)/shard_map/ppermute | solution.py:452
  212.0 5.6 %collective-permute-start.25 = (bf16[104,256]{1,0:T(8,128)(2,1)}, bf16[104,256]{1,0:T(8,128)(2,1)}, u32[]{:S(2)}, u32[]{:S(2)}) collective-permute-start(bf16[104,256]{1,0:T(8,128)(2,1)} %get-tuple-element.258), channel_id=1, source_target_pairs={{0,24},{4,28},{8,16},{12,20},{16,8},{20,12},{24,0},{28,4},{1,25},{... | collective-permute-start | bytes 159752 | tf_op jit(solution)/shard_map/ppermute | solution.py:452
  215.6 22.5 %collective-permute-start.31 = (bf16[128,1280]{1,0:T(8,128)(2,1)}, bf16[128,1280]{1,0:T(8,128)(2,1)}, u32[]{:S(2)}, u32[]{:S(2)}) collective-permute-start(bf16[128,1280]{1,0:T(8,128)(2,1)} %get-tuple-element.268), channel_id=1, source_target_pairs={{0,16},{4,20},{8,24},{12,28},{16,0},{20,4},{24,8},{28,12},{1,17},{... | collective-permute-start | bytes 983048 | tf_op jit(solution)/shard_map/ppermute | solution.py:452
  219.1 5.4 %collective-permute-start.27 = (bf16[104,256]{1,0:T(8,128)(2,1)}, bf16[104,256]{1,0:T(8,128)(2,1)}, u32[]{:S(2)}, u32[]{:S(2)}) collective-permute-start(bf16[104,256]{1,0:T(8,128)(2,1)} %z_sum.1.refs_0_), channel_id=1, source_target_pairs={{0,8},{4,12},{8,0},{12,4},{16,24},{20,28},{24,16},{28,20},{1,9},{5... | collective-permute-start | bytes 159752 | tf_op jit(solution)/shard_map/ppermute | solution.py:452
  219.5 17.9 %collective-permute-start.28 = (bf16[104,256]{1,0:T(8,128)(2,1)}, bf16[104,256]{1,0:T(8,128)(2,1)}, u32[]{:S(2)}, u32[]{:S(2)}) collective-permute-start(bf16[104,256]{1,0:T(8,128)(2,1)} %z_sum.1.refs_0_), channel_id=1, source_target_pairs={{0,16},{4,20},{8,24},{12,28},{16,0},{20,4},{24,8},{28,12},{1,17},{... | collective-permute-start | bytes 159752 | tf_op jit(solution)/shard_map/ppermute | solution.py:452
  220.2 17.9 %collective-permute-start.29 = (bf16[104,256]{1,0:T(8,128)(2,1)}, bf16[104,256]{1,0:T(8,128)(2,1)}, u32[]{:S(2)}, u32[]{:S(2)}) collective-permute-start(bf16[104,256]{1,0:T(8,128)(2,1)} %z_sum.1.refs_0_), channel_id=1, source_target_pairs={{0,24},{4,28},{8,16},{12,20},{16,8},{20,12},{24,0},{28,4},{1,25},{... | collective-permute-start | bytes 159752 | tf_op jit(solution)/shard_map/ppermute | solution.py:452
  224.4 26.5 %collective-permute-start.33 = (bf16[128,1024]{1,0:T(8,128)(2,1)}, bf16[128,1024]{1,0:T(8,128)(2,1)}, u32[]{:S(2)}, u32[]{:S(2)}) collective-permute-start(bf16[128,1024]{1,0:T(8,128)(2,1)} %z_last_sum.3.refs_0_), channel_id=1, source_target_pairs={{0,2},{1,3},{2,0},{3,1},{4,6},{5,7},{6,4},{7,5},{8,10},{9,11},{10,... | collective-permute-start | bytes 786440 | tf_op jit(solution)/shard_map/ppermute | solution.py:452
  237.4 21.7 %collective-permute-start.36 = (bf16[128,1024]{1,0:T(8,128)(2,1)}, bf16[128,1024]{1,0:T(8,128)(2,1)}, u32[]{:S(2)}, u32[]{:S(2)}) collective-permute-start(bf16[128,1024]{1,0:T(8,128)(2,1)} %z_last_sum.3.refs_0_), channel_id=1, source_target_pairs={{0,1},{1,0},{2,3},{3,2},{4,5},{5,4},{6,7},{7,6},{8,9},{9,8},{10,11... | collective-permute-start | bytes 786440 | tf_op jit(solution)/shard_map/ppermute | solution.py:452
  240.4 15.3 %collective-permute-start.38 = (bf16[2,128,1024]{2,1,0:T(8,128)(2,1)}, bf16[2,128,1024]{2,1,0:T(8,128)(2,1)}, u32[]{:S(2)}, u32[]{:S(2)}) collective-permute-start(bf16[2,128,1024]{2,1,0:T(8,128)(2,1)} %pair_sum.5), channel_id=1, source_target_pairs={{0,8},{4,12},{8,0},{12,4},{16,24},{20,28},{24,16},{28,20},{1,9},{5... | collective-permute-start | bytes 1572872 | tf_op jit(solution)/shard_map/ppermute | solution.py:452
  242.7 10.8 %collective-permute-start.32 = (bf16[416,256]{1,0:T(8,128)(2,1)}, bf16[416,256]{1,0:T(8,128)(2,1)}, u32[]{:S(2)}, u32[]{:S(2)}) collective-permute-start(bf16[416,256]{1,0:T(8,128)(2,1)} %bitcast.84), channel_id=1, source_target_pairs={{0,4},{4,0},{8,12},{12,8},{16,20},{20,16},{24,28},{28,24},{1,5},{5... | collective-permute-start | bytes 638984 | tf_op jit(solution)/shard_map/ppermute | solution.py:452
  243.9 9.6 %all-to-all-start.6 = ((bf16[4,192,128]{2,1,0:T(8,128)(2,1)}), bf16[4,192,128]{2,1,0:T(8,128)(2,1)}, u32[]{:S(2)}, u32[]{:S(2)}) async-start(bf16[4,192,128]{2,1,0:T(8,128)(2,1)} %bitcast.30), calls=%async_computation.6 | async-start | bytes 393216 | tf_op jit(solution)/shard_map/all_to_all | solution.py:1115
  250.9 29.6 %collective-permute-start.44 = (bf16[128,1280]{1,0:T(8,128)(2,1)}, bf16[128,1280]{1,0:T(8,128)(2,1)}, u32[]{:S(2)}, u32[]{:S(2)}) collective-permute-start(bf16[128,1280]{1,0:T(8,128)(2,1)} %z_last_sum.5.refs_0_), channel_id=1, source_target_pairs={{0,1},{1,0},{2,3},{3,2},{4,5},{5,4},{6,7},{7,6},{8,9},{9,8},{10,11... | collective-permute-start | bytes 983048 | tf_op jit(solution)/shard_map/ppermute | solution.py:452
  250.9 9.6 %collective-permute-start.45 = (bf16[128,1280]{1,0:T(8,128)(2,1)}, bf16[128,1280]{1,0:T(8,128)(2,1)}, u32[]{:S(2)}, u32[]{:S(2)}) collective-permute-start(bf16[128,1280]{1,0:T(8,128)(2,1)} %z_last_sum.5.refs_0_), channel_id=1, source_target_pairs={{0,2},{1,3},{2,0},{3,1},{4,6},{5,7},{6,4},{7,5},{8,10},{9,11},{10,... | collective-permute-start | bytes 983048 | tf_op jit(solution)/shard_map/ppermute | solution.py:452
  255.4 14.3 %collective-permute-start.35 = (bf16[832,256]{1,0:T(8,128)(2,1)}, bf16[832,256]{1,0:T(8,128)(2,1)}, u32[]{:S(2)}, u32[]{:S(2)}) collective-permute-start(bf16[832,256]{1,0:T(8,128)(2,1)} %bitcast.33.m0), channel_id=1, source_target_pairs={{0,2},{1,3},{2,0},{3,1},{4,6},{5,7},{6,4},{7,5},{8,10},{9,11},{10,... | collective-permute-start | bytes 1277960 | tf_op jit(solution)/shard_map/ppermute | solution.py:452
  255.7 6.5 %collective-permute-start.37 = (bf16[128,1024]{1,0:T(8,128)(2,1)}, bf16[128,1024]{1,0:T(8,128)(2,1)}, u32[]{:S(2)}, u32[]{:S(2)}) collective-permute-start(bf16[128,1024]{1,0:T(8,128)(2,1)} %collective-permute-done.33.refs_2_), channel_id=1, source_target_pairs={{0,1},{1,0},{2,3},{3,2},{4,5},{5,4},{6,7},{7,6},{8,9},{9,8},{10,11... | collective-permute-start | bytes 786440 | tf_op jit(solution)/shard_map/ppermute | solution.py:452
  259.0 29.1 %collective-permute-start.34 = (bf16[832,256]{1,0:T(8,128)(2,1)}, bf16[832,256]{1,0:T(8,128)(2,1)}, u32[]{:S(2)}, u32[]{:S(2)}) collective-permute-start(bf16[832,256]{1,0:T(8,128)(2,1)} %bitcast.33.m0), channel_id=1, source_target_pairs={{0,1},{1,0},{2,3},{3,2},{4,5},{5,4},{6,7},{7,6},{8,9},{9,8},{10,11... | collective-permute-start | bytes 1277960 | tf_op jit(solution)/shard_map/ppermute | solution.py:452
  260.6 20.0 %collective-permute-start.46 = (bf16[128,1280]{1,0:T(8,128)(2,1)}, bf16[128,1280]{1,0:T(8,128)(2,1)}, u32[]{:S(2)}, u32[]{:S(2)}) collective-permute-start(bf16[128,1280]{1,0:T(8,128)(2,1)} %collective-permute-done.45.refs_2_), channel_id=1, source_target_pairs={{0,1},{1,0},{2,3},{3,2},{4,5},{5,4},{6,7},{7,6},{8,9},{9,8},{10,11... | collective-permute-start | bytes 983048 | tf_op jit(solution)/shard_map/ppermute | solution.py:452
  262.2 15.1 %collective-permute-start.40 = (bf16[128,1024]{1,0:T(8,128)(2,1)}, bf16[128,1024]{1,0:T(8,128)(2,1)}, u32[]{:S(2)}, u32[]{:S(2)}) collective-permute-start(bf16[128,1024]{1,0:T(8,128)(2,1)} %get-tuple-element.299), channel_id=1, source_target_pairs={{0,16},{4,20},{8,24},{12,28},{16,0},{20,4},{24,8},{28,12},{1,17},{... | collective-permute-start | bytes 786440 | tf_op jit(solution)/shard_map/ppermute | solution.py:452
  269.7 18.5 %collective-permute-start.39 = (bf16[832,256]{1,0:T(8,128)(2,1)}, bf16[832,256]{1,0:T(8,128)(2,1)}, u32[]{:S(2)}, u32[]{:S(2)}) collective-permute-start(bf16[832,256]{1,0:T(8,128)(2,1)} %collective-permute-done.35.m2), channel_id=1, source_target_pairs={{0,1},{1,0},{2,3},{3,2},{4,5},{5,4},{6,7},{7,6},{8,9},{9,8},{10,11... | collective-permute-start | bytes 1277960 | tf_op jit(solution)/shard_map/ppermute | solution.py:452
  279.1 7.8 %collective-permute-start.42 = (bf16[128,1024]{1,0:T(8,128)(2,1)}, bf16[128,1024]{1,0:T(8,128)(2,1)}, u32[]{:S(2)}, u32[]{:S(2)}) collective-permute-start(bf16[128,1024]{1,0:T(8,128)(2,1)} %z_last_sum.4.refs_0_), channel_id=1, source_target_pairs={{0,2},{1,3},{2,0},{3,1},{4,6},{5,7},{6,4},{7,5},{8,10},{9,11},{10,... | collective-permute-start | bytes 786440 | tf_op jit(solution)/shard_map/ppermute | solution.py:452
  283.4 10.9 %collective-permute-start.41 = (bf16[128,1024]{1,0:T(8,128)(2,1)}, bf16[128,1024]{1,0:T(8,128)(2,1)}, u32[]{:S(2)}, u32[]{:S(2)}) collective-permute-start(bf16[128,1024]{1,0:T(8,128)(2,1)} %z_last_sum.4.refs_0_), channel_id=1, source_target_pairs={{0,1},{1,0},{2,3},{3,2},{4,5},{5,4},{6,7},{7,6},{8,9},{9,8},{10,11... | collective-permute-start | bytes 786440 | tf_op jit(solution)/shard_map/ppermute | solution.py:452
  286.9 7.5 %collective-permute-start.43 = (bf16[128,1024]{1,0:T(8,128)(2,1)}, bf16[128,1024]{1,0:T(8,128)(2,1)}, u32[]{:S(2)}, u32[]{:S(2)}) collective-permute-start(bf16[128,1024]{1,0:T(8,128)(2,1)} %collective-permute-done.42.refs_2_), channel_id=1, source_target_pairs={{0,1},{1,0},{2,3},{3,2},{4,5},{5,4},{6,7},{7,6},{8,9},{9,8},{10,11... | collective-permute-start | bytes 786440 | tf_op jit(solution)/shard_map/ppermute | solution.py:452
  (18 other events, 72.4 us)

commit v4 on v3

--- a/solution.py
+++ b/solution.py
@@ -415,11 +415,7 @@
         values = [member(right, s)[:, pl.ds(right_start, cols)] for s in range(4)]
         values = jnp.concatenate(values, axis=0)
         for out, side, blocks in zip(outs, sides, away + near):
-
-            def step(slot, carry, out=out, side=side, blocks=blocks, start=start):
-                k = blocks[0] + 2 * slot
-                if len(blocks) == 4:
-                    k = jnp.where(slot < 2, k, 2 * slot - 4)
+            for slot, k in enumerate(blocks):
                 source = 2 * (place_ref[Z] ^ k) + side
                 group = [member(left, s) for s in range(4)]
                 if len(group[0].shape) == 3:
@@ -429,9 +425,6 @@
                     factor = [ref[:, block] for ref in group]
                 factor = jnp.concatenate(factor, axis=0)
                 out[slot, :, start : start + cols] = mm(factor, values, TN).astype(BF16)
-                return carry
-
-            lax.fori_loop(0, len(blocks), step, 0)
         start += cols
 
 
@@ -697,7 +690,7 @@
     seg, width = front_out.shape
     hidden = mlp_in.shape[1]
     parts = attended.shape[0]
-    sub = 2
+    sub = 1
     block = hidden * sub // parts
     shape = jax.ShapeDtypeStruct
 

time: 300 us -> 296 us (0.987)
  Pallas kernels: 123 us -> 117 us
    pallas_call x22, Pallas kernels: 67 us -> 59.1 us  [small_call(): pl.pallas_call(kernel, out_shape=tuple((jax.ShapeDtypeStruct(dims, dtype)...]
  transfers between devices with their start and end apart: 54 -> 54, of which waited for: 14 -> 15; matrix products, arithmetic and copies ran while one was open for 9% -> 9% of each run, Pallas kernels for 39% -> 37%
where the time goes in v4:
time: 296 us; the launch traced here: 294 us
  Pallas kernels  117 us (40%)
  starting transfers between devices  76.6 us (26%)
  waiting for transfers between devices  61.8 us (21%)
  matrix products  17.1 us (6%)
  local copies, waits for them, and re-layouts  13.2 us (4%)
  other arithmetic  7.1 us (2%)
    pallas_call x22, Pallas kernels, small_call(): pl.pallas_call(kernel, out_shape=tuple((jax.ShapeDtypeStruct(dims, dtype)...  59.1 us
    ppermute x47, waiting for transfers between devices, swap(): lax.ppermute(values, axis, [(i, i ^ bit) for i in range(lax.axis_size(axi...  44.3 us
    ppermute x47, starting transfers between devices, swap(): lax.ppermute(values, axis, [(i, i ^ bit) for i in range(lax.axis_size(axi...  43.8 us
    all_to_all x4, starting transfers between devices, to_heads(): lax.all_to_all(values, 'patch', split_axis=0, concat_axis=0, tiled=True)  19 us
    pallas_call x1, Pallas kernels, middle(): pl.pallas_call(functools.partial(middle_kernel, sub), grid=(parts // sub,...  18.1 us
    dot_general x10, matrix products, mm(): lax.dot_general(a, b, dims, precision=precision, preferred_element_type=F32)  17.1 us
    all_to_all x4, waiting for transfers between devices, to_heads(): lax.all_to_all(values, 'patch', split_axis=0, concat_axis=0, tiled=True)  15.1 us
    pallas_call x1, Pallas kernels, attend_backward(): pl.pallas_call(functools.partial(attend_backward_kernel, head_dim, block)...  11 us
  transfers between devices with their start and end apart: 54, of which 15 were waited for; matrix products, arithmetic and copies ran while one was open for 9% of the time, Pallas kernels for 37%

profile of v4, /device:TPU:1, one launch (start us, length us, event | category | flops | bytes accessed | tf_op | source)
XLA Modules:
  0.0 294.2 jit_solution(12021775317643167703)
XLA Ops:
  0.7 4.3 %all-to-all-start = ((bf16[4,192,128]{2,1,0:T(8,128)(2,1)}), bf16[4,192,128]{2,1,0:T(8,128)(2,1)S(1)}, u32[]{:S(2)}, u32[]{:S(2)}) async-start(bf16[4,192,128]{2,1,0:T(8,128)(2,1)} %bitcast.79), calls=%async_computation | async-start | bytes 393216 | tf_op jit(solution)/shard_map/all_to_all | solution.py:936
  5.8 2.1 fusion.18.aggq_ref
  10.1 3.0 %convolution_convert_fusion.2.vwt_ref = bf16[1024,768]{1,0:T(8,128)(2,1)} fusion(bf16[1024,1024]{1,0:T(8,128)(2,1)S(1)} %copy-done.2, bf16[768,1024]{1,0:T(8,128)(2,1)S(1)} %bitcast.75), kind=kOutput, calls=%fused_computation.2 | convolution fusion | flops 1611399168 | bytes 5242880 | tf_op jit(solution)/shard_map/dot_general | solution.py:28
  18.4 4.8 %front_forward.1 = (bf16[768,128]{1,0:T(8,128)(2,1)}, f32[768,128]{1,0:T(8,128)}, bf16[128,1024]{1,0:T(8,128)(2,1)}, bf16[768,768]{1,0:T(8,128)(2,1)}) custom-call(s32[1,48]{1,0:T(1,128)} %constant_dynamic-slice_fusion.4.ids_ref, bf16[768,128]{1,0:T(8,128)(2,1)} %bitcast.80, f32[16,768]{1,0:T(8,128)} %slice_add_fusion.1.weight_ref, ...), custom_call_target="tpu_custom_call" | custom-call | flops 60000002048 | bytes 1048576 | tf_op jit(solution)/shard_map/front_forward/pallas_call | solution.py:86
  23.1 2.2 fusion.17
  25.7 3.8 %convolution_convert_fusion = bf16[128,3072]{1,0:T(8,128)(2,1)S(1)} fusion(bf16[128,1024]{1,0:T(8,128)(2,1)S(1)} %multiply_convert_fusion, bf16[1024,3072]{1,0:T(8,128)(2,1)} %wqkv_ref.1), kind=kOutput, calls=%fused_computation | convolution fusion | flops 805699584 | bytes 7340032 | tf_op jit(solution)/shard_map/dot_general | solution.py:28
  30.8 6.1 %all-to-all-start.1 = ((bf16[8,384,128]{2,1,0:T(8,128)(2,1)}), bf16[8,384,128]{2,1,0:T(8,128)(2,1)}, u32[]{:S(2)}, u32[]{:S(2)}) async-start(bf16[8,384,128]{2,1,0:T(8,128)(2,1)} %bitcast.14), calls=%async_computation.1 | async-start | bytes 1572864 | tf_op jit(solution)/shard_map/all_to_all | solution.py:392
  41.8 1.6 constant_dynamic-slice_fusion.3.weight_own_ref
  43.4 1.8 constant_dynamic-slice_fusion
  46.3 3.0 %fusion.vw_ref = bf16[768,1024]{1,0:T(8,128)(2,1)} fusion(bf16[768,1024]{1,0:T(8,128)(2,1)S(1)} %bitcast.76, bf16[1024,1024]{1,0:T(8,128)(2,1)S(1)} %copy-done.2), kind=kOutput, calls=%fused_computation.3 | convolution fusion | flops 1611399168 | bytes 5242880 | tf_op jit(solution)/shard_map/dot_general | solution.py:28
  49.3 7.6 %all-to-all-done.1.qkv_ref = bf16[8,384,128]{2,1,0:T(8,128)(2,1)} async-done(((bf16[8,384,128]{2,1,0:T(8,128)(2,1)}), bf16[8,384,128]{2,1,0:T(8,128)(2,1)}, u32[]{:S(2)}, u32[]{:S(2)}) %all-to-all-start.1) | async-done | bytes 786464 | tf_op jit(solution)/shard_map/all_to_all | solution.py:392
  57.0 6.8 %attend_forward.1 = (bf16[1024,128]{1,0:T(8,128)(2,1)}, f32[2,1024]{1,0:T(2,128)}) custom-call(s32[1,1]{1,0:T(1,128)} %bitcast.5.count_ref, bf16[8,384,128]{2,1,0:T(8,128)(2,1)} %all-to-all-done.1.qkv_ref), custom_call_target="tpu_custom_call" | custom-call | flops 60000002048 | bytes 1048576 | tf_op jit(solution)/shard_map/attend_forward/pallas_call | solution.py:266
  63.8 4.1 %all-to-all-start.2 = ((bf16[8,128,128]{2,1,0:T(8,128)(2,1)}), bf16[8,128,128]{2,1,0:T(8,128)(2,1)S(1)}, u32[]{:S(2)}, u32[]{:S(2)}) async-start(bf16[8,128,128]{2,1,0:T(8,128)(2,1)} %bitcast.77), calls=%async_computation.2 | async-start | bytes 524288 | tf_op jit(solution)/shard_map/all_to_all | solution.py:392
  71.0 4.4 %all-to-all-done.2.att_ref.refs_4_ = bf16[8,128,128]{2,1,0:T(8,128)(2,1)S(1)} async-done(((bf16[8,128,128]{2,1,0:T(8,128)(2,1)}), bf16[8,128,128]{2,1,0:T(8,128)(2,1)S(1)}, u32[]{:S(2)}, u32[]{:S(2)}) %all-to-all-start.2) | async-done | bytes 262176 | tf_op jit(solution)/shard_map/all_to_all | solution.py:392
  75.4 2.3 collective-permute-start
  79.3 18.1 %trunk_middle.1 = (bf16[128,1024]{1,0:T(8,128)(2,1)}, bf16[128,1024]{1,0:T(8,128)(2,1)}, bf16[128,1024]{1,0:T(8,128)(2,1)}, bf16[128,1024]{1,0:T(8,128)(2,1)}, b...) custom-call(s32[5]{0:T(128)} %stack.23.place_ref, ...), custom_call_target="tpu_custom_call" | custom-call | flops 99999997952 | bytes 1048576 | tf_op jit(solution)/shard_map/trunk_middle/pallas_call | solution.py:701
  97.5 3.4 %all-to-all-start.3 = ((bf16[8,128,128]{2,1,0:T(8,128)(2,1)}), bf16[8,128,128]{2,1,0:T(8,128)(2,1)S(1)}, u32[]{:S(2)}, u32[]{:S(2)}) async-start(bf16[8,128,128]{2,1,0:T(8,128)(2,1)} %get-tuple-element.188), calls=%async_computation.3 | async-start | bytes 524288 | tf_op jit(solution)/shard_map/all_to_all | solution.py:392
  103.8 2.0 collective-permute-start.9
  105.8 3.1 %all-to-all-done.3 = bf16[8,128,128]{2,1,0:T(8,128)(2,1)S(1)} async-done(((bf16[8,128,128]{2,1,0:T(8,128)(2,1)}), bf16[8,128,128]{2,1,0:T(8,128)(2,1)S(1)}, u32[]{:S(2)}, u32[]{:S(2)}) %all-to-all-start.3) | async-done | bytes 262176 | tf_op jit(solution)/shard_map/all_to_all | solution.py:392
  109.6 11.0 %attend_backward.1 = bf16[8,384,128]{2,1,0:T(8,128)(2,1)} custom-call(s32[1,1]{1,0:T(1,128)} %bitcast.5.count_ref, bf16[8,384,128]{2,1,0:T(8,128)(2,1)} %all-to-all-done.1.qkv_ref, bf16[1024,128]{1,0:T(8,128)(2,1)} %bitcast.78, f32[2,1024]{1,0:T(2,128)} %get-tuple-element.189.lse_ref), custom_call_target="tpu_custom_call" | custom-call | flops 99999997952 | bytes 1048576 | tf_op jit(solution)/shard_map/attend_backward/pallas_call | solution.py:334
  121.2 5.4 %all-to-all-start.4 = ((bf16[8,384,128]{2,1,0:T(8,128)(2,1)}), bf16[8,384,128]{2,1,0:T(8,128)(2,1)}, u32[]{:S(2)}, u32[]{:S(2)}) async-start(bf16[8,384,128]{2,1,0:T(8,128)(2,1)} %attend_backward.1), calls=%async_computation.4 | async-start | bytes 1572864 | tf_op jit(solution)/shard_map/all_to_all | solution.py:392
  129.0 4.3 %weight_grads.3 = (bf16[4,128,1024]{2,1,0:T(8,128)(2,1)}, bf16[2,128,1024]{2,1,0:T(8,128)(2,1)}, bf16[2,128,1024]{2,1,0:T(8,128)(2,1)}) custom-call(s32[5]{0:T(128)} %stack.23.place_ref, bf16[128,1024]{1,0:T(8,128)(2,1)} %get-tuple-element.200.refs_0_, bf16[128,1024]{1,0:T(8,128)(2,1)} %copy-done.24, bf16[128,1024]{1,0:T(8,128)(2,1)} %copy-done.25, ...), custom_call_target="tpu_custom_call" | custom-call | flops 1999999991808 | bytes 1048576 | tf_op jit(solution)/shard_map/weight_grads/pallas_call | solution.py:458
  133.3 1.6 collective-permute-start.15
  134.9 1.5 collective-permute-done.13.refs_10_
  136.4 7.7 %collective-permute-done.14.refs_11_ = bf16[128,1280]{1,0:T(8,128)(2,1)} collective-permute-done((bf16[128,1280]{1,0:T(8,128)(2,1)}, bf16[128,1280]{1,0:T(8,128)(2,1)}, u32[]{:S(2)}, u32[]{:S(2)}) %collective-permute-start.14) | collective-permute-done | bytes 327712 | tf_op jit(solution)/shard_map/ppermute | solution.py:445
  144.1 4.8 %weight_grads.4 = (bf16[2,128,1280]{2,1,0:T(8,128)(2,1)}, bf16[2,128,1280]{2,1,0:T(8,128)(2,1)}, bf16[2,128,1280]{2,1,0:T(8,128)(2,1)}, bf16[2,128,1280]{2,1,0:T(8,128)(2,1)}) custom-call(s32[5]{0:T(128)} %stack.23.place_ref, bf16[128,1024]{1,0:T(8,128)(2,1)} %get-tuple-element.210.refs_0_, bf16[128,1024]{1,0:T(8,128)(2,1)} %collective-permute-done.10.refs_1_, ...), custom_call_target="tpu_custom_call" | custom-call | flops 1999999991808 | bytes 1048576 | tf_op jit(solution)/shard_map/weight_grads/pallas_call | solution.py:458
  149.0 1.5 collective-permute-start.16
  150.4 8.5 %trunk_back.1 = (bf16[128,1024]{1,0:T(8,128)(2,1)}, f32[1,1024]{1,0:T(1,128)}, bf16[4,128,1024]{2,1,0:T(8,128)(2,1)}) custom-call(s32[5]{0:T(128)} %stack.23.place_ref, bf16[8,384,128]{2,1,0:T(8,128)(2,1)} %all-to-all-done.4.grads_ref, f32[128,1024]{1,0:T(8,128)} %copy-done.3, f32[1,1024]{1,0:T(1,128)} %bitcast.82, ...), custom_call_target="tpu_custom_call" | custom-call | flops 99999997952 | bytes 1048576 | tf_op jit(solution)/shard_map/trunk_back/pallas_call | solution.py:797
  159.0 4.5 %all-to-all-start.5 = ((bf16[4,128,1024]{2,1,0:T(8,128)(2,1)}), bf16[4,128,1024]{2,1,0:T(8,128)(2,1)}, u32[]{:S(2)}, u32[]{:S(2)}) async-start(bf16[4,128,1024]{2,1,0:T(8,128)(2,1)} %get-tuple-element.236), calls=%async_computation.5 | async-start | bytes 2097152 | tf_op jit(solution)/shard_map/all_to_all | solution.py:1044
  163.4 2.3 pair_sum.3
  166.9 8.9 %front_backward.1 = (bf16[768,128]{1,0:T(8,128)(2,1)}, bf16[2,832,256]{2,1,0:T(8,128)(2,1)}, bf16[2,832,256]{2,1,0:T(8,128)(2,1)}) custom-call(s32[5]{0:T(128)} %stack.23.place_ref, s32[1,48]{1,0:T(1,128)} %constant_dynamic-slice_fusion.4.ids_ref, bf16[768,128]{1,0:T(8,128)(2,1)} %get-tuple-element.186.x_ref, f32[768,128]{1,0:T(8,128)} %get-tuple-element.187.p_ref, ...), custom_call_target="tpu_custom_call" | custom-call | flops 100000000 | bytes 1048576 | tf_op jit(solution)/shard_map/front_backward/pallas_call | solution.py:209
  175.9 1.5 all-to-all-done.5.refs_4_
  177.9 2.3 pair_sum.4
  180.2 1.4 collective-permute-start.22
  181.6 2.4 core_sum.1
  185.1 2.4 z_first_sum.3
  188.7 6.5 %collective-permute-done.18 = bf16[832,256]{1,0:T(8,128)(2,1)} collective-permute-done((bf16[832,256]{1,0:T(8,128)(2,1)}, bf16[832,256]{1,0:T(8,128)(2,1)}, u32[]{:S(2)}, u32[]{:S(2)}) %collective-permute-start.18) | collective-permute-done | bytes 426016 | tf_op jit(solution)/shard_map/ppermute | solution.py:445
  195.2 2.0 x_sum.1
  198.4 4.7 %weight_grads.5 = (bf16[4,128,1024]{2,1,0:T(8,128)(2,1)}, bf16[2,128,1024]{2,1,0:T(8,128)(2,1)}, bf16[2,128,1024]{2,1,0:T(8,128)(2,1)}) custom-call(s32[5]{0:T(128)} %stack.23.place_ref, bf16[128,3072]{1,0:T(8,128)(2,1)} %pad_maximum_fusion.refs_4_.refs_0_, bf16[128,3072]{1,0:T(8,128)(2,1)} %copy-done.19, ...), custom_call_target="tpu_custom_call" | custom-call | flops 1999999991808 | bytes 1048576 | tf_op jit(solution)/shard_map/weight_grads/pallas_call | solution.py:458
  203.4 1.8 z_pieces.1
  205.2 2.3 collective-permute-start.24
  208.7 2.5 z_first_sum.4
  213.1 1.5 z_sum.1.refs_0_
  215.7 2.4 collective-permute-start.29
  218.2 1.8 z_last_sum.3.refs_0_
  220.6 12.3 %collective-permute-done.28.refs_2_ = bf16[104,256]{1,0:T(8,128)(2,1)} collective-permute-done((bf16[104,256]{1,0:T(8,128)(2,1)}, bf16[104,256]{1,0:T(8,128)(2,1)}, u32[]{:S(2)}, u32[]{:S(2)}) %collective-permute-start.28) | collective-permute-done | bytes 53280 | tf_op jit(solution)/shard_map/ppermute | solution.py:445
  233.7 2.3 pair_sum.5
  236.7 1.6 z_join.1
  239.4 5.1 %all-to-all-start.6 = ((bf16[4,192,128]{2,1,0:T(8,128)(2,1)}), bf16[4,192,128]{2,1,0:T(8,128)(2,1)}, u32[]{:S(2)}, u32[]{:S(2)}) async-start(bf16[4,192,128]{2,1,0:T(8,128)(2,1)} %bitcast.30), calls=%async_computation.6 | async-start | bytes 393216 | tf_op jit(solution)/shard_map/all_to_all | solution.py:1108
  244.5 1.9 z_last_sum.5.refs_0_
  246.5 1.7 collective-permute-start.45
  249.1 1.8 y_join.1
  252.2 2.4 z_first_sum.5
  254.6 1.5 collective-permute-done.45.refs_2_
  256.1 1.7 collective-permute-start.46
  258.4 6.8 %collective-permute-done.35.m2 = bf16[832,256]{1,0:T(8,128)(2,1)} collective-permute-done((bf16[832,256]{1,0:T(8,128)(2,1)}, bf16[832,256]{1,0:T(8,128)(2,1)}, u32[]{:S(2)}, u32[]{:S(2)}) %collective-permute-start.35) | collective-permute-done | bytes 426016 | tf_op jit(solution)/shard_map/ppermute | solution.py:445
  266.3 2.7 join.5
  268.9 3.9 %collective-permute-done.40.got_ref = bf16[128,1024]{1,0:T(8,128)(2,1)} collective-permute-done((bf16[128,1024]{1,0:T(8,128)(2,1)}, bf16[128,1024]{1,0:T(8,128)(2,1)}, u32[]{:S(2)}, u32[]{:S(2)}) %collective-permute-start.40) | collective-permute-done | bytes 262176 | tf_op jit(solution)/shard_map/ppermute | solution.py:445
  272.8 1.8 z_last_sum.4.refs_0_
  276.1 2.9 join.4
  279.7 2.7 collective-permute-done.42.refs_2_
  283.7 6.2 %front_last.1 = (f32[128,1024]{1,0:T(8,128)}, f32[768,128]{1,0:T(8,128)}, f32[48,128]{1,0:T(8,128)}, f32[128,1024]{1,0:T(8,128)}, f32[128,1024]{1,0:T(8,128)}, /...) custom-call(s32[5]{0:T(128)} %stack.23.place_ref, bf16[832,256]{1,0:T(8,128)(2,1)} %bitcast.33.m0, ...), custom_call_target="tpu_custom_call" | custom-call | flops 199999995904 | bytes 1048576 | tf_op jit(solution)/shard_map/front_last/pallas_call | solution.py:458
  289.9 2.6 join.3
  292.6 1.6 copy.47
  (171 shorter events, 47.5 us)
Async XLA Ops:
  0.6 16.5 %copy-start = (s32[4,48]{1,0:T(4,128)S(1)}, s32[4,48]{1,0:T(4,128)}, u32[]{:S(2)}) copy-start(s32[4,48]{1,0:T(4,128)} %param.19) | copy-start | bytes 2308
  0.7 17.0 %all-to-all-start = ((bf16[4,192,128]{2,1,0:T(8,128)(2,1)}), bf16[4,192,128]{2,1,0:T(8,128)(2,1)S(1)}, u32[]{:S(2)}, u32[]{:S(2)}) async-start(bf16[4,192,128]{2,1,0:T(8,128)(2,1)} %bitcast.79), calls=%async_computation | async-start | bytes 393216 | tf_op jit(solution)/shard_map/all_to_all | solution.py:936
  15.7 21.3 %copy-start.7 = (bf16[128,1024]{1,0:T(8,128)(2,1)}, bf16[128,1024]{1,0:T(8,128)(2,1)S(1)}, u32[]{:S(2)}) copy-start(bf16[128,1024]{1,0:T(8,128)(2,1)S(1)} %fusion.2.og_ref) | copy-start | bytes 786436
  30.8 26.2 %all-to-all-start.1 = ((bf16[8,384,128]{2,1,0:T(8,128)(2,1)}), bf16[8,384,128]{2,1,0:T(8,128)(2,1)}, u32[]{:S(2)}, u32[]{:S(2)}) async-start(bf16[8,384,128]{2,1,0:T(8,128)(2,1)} %bitcast.14), calls=%async_computation.1 | async-start | bytes 1572864 | tf_op jit(solution)/shard_map/all_to_all | solution.py:392
  37.9 8.5 %copy-start.6 = (bf16[48,16,1024]{2,1,0:T(8,128)(2,1)S(1)}, bf16[48,16,1024]{2,1,0:T(8,128)(2,1)}, u32[]{:S(2)}) copy-start(bf16[48,16,1024]{2,1,0:T(8,128)(2,1)} %param.20) | copy-start | bytes 4718596
  37.9 33.2 %collective-permute-start.4 = (bf16[128,3072]{1,0:T(8,128)(2,1)}, bf16[128,3072]{1,0:T(8,128)(2,1)}, u32[]{:S(2)}, u32[]{:S(2)}) collective-permute-start(bf16[128,3072]{1,0:T(8,128)(2,1)} %pad_maximum_fusion.refs_4_.refs_0_), channel_id=1, source_target_pairs={{0,2},{1,3},{2,0},{3,1},{4,6},{5,7},{6,4},{7,5},{8,10},{9,11},{10,... | collective-permute-start | bytes 2359304 | tf_op jit(solution)/shard_map/ppermute | solution.py:445
  57.0 10.9 %copy-start.17 = (bf16[1024]{0:T(1024)(128)(2,1)S(1)}, bf16[1024]{0:T(1024)(128)(2,1)}, u32[]{:S(2)}) copy-start(bf16[1024]{0:T(1024)(128)(2,1)} %param.30) | copy-start | bytes 6148
  63.8 11.6 %all-to-all-start.2 = ((bf16[8,128,128]{2,1,0:T(8,128)(2,1)}), bf16[8,128,128]{2,1,0:T(8,128)(2,1)S(1)}, u32[]{:S(2)}, u32[]{:S(2)}) async-start(bf16[8,128,128]{2,1,0:T(8,128)(2,1)} %bitcast.77), calls=%async_computation.2 | async-start | bytes 524288 | tf_op jit(solution)/shard_map/all_to_all | solution.py:392
  70.3 27.2 %collective-permute-start.3 = (bf16[128,3072]{1,0:T(8,128)(2,1)}, bf16[128,3072]{1,0:T(8,128)(2,1)S(1)}, u32[]{:S(2)}, u32[]{:S(2)}) collective-permute-start(bf16[128,3072]{1,0:T(8,128)(2,1)} %pad_maximum_fusion.refs_4_.refs_0_), channel_id=1, source_target_pairs={{0,1},{1,0},{2,3},{3,2},{4,5},{5,4},{6,7},{7,6},{8,9},{9,8},{10,11... | collective-permute-start | bytes 2359304 | tf_op jit(solution)/shard_map/ppermute | solution.py:445
  71.0 26.4 %collective-permute-start.5 = (bf16[128,3072]{1,0:T(8,128)(2,1)}, bf16[128,3072]{1,0:T(8,128)(2,1)S(1)}, u32[]{:S(2)}, u32[]{:S(2)}) collective-permute-start(bf16[128,3072]{1,0:T(8,128)(2,1)} %collective-permute-done.4.refs_6_.refs_2_), channel_id=1, source_target_pairs={{0,1},{1,0},{2,3},{3,2},{4,5},{5,4},{6,7},{7,6},{8,9},{9,8},{10,11... | collective-permute-start | bytes 2359304 | tf_op jit(solution)/shard_map/ppermute | solution.py:445
  75.4 22.0 %collective-permute-start = (bf16[8,128,128]{2,1,0:T(8,128)(2,1)S(1)}, bf16[8,128,128]{2,1,0:T(8,128)(2,1)S(1)}, u32[]{:S(2)}, u32[]{:S(2)}) collective-permute-start(bf16[8,128,128]{2,1,0:T(8,128)(2,1)S(1)} %all-to-all-done.2.att_ref.refs_4_), channel_id=1, source_target_pairs={{0,1},{1,0},{2,3},{3,2},{4,5},{5,4},{6,7},{7,6},{8,9},{9,8},{10,11... | collective-permute-start | bytes 786440 | tf_op jit(solution)/shard_map/ppermute | solution.py:445
  77.7 19.8 %collective-permute-start.1 = (bf16[8,128,128]{2,1,0:T(8,128)(2,1)S(1)}, bf16[8,128,128]{2,1,0:T(8,128)(2,1)S(1)}, u32[]{:S(2)}, u32[]{:S(2)}) collective-permute-start(bf16[8,128,128]{2,1,0:T(8,128)(2,1)S(1)} %all-to-all-done.2.att_ref.refs_4_), channel_id=1, source_target_pairs={{0,2},{1,3},{2,0},{3,1},{4,6},{5,7},{6,4},{7,5},{8,10},{9,11},{10,... | collective-permute-start | bytes 786440 | tf_op jit(solution)/shard_map/ppermute | solution.py:445
  79.0 18.5 %collective-permute-start.2 = (bf16[8,128,128]{2,1,0:T(8,128)(2,1)S(1)}, bf16[8,128,128]{2,1,0:T(8,128)(2,1)S(1)}, u32[]{:S(2)}, u32[]{:S(2)}) collective-permute-start(bf16[8,128,128]{2,1,0:T(8,128)(2,1)S(1)} %all-to-all-done.2.att_ref.refs_4_), channel_id=1, source_target_pairs={{0,3},{1,2},{2,1},{3,0},{4,7},{5,6},{6,5},{7,4},{8,11},{9,10},{10,... | collective-permute-start | bytes 786440 | tf_op jit(solution)/shard_map/ppermute | solution.py:445
  79.3 21.6 %copy-start.18 = (f32[128,1]{0,1:T(1,128)S(1)}, f32[128,1]{0,1:T(1,128)}, u32[]{:S(2)}) copy-start(f32[128,1]{0,1:T(1,128)} %bitcast_convert_fusion) | copy-start | bytes 1540
  97.4 23.1 %copy-start.19 = (bf16[128,3072]{1,0:T(8,128)(2,1)}, bf16[128,3072]{1,0:T(8,128)(2,1)S(1)}, u32[]{:S(2)}) copy-start(bf16[128,3072]{1,0:T(8,128)(2,1)S(1)} %collective-permute-done.3.refs_5_.refs_1_) | copy-start | bytes 2359300
  97.4 23.1 %copy-start.20 = (bf16[128,3072]{1,0:T(8,128)(2,1)}, bf16[128,3072]{1,0:T(8,128)(2,1)S(1)}, u32[]{:S(2)}) copy-start(bf16[128,3072]{1,0:T(8,128)(2,1)S(1)} %collective-permute-done.5.refs_7_.refs_3_) | copy-start | bytes 2359300
  97.5 23.1 %copy-start.21 = (bf16[8,128,128]{2,1,0:T(8,128)(2,1)}, bf16[8,128,128]{2,1,0:T(8,128)(2,1)S(1)}, u32[]{:S(2)}) copy-start(bf16[8,128,128]{2,1,0:T(8,128)(2,1)S(1)} %collective-permute-done.refs_5_) | copy-start | bytes 786436
  97.5 23.1 %copy-start.22 = (bf16[8,128,128]{2,1,0:T(8,128)(2,1)}, bf16[8,128,128]{2,1,0:T(8,128)(2,1)S(1)}, u32[]{:S(2)}) copy-start(bf16[8,128,128]{2,1,0:T(8,128)(2,1)S(1)} %collective-permute-done.1.refs_6_) | copy-start | bytes 786436
  97.5 23.1 %copy-start.23 = (bf16[8,128,128]{2,1,0:T(8,128)(2,1)}, bf16[8,128,128]{2,1,0:T(8,128)(2,1)S(1)}, u32[]{:S(2)}) copy-start(bf16[8,128,128]{2,1,0:T(8,128)(2,1)S(1)} %collective-permute-done.2.refs_7_) | copy-start | bytes 786436
  97.5 11.3 %all-to-all-start.3 = ((bf16[8,128,128]{2,1,0:T(8,128)(2,1)}), bf16[8,128,128]{2,1,0:T(8,128)(2,1)S(1)}, u32[]{:S(2)}, u32[]{:S(2)}) async-start(bf16[8,128,128]{2,1,0:T(8,128)(2,1)} %get-tuple-element.188), calls=%async_computation.3 | async-start | bytes 524288 | tf_op jit(solution)/shard_map/all_to_all | solution.py:392
  101.7 18.9 %collective-permute-start.6 = (bf16[128,1024]{1,0:T(8,128)(2,1)}, bf16[128,1024]{1,0:T(8,128)(2,1)}, u32[]{:S(2)}, u32[]{:S(2)}) collective-permute-start(bf16[128,1024]{1,0:T(8,128)(2,1)} %get-tuple-element.210.refs_0_), channel_id=1, source_target_pairs={{0,2},{1,3},{2,0},{3,1},{4,6},{5,7},{6,4},{7,5},{8,10},{9,11},{10,... | collective-permute-start | bytes 786440 | tf_op jit(solution)/shard_map/ppermute | solution.py:445
  103.0 30.3 %collective-permute-start.10 = (bf16[128,1024]{1,0:T(8,128)(2,1)}, bf16[128,1024]{1,0:T(8,128)(2,1)}, u32[]{:S(2)}, u32[]{:S(2)}) collective-permute-start(bf16[128,1024]{1,0:T(8,128)(2,1)} %get-tuple-element.210.refs_0_), channel_id=1, source_target_pairs={{0,1},{1,0},{2,3},{3,2},{4,5},{5,4},{6,7},{7,6},{8,9},{9,8},{10,11... | collective-permute-start | bytes 786440 | tf_op jit(solution)/shard_map/ppermute | solution.py:445
  103.7 16.9 %collective-permute-start.7 = (bf16[128,1024]{1,0:T(8,128)(2,1)}, bf16[128,1024]{1,0:T(8,128)(2,1)S(1)}, u32[]{:S(2)}, u32[]{:S(2)}) collective-permute-start(bf16[128,1024]{1,0:T(8,128)(2,1)} %get-tuple-element.192), channel_id=1, source_target_pairs={{0,1},{1,0},{2,3},{3,2},{4,5},{5,4},{6,7},{7,6},{8,9},{9,8},{10,11... | collective-permute-start | bytes 786440 | tf_op jit(solution)/shard_map/ppermute | solution.py:445
  103.7 16.9 %collective-permute-start.8 = (bf16[128,1024]{1,0:T(8,128)(2,1)}, bf16[128,1024]{1,0:T(8,128)(2,1)S(1)}, u32[]{:S(2)}, u32[]{:S(2)}) collective-permute-start(bf16[128,1024]{1,0:T(8,128)(2,1)} %get-tuple-element.193), channel_id=1, source_target_pairs={{0,2},{1,3},{2,0},{3,1},{4,6},{5,7},{6,4},{7,5},{8,10},{9,11},{10,... | collective-permute-start | bytes 786440 | tf_op jit(solution)/shard_map/ppermute | solution.py:445
  103.8 17.4 %collective-permute-start.9 = (bf16[128,1024]{1,0:T(8,128)(2,1)}, bf16[128,1024]{1,0:T(8,128)(2,1)S(1)}, u32[]{:S(2)}, u32[]{:S(2)}) collective-permute-start(bf16[128,1024]{1,0:T(8,128)(2,1)} %get-tuple-element.194), channel_id=1, source_target_pairs={{0,3},{1,2},{2,1},{3,0},{4,7},{5,6},{6,5},{7,4},{8,11},{9,10},{10,... | collective-permute-start | bytes 786440 | tf_op jit(solution)/shard_map/ppermute | solution.py:445
  121.2 29.2 %all-to-all-start.4 = ((bf16[8,384,128]{2,1,0:T(8,128)(2,1)}), bf16[8,384,128]{2,1,0:T(8,128)(2,1)}, u32[]{:S(2)}, u32[]{:S(2)}) async-start(bf16[8,384,128]{2,1,0:T(8,128)(2,1)} %attend_backward.1), calls=%async_computation.4 | async-start | bytes 1572864 | tf_op jit(solution)/shard_map/all_to_all | solution.py:392
  126.5 8.4 %collective-permute-start.11 = (bf16[128,1024]{1,0:T(8,128)(2,1)}, bf16[128,1024]{1,0:T(8,128)(2,1)}, u32[]{:S(2)}, u32[]{:S(2)}) collective-permute-start(bf16[128,1024]{1,0:T(8,128)(2,1)} %collective-permute-done.6.refs_2_), channel_id=1, source_target_pairs={{0,1},{1,0},{2,3},{3,2},{4,5},{5,4},{6,7},{7,6},{8,9},{9,8},{10,11... | collective-permute-start | bytes 786440 | tf_op jit(solution)/shard_map/ppermute | solution.py:445
  126.8 8.1 %collective-permute-start.12 = (bf16[128,1280]{1,0:T(8,128)(2,1)}, bf16[128,1280]{1,0:T(8,128)(2,1)}, u32[]{:S(2)}, u32[]{:S(2)}) collective-permute-start(bf16[128,1280]{1,0:T(8,128)(2,1)} %get-tuple-element.217), channel_id=1, source_target_pairs={{0,1},{1,0},{2,3},{3,2},{4,5},{5,4},{6,7},{7,6},{8,9},{9,8},{10,11... | collective-permute-start | bytes 983048 | tf_op jit(solution)/shard_map/ppermute | solution.py:445
  127.1 9.3 %collective-permute-start.13 = (bf16[128,1280]{1,0:T(8,128)(2,1)}, bf16[128,1280]{1,0:T(8,128)(2,1)}, u32[]{:S(2)}, u32[]{:S(2)}) collective-permute-start(bf16[128,1280]{1,0:T(8,128)(2,1)} %get-tuple-element.218), channel_id=1, source_target_pairs={{0,2},{1,3},{2,0},{3,1},{4,6},{5,7},{6,4},{7,5},{8,10},{9,11},{10,... | collective-permute-start | bytes 983048 | tf_op jit(solution)/shard_map/ppermute | solution.py:445
  128.4 15.8 %collective-permute-start.14 = (bf16[128,1280]{1,0:T(8,128)(2,1)}, bf16[128,1280]{1,0:T(8,128)(2,1)}, u32[]{:S(2)}, u32[]{:S(2)}) collective-permute-start(bf16[128,1280]{1,0:T(8,128)(2,1)} %get-tuple-element.219), channel_id=1, source_target_pairs={{0,3},{1,2},{2,1},{3,0},{4,7},{5,6},{6,5},{7,4},{8,11},{9,10},{10,... | collective-permute-start | bytes 983048 | tf_op jit(solution)/shard_map/ppermute | solution.py:445
  133.3 30.1 %collective-permute-start.15 = (bf16[4,128,1024]{2,1,0:T(8,128)(2,1)}, bf16[4,128,1024]{2,1,0:T(8,128)(2,1)}, u32[]{:S(2)}, u32[]{:S(2)}) collective-permute-start(bf16[4,128,1024]{2,1,0:T(8,128)(2,1)} %get-tuple-element.226), channel_id=1, source_target_pairs={{0,4},{4,0},{8,12},{12,8},{16,20},{20,16},{24,28},{28,24},{1,5},{5... | collective-permute-start | bytes 3145736 | tf_op jit(solution)/shard_map/ppermute | solution.py:445
  149.0 26.9 %collective-permute-start.16 = (bf16[2,128,1280]{2,1,0:T(8,128)(2,1)}, bf16[2,128,1280]{2,1,0:T(8,128)(2,1)}, u32[]{:S(2)}, u32[]{:S(2)}) collective-permute-start(bf16[2,128,1280]{2,1,0:T(8,128)(2,1)} %get-tuple-element.235), channel_id=1, source_target_pairs={{0,4},{4,0},{8,12},{12,8},{16,20},{20,16},{24,28},{28,24},{1,5},{5... | collective-permute-start | bytes 1966088 | tf_op jit(solution)/shard_map/ppermute | solution.py:445
  159.0 18.4 %all-to-all-start.5 = ((bf16[4,128,1024]{2,1,0:T(8,128)(2,1)}), bf16[4,128,1024]{2,1,0:T(8,128)(2,1)}, u32[]{:S(2)}, u32[]{:S(2)}) async-start(bf16[4,128,1024]{2,1,0:T(8,128)(2,1)} %get-tuple-element.236), calls=%async_computation.5 | async-start | bytes 2097152 | tf_op jit(solution)/shard_map/all_to_all | solution.py:1044
  165.8 19.3 %collective-permute-start.19 = (bf16[2,128,1024]{2,1,0:T(8,128)(2,1)}, bf16[2,128,1024]{2,1,0:T(8,128)(2,1)}, u32[]{:S(2)}, u32[]{:S(2)}) collective-permute-start(bf16[2,128,1024]{2,1,0:T(8,128)(2,1)} %pair_sum.3), channel_id=1, source_target_pairs={{0,8},{4,12},{8,0},{12,4},{16,24},{20,28},{24,16},{28,20},{1,9},{5... | collective-permute-start | bytes 1572872 | tf_op jit(solution)/shard_map/ppermute | solution.py:445
  177.3 4.3 %collective-permute-start.17 = (bf16[2,832,256]{2,1,0:T(8,128)(2,1)}, bf16[2,832,256]{2,1,0:T(8,128)(2,1)}, u32[]{:S(2)}, u32[]{:S(2)}) collective-permute-start(bf16[2,832,256]{2,1,0:T(8,128)(2,1)} %get-tuple-element.238), channel_id=1, source_target_pairs={{0,1},{1,0},{2,3},{3,2},{4,5},{5,4},{6,7},{7,6},{8,9},{9,8},{10,11... | collective-permute-start | bytes 2555912 | tf_op jit(solution)/shard_map/ppermute | solution.py:445
  180.2 23.2 %collective-permute-start.21 = (bf16[2,128,1280]{2,1,0:T(8,128)(2,1)}, bf16[2,128,1280]{2,1,0:T(8,128)(2,1)}, u32[]{:S(2)}, u32[]{:S(2)}) collective-permute-start(bf16[2,128,1280]{2,1,0:T(8,128)(2,1)} %get-tuple-element.249), channel_id=1, source_target_pairs={{0,4},{4,0},{8,12},{12,8},{16,20},{20,16},{24,28},{28,24},{1,5},{5... | collective-permute-start | bytes 1966088 | tf_op jit(solution)/shard_map/ppermute | solution.py:445
  180.2 23.2 %collective-permute-start.22 = (bf16[2,128,1280]{2,1,0:T(8,128)(2,1)}, bf16[2,128,1280]{2,1,0:T(8,128)(2,1)}, u32[]{:S(2)}, u32[]{:S(2)}) collective-permute-start(bf16[2,128,1280]{2,1,0:T(8,128)(2,1)} %pair_sum.4), channel_id=1, source_target_pairs={{0,8},{4,12},{8,0},{12,4},{16,24},{20,28},{24,16},{28,20},{1,9},{5... | collective-permute-start | bytes 1966088 | tf_op jit(solution)/shard_map/ppermute | solution.py:445
  184.1 11.1 %collective-permute-start.18 = (bf16[832,256]{1,0:T(8,128)(2,1)}, bf16[832,256]{1,0:T(8,128)(2,1)}, u32[]{:S(2)}, u32[]{:S(2)}) collective-permute-start(bf16[832,256]{1,0:T(8,128)(2,1)} %get-tuple-element.240), channel_id=1, source_target_pairs={{0,2},{1,3},{2,0},{3,1},{4,6},{5,7},{6,4},{7,5},{8,10},{9,11},{10,... | collective-permute-start | bytes 1277960 | tf_op jit(solution)/shard_map/ppermute | solution.py:445
  187.5 23.6 %collective-permute-start.26 = (bf16[128,1024]{1,0:T(8,128)(2,1)}, bf16[128,1024]{1,0:T(8,128)(2,1)}, u32[]{:S(2)}, u32[]{:S(2)}) collective-permute-start(bf16[128,1024]{1,0:T(8,128)(2,1)} %get-tuple-element.259), channel_id=1, source_target_pairs={{0,16},{4,20},{8,24},{12,28},{16,0},{20,4},{24,8},{28,12},{1,17},{... | collective-permute-start | bytes 786440 | tf_op jit(solution)/shard_map/ppermute | solution.py:445
  197.2 6.2 %collective-permute-start.20 = (bf16[416,256]{1,0:T(8,128)(2,1)}, bf16[416,256]{1,0:T(8,128)(2,1)}, u32[]{:S(2)}, u32[]{:S(2)}) collective-permute-start(bf16[416,256]{1,0:T(8,128)(2,1)} %get-tuple-element.246), channel_id=1, source_target_pairs={{0,4},{4,0},{8,12},{12,8},{16,20},{20,16},{24,28},{28,24},{1,5},{5... | collective-permute-start | bytes 638984 | tf_op jit(solution)/shard_map/ppermute | solution.py:445
  203.1 30.6 %collective-permute-start.30 = (bf16[4,128,1024]{2,1,0:T(8,128)(2,1)}, bf16[4,128,1024]{2,1,0:T(8,128)(2,1)}, u32[]{:S(2)}, u32[]{:S(2)}) collective-permute-start(bf16[4,128,1024]{2,1,0:T(8,128)(2,1)} %get-tuple-element.267), channel_id=1, source_target_pairs={{0,4},{4,0},{8,12},{12,8},{16,20},{20,16},{24,28},{28,24},{1,5},{5... | collective-permute-start | bytes 3145736 | tf_op jit(solution)/shard_map/ppermute | solution.py:445
  205.1 7.2 %collective-permute-start.23 = (bf16[104,256]{1,0:T(8,128)(2,1)}, bf16[104,256]{1,0:T(8,128)(2,1)}, u32[]{:S(2)}, u32[]{:S(2)}) collective-permute-start(bf16[104,256]{1,0:T(8,128)(2,1)} %get-tuple-element.256), channel_id=1, source_target_pairs={{0,8},{4,12},{8,0},{12,4},{16,24},{20,28},{24,16},{28,20},{1,9},{5... | collective-permute-start | bytes 159752 | tf_op jit(solution)/shard_map/ppermute | solution.py:445
  205.2 7.2 %collective-permute-start.24 = (bf16[104,256]{1,0:T(8,128)(2,1)}, bf16[104,256]{1,0:T(8,128)(2,1)}, u32[]{:S(2)}, u32[]{:S(2)}) collective-permute-start(bf16[104,256]{1,0:T(8,128)(2,1)} %get-tuple-element.257), channel_id=1, source_target_pairs={{0,16},{4,20},{8,24},{12,28},{16,0},{20,4},{24,8},{28,12},{1,17},{... | collective-permute-start | bytes 159752 | tf_op jit(solution)/shard_map/ppermute | solution.py:445
  207.5 5.6 %collective-permute-start.25 = (bf16[104,256]{1,0:T(8,128)(2,1)}, bf16[104,256]{1,0:T(8,128)(2,1)}, u32[]{:S(2)}, u32[]{:S(2)}) collective-permute-start(bf16[104,256]{1,0:T(8,128)(2,1)} %get-tuple-element.258), channel_id=1, source_target_pairs={{0,24},{4,28},{8,16},{12,20},{16,8},{20,12},{24,0},{28,4},{1,25},{... | collective-permute-start | bytes 159752 | tf_op jit(solution)/shard_map/ppermute | solution.py:445
  211.1 22.5 %collective-permute-start.31 = (bf16[128,1280]{1,0:T(8,128)(2,1)}, bf16[128,1280]{1,0:T(8,128)(2,1)}, u32[]{:S(2)}, u32[]{:S(2)}) collective-permute-start(bf16[128,1280]{1,0:T(8,128)(2,1)} %get-tuple-element.268), channel_id=1, source_target_pairs={{0,16},{4,20},{8,24},{12,28},{16,0},{20,4},{24,8},{28,12},{1,17},{... | collective-permute-start | bytes 983048 | tf_op jit(solution)/shard_map/ppermute | solution.py:445
  214.6 5.4 %collective-permute-start.27 = (bf16[104,256]{1,0:T(8,128)(2,1)}, bf16[104,256]{1,0:T(8,128)(2,1)}, u32[]{:S(2)}, u32[]{:S(2)}) collective-permute-start(bf16[104,256]{1,0:T(8,128)(2,1)} %z_sum.1.refs_0_), channel_id=1, source_target_pairs={{0,8},{4,12},{8,0},{12,4},{16,24},{20,28},{24,16},{28,20},{1,9},{5... | collective-permute-start | bytes 159752 | tf_op jit(solution)/shard_map/ppermute | solution.py:445
  215.1 17.8 %collective-permute-start.28 = (bf16[104,256]{1,0:T(8,128)(2,1)}, bf16[104,256]{1,0:T(8,128)(2,1)}, u32[]{:S(2)}, u32[]{:S(2)}) collective-permute-start(bf16[104,256]{1,0:T(8,128)(2,1)} %z_sum.1.refs_0_), channel_id=1, source_target_pairs={{0,16},{4,20},{8,24},{12,28},{16,0},{20,4},{24,8},{28,12},{1,17},{... | collective-permute-start | bytes 159752 | tf_op jit(solution)/shard_map/ppermute | solution.py:445
  215.7 17.9 %collective-permute-start.29 = (bf16[104,256]{1,0:T(8,128)(2,1)}, bf16[104,256]{1,0:T(8,128)(2,1)}, u32[]{:S(2)}, u32[]{:S(2)}) collective-permute-start(bf16[104,256]{1,0:T(8,128)(2,1)} %z_sum.1.refs_0_), channel_id=1, source_target_pairs={{0,24},{4,28},{8,16},{12,20},{16,8},{20,12},{24,0},{28,4},{1,25},{... | collective-permute-start | bytes 159752 | tf_op jit(solution)/shard_map/ppermute | solution.py:445
  220.0 26.5 %collective-permute-start.33 = (bf16[128,1024]{1,0:T(8,128)(2,1)}, bf16[128,1024]{1,0:T(8,128)(2,1)}, u32[]{:S(2)}, u32[]{:S(2)}) collective-permute-start(bf16[128,1024]{1,0:T(8,128)(2,1)} %z_last_sum.3.refs_0_), channel_id=1, source_target_pairs={{0,2},{1,3},{2,0},{3,1},{4,6},{5,7},{6,4},{7,5},{8,10},{9,11},{10,... | collective-permute-start | bytes 786440 | tf_op jit(solution)/shard_map/ppermute | solution.py:445
  232.9 21.7 %collective-permute-start.36 = (bf16[128,1024]{1,0:T(8,128)(2,1)}, bf16[128,1024]{1,0:T(8,128)(2,1)}, u32[]{:S(2)}, u32[]{:S(2)}) collective-permute-start(bf16[128,1024]{1,0:T(8,128)(2,1)} %z_last_sum.3.refs_0_), channel_id=1, source_target_pairs={{0,1},{1,0},{2,3},{3,2},{4,5},{5,4},{6,7},{7,6},{8,9},{9,8},{10,11... | collective-permute-start | bytes 786440 | tf_op jit(solution)/shard_map/ppermute | solution.py:445
  236.0 15.3 %collective-permute-start.38 = (bf16[2,128,1024]{2,1,0:T(8,128)(2,1)}, bf16[2,128,1024]{2,1,0:T(8,128)(2,1)}, u32[]{:S(2)}, u32[]{:S(2)}) collective-permute-start(bf16[2,128,1024]{2,1,0:T(8,128)(2,1)} %pair_sum.5), channel_id=1, source_target_pairs={{0,8},{4,12},{8,0},{12,4},{16,24},{20,28},{24,16},{28,20},{1,9},{5... | collective-permute-start | bytes 1572872 | tf_op jit(solution)/shard_map/ppermute | solution.py:445
  238.3 10.8 %collective-permute-start.32 = (bf16[416,256]{1,0:T(8,128)(2,1)}, bf16[416,256]{1,0:T(8,128)(2,1)}, u32[]{:S(2)}, u32[]{:S(2)}) collective-permute-start(bf16[416,256]{1,0:T(8,128)(2,1)} %bitcast.84), channel_id=1, source_target_pairs={{0,4},{4,0},{8,12},{12,8},{16,20},{20,16},{24,28},{28,24},{1,5},{5... | collective-permute-start | bytes 638984 | tf_op jit(solution)/shard_map/ppermute | solution.py:445
  239.4 9.7 %all-to-all-start.6 = ((bf16[4,192,128]{2,1,0:T(8,128)(2,1)}), bf16[4,192,128]{2,1,0:T(8,128)(2,1)}, u32[]{:S(2)}, u32[]{:S(2)}) async-start(bf16[4,192,128]{2,1,0:T(8,128)(2,1)} %bitcast.30), calls=%async_computation.6 | async-start | bytes 393216 | tf_op jit(solution)/shard_map/all_to_all | solution.py:1108
  246.4 29.7 %collective-permute-start.44 = (bf16[128,1280]{1,0:T(8,128)(2,1)}, bf16[128,1280]{1,0:T(8,128)(2,1)}, u32[]{:S(2)}, u32[]{:S(2)}) collective-permute-start(bf16[128,1280]{1,0:T(8,128)(2,1)} %z_last_sum.5.refs_0_), channel_id=1, source_target_pairs={{0,1},{1,0},{2,3},{3,2},{4,5},{5,4},{6,7},{7,6},{8,9},{9,8},{10,11... | collective-permute-start | bytes 983048 | tf_op jit(solution)/shard_map/ppermute | solution.py:445
  246.5 9.6 %collective-permute-start.45 = (bf16[128,1280]{1,0:T(8,128)(2,1)}, bf16[128,1280]{1,0:T(8,128)(2,1)}, u32[]{:S(2)}, u32[]{:S(2)}) collective-permute-start(bf16[128,1280]{1,0:T(8,128)(2,1)} %z_last_sum.5.refs_0_), channel_id=1, source_target_pairs={{0,2},{1,3},{2,0},{3,1},{4,6},{5,7},{6,4},{7,5},{8,10},{9,11},{10,... | collective-permute-start | bytes 983048 | tf_op jit(solution)/shard_map/ppermute | solution.py:445
  250.9 14.3 %collective-permute-start.35 = (bf16[832,256]{1,0:T(8,128)(2,1)}, bf16[832,256]{1,0:T(8,128)(2,1)}, u32[]{:S(2)}, u32[]{:S(2)}) collective-permute-start(bf16[832,256]{1,0:T(8,128)(2,1)} %bitcast.33.m0), channel_id=1, source_target_pairs={{0,2},{1,3},{2,0},{3,1},{4,6},{5,7},{6,4},{7,5},{8,10},{9,11},{10,... | collective-permute-start | bytes 1277960 | tf_op jit(solution)/shard_map/ppermute | solution.py:445
  251.3 6.5 %collective-permute-start.37 = (bf16[128,1024]{1,0:T(8,128)(2,1)}, bf16[128,1024]{1,0:T(8,128)(2,1)}, u32[]{:S(2)}, u32[]{:S(2)}) collective-permute-start(bf16[128,1024]{1,0:T(8,128)(2,1)} %collective-permute-done.33.refs_2_), channel_id=1, source_target_pairs={{0,1},{1,0},{2,3},{3,2},{4,5},{5,4},{6,7},{7,6},{8,9},{9,8},{10,11... | collective-permute-start | bytes 786440 | tf_op jit(solution)/shard_map/ppermute | solution.py:445
  254.6 29.1 %collective-permute-start.34 = (bf16[832,256]{1,0:T(8,128)(2,1)}, bf16[832,256]{1,0:T(8,128)(2,1)}, u32[]{:S(2)}, u32[]{:S(2)}) collective-permute-start(bf16[832,256]{1,0:T(8,128)(2,1)} %bitcast.33.m0), channel_id=1, source_target_pairs={{0,1},{1,0},{2,3},{3,2},{4,5},{5,4},{6,7},{7,6},{8,9},{9,8},{10,11... | collective-permute-start | bytes 1277960 | tf_op jit(solution)/shard_map/ppermute | solution.py:445
  256.1 20.0 %collective-permute-start.46 = (bf16[128,1280]{1,0:T(8,128)(2,1)}, bf16[128,1280]{1,0:T(8,128)(2,1)}, u32[]{:S(2)}, u32[]{:S(2)}) collective-permute-start(bf16[128,1280]{1,0:T(8,128)(2,1)} %collective-permute-done.45.refs_2_), channel_id=1, source_target_pairs={{0,1},{1,0},{2,3},{3,2},{4,5},{5,4},{6,7},{7,6},{8,9},{9,8},{10,11... | collective-permute-start | bytes 983048 | tf_op jit(solution)/shard_map/ppermute | solution.py:445
  257.8 15.1 %collective-permute-start.40 = (bf16[128,1024]{1,0:T(8,128)(2,1)}, bf16[128,1024]{1,0:T(8,128)(2,1)}, u32[]{:S(2)}, u32[]{:S(2)}) collective-permute-start(bf16[128,1024]{1,0:T(8,128)(2,1)} %get-tuple-element.299), channel_id=1, source_target_pairs={{0,16},{4,20},{8,24},{12,28},{16,0},{20,4},{24,8},{28,12},{1,17},{... | collective-permute-start | bytes 786440 | tf_op jit(solution)/shard_map/ppermute | solution.py:445
  265.2 18.5 %collective-permute-start.39 = (bf16[832,256]{1,0:T(8,128)(2,1)}, bf16[832,256]{1,0:T(8,128)(2,1)}, u32[]{:S(2)}, u32[]{:S(2)}) collective-permute-start(bf16[832,256]{1,0:T(8,128)(2,1)} %collective-permute-done.35.m2), channel_id=1, source_target_pairs={{0,1},{1,0},{2,3},{3,2},{4,5},{5,4},{6,7},{7,6},{8,9},{9,8},{10,11... | collective-permute-start | bytes 1277960 | tf_op jit(solution)/shard_map/ppermute | solution.py:445
  274.7 7.8 %collective-permute-start.42 = (bf16[128,1024]{1,0:T(8,128)(2,1)}, bf16[128,1024]{1,0:T(8,128)(2,1)}, u32[]{:S(2)}, u32[]{:S(2)}) collective-permute-start(bf16[128,1024]{1,0:T(8,128)(2,1)} %z_last_sum.4.refs_0_), channel_id=1, source_target_pairs={{0,2},{1,3},{2,0},{3,1},{4,6},{5,7},{6,4},{7,5},{8,10},{9,11},{10,... | collective-permute-start | bytes 786440 | tf_op jit(solution)/shard_map/ppermute | solution.py:445
  279.0 10.9 %collective-permute-start.41 = (bf16[128,1024]{1,0:T(8,128)(2,1)}, bf16[128,1024]{1,0:T(8,128)(2,1)}, u32[]{:S(2)}, u32[]{:S(2)}) collective-permute-start(bf16[128,1024]{1,0:T(8,128)(2,1)} %z_last_sum.4.refs_0_), channel_id=1, source_target_pairs={{0,1},{1,0},{2,3},{3,2},{4,5},{5,4},{6,7},{7,6},{8,9},{9,8},{10,11... | collective-permute-start | bytes 786440 | tf_op jit(solution)/shard_map/ppermute | solution.py:445
  282.4 7.5 %collective-permute-start.43 = (bf16[128,1024]{1,0:T(8,128)(2,1)}, bf16[128,1024]{1,0:T(8,128)(2,1)}, u32[]{:S(2)}, u32[]{:S(2)}) collective-permute-start(bf16[128,1024]{1,0:T(8,128)(2,1)} %collective-permute-done.42.refs_2_), channel_id=1, source_target_pairs={{0,1},{1,0},{2,3},{3,2},{4,5},{5,4},{6,7},{7,6},{8,9},{9,8},{10,11... | collective-permute-start | bytes 786440 | tf_op jit(solution)/shard_map/ppermute | solution.py:445
  (18 other events, 72.2 us)

commit v5 on v4

--- a/solution.py
+++ b/solution.py
@@ -75,7 +75,7 @@
         mt_ref[rows, :] = mm(vwt_ref[rows, :], scaled) + mm(vet_ref[rows, :], shares.astype(BF16))
         return carry
 
-    lax.fori_loop(0, HEADS, head, 0, unroll=4)
+    lax.fori_loop(0, HEADS, head, 0, unroll=2)
     mixed_ref[...] = mt_ref[...].T.astype(BF16)
 
 
@@ -690,7 +690,7 @@
     seg, width = front_out.shape
     hidden = mlp_in.shape[1]
     parts = attended.shape[0]
-    sub = 1
+    sub = 2
     block = hidden * sub // parts
     shape = jax.ShapeDtypeStruct
 

time: 296 us -> 295 us (level)
  no operation moved by 1% of the time
where the time goes in v5:
time: 295 us; the launch traced here: 293 us
  Pallas kernels  116 us (39%)
  starting transfers between devices  76.7 us (26%)
  waiting for transfers between devices  61.8 us (21%)
  matrix products  17.1 us (6%)
  local copies, waits for them, and re-layouts  13.2 us (4%)
  other arithmetic  7.1 us (2%)
    pallas_call x22, Pallas kernels, small_call(): pl.pallas_call(kernel, out_shape=tuple((jax.ShapeDtypeStruct(dims, dtype)...  59.1 us
    ppermute x47, waiting for transfers between devices, swap(): lax.ppermute(values, axis, [(i, i ^ bit) for i in range(lax.axis_size(axi...  44.3 us
    ppermute x47, starting transfers between devices, swap(): lax.ppermute(values, axis, [(i, i ^ bit) for i in range(lax.axis_size(axi...  43.9 us
    all_to_all x4, starting transfers between devices, to_heads(): lax.all_to_all(values, 'patch', split_axis=0, concat_axis=0, tiled=True)  19 us
    dot_general x10, matrix products, mm(): lax.dot_general(a, b, dims, precision=precision, preferred_element_type=F32)  17.1 us
    pallas_call x1, Pallas kernels, middle(): pl.pallas_call(functools.partial(middle_kernel, sub), grid=(parts // sub,...  16.3 us
    all_to_all x4, waiting for transfers between devices, to_heads(): lax.all_to_all(values, 'patch', split_axis=0, concat_axis=0, tiled=True)  15 us
    pallas_call x1, Pallas kernels, attend_backward(): pl.pallas_call(functools.partial(attend_backward_kernel, head_dim, block)...  11 us
  transfers between devices with their start and end apart: 54, of which 15 were waited for; matrix products, arithmetic and copies ran while one was open for 9% of the time, Pallas kernels for 37%

profile of v5, /device:TPU:1, one launch (start us, length us, event | category | flops | bytes accessed | tf_op | source)
XLA Modules:
  0.0 293.0 jit_solution(17961141290482739195)
XLA Ops:
  0.7 4.3 %all-to-all-start = ((bf16[4,192,128]{2,1,0:T(8,128)(2,1)}), bf16[4,192,128]{2,1,0:T(8,128)(2,1)S(1)}, u32[]{:S(2)}, u32[]{:S(2)}) async-start(bf16[4,192,128]{2,1,0:T(8,128)(2,1)} %bitcast.79), calls=%async_computation | async-start | bytes 393216 | tf_op jit(solution)/shard_map/all_to_all | solution.py:936
  5.8 2.1 fusion.18.aggq_ref
  10.1 3.0 %convolution_convert_fusion.2.vwt_ref = bf16[1024,768]{1,0:T(8,128)(2,1)} fusion(bf16[1024,1024]{1,0:T(8,128)(2,1)S(1)} %copy-done.2, bf16[768,1024]{1,0:T(8,128)(2,1)S(1)} %bitcast.75), kind=kOutput, calls=%fused_computation.2 | convolution fusion | flops 1611399168 | bytes 5242880 | tf_op jit(solution)/shard_map/dot_general | solution.py:28
  18.4 5.3 %front_forward.1 = (bf16[768,128]{1,0:T(8,128)(2,1)}, f32[768,128]{1,0:T(8,128)}, bf16[128,1024]{1,0:T(8,128)(2,1)}, bf16[768,768]{1,0:T(8,128)(2,1)}) custom-call(s32[1,48]{1,0:T(1,128)} %constant_dynamic-slice_fusion.4.ids_ref, bf16[768,128]{1,0:T(8,128)(2,1)} %bitcast.80, f32[16,768]{1,0:T(8,128)} %slice_add_fusion.1.weight_ref, ...), custom_call_target="tpu_custom_call" | custom-call | flops 60000002048 | bytes 1048576 | tf_op jit(solution)/shard_map/front_forward/pallas_call | solution.py:86
  23.7 2.2 fusion.17
  26.3 3.8 %convolution_convert_fusion = bf16[128,3072]{1,0:T(8,128)(2,1)S(1)} fusion(bf16[128,1024]{1,0:T(8,128)(2,1)S(1)} %multiply_convert_fusion, bf16[1024,3072]{1,0:T(8,128)(2,1)} %wqkv_ref.1), kind=kOutput, calls=%fused_computation | convolution fusion | flops 805699584 | bytes 7340032 | tf_op jit(solution)/shard_map/dot_general | solution.py:28
  31.3 6.1 %all-to-all-start.1 = ((bf16[8,384,128]{2,1,0:T(8,128)(2,1)}), bf16[8,384,128]{2,1,0:T(8,128)(2,1)}, u32[]{:S(2)}, u32[]{:S(2)}) async-start(bf16[8,384,128]{2,1,0:T(8,128)(2,1)} %bitcast.14), calls=%async_computation.1 | async-start | bytes 1572864 | tf_op jit(solution)/shard_map/all_to_all | solution.py:392
  42.3 1.6 constant_dynamic-slice_fusion.3.weight_own_ref
  43.9 1.8 constant_dynamic-slice_fusion
  46.9 3.0 %fusion.vw_ref = bf16[768,1024]{1,0:T(8,128)(2,1)} fusion(bf16[768,1024]{1,0:T(8,128)(2,1)S(1)} %bitcast.76, bf16[1024,1024]{1,0:T(8,128)(2,1)S(1)} %copy-done.2), kind=kOutput, calls=%fused_computation.3 | convolution fusion | flops 1611399168 | bytes 5242880 | tf_op jit(solution)/shard_map/dot_general | solution.py:28
  49.9 7.7 %all-to-all-done.1.qkv_ref = bf16[8,384,128]{2,1,0:T(8,128)(2,1)} async-done(((bf16[8,384,128]{2,1,0:T(8,128)(2,1)}), bf16[8,384,128]{2,1,0:T(8,128)(2,1)}, u32[]{:S(2)}, u32[]{:S(2)}) %all-to-all-start.1) | async-done | bytes 786464 | tf_op jit(solution)/shard_map/all_to_all | solution.py:392
  57.5 6.8 %attend_forward.1 = (bf16[1024,128]{1,0:T(8,128)(2,1)}, f32[2,1024]{1,0:T(2,128)}) custom-call(s32[1,1]{1,0:T(1,128)} %bitcast.5.count_ref, bf16[8,384,128]{2,1,0:T(8,128)(2,1)} %all-to-all-done.1.qkv_ref), custom_call_target="tpu_custom_call" | custom-call | flops 60000002048 | bytes 1048576 | tf_op jit(solution)/shard_map/attend_forward/pallas_call | solution.py:266
  64.3 4.0 %all-to-all-start.2 = ((bf16[8,128,128]{2,1,0:T(8,128)(2,1)}), bf16[8,128,128]{2,1,0:T(8,128)(2,1)S(1)}, u32[]{:S(2)}, u32[]{:S(2)}) async-start(bf16[8,128,128]{2,1,0:T(8,128)(2,1)} %bitcast.77), calls=%async_computation.2 | async-start | bytes 524288 | tf_op jit(solution)/shard_map/all_to_all | solution.py:392
  71.6 4.4 %all-to-all-done.2.att_ref.refs_4_ = bf16[8,128,128]{2,1,0:T(8,128)(2,1)S(1)} async-done(((bf16[8,128,128]{2,1,0:T(8,128)(2,1)}), bf16[8,128,128]{2,1,0:T(8,128)(2,1)S(1)}, u32[]{:S(2)}, u32[]{:S(2)}) %all-to-all-start.2) | async-done | bytes 262176 | tf_op jit(solution)/shard_map/all_to_all | solution.py:392
  76.0 2.3 collective-permute-start
  79.9 16.3 %trunk_middle.1 = (bf16[128,1024]{1,0:T(8,128)(2,1)}, bf16[128,1024]{1,0:T(8,128)(2,1)}, bf16[128,1024]{1,0:T(8,128)(2,1)}, bf16[128,1024]{1,0:T(8,128)(2,1)}, b...) custom-call(s32[5]{0:T(128)} %stack.23.place_ref, ...), custom_call_target="tpu_custom_call" | custom-call | flops 99999997952 | bytes 1048576 | tf_op jit(solution)/shard_map/trunk_middle/pallas_call | solution.py:701
  96.3 3.4 %all-to-all-start.3 = ((bf16[8,128,128]{2,1,0:T(8,128)(2,1)}), bf16[8,128,128]{2,1,0:T(8,128)(2,1)S(1)}, u32[]{:S(2)}, u32[]{:S(2)}) async-start(bf16[8,128,128]{2,1,0:T(8,128)(2,1)} %get-tuple-element.188), calls=%async_computation.3 | async-start | bytes 524288 | tf_op jit(solution)/shard_map/all_to_all | solution.py:392
  102.6 2.0 collective-permute-start.9
  104.6 3.0 %all-to-all-done.3 = bf16[8,128,128]{2,1,0:T(8,128)(2,1)S(1)} async-done(((bf16[8,128,128]{2,1,0:T(8,128)(2,1)}), bf16[8,128,128]{2,1,0:T(8,128)(2,1)S(1)}, u32[]{:S(2)}, u32[]{:S(2)}) %all-to-all-start.3) | async-done | bytes 262176 | tf_op jit(solution)/shard_map/all_to_all | solution.py:392
  108.2 11.0 %attend_backward.1 = bf16[8,384,128]{2,1,0:T(8,128)(2,1)} custom-call(s32[1,1]{1,0:T(1,128)} %bitcast.5.count_ref, bf16[8,384,128]{2,1,0:T(8,128)(2,1)} %all-to-all-done.1.qkv_ref, bf16[1024,128]{1,0:T(8,128)(2,1)} %bitcast.78, f32[2,1024]{1,0:T(2,128)} %get-tuple-element.189.lse_ref), custom_call_target="tpu_custom_call" | custom-call | flops 99999997952 | bytes 1048576 | tf_op jit(solution)/shard_map/attend_backward/pallas_call | solution.py:334
  119.9 5.4 %all-to-all-start.4 = ((bf16[8,384,128]{2,1,0:T(8,128)(2,1)}), bf16[8,384,128]{2,1,0:T(8,128)(2,1)}, u32[]{:S(2)}, u32[]{:S(2)}) async-start(bf16[8,384,128]{2,1,0:T(8,128)(2,1)} %attend_backward.1), calls=%async_computation.4 | async-start | bytes 1572864 | tf_op jit(solution)/shard_map/all_to_all | solution.py:392
  127.7 4.3 %weight_grads.3 = (bf16[4,128,1024]{2,1,0:T(8,128)(2,1)}, bf16[2,128,1024]{2,1,0:T(8,128)(2,1)}, bf16[2,128,1024]{2,1,0:T(8,128)(2,1)}) custom-call(s32[5]{0:T(128)} %stack.23.place_ref, bf16[128,1024]{1,0:T(8,128)(2,1)} %get-tuple-element.200.refs_0_, bf16[128,1024]{1,0:T(8,128)(2,1)} %copy-done.24, bf16[128,1024]{1,0:T(8,128)(2,1)} %copy-done.25, ...), custom_call_target="tpu_custom_call" | custom-call | flops 1999999991808 | bytes 1048576 | tf_op jit(solution)/shard_map/weight_grads/pallas_call | solution.py:458
  132.1 1.6 collective-permute-start.15
  133.7 1.4 collective-permute-done.13.refs_10_
  135.1 7.8 %collective-permute-done.14.refs_11_ = bf16[128,1280]{1,0:T(8,128)(2,1)} collective-permute-done((bf16[128,1280]{1,0:T(8,128)(2,1)}, bf16[128,1280]{1,0:T(8,128)(2,1)}, u32[]{:S(2)}, u32[]{:S(2)}) %collective-permute-start.14) | collective-permute-done | bytes 327712 | tf_op jit(solution)/shard_map/ppermute | solution.py:445
  142.9 4.8 %weight_grads.4 = (bf16[2,128,1280]{2,1,0:T(8,128)(2,1)}, bf16[2,128,1280]{2,1,0:T(8,128)(2,1)}, bf16[2,128,1280]{2,1,0:T(8,128)(2,1)}, bf16[2,128,1280]{2,1,0:T(8,128)(2,1)}) custom-call(s32[5]{0:T(128)} %stack.23.place_ref, bf16[128,1024]{1,0:T(8,128)(2,1)} %get-tuple-element.210.refs_0_, bf16[128,1024]{1,0:T(8,128)(2,1)} %collective-permute-done.10.refs_1_, ...), custom_call_target="tpu_custom_call" | custom-call | flops 1999999991808 | bytes 1048576 | tf_op jit(solution)/shard_map/weight_grads/pallas_call | solution.py:458
  147.7 1.5 collective-permute-start.16
  149.2 8.5 %trunk_back.1 = (bf16[128,1024]{1,0:T(8,128)(2,1)}, f32[1,1024]{1,0:T(1,128)}, bf16[4,128,1024]{2,1,0:T(8,128)(2,1)}) custom-call(s32[5]{0:T(128)} %stack.23.place_ref, bf16[8,384,128]{2,1,0:T(8,128)(2,1)} %all-to-all-done.4.grads_ref, f32[128,1024]{1,0:T(8,128)} %copy-done.3, f32[1,1024]{1,0:T(1,128)} %bitcast.82, ...), custom_call_target="tpu_custom_call" | custom-call | flops 99999997952 | bytes 1048576 | tf_op jit(solution)/shard_map/trunk_back/pallas_call | solution.py:797
  157.7 4.5 %all-to-all-start.5 = ((bf16[4,128,1024]{2,1,0:T(8,128)(2,1)}), bf16[4,128,1024]{2,1,0:T(8,128)(2,1)}, u32[]{:S(2)}, u32[]{:S(2)}) async-start(bf16[4,128,1024]{2,1,0:T(8,128)(2,1)} %get-tuple-element.236), calls=%async_computation.5 | async-start | bytes 2097152 | tf_op jit(solution)/shard_map/all_to_all | solution.py:1044
  162.2 2.3 pair_sum.3
  165.7 8.9 %front_backward.1 = (bf16[768,128]{1,0:T(8,128)(2,1)}, bf16[2,832,256]{2,1,0:T(8,128)(2,1)}, bf16[2,832,256]{2,1,0:T(8,128)(2,1)}) custom-call(s32[5]{0:T(128)} %stack.23.place_ref, s32[1,48]{1,0:T(1,128)} %constant_dynamic-slice_fusion.4.ids_ref, bf16[768,128]{1,0:T(8,128)(2,1)} %get-tuple-element.186.x_ref, f32[768,128]{1,0:T(8,128)} %get-tuple-element.187.p_ref, ...), custom_call_target="tpu_custom_call" | custom-call | flops 100000000 | bytes 1048576 | tf_op jit(solution)/shard_map/front_backward/pallas_call | solution.py:209
  174.6 1.5 all-to-all-done.5.refs_4_
  176.7 2.3 pair_sum.4
  179.0 1.4 collective-permute-start.22
  180.4 2.4 core_sum.1
  183.8 2.4 z_first_sum.3
  187.5 6.5 %collective-permute-done.18 = bf16[832,256]{1,0:T(8,128)(2,1)} collective-permute-done((bf16[832,256]{1,0:T(8,128)(2,1)}, bf16[832,256]{1,0:T(8,128)(2,1)}, u32[]{:S(2)}, u32[]{:S(2)}) %collective-permute-start.18) | collective-permute-done | bytes 426016 | tf_op jit(solution)/shard_map/ppermute | solution.py:445
  194.0 2.0 x_sum.1
  197.1 4.7 %weight_grads.5 = (bf16[4,128,1024]{2,1,0:T(8,128)(2,1)}, bf16[2,128,1024]{2,1,0:T(8,128)(2,1)}, bf16[2,128,1024]{2,1,0:T(8,128)(2,1)}) custom-call(s32[5]{0:T(128)} %stack.23.place_ref, bf16[128,3072]{1,0:T(8,128)(2,1)} %pad_maximum_fusion.refs_4_.refs_0_, bf16[128,3072]{1,0:T(8,128)(2,1)} %copy-done.19, ...), custom_call_target="tpu_custom_call" | custom-call | flops 1999999991808 | bytes 1048576 | tf_op jit(solution)/shard_map/weight_grads/pallas_call | solution.py:458
  202.1 1.8 z_pieces.1
  204.0 2.3 collective-permute-start.24
  207.5 2.5 z_first_sum.4
  211.8 1.5 z_sum.1.refs_0_
  214.5 2.4 collective-permute-start.29
  216.9 1.8 z_last_sum.3.refs_0_
  219.4 12.3 %collective-permute-done.28.refs_2_ = bf16[104,256]{1,0:T(8,128)(2,1)} collective-permute-done((bf16[104,256]{1,0:T(8,128)(2,1)}, bf16[104,256]{1,0:T(8,128)(2,1)}, u32[]{:S(2)}, u32[]{:S(2)}) %collective-permute-start.28) | collective-permute-done | bytes 53280 | tf_op jit(solution)/shard_map/ppermute | solution.py:445
  232.4 2.3 pair_sum.5
  235.4 1.6 z_join.1
  238.2 5.1 %all-to-all-start.6 = ((bf16[4,192,128]{2,1,0:T(8,128)(2,1)}), bf16[4,192,128]{2,1,0:T(8,128)(2,1)}, u32[]{:S(2)}, u32[]{:S(2)}) async-start(bf16[4,192,128]{2,1,0:T(8,128)(2,1)} %bitcast.30), calls=%async_computation.6 | async-start | bytes 393216 | tf_op jit(solution)/shard_map/all_to_all | solution.py:1108
  243.3 1.9 z_last_sum.5.refs_0_
  245.2 1.7 collective-permute-start.45
  247.9 1.8 y_join.1
  250.9 2.4 z_first_sum.5
  253.4 1.5 collective-permute-done.45.refs_2_
  254.9 1.7 collective-permute-start.46
  257.2 6.8 %collective-permute-done.35.m2 = bf16[832,256]{1,0:T(8,128)(2,1)} collective-permute-done((bf16[832,256]{1,0:T(8,128)(2,1)}, bf16[832,256]{1,0:T(8,128)(2,1)}, u32[]{:S(2)}, u32[]{:S(2)}) %collective-permute-start.35) | collective-permute-done | bytes 426016 | tf_op jit(solution)/shard_map/ppermute | solution.py:445
  265.0 2.7 join.5
  267.7 3.9 %collective-permute-done.40.got_ref = bf16[128,1024]{1,0:T(8,128)(2,1)} collective-permute-done((bf16[128,1024]{1,0:T(8,128)(2,1)}, bf16[128,1024]{1,0:T(8,128)(2,1)}, u32[]{:S(2)}, u32[]{:S(2)}) %collective-permute-start.40) | collective-permute-done | bytes 262176 | tf_op jit(solution)/shard_map/ppermute | solution.py:445
  271.6 1.8 z_last_sum.4.refs_0_
  274.8 2.9 join.4
  278.5 2.7 collective-permute-done.42.refs_2_
  282.5 6.2 %front_last.1 = (f32[128,1024]{1,0:T(8,128)}, f32[768,128]{1,0:T(8,128)}, f32[48,128]{1,0:T(8,128)}, f32[128,1024]{1,0:T(8,128)}, f32[128,1024]{1,0:T(8,128)}, /...) custom-call(s32[5]{0:T(128)} %stack.23.place_ref, bf16[832,256]{1,0:T(8,128)(2,1)} %bitcast.33.m0, ...), custom_call_target="tpu_custom_call" | custom-call | flops 199999995904 | bytes 1048576 | tf_op jit(solution)/shard_map/front_last/pallas_call | solution.py:458
  288.7 2.6 join.3
  291.3 1.6 copy.47
  (171 shorter events, 47.6 us)
Async XLA Ops:
  0.6 16.5 %copy-start = (s32[4,48]{1,0:T(4,128)S(1)}, s32[4,48]{1,0:T(4,128)}, u32[]{:S(2)}) copy-start(s32[4,48]{1,0:T(4,128)} %param.19) | copy-start | bytes 2308
  0.7 17.0 %all-to-all-start = ((bf16[4,192,128]{2,1,0:T(8,128)(2,1)}), bf16[4,192,128]{2,1,0:T(8,128)(2,1)S(1)}, u32[]{:S(2)}, u32[]{:S(2)}) async-start(bf16[4,192,128]{2,1,0:T(8,128)(2,1)} %bitcast.79), calls=%async_computation | async-start | bytes 393216 | tf_op jit(solution)/shard_map/all_to_all | solution.py:936
  15.7 21.8 %copy-start.7 = (bf16[128,1024]{1,0:T(8,128)(2,1)}, bf16[128,1024]{1,0:T(8,128)(2,1)S(1)}, u32[]{:S(2)}) copy-start(bf16[128,1024]{1,0:T(8,128)(2,1)S(1)} %fusion.2.og_ref) | copy-start | bytes 786436
  17.2 9.0 %copy-start.15 = (f32[1024]{0:T(1024)}, f32[1024]{0:T(1024)S(1)}, u32[]{:S(2)}) copy-start(f32[1024]{0:T(1024)S(1)} %convert_element_type.88) | copy-start | bytes 12292
  31.3 26.2 %all-to-all-start.1 = ((bf16[8,384,128]{2,1,0:T(8,128)(2,1)}), bf16[8,384,128]{2,1,0:T(8,128)(2,1)}, u32[]{:S(2)}, u32[]{:S(2)}) async-start(bf16[8,384,128]{2,1,0:T(8,128)(2,1)} %bitcast.14), calls=%async_computation.1 | async-start | bytes 1572864 | tf_op jit(solution)/shard_map/all_to_all | solution.py:392
  38.4 33.2 %collective-permute-start.4 = (bf16[128,3072]{1,0:T(8,128)(2,1)}, bf16[128,3072]{1,0:T(8,128)(2,1)}, u32[]{:S(2)}, u32[]{:S(2)}) collective-permute-start(bf16[128,3072]{1,0:T(8,128)(2,1)} %pad_maximum_fusion.refs_4_.refs_0_), channel_id=1, source_target_pairs={{0,2},{1,3},{2,0},{3,1},{4,6},{5,7},{6,4},{7,5},{8,10},{9,11},{10,... | collective-permute-start | bytes 2359304 | tf_op jit(solution)/shard_map/ppermute | solution.py:445
  57.5 10.9 %copy-start.17 = (bf16[1024]{0:T(1024)(128)(2,1)S(1)}, bf16[1024]{0:T(1024)(128)(2,1)}, u32[]{:S(2)}) copy-start(bf16[1024]{0:T(1024)(128)(2,1)} %param.30) | copy-start | bytes 6148
  64.3 11.6 %all-to-all-start.2 = ((bf16[8,128,128]{2,1,0:T(8,128)(2,1)}), bf16[8,128,128]{2,1,0:T(8,128)(2,1)S(1)}, u32[]{:S(2)}, u32[]{:S(2)}) async-start(bf16[8,128,128]{2,1,0:T(8,128)(2,1)} %bitcast.77), calls=%async_computation.2 | async-start | bytes 524288 | tf_op jit(solution)/shard_map/all_to_all | solution.py:392
  70.8 25.3 %collective-permute-start.3 = (bf16[128,3072]{1,0:T(8,128)(2,1)}, bf16[128,3072]{1,0:T(8,128)(2,1)S(1)}, u32[]{:S(2)}, u32[]{:S(2)}) collective-permute-start(bf16[128,3072]{1,0:T(8,128)(2,1)} %pad_maximum_fusion.refs_4_.refs_0_), channel_id=1, source_target_pairs={{0,1},{1,0},{2,3},{3,2},{4,5},{5,4},{6,7},{7,6},{8,9},{9,8},{10,11... | collective-permute-start | bytes 2359304 | tf_op jit(solution)/shard_map/ppermute | solution.py:445
  71.6 24.6 %collective-permute-start.5 = (bf16[128,3072]{1,0:T(8,128)(2,1)}, bf16[128,3072]{1,0:T(8,128)(2,1)S(1)}, u32[]{:S(2)}, u32[]{:S(2)}) collective-permute-start(bf16[128,3072]{1,0:T(8,128)(2,1)} %collective-permute-done.4.refs_6_.refs_2_), channel_id=1, source_target_pairs={{0,1},{1,0},{2,3},{3,2},{4,5},{5,4},{6,7},{7,6},{8,9},{9,8},{10,11... | collective-permute-start | bytes 2359304 | tf_op jit(solution)/shard_map/ppermute | solution.py:445
  76.0 20.2 %collective-permute-start = (bf16[8,128,128]{2,1,0:T(8,128)(2,1)S(1)}, bf16[8,128,128]{2,1,0:T(8,128)(2,1)S(1)}, u32[]{:S(2)}, u32[]{:S(2)}) collective-permute-start(bf16[8,128,128]{2,1,0:T(8,128)(2,1)S(1)} %all-to-all-done.2.att_ref.refs_4_), channel_id=1, source_target_pairs={{0,1},{1,0},{2,3},{3,2},{4,5},{5,4},{6,7},{7,6},{8,9},{9,8},{10,11... | collective-permute-start | bytes 786440 | tf_op jit(solution)/shard_map/ppermute | solution.py:445
  78.2 18.0 %collective-permute-start.1 = (bf16[8,128,128]{2,1,0:T(8,128)(2,1)S(1)}, bf16[8,128,128]{2,1,0:T(8,128)(2,1)S(1)}, u32[]{:S(2)}, u32[]{:S(2)}) collective-permute-start(bf16[8,128,128]{2,1,0:T(8,128)(2,1)S(1)} %all-to-all-done.2.att_ref.refs_4_), channel_id=1, source_target_pairs={{0,2},{1,3},{2,0},{3,1},{4,6},{5,7},{6,4},{7,5},{8,10},{9,11},{10,... | collective-permute-start | bytes 786440 | tf_op jit(solution)/shard_map/ppermute | solution.py:445
  79.6 16.7 %collective-permute-start.2 = (bf16[8,128,128]{2,1,0:T(8,128)(2,1)S(1)}, bf16[8,128,128]{2,1,0:T(8,128)(2,1)S(1)}, u32[]{:S(2)}, u32[]{:S(2)}) collective-permute-start(bf16[8,128,128]{2,1,0:T(8,128)(2,1)S(1)} %all-to-all-done.2.att_ref.refs_4_), channel_id=1, source_target_pairs={{0,3},{1,2},{2,1},{3,0},{4,7},{5,6},{6,5},{7,4},{8,11},{9,10},{10,... | collective-permute-start | bytes 786440 | tf_op jit(solution)/shard_map/ppermute | solution.py:445
  79.9 19.8 %copy-start.18 = (f32[128,1]{0,1:T(1,128)S(1)}, f32[128,1]{0,1:T(1,128)}, u32[]{:S(2)}) copy-start(f32[128,1]{0,1:T(1,128)} %bitcast_convert_fusion) | copy-start | bytes 1540
  96.2 23.1 %copy-start.19 = (bf16[128,3072]{1,0:T(8,128)(2,1)}, bf16[128,3072]{1,0:T(8,128)(2,1)S(1)}, u32[]{:S(2)}) copy-start(bf16[128,3072]{1,0:T(8,128)(2,1)S(1)} %collective-permute-done.3.refs_5_.refs_1_) | copy-start | bytes 2359300
  96.2 23.0 %copy-start.20 = (bf16[128,3072]{1,0:T(8,128)(2,1)}, bf16[128,3072]{1,0:T(8,128)(2,1)S(1)}, u32[]{:S(2)}) copy-start(bf16[128,3072]{1,0:T(8,128)(2,1)S(1)} %collective-permute-done.5.refs_7_.refs_3_) | copy-start | bytes 2359300
  96.2 23.0 %copy-start.21 = (bf16[8,128,128]{2,1,0:T(8,128)(2,1)}, bf16[8,128,128]{2,1,0:T(8,128)(2,1)S(1)}, u32[]{:S(2)}) copy-start(bf16[8,128,128]{2,1,0:T(8,128)(2,1)S(1)} %collective-permute-done.refs_5_) | copy-start | bytes 786436
  96.2 23.0 %copy-start.22 = (bf16[8,128,128]{2,1,0:T(8,128)(2,1)}, bf16[8,128,128]{2,1,0:T(8,128)(2,1)S(1)}, u32[]{:S(2)}) copy-start(bf16[8,128,128]{2,1,0:T(8,128)(2,1)S(1)} %collective-permute-done.1.refs_6_) | copy-start | bytes 786436
  96.2 23.0 %copy-start.23 = (bf16[8,128,128]{2,1,0:T(8,128)(2,1)}, bf16[8,128,128]{2,1,0:T(8,128)(2,1)S(1)}, u32[]{:S(2)}) copy-start(bf16[8,128,128]{2,1,0:T(8,128)(2,1)S(1)} %collective-permute-done.2.refs_7_) | copy-start | bytes 786436
  96.3 11.3 %all-to-all-start.3 = ((bf16[8,128,128]{2,1,0:T(8,128)(2,1)}), bf16[8,128,128]{2,1,0:T(8,128)(2,1)S(1)}, u32[]{:S(2)}, u32[]{:S(2)}) async-start(bf16[8,128,128]{2,1,0:T(8,128)(2,1)} %get-tuple-element.188), calls=%async_computation.3 | async-start | bytes 524288 | tf_op jit(solution)/shard_map/all_to_all | solution.py:392
  100.4 18.8 %collective-permute-start.6 = (bf16[128,1024]{1,0:T(8,128)(2,1)}, bf16[128,1024]{1,0:T(8,128)(2,1)}, u32[]{:S(2)}, u32[]{:S(2)}) collective-permute-start(bf16[128,1024]{1,0:T(8,128)(2,1)} %get-tuple-element.210.refs_0_), channel_id=1, source_target_pairs={{0,2},{1,3},{2,0},{3,1},{4,6},{5,7},{6,4},{7,5},{8,10},{9,11},{10,... | collective-permute-start | bytes 786440 | tf_op jit(solution)/shard_map/ppermute | solution.py:445
  101.8 30.3 %collective-permute-start.10 = (bf16[128,1024]{1,0:T(8,128)(2,1)}, bf16[128,1024]{1,0:T(8,128)(2,1)}, u32[]{:S(2)}, u32[]{:S(2)}) collective-permute-start(bf16[128,1024]{1,0:T(8,128)(2,1)} %get-tuple-element.210.refs_0_), channel_id=1, source_target_pairs={{0,1},{1,0},{2,3},{3,2},{4,5},{5,4},{6,7},{7,6},{8,9},{9,8},{10,11... | collective-permute-start | bytes 786440 | tf_op jit(solution)/shard_map/ppermute | solution.py:445
  102.4 16.8 %collective-permute-start.7 = (bf16[128,1024]{1,0:T(8,128)(2,1)}, bf16[128,1024]{1,0:T(8,128)(2,1)S(1)}, u32[]{:S(2)}, u32[]{:S(2)}) collective-permute-start(bf16[128,1024]{1,0:T(8,128)(2,1)} %get-tuple-element.192), channel_id=1, source_target_pairs={{0,1},{1,0},{2,3},{3,2},{4,5},{5,4},{6,7},{7,6},{8,9},{9,8},{10,11... | collective-permute-start | bytes 786440 | tf_op jit(solution)/shard_map/ppermute | solution.py:445
  102.4 16.8 %collective-permute-start.8 = (bf16[128,1024]{1,0:T(8,128)(2,1)}, bf16[128,1024]{1,0:T(8,128)(2,1)S(1)}, u32[]{:S(2)}, u32[]{:S(2)}) collective-permute-start(bf16[128,1024]{1,0:T(8,128)(2,1)} %get-tuple-element.193), channel_id=1, source_target_pairs={{0,2},{1,3},{2,0},{3,1},{4,6},{5,7},{6,4},{7,5},{8,10},{9,11},{10,... | collective-permute-start | bytes 786440 | tf_op jit(solution)/shard_map/ppermute | solution.py:445
  102.6 17.3 %collective-permute-start.9 = (bf16[128,1024]{1,0:T(8,128)(2,1)}, bf16[128,1024]{1,0:T(8,128)(2,1)S(1)}, u32[]{:S(2)}, u32[]{:S(2)}) collective-permute-start(bf16[128,1024]{1,0:T(8,128)(2,1)} %get-tuple-element.194), channel_id=1, source_target_pairs={{0,3},{1,2},{2,1},{3,0},{4,7},{5,6},{6,5},{7,4},{8,11},{9,10},{10,... | collective-permute-start | bytes 786440 | tf_op jit(solution)/shard_map/ppermute | solution.py:445
  119.9 29.2 %all-to-all-start.4 = ((bf16[8,384,128]{2,1,0:T(8,128)(2,1)}), bf16[8,384,128]{2,1,0:T(8,128)(2,1)}, u32[]{:S(2)}, u32[]{:S(2)}) async-start(bf16[8,384,128]{2,1,0:T(8,128)(2,1)} %attend_backward.1), calls=%async_computation.4 | async-start | bytes 1572864 | tf_op jit(solution)/shard_map/all_to_all | solution.py:392
  125.3 8.4 %collective-permute-start.11 = (bf16[128,1024]{1,0:T(8,128)(2,1)}, bf16[128,1024]{1,0:T(8,128)(2,1)}, u32[]{:S(2)}, u32[]{:S(2)}) collective-permute-start(bf16[128,1024]{1,0:T(8,128)(2,1)} %collective-permute-done.6.refs_2_), channel_id=1, source_target_pairs={{0,1},{1,0},{2,3},{3,2},{4,5},{5,4},{6,7},{7,6},{8,9},{9,8},{10,11... | collective-permute-start | bytes 786440 | tf_op jit(solution)/shard_map/ppermute | solution.py:445
  125.6 8.1 %collective-permute-start.12 = (bf16[128,1280]{1,0:T(8,128)(2,1)}, bf16[128,1280]{1,0:T(8,128)(2,1)}, u32[]{:S(2)}, u32[]{:S(2)}) collective-permute-start(bf16[128,1280]{1,0:T(8,128)(2,1)} %get-tuple-element.217), channel_id=1, source_target_pairs={{0,1},{1,0},{2,3},{3,2},{4,5},{5,4},{6,7},{7,6},{8,9},{9,8},{10,11... | collective-permute-start | bytes 983048 | tf_op jit(solution)/shard_map/ppermute | solution.py:445
  125.8 9.3 %collective-permute-start.13 = (bf16[128,1280]{1,0:T(8,128)(2,1)}, bf16[128,1280]{1,0:T(8,128)(2,1)}, u32[]{:S(2)}, u32[]{:S(2)}) collective-permute-start(bf16[128,1280]{1,0:T(8,128)(2,1)} %get-tuple-element.218), channel_id=1, source_target_pairs={{0,2},{1,3},{2,0},{3,1},{4,6},{5,7},{6,4},{7,5},{8,10},{9,11},{10,... | collective-permute-start | bytes 983048 | tf_op jit(solution)/shard_map/ppermute | solution.py:445
  127.1 15.7 %collective-permute-start.14 = (bf16[128,1280]{1,0:T(8,128)(2,1)}, bf16[128,1280]{1,0:T(8,128)(2,1)}, u32[]{:S(2)}, u32[]{:S(2)}) collective-permute-start(bf16[128,1280]{1,0:T(8,128)(2,1)} %get-tuple-element.219), channel_id=1, source_target_pairs={{0,3},{1,2},{2,1},{3,0},{4,7},{5,6},{6,5},{7,4},{8,11},{9,10},{10,... | collective-permute-start | bytes 983048 | tf_op jit(solution)/shard_map/ppermute | solution.py:445
  132.1 30.1 %collective-permute-start.15 = (bf16[4,128,1024]{2,1,0:T(8,128)(2,1)}, bf16[4,128,1024]{2,1,0:T(8,128)(2,1)}, u32[]{:S(2)}, u32[]{:S(2)}) collective-permute-start(bf16[4,128,1024]{2,1,0:T(8,128)(2,1)} %get-tuple-element.226), channel_id=1, source_target_pairs={{0,4},{4,0},{8,12},{12,8},{16,20},{20,16},{24,28},{28,24},{1,5},{5... | collective-permute-start | bytes 3145736 | tf_op jit(solution)/shard_map/ppermute | solution.py:445
  147.7 26.9 %collective-permute-start.16 = (bf16[2,128,1280]{2,1,0:T(8,128)(2,1)}, bf16[2,128,1280]{2,1,0:T(8,128)(2,1)}, u32[]{:S(2)}, u32[]{:S(2)}) collective-permute-start(bf16[2,128,1280]{2,1,0:T(8,128)(2,1)} %get-tuple-element.235), channel_id=1, source_target_pairs={{0,4},{4,0},{8,12},{12,8},{16,20},{20,16},{24,28},{28,24},{1,5},{5... | collective-permute-start | bytes 1966088 | tf_op jit(solution)/shard_map/ppermute | solution.py:445
  157.7 18.4 %all-to-all-start.5 = ((bf16[4,128,1024]{2,1,0:T(8,128)(2,1)}), bf16[4,128,1024]{2,1,0:T(8,128)(2,1)}, u32[]{:S(2)}, u32[]{:S(2)}) async-start(bf16[4,128,1024]{2,1,0:T(8,128)(2,1)} %get-tuple-element.236), calls=%async_computation.5 | async-start | bytes 2097152 | tf_op jit(solution)/shard_map/all_to_all | solution.py:1044
  164.5 19.3 %collective-permute-start.19 = (bf16[2,128,1024]{2,1,0:T(8,128)(2,1)}, bf16[2,128,1024]{2,1,0:T(8,128)(2,1)}, u32[]{:S(2)}, u32[]{:S(2)}) collective-permute-start(bf16[2,128,1024]{2,1,0:T(8,128)(2,1)} %pair_sum.3), channel_id=1, source_target_pairs={{0,8},{4,12},{8,0},{12,4},{16,24},{20,28},{24,16},{28,20},{1,9},{5... | collective-permute-start | bytes 1572872 | tf_op jit(solution)/shard_map/ppermute | solution.py:445
  176.1 4.3 %collective-permute-start.17 = (bf16[2,832,256]{2,1,0:T(8,128)(2,1)}, bf16[2,832,256]{2,1,0:T(8,128)(2,1)}, u32[]{:S(2)}, u32[]{:S(2)}) collective-permute-start(bf16[2,832,256]{2,1,0:T(8,128)(2,1)} %get-tuple-element.238), channel_id=1, source_target_pairs={{0,1},{1,0},{2,3},{3,2},{4,5},{5,4},{6,7},{7,6},{8,9},{9,8},{10,11... | collective-permute-start | bytes 2555912 | tf_op jit(solution)/shard_map/ppermute | solution.py:445
  179.0 23.2 %collective-permute-start.21 = (bf16[2,128,1280]{2,1,0:T(8,128)(2,1)}, bf16[2,128,1280]{2,1,0:T(8,128)(2,1)}, u32[]{:S(2)}, u32[]{:S(2)}) collective-permute-start(bf16[2,128,1280]{2,1,0:T(8,128)(2,1)} %get-tuple-element.249), channel_id=1, source_target_pairs={{0,4},{4,0},{8,12},{12,8},{16,20},{20,16},{24,28},{28,24},{1,5},{5... | collective-permute-start | bytes 1966088 | tf_op jit(solution)/shard_map/ppermute | solution.py:445
  179.0 23.2 %collective-permute-start.22 = (bf16[2,128,1280]{2,1,0:T(8,128)(2,1)}, bf16[2,128,1280]{2,1,0:T(8,128)(2,1)}, u32[]{:S(2)}, u32[]{:S(2)}) collective-permute-start(bf16[2,128,1280]{2,1,0:T(8,128)(2,1)} %pair_sum.4), channel_id=1, source_target_pairs={{0,8},{4,12},{8,0},{12,4},{16,24},{20,28},{24,16},{28,20},{1,9},{5... | collective-permute-start | bytes 1966088 | tf_op jit(solution)/shard_map/ppermute | solution.py:445
  182.8 11.1 %collective-permute-start.18 = (bf16[832,256]{1,0:T(8,128)(2,1)}, bf16[832,256]{1,0:T(8,128)(2,1)}, u32[]{:S(2)}, u32[]{:S(2)}) collective-permute-start(bf16[832,256]{1,0:T(8,128)(2,1)} %get-tuple-element.240), channel_id=1, source_target_pairs={{0,2},{1,3},{2,0},{3,1},{4,6},{5,7},{6,4},{7,5},{8,10},{9,11},{10,... | collective-permute-start | bytes 1277960 | tf_op jit(solution)/shard_map/ppermute | solution.py:445
  186.3 23.6 %collective-permute-start.26 = (bf16[128,1024]{1,0:T(8,128)(2,1)}, bf16[128,1024]{1,0:T(8,128)(2,1)}, u32[]{:S(2)}, u32[]{:S(2)}) collective-permute-start(bf16[128,1024]{1,0:T(8,128)(2,1)} %get-tuple-element.259), channel_id=1, source_target_pairs={{0,16},{4,20},{8,24},{12,28},{16,0},{20,4},{24,8},{28,12},{1,17},{... | collective-permute-start | bytes 786440 | tf_op jit(solution)/shard_map/ppermute | solution.py:445
  195.9 6.2 %collective-permute-start.20 = (bf16[416,256]{1,0:T(8,128)(2,1)}, bf16[416,256]{1,0:T(8,128)(2,1)}, u32[]{:S(2)}, u32[]{:S(2)}) collective-permute-start(bf16[416,256]{1,0:T(8,128)(2,1)} %get-tuple-element.246), channel_id=1, source_target_pairs={{0,4},{4,0},{8,12},{12,8},{16,20},{20,16},{24,28},{28,24},{1,5},{5... | collective-permute-start | bytes 638984 | tf_op jit(solution)/shard_map/ppermute | solution.py:445
  201.9 30.6 %collective-permute-start.30 = (bf16[4,128,1024]{2,1,0:T(8,128)(2,1)}, bf16[4,128,1024]{2,1,0:T(8,128)(2,1)}, u32[]{:S(2)}, u32[]{:S(2)}) collective-permute-start(bf16[4,128,1024]{2,1,0:T(8,128)(2,1)} %get-tuple-element.267), channel_id=1, source_target_pairs={{0,4},{4,0},{8,12},{12,8},{16,20},{20,16},{24,28},{28,24},{1,5},{5... | collective-permute-start | bytes 3145736 | tf_op jit(solution)/shard_map/ppermute | solution.py:445
  203.9 7.2 %collective-permute-start.23 = (bf16[104,256]{1,0:T(8,128)(2,1)}, bf16[104,256]{1,0:T(8,128)(2,1)}, u32[]{:S(2)}, u32[]{:S(2)}) collective-permute-start(bf16[104,256]{1,0:T(8,128)(2,1)} %get-tuple-element.256), channel_id=1, source_target_pairs={{0,8},{4,12},{8,0},{12,4},{16,24},{20,28},{24,16},{28,20},{1,9},{5... | collective-permute-start | bytes 159752 | tf_op jit(solution)/shard_map/ppermute | solution.py:445
  204.0 7.1 %collective-permute-start.24 = (bf16[104,256]{1,0:T(8,128)(2,1)}, bf16[104,256]{1,0:T(8,128)(2,1)}, u32[]{:S(2)}, u32[]{:S(2)}) collective-permute-start(bf16[104,256]{1,0:T(8,128)(2,1)} %get-tuple-element.257), channel_id=1, source_target_pairs={{0,16},{4,20},{8,24},{12,28},{16,0},{20,4},{24,8},{28,12},{1,17},{... | collective-permute-start | bytes 159752 | tf_op jit(solution)/shard_map/ppermute | solution.py:445
  206.2 5.6 %collective-permute-start.25 = (bf16[104,256]{1,0:T(8,128)(2,1)}, bf16[104,256]{1,0:T(8,128)(2,1)}, u32[]{:S(2)}, u32[]{:S(2)}) collective-permute-start(bf16[104,256]{1,0:T(8,128)(2,1)} %get-tuple-element.258), channel_id=1, source_target_pairs={{0,24},{4,28},{8,16},{12,20},{16,8},{20,12},{24,0},{28,4},{1,25},{... | collective-permute-start | bytes 159752 | tf_op jit(solution)/shard_map/ppermute | solution.py:445
  209.9 22.5 %collective-permute-start.31 = (bf16[128,1280]{1,0:T(8,128)(2,1)}, bf16[128,1280]{1,0:T(8,128)(2,1)}, u32[]{:S(2)}, u32[]{:S(2)}) collective-permute-start(bf16[128,1280]{1,0:T(8,128)(2,1)} %get-tuple-element.268), channel_id=1, source_target_pairs={{0,16},{4,20},{8,24},{12,28},{16,0},{20,4},{24,8},{28,12},{1,17},{... | collective-permute-start | bytes 983048 | tf_op jit(solution)/shard_map/ppermute | solution.py:445
  213.4 5.4 %collective-permute-start.27 = (bf16[104,256]{1,0:T(8,128)(2,1)}, bf16[104,256]{1,0:T(8,128)(2,1)}, u32[]{:S(2)}, u32[]{:S(2)}) collective-permute-start(bf16[104,256]{1,0:T(8,128)(2,1)} %z_sum.1.refs_0_), channel_id=1, source_target_pairs={{0,8},{4,12},{8,0},{12,4},{16,24},{20,28},{24,16},{28,20},{1,9},{5... | collective-permute-start | bytes 159752 | tf_op jit(solution)/shard_map/ppermute | solution.py:445
  213.8 17.9 %collective-permute-start.28 = (bf16[104,256]{1,0:T(8,128)(2,1)}, bf16[104,256]{1,0:T(8,128)(2,1)}, u32[]{:S(2)}, u32[]{:S(2)}) collective-permute-start(bf16[104,256]{1,0:T(8,128)(2,1)} %z_sum.1.refs_0_), channel_id=1, source_target_pairs={{0,16},{4,20},{8,24},{12,28},{16,0},{20,4},{24,8},{28,12},{1,17},{... | collective-permute-start | bytes 159752 | tf_op jit(solution)/shard_map/ppermute | solution.py:445
  214.5 17.9 %collective-permute-start.29 = (bf16[104,256]{1,0:T(8,128)(2,1)}, bf16[104,256]{1,0:T(8,128)(2,1)}, u32[]{:S(2)}, u32[]{:S(2)}) collective-permute-start(bf16[104,256]{1,0:T(8,128)(2,1)} %z_sum.1.refs_0_), channel_id=1, source_target_pairs={{0,24},{4,28},{8,16},{12,20},{16,8},{20,12},{24,0},{28,4},{1,25},{... | collective-permute-start | bytes 159752 | tf_op jit(solution)/shard_map/ppermute | solution.py:445
  218.7 26.5 %collective-permute-start.33 = (bf16[128,1024]{1,0:T(8,128)(2,1)}, bf16[128,1024]{1,0:T(8,128)(2,1)}, u32[]{:S(2)}, u32[]{:S(2)}) collective-permute-start(bf16[128,1024]{1,0:T(8,128)(2,1)} %z_last_sum.3.refs_0_), channel_id=1, source_target_pairs={{0,2},{1,3},{2,0},{3,1},{4,6},{5,7},{6,4},{7,5},{8,10},{9,11},{10,... | collective-permute-start | bytes 786440 | tf_op jit(solution)/shard_map/ppermute | solution.py:445
  231.7 21.7 %collective-permute-start.36 = (bf16[128,1024]{1,0:T(8,128)(2,1)}, bf16[128,1024]{1,0:T(8,128)(2,1)}, u32[]{:S(2)}, u32[]{:S(2)}) collective-permute-start(bf16[128,1024]{1,0:T(8,128)(2,1)} %z_last_sum.3.refs_0_), channel_id=1, source_target_pairs={{0,1},{1,0},{2,3},{3,2},{4,5},{5,4},{6,7},{7,6},{8,9},{9,8},{10,11... | collective-permute-start | bytes 786440 | tf_op jit(solution)/shard_map/ppermute | solution.py:445
  234.7 15.3 %collective-permute-start.38 = (bf16[2,128,1024]{2,1,0:T(8,128)(2,1)}, bf16[2,128,1024]{2,1,0:T(8,128)(2,1)}, u32[]{:S(2)}, u32[]{:S(2)}) collective-permute-start(bf16[2,128,1024]{2,1,0:T(8,128)(2,1)} %pair_sum.5), channel_id=1, source_target_pairs={{0,8},{4,12},{8,0},{12,4},{16,24},{20,28},{24,16},{28,20},{1,9},{5... | collective-permute-start | bytes 1572872 | tf_op jit(solution)/shard_map/ppermute | solution.py:445
  237.0 10.8 %collective-permute-start.32 = (bf16[416,256]{1,0:T(8,128)(2,1)}, bf16[416,256]{1,0:T(8,128)(2,1)}, u32[]{:S(2)}, u32[]{:S(2)}) collective-permute-start(bf16[416,256]{1,0:T(8,128)(2,1)} %bitcast.84), channel_id=1, source_target_pairs={{0,4},{4,0},{8,12},{12,8},{16,20},{20,16},{24,28},{28,24},{1,5},{5... | collective-permute-start | bytes 638984 | tf_op jit(solution)/shard_map/ppermute | solution.py:445
  238.2 9.7 %all-to-all-start.6 = ((bf16[4,192,128]{2,1,0:T(8,128)(2,1)}), bf16[4,192,128]{2,1,0:T(8,128)(2,1)}, u32[]{:S(2)}, u32[]{:S(2)}) async-start(bf16[4,192,128]{2,1,0:T(8,128)(2,1)} %bitcast.30), calls=%async_computation.6 | async-start | bytes 393216 | tf_op jit(solution)/shard_map/all_to_all | solution.py:1108
  245.2 29.7 %collective-permute-start.44 = (bf16[128,1280]{1,0:T(8,128)(2,1)}, bf16[128,1280]{1,0:T(8,128)(2,1)}, u32[]{:S(2)}, u32[]{:S(2)}) collective-permute-start(bf16[128,1280]{1,0:T(8,128)(2,1)} %z_last_sum.5.refs_0_), channel_id=1, source_target_pairs={{0,1},{1,0},{2,3},{3,2},{4,5},{5,4},{6,7},{7,6},{8,9},{9,8},{10,11... | collective-permute-start | bytes 983048 | tf_op jit(solution)/shard_map/ppermute | solution.py:445
  245.2 9.6 %collective-permute-start.45 = (bf16[128,1280]{1,0:T(8,128)(2,1)}, bf16[128,1280]{1,0:T(8,128)(2,1)}, u32[]{:S(2)}, u32[]{:S(2)}) collective-permute-start(bf16[128,1280]{1,0:T(8,128)(2,1)} %z_last_sum.5.refs_0_), channel_id=1, source_target_pairs={{0,2},{1,3},{2,0},{3,1},{4,6},{5,7},{6,4},{7,5},{8,10},{9,11},{10,... | collective-permute-start | bytes 983048 | tf_op jit(solution)/shard_map/ppermute | solution.py:445
  249.7 14.3 %collective-permute-start.35 = (bf16[832,256]{1,0:T(8,128)(2,1)}, bf16[832,256]{1,0:T(8,128)(2,1)}, u32[]{:S(2)}, u32[]{:S(2)}) collective-permute-start(bf16[832,256]{1,0:T(8,128)(2,1)} %bitcast.33.m0), channel_id=1, source_target_pairs={{0,2},{1,3},{2,0},{3,1},{4,6},{5,7},{6,4},{7,5},{8,10},{9,11},{10,... | collective-permute-start | bytes 1277960 | tf_op jit(solution)/shard_map/ppermute | solution.py:445
  250.0 6.5 %collective-permute-start.37 = (bf16[128,1024]{1,0:T(8,128)(2,1)}, bf16[128,1024]{1,0:T(8,128)(2,1)}, u32[]{:S(2)}, u32[]{:S(2)}) collective-permute-start(bf16[128,1024]{1,0:T(8,128)(2,1)} %collective-permute-done.33.refs_2_), channel_id=1, source_target_pairs={{0,1},{1,0},{2,3},{3,2},{4,5},{5,4},{6,7},{7,6},{8,9},{9,8},{10,11... | collective-permute-start | bytes 786440 | tf_op jit(solution)/shard_map/ppermute | solution.py:445
  253.3 29.1 %collective-permute-start.34 = (bf16[832,256]{1,0:T(8,128)(2,1)}, bf16[832,256]{1,0:T(8,128)(2,1)}, u32[]{:S(2)}, u32[]{:S(2)}) collective-permute-start(bf16[832,256]{1,0:T(8,128)(2,1)} %bitcast.33.m0), channel_id=1, source_target_pairs={{0,1},{1,0},{2,3},{3,2},{4,5},{5,4},{6,7},{7,6},{8,9},{9,8},{10,11... | collective-permute-start | bytes 1277960 | tf_op jit(solution)/shard_map/ppermute | solution.py:445
  254.9 20.0 %collective-permute-start.46 = (bf16[128,1280]{1,0:T(8,128)(2,1)}, bf16[128,1280]{1,0:T(8,128)(2,1)}, u32[]{:S(2)}, u32[]{:S(2)}) collective-permute-start(bf16[128,1280]{1,0:T(8,128)(2,1)} %collective-permute-done.45.refs_2_), channel_id=1, source_target_pairs={{0,1},{1,0},{2,3},{3,2},{4,5},{5,4},{6,7},{7,6},{8,9},{9,8},{10,11... | collective-permute-start | bytes 983048 | tf_op jit(solution)/shard_map/ppermute | solution.py:445
  256.5 15.1 %collective-permute-start.40 = (bf16[128,1024]{1,0:T(8,128)(2,1)}, bf16[128,1024]{1,0:T(8,128)(2,1)}, u32[]{:S(2)}, u32[]{:S(2)}) collective-permute-start(bf16[128,1024]{1,0:T(8,128)(2,1)} %get-tuple-element.299), channel_id=1, source_target_pairs={{0,16},{4,20},{8,24},{12,28},{16,0},{20,4},{24,8},{28,12},{1,17},{... | collective-permute-start | bytes 786440 | tf_op jit(solution)/shard_map/ppermute | solution.py:445
  264.0 18.5 %collective-permute-start.39 = (bf16[832,256]{1,0:T(8,128)(2,1)}, bf16[832,256]{1,0:T(8,128)(2,1)}, u32[]{:S(2)}, u32[]{:S(2)}) collective-permute-start(bf16[832,256]{1,0:T(8,128)(2,1)} %collective-permute-done.35.m2), channel_id=1, source_target_pairs={{0,1},{1,0},{2,3},{3,2},{4,5},{5,4},{6,7},{7,6},{8,9},{9,8},{10,11... | collective-permute-start | bytes 1277960 | tf_op jit(solution)/shard_map/ppermute | solution.py:445
  273.4 7.8 %collective-permute-start.42 = (bf16[128,1024]{1,0:T(8,128)(2,1)}, bf16[128,1024]{1,0:T(8,128)(2,1)}, u32[]{:S(2)}, u32[]{:S(2)}) collective-permute-start(bf16[128,1024]{1,0:T(8,128)(2,1)} %z_last_sum.4.refs_0_), channel_id=1, source_target_pairs={{0,2},{1,3},{2,0},{3,1},{4,6},{5,7},{6,4},{7,5},{8,10},{9,11},{10,... | collective-permute-start | bytes 786440 | tf_op jit(solution)/shard_map/ppermute | solution.py:445
  277.7 10.9 %collective-permute-start.41 = (bf16[128,1024]{1,0:T(8,128)(2,1)}, bf16[128,1024]{1,0:T(8,128)(2,1)}, u32[]{:S(2)}, u32[]{:S(2)}) collective-permute-start(bf16[128,1024]{1,0:T(8,128)(2,1)} %z_last_sum.4.refs_0_), channel_id=1, source_target_pairs={{0,1},{1,0},{2,3},{3,2},{4,5},{5,4},{6,7},{7,6},{8,9},{9,8},{10,11... | collective-permute-start | bytes 786440 | tf_op jit(solution)/shard_map/ppermute | solution.py:445
  281.2 7.5 %collective-permute-start.43 = (bf16[128,1024]{1,0:T(8,128)(2,1)}, bf16[128,1024]{1,0:T(8,128)(2,1)}, u32[]{:S(2)}, u32[]{:S(2)}) collective-permute-start(bf16[128,1024]{1,0:T(8,128)(2,1)} %collective-permute-done.42.refs_2_), channel_id=1, source_target_pairs={{0,1},{1,0},{2,3},{3,2},{4,5},{5,4},{6,7},{7,6},{8,9},{9,8},{10,11... | collective-permute-start | bytes 786440 | tf_op jit(solution)/shard_map/ppermute | solution.py:445
  (18 other events, 72.5 us)

commit v6 on v5

--- a/solution.py
+++ b/solution.py
@@ -1112,6 +1112,12 @@
 
         def y_back(values):
             values, one["across"], last["field"] = together(values, swap(one["own"], "var", 2), last["field"])
+
+            def field_kernel(place_ref, field_ref, out):
+                out[...] = field_ref[...]
+
+            field = last["field"]
+            last["field"] = small_call(field_kernel, place, (field,), [(field.shape, BF16)], name="field_out")[0]
             return values
 
         def var_done(values):
@@ -1120,7 +1126,8 @@
             two["parts"] = (two["own"], swap(two["own"], "var", 1), across, swap(across, "var", 1))
             last["own"] = z_last_sum(place, near, swap(away, "patch", 4))
             own, across = one["own"], one["across"]
-            values, inner, corner, _ = together(values, swap(own, "var", 1), swap(across, "var", 1), near)
+            moved = (swap(own, "var", 1), swap(across, "var", 1), near)
+            values, inner, corner, *_ = together(values, *moved, last["field"])
             one["parts"] = (own, inner, across, corner)
             return values
 

time: 295 us -> 293 us (level)
    pallas_call x22 -> x23, Pallas kernels: 59.1 us -> 60.8 us  [small_call(): pl.pallas_call(kernel, out_shape=tuple((jax.ShapeDtypeStruct(dims, dtype)...]
  transfers between devices with their start and end apart: 54 -> 54, of which waited for: 15 -> 14; matrix products, arithmetic and copies ran while one was open for 9% -> 9% of each run, Pallas kernels for 37% -> 38%
where the time goes in v6:
time: 293 us; the launch traced here: 291 us
  Pallas kernels  118 us (40%)
  starting transfers between devices  76.5 us (26%)
  waiting for transfers between devices  60.3 us (21%)
  matrix products  17.1 us (6%)
  local copies, waits for them, and re-layouts  11.6 us (4%)
  other arithmetic  7.1 us (2%)
    pallas_call x23, Pallas kernels, small_call(): pl.pallas_call(kernel, out_shape=tuple((jax.ShapeDtypeStruct(dims, dtype)...  60.8 us
    ppermute x47, starting transfers between devices, swap(): lax.ppermute(values, axis, [(i, i ^ bit) for i in range(lax.axis_size(axi...  43.7 us
    ppermute x47, waiting for transfers between devices, swap(): lax.ppermute(values, axis, [(i, i ^ bit) for i in range(lax.axis_size(axi...  42.8 us
    all_to_all x4, starting transfers between devices, to_heads(): lax.all_to_all(values, 'patch', split_axis=0, concat_axis=0, tiled=True)  19 us
    dot_general x10, matrix products, mm(): lax.dot_general(a, b, dims, precision=precision, preferred_element_type=F32)  17.1 us
    pallas_call x1, Pallas kernels, middle(): pl.pallas_call(functools.partial(middle_kernel, sub), grid=(parts // sub,...  16.3 us
    all_to_all x4, waiting for transfers between devices, to_heads(): lax.all_to_all(values, 'patch', split_axis=0, concat_axis=0, tiled=True)  15 us
    pallas_call x1, Pallas kernels, attend_backward(): pl.pallas_call(functools.partial(attend_backward_kernel, head_dim, block)...  11 us
  transfers between devices with their start and end apart: 54, of which 14 were waited for; matrix products, arithmetic and copies ran while one was open for 9% of the time, Pallas kernels for 38%

profile of v6, /device:TPU:1, one launch (start us, length us, event | category | flops | bytes accessed | tf_op | source)
XLA Modules:
  0.0 291.3 jit_solution(14423456082897156637)
XLA Ops:
  0.7 4.3 %all-to-all-start = ((bf16[4,192,128]{2,1,0:T(8,128)(2,1)}), bf16[4,192,128]{2,1,0:T(8,128)(2,1)S(1)}, u32[]{:S(2)}, u32[]{:S(2)}) async-start(bf16[4,192,128]{2,1,0:T(8,128)(2,1)} %bitcast.79), calls=%async_computation | async-start | bytes 393216 | tf_op jit(solution)/shard_map/all_to_all | solution.py:936
  5.8 2.1 fusion.18.aggq_ref
  10.1 3.0 %convolution_convert_fusion.2.vwt_ref = bf16[1024,768]{1,0:T(8,128)(2,1)} fusion(bf16[1024,1024]{1,0:T(8,128)(2,1)S(1)} %copy-done.2, bf16[768,1024]{1,0:T(8,128)(2,1)S(1)} %bitcast.75), kind=kOutput, calls=%fused_computation.2 | convolution fusion | flops 1611399168 | bytes 5242880 | tf_op jit(solution)/shard_map/dot_general | solution.py:28
  18.4 5.3 %front_forward.1 = (bf16[768,128]{1,0:T(8,128)(2,1)}, f32[768,128]{1,0:T(8,128)}, bf16[128,1024]{1,0:T(8,128)(2,1)}, bf16[768,768]{1,0:T(8,128)(2,1)}) custom-call(s32[1,48]{1,0:T(1,128)} %constant_dynamic-slice_fusion.4.ids_ref, bf16[768,128]{1,0:T(8,128)(2,1)} %bitcast.80, f32[16,768]{1,0:T(8,128)} %slice_add_fusion.1.weight_ref, ...), custom_call_target="tpu_custom_call" | custom-call | flops 60000002048 | bytes 1048576 | tf_op jit(solution)/shard_map/front_forward/pallas_call | solution.py:86
  23.7 2.2 fusion.17
  26.3 3.8 %convolution_convert_fusion = bf16[128,3072]{1,0:T(8,128)(2,1)S(1)} fusion(bf16[128,1024]{1,0:T(8,128)(2,1)S(1)} %multiply_convert_fusion, bf16[1024,3072]{1,0:T(8,128)(2,1)} %wqkv_ref.1), kind=kOutput, calls=%fused_computation | convolution fusion | flops 805699584 | bytes 7340032 | tf_op jit(solution)/shard_map/dot_general | solution.py:28
  31.3 6.1 %all-to-all-start.1 = ((bf16[8,384,128]{2,1,0:T(8,128)(2,1)}), bf16[8,384,128]{2,1,0:T(8,128)(2,1)}, u32[]{:S(2)}, u32[]{:S(2)}) async-start(bf16[8,384,128]{2,1,0:T(8,128)(2,1)} %bitcast.14), calls=%async_computation.1 | async-start | bytes 1572864 | tf_op jit(solution)/shard_map/all_to_all | solution.py:392
  42.3 1.6 constant_dynamic-slice_fusion.3.weight_own_ref
  43.9 1.8 constant_dynamic-slice_fusion
  46.9 3.0 %fusion.vw_ref = bf16[768,1024]{1,0:T(8,128)(2,1)} fusion(bf16[768,1024]{1,0:T(8,128)(2,1)S(1)} %bitcast.76, bf16[1024,1024]{1,0:T(8,128)(2,1)S(1)} %copy-done.2), kind=kOutput, calls=%fused_computation.3 | convolution fusion | flops 1611399168 | bytes 5242880 | tf_op jit(solution)/shard_map/dot_general | solution.py:28
  49.9 7.7 %all-to-all-done.1.qkv_ref = bf16[8,384,128]{2,1,0:T(8,128)(2,1)} async-done(((bf16[8,384,128]{2,1,0:T(8,128)(2,1)}), bf16[8,384,128]{2,1,0:T(8,128)(2,1)}, u32[]{:S(2)}, u32[]{:S(2)}) %all-to-all-start.1) | async-done | bytes 786464 | tf_op jit(solution)/shard_map/all_to_all | solution.py:392
  57.5 6.8 %attend_forward.1 = (bf16[1024,128]{1,0:T(8,128)(2,1)}, f32[2,1024]{1,0:T(2,128)}) custom-call(s32[1,1]{1,0:T(1,128)} %bitcast.5.count_ref, bf16[8,384,128]{2,1,0:T(8,128)(2,1)} %all-to-all-done.1.qkv_ref), custom_call_target="tpu_custom_call" | custom-call | flops 60000002048 | bytes 1048576 | tf_op jit(solution)/shard_map/attend_forward/pallas_call | solution.py:266
  64.3 4.0 %all-to-all-start.2 = ((bf16[8,128,128]{2,1,0:T(8,128)(2,1)}), bf16[8,128,128]{2,1,0:T(8,128)(2,1)S(1)}, u32[]{:S(2)}, u32[]{:S(2)}) async-start(bf16[8,128,128]{2,1,0:T(8,128)(2,1)} %bitcast.77), calls=%async_computation.2 | async-start | bytes 524288 | tf_op jit(solution)/shard_map/all_to_all | solution.py:392
  71.6 4.4 %all-to-all-done.2.att_ref.refs_4_ = bf16[8,128,128]{2,1,0:T(8,128)(2,1)S(1)} async-done(((bf16[8,128,128]{2,1,0:T(8,128)(2,1)}), bf16[8,128,128]{2,1,0:T(8,128)(2,1)S(1)}, u32[]{:S(2)}, u32[]{:S(2)}) %all-to-all-start.2) | async-done | bytes 262176 | tf_op jit(solution)/shard_map/all_to_all | solution.py:392
  76.0 2.3 collective-permute-start
  79.9 16.3 %trunk_middle.1 = (bf16[128,1024]{1,0:T(8,128)(2,1)}, bf16[128,1024]{1,0:T(8,128)(2,1)}, bf16[128,1024]{1,0:T(8,128)(2,1)}, bf16[128,1024]{1,0:T(8,128)(2,1)}, b...) custom-call(s32[5]{0:T(128)} %stack.23.place_ref, ...), custom_call_target="tpu_custom_call" | custom-call | flops 99999997952 | bytes 1048576 | tf_op jit(solution)/shard_map/trunk_middle/pallas_call | solution.py:701
  96.3 3.4 %all-to-all-start.3 = ((bf16[8,128,128]{2,1,0:T(8,128)(2,1)}), bf16[8,128,128]{2,1,0:T(8,128)(2,1)S(1)}, u32[]{:S(2)}, u32[]{:S(2)}) async-start(bf16[8,128,128]{2,1,0:T(8,128)(2,1)} %get-tuple-element.188), calls=%async_computation.3 | async-start | bytes 524288 | tf_op jit(solution)/shard_map/all_to_all | solution.py:392
  102.6 2.0 collective-permute-start.9
  104.6 3.0 %all-to-all-done.3 = bf16[8,128,128]{2,1,0:T(8,128)(2,1)S(1)} async-done(((bf16[8,128,128]{2,1,0:T(8,128)(2,1)}), bf16[8,128,128]{2,1,0:T(8,128)(2,1)S(1)}, u32[]{:S(2)}, u32[]{:S(2)}) %all-to-all-start.3) | async-done | bytes 262176 | tf_op jit(solution)/shard_map/all_to_all | solution.py:392
  108.2 11.0 %attend_backward.1 = bf16[8,384,128]{2,1,0:T(8,128)(2,1)} custom-call(s32[1,1]{1,0:T(1,128)} %bitcast.5.count_ref, bf16[8,384,128]{2,1,0:T(8,128)(2,1)} %all-to-all-done.1.qkv_ref, bf16[1024,128]{1,0:T(8,128)(2,1)} %bitcast.78, f32[2,1024]{1,0:T(2,128)} %get-tuple-element.189.lse_ref), custom_call_target="tpu_custom_call" | custom-call | flops 99999997952 | bytes 1048576 | tf_op jit(solution)/shard_map/attend_backward/pallas_call | solution.py:334
  119.9 5.4 %all-to-all-start.4 = ((bf16[8,384,128]{2,1,0:T(8,128)(2,1)}), bf16[8,384,128]{2,1,0:T(8,128)(2,1)}, u32[]{:S(2)}, u32[]{:S(2)}) async-start(bf16[8,384,128]{2,1,0:T(8,128)(2,1)} %attend_backward.1), calls=%async_computation.4 | async-start | bytes 1572864 | tf_op jit(solution)/shard_map/all_to_all | solution.py:392
  127.7 4.3 %weight_grads.3 = (bf16[4,128,1024]{2,1,0:T(8,128)(2,1)}, bf16[2,128,1024]{2,1,0:T(8,128)(2,1)}, bf16[2,128,1024]{2,1,0:T(8,128)(2,1)}) custom-call(s32[5]{0:T(128)} %stack.23.place_ref, bf16[128,1024]{1,0:T(8,128)(2,1)} %get-tuple-element.200.refs_0_, bf16[128,1024]{1,0:T(8,128)(2,1)} %copy-done.24, bf16[128,1024]{1,0:T(8,128)(2,1)} %copy-done.25, ...), custom_call_target="tpu_custom_call" | custom-call | flops 1999999991808 | bytes 1048576 | tf_op jit(solution)/shard_map/weight_grads/pallas_call | solution.py:458
  132.1 1.6 collective-permute-start.15
  133.7 1.4 collective-permute-done.13.refs_10_
  135.1 7.8 %collective-permute-done.14.refs_11_ = bf16[128,1280]{1,0:T(8,128)(2,1)} collective-permute-done((bf16[128,1280]{1,0:T(8,128)(2,1)}, bf16[128,1280]{1,0:T(8,128)(2,1)}, u32[]{:S(2)}, u32[]{:S(2)}) %collective-permute-start.14) | collective-permute-done | bytes 327712 | tf_op jit(solution)/shard_map/ppermute | solution.py:445
  142.9 4.8 %weight_grads.4 = (bf16[2,128,1280]{2,1,0:T(8,128)(2,1)}, bf16[2,128,1280]{2,1,0:T(8,128)(2,1)}, bf16[2,128,1280]{2,1,0:T(8,128)(2,1)}, bf16[2,128,1280]{2,1,0:T(8,128)(2,1)}) custom-call(s32[5]{0:T(128)} %stack.23.place_ref, bf16[128,1024]{1,0:T(8,128)(2,1)} %get-tuple-element.210.refs_0_, bf16[128,1024]{1,0:T(8,128)(2,1)} %collective-permute-done.10.refs_1_, ...), custom_call_target="tpu_custom_call" | custom-call | flops 1999999991808 | bytes 1048576 | tf_op jit(solution)/shard_map/weight_grads/pallas_call | solution.py:458
  147.7 1.5 collective-permute-start.16
  149.2 8.5 %trunk_back.1 = (bf16[128,1024]{1,0:T(8,128)(2,1)}, f32[1,1024]{1,0:T(1,128)}, bf16[4,128,1024]{2,1,0:T(8,128)(2,1)}) custom-call(s32[5]{0:T(128)} %stack.23.place_ref, bf16[8,384,128]{2,1,0:T(8,128)(2,1)} %all-to-all-done.4.grads_ref, f32[128,1024]{1,0:T(8,128)} %copy-done.3, f32[1,1024]{1,0:T(1,128)} %bitcast.82, ...), custom_call_target="tpu_custom_call" | custom-call | flops 99999997952 | bytes 1048576 | tf_op jit(solution)/shard_map/trunk_back/pallas_call | solution.py:797
  157.7 4.5 %all-to-all-start.5 = ((bf16[4,128,1024]{2,1,0:T(8,128)(2,1)}), bf16[4,128,1024]{2,1,0:T(8,128)(2,1)}, u32[]{:S(2)}, u32[]{:S(2)}) async-start(bf16[4,128,1024]{2,1,0:T(8,128)(2,1)} %get-tuple-element.236), calls=%async_computation.5 | async-start | bytes 2097152 | tf_op jit(solution)/shard_map/all_to_all | solution.py:1044
  162.2 2.3 pair_sum.3
  165.7 8.9 %front_backward.1 = (bf16[768,128]{1,0:T(8,128)(2,1)}, bf16[2,832,256]{2,1,0:T(8,128)(2,1)}, bf16[2,832,256]{2,1,0:T(8,128)(2,1)}) custom-call(s32[5]{0:T(128)} %stack.23.place_ref, s32[1,48]{1,0:T(1,128)} %constant_dynamic-slice_fusion.4.ids_ref, bf16[768,128]{1,0:T(8,128)(2,1)} %get-tuple-element.186.x_ref, f32[768,128]{1,0:T(8,128)} %get-tuple-element.187.p_ref, ...), custom_call_target="tpu_custom_call" | custom-call | flops 100000000 | bytes 1048576 | tf_op jit(solution)/shard_map/front_backward/pallas_call | solution.py:209
  174.6 1.5 all-to-all-done.5.refs_4_
  176.7 2.3 pair_sum.4
  179.0 1.4 collective-permute-start.22
  180.4 2.4 core_sum.1
  183.8 2.4 z_first_sum.3
  187.5 6.5 %collective-permute-done.18 = bf16[832,256]{1,0:T(8,128)(2,1)} collective-permute-done((bf16[832,256]{1,0:T(8,128)(2,1)}, bf16[832,256]{1,0:T(8,128)(2,1)}, u32[]{:S(2)}, u32[]{:S(2)}) %collective-permute-start.18) | collective-permute-done | bytes 426016 | tf_op jit(solution)/shard_map/ppermute | solution.py:445
  194.0 2.0 x_sum.1
  197.1 4.7 %weight_grads.5 = (bf16[4,128,1024]{2,1,0:T(8,128)(2,1)}, bf16[2,128,1024]{2,1,0:T(8,128)(2,1)}, bf16[2,128,1024]{2,1,0:T(8,128)(2,1)}) custom-call(s32[5]{0:T(128)} %stack.23.place_ref, bf16[128,3072]{1,0:T(8,128)(2,1)} %pad_maximum_fusion.refs_4_.refs_0_, bf16[128,3072]{1,0:T(8,128)(2,1)} %copy-done.19, ...), custom_call_target="tpu_custom_call" | custom-call | flops 1999999991808 | bytes 1048576 | tf_op jit(solution)/shard_map/weight_grads/pallas_call | solution.py:458
  202.1 1.8 z_pieces.1
  204.0 2.3 collective-permute-start.24
  207.5 2.5 z_first_sum.4
  211.8 1.5 z_sum.1.refs_0_
  214.5 2.4 collective-permute-start.29
  216.9 1.8 z_last_sum.3.refs_0_
  219.4 12.3 %collective-permute-done.28.refs_2_ = bf16[104,256]{1,0:T(8,128)(2,1)} collective-permute-done((bf16[104,256]{1,0:T(8,128)(2,1)}, bf16[104,256]{1,0:T(8,128)(2,1)}, u32[]{:S(2)}, u32[]{:S(2)}) %collective-permute-start.28) | collective-permute-done | bytes 53280 | tf_op jit(solution)/shard_map/ppermute | solution.py:445
  232.4 2.3 pair_sum.5
  235.4 1.6 z_join.1
  238.2 5.1 %all-to-all-start.6 = ((bf16[4,192,128]{2,1,0:T(8,128)(2,1)}), bf16[4,192,128]{2,1,0:T(8,128)(2,1)}, u32[]{:S(2)}, u32[]{:S(2)}) async-start(bf16[4,192,128]{2,1,0:T(8,128)(2,1)} %bitcast.30), calls=%async_computation.6 | async-start | bytes 393216 | tf_op jit(solution)/shard_map/all_to_all | solution.py:1108
  243.3 1.9 z_last_sum.5.refs_0_
  245.2 1.7 collective-permute-start.45
  247.9 1.6 field_out.1
  249.5 1.8 y_join.1
  252.5 2.4 z_first_sum.5
  255.0 1.5 collective-permute-start.46
  257.2 6.8 %collective-permute-done.35.m2 = bf16[832,256]{1,0:T(8,128)(2,1)} collective-permute-done((bf16[832,256]{1,0:T(8,128)(2,1)}, bf16[832,256]{1,0:T(8,128)(2,1)}, u32[]{:S(2)}, u32[]{:S(2)}) %collective-permute-start.35) | collective-permute-done | bytes 426016 | tf_op jit(solution)/shard_map/ppermute | solution.py:445
  265.0 2.7 join.5
  267.7 3.9 %collective-permute-done.40.got_ref = bf16[128,1024]{1,0:T(8,128)(2,1)} collective-permute-done((bf16[128,1024]{1,0:T(8,128)(2,1)}, bf16[128,1024]{1,0:T(8,128)(2,1)}, u32[]{:S(2)}, u32[]{:S(2)}) %collective-permute-start.40) | collective-permute-done | bytes 262176 | tf_op jit(solution)/shard_map/ppermute | solution.py:445
  271.6 1.8 z_last_sum.4.refs_0_
  273.4 1.4 collective-permute-start.42
  274.8 2.9 %join.4 = (f32[128,4096]{1,0:T(8,128)}, f32[128,1024]{1,0:T(8,128)}) custom-call(s32[5]{0:T(128)} %stack.23.place_ref, bf16[128,1280]{1,0:T(8,128)(2,1)} %z_last_sum.5.refs_0_, bf16[128,1280]{1,0:T(8,128)(2,1)} %collective-permute-done.44.refs_1_, bf16[128,1280]{1,0:T(8,128)(2,1)} %collective-permute-done.45.refs_2_, ...), custom_call_target="tpu_custom_call" | custom-call | flops 199999995904 | bytes 1048576 | tf_op jit(solution)/shard_map/join/pallas_call | solution.py:458
  278.5 2.7 collective-permute-done.42.refs_2_
  282.5 6.2 %front_last.1 = (f32[128,1024]{1,0:T(8,128)}, f32[768,128]{1,0:T(8,128)}, f32[48,128]{1,0:T(8,128)}, f32[128,1024]{1,0:T(8,128)}, f32[128,1024]{1,0:T(8,128)}, /...) custom-call(s32[5]{0:T(128)} %stack.23.place_ref, bf16[832,256]{1,0:T(8,128)(2,1)} %bitcast.33.m0, ...), custom_call_target="tpu_custom_call" | custom-call | flops 199999995904 | bytes 1048576 | tf_op jit(solution)/shard_map/front_last/pallas_call | solution.py:458
  288.7 2.6 join.3
  (171 shorter events, 46.2 us)
Async XLA Ops:
  0.6 16.5 %copy-start = (s32[4,48]{1,0:T(4,128)S(1)}, s32[4,48]{1,0:T(4,128)}, u32[]{:S(2)}) copy-start(s32[4,48]{1,0:T(4,128)} %param.19) | copy-start | bytes 2308
  0.7 17.0 %all-to-all-start = ((bf16[4,192,128]{2,1,0:T(8,128)(2,1)}), bf16[4,192,128]{2,1,0:T(8,128)(2,1)S(1)}, u32[]{:S(2)}, u32[]{:S(2)}) async-start(bf16[4,192,128]{2,1,0:T(8,128)(2,1)} %bitcast.79), calls=%async_computation | async-start | bytes 393216 | tf_op jit(solution)/shard_map/all_to_all | solution.py:936
  15.7 21.8 %copy-start.7 = (bf16[128,1024]{1,0:T(8,128)(2,1)}, bf16[128,1024]{1,0:T(8,128)(2,1)S(1)}, u32[]{:S(2)}) copy-start(bf16[128,1024]{1,0:T(8,128)(2,1)S(1)} %fusion.2.og_ref) | copy-start | bytes 786436
  17.2 9.0 %copy-start.15 = (f32[1024]{0:T(1024)}, f32[1024]{0:T(1024)S(1)}, u32[]{:S(2)}) copy-start(f32[1024]{0:T(1024)S(1)} %convert_element_type.88) | copy-start | bytes 12292
  31.3 26.2 %all-to-all-start.1 = ((bf16[8,384,128]{2,1,0:T(8,128)(2,1)}), bf16[8,384,128]{2,1,0:T(8,128)(2,1)}, u32[]{:S(2)}, u32[]{:S(2)}) async-start(bf16[8,384,128]{2,1,0:T(8,128)(2,1)} %bitcast.14), calls=%async_computation.1 | async-start | bytes 1572864 | tf_op jit(solution)/shard_map/all_to_all | solution.py:392
  38.4 33.2 %collective-permute-start.4 = (bf16[128,3072]{1,0:T(8,128)(2,1)}, bf16[128,3072]{1,0:T(8,128)(2,1)}, u32[]{:S(2)}, u32[]{:S(2)}) collective-permute-start(bf16[128,3072]{1,0:T(8,128)(2,1)} %pad_maximum_fusion.refs_4_.refs_0_), channel_id=1, source_target_pairs={{0,2},{1,3},{2,0},{3,1},{4,6},{5,7},{6,4},{7,5},{8,10},{9,11},{10,... | collective-permute-start | bytes 2359304 | tf_op jit(solution)/shard_map/ppermute | solution.py:445
  57.5 10.9 %copy-start.17 = (bf16[1024]{0:T(1024)(128)(2,1)S(1)}, bf16[1024]{0:T(1024)(128)(2,1)}, u32[]{:S(2)}) copy-start(bf16[1024]{0:T(1024)(128)(2,1)} %param.30) | copy-start | bytes 6148
  64.3 11.6 %all-to-all-start.2 = ((bf16[8,128,128]{2,1,0:T(8,128)(2,1)}), bf16[8,128,128]{2,1,0:T(8,128)(2,1)S(1)}, u32[]{:S(2)}, u32[]{:S(2)}) async-start(bf16[8,128,128]{2,1,0:T(8,128)(2,1)} %bitcast.77), calls=%async_computation.2 | async-start | bytes 524288 | tf_op jit(solution)/shard_map/all_to_all | solution.py:392
  70.8 25.3 %collective-permute-start.3 = (bf16[128,3072]{1,0:T(8,128)(2,1)}, bf16[128,3072]{1,0:T(8,128)(2,1)S(1)}, u32[]{:S(2)}, u32[]{:S(2)}) collective-permute-start(bf16[128,3072]{1,0:T(8,128)(2,1)} %pad_maximum_fusion.refs_4_.refs_0_), channel_id=1, source_target_pairs={{0,1},{1,0},{2,3},{3,2},{4,5},{5,4},{6,7},{7,6},{8,9},{9,8},{10,11... | collective-permute-start | bytes 2359304 | tf_op jit(solution)/shard_map/ppermute | solution.py:445
  71.6 24.6 %collective-permute-start.5 = (bf16[128,3072]{1,0:T(8,128)(2,1)}, bf16[128,3072]{1,0:T(8,128)(2,1)S(1)}, u32[]{:S(2)}, u32[]{:S(2)}) collective-permute-start(bf16[128,3072]{1,0:T(8,128)(2,1)} %collective-permute-done.4.refs_6_.refs_2_), channel_id=1, source_target_pairs={{0,1},{1,0},{2,3},{3,2},{4,5},{5,4},{6,7},{7,6},{8,9},{9,8},{10,11... | collective-permute-start | bytes 2359304 | tf_op jit(solution)/shard_map/ppermute | solution.py:445
  76.0 20.2 %collective-permute-start = (bf16[8,128,128]{2,1,0:T(8,128)(2,1)S(1)}, bf16[8,128,128]{2,1,0:T(8,128)(2,1)S(1)}, u32[]{:S(2)}, u32[]{:S(2)}) collective-permute-start(bf16[8,128,128]{2,1,0:T(8,128)(2,1)S(1)} %all-to-all-done.2.att_ref.refs_4_), channel_id=1, source_target_pairs={{0,1},{1,0},{2,3},{3,2},{4,5},{5,4},{6,7},{7,6},{8,9},{9,8},{10,11... | collective-permute-start | bytes 786440 | tf_op jit(solution)/shard_map/ppermute | solution.py:445
  78.2 18.0 %collective-permute-start.1 = (bf16[8,128,128]{2,1,0:T(8,128)(2,1)S(1)}, bf16[8,128,128]{2,1,0:T(8,128)(2,1)S(1)}, u32[]{:S(2)}, u32[]{:S(2)}) collective-permute-start(bf16[8,128,128]{2,1,0:T(8,128)(2,1)S(1)} %all-to-all-done.2.att_ref.refs_4_), channel_id=1, source_target_pairs={{0,2},{1,3},{2,0},{3,1},{4,6},{5,7},{6,4},{7,5},{8,10},{9,11},{10,... | collective-permute-start | bytes 786440 | tf_op jit(solution)/shard_map/ppermute | solution.py:445
  79.6 16.7 %collective-permute-start.2 = (bf16[8,128,128]{2,1,0:T(8,128)(2,1)S(1)}, bf16[8,128,128]{2,1,0:T(8,128)(2,1)S(1)}, u32[]{:S(2)}, u32[]{:S(2)}) collective-permute-start(bf16[8,128,128]{2,1,0:T(8,128)(2,1)S(1)} %all-to-all-done.2.att_ref.refs_4_), channel_id=1, source_target_pairs={{0,3},{1,2},{2,1},{3,0},{4,7},{5,6},{6,5},{7,4},{8,11},{9,10},{10,... | collective-permute-start | bytes 786440 | tf_op jit(solution)/shard_map/ppermute | solution.py:445
  79.9 19.8 %copy-start.18 = (f32[128,1]{0,1:T(1,128)S(1)}, f32[128,1]{0,1:T(1,128)}, u32[]{:S(2)}) copy-start(f32[128,1]{0,1:T(1,128)} %bitcast_convert_fusion) | copy-start | bytes 1540
  96.2 23.1 %copy-start.19 = (bf16[128,3072]{1,0:T(8,128)(2,1)}, bf16[128,3072]{1,0:T(8,128)(2,1)S(1)}, u32[]{:S(2)}) copy-start(bf16[128,3072]{1,0:T(8,128)(2,1)S(1)} %collective-permute-done.3.refs_5_.refs_1_) | copy-start | bytes 2359300
  96.2 23.0 %copy-start.20 = (bf16[128,3072]{1,0:T(8,128)(2,1)}, bf16[128,3072]{1,0:T(8,128)(2,1)S(1)}, u32[]{:S(2)}) copy-start(bf16[128,3072]{1,0:T(8,128)(2,1)S(1)} %collective-permute-done.5.refs_7_.refs_3_) | copy-start | bytes 2359300
  96.2 23.0 %copy-start.21 = (bf16[8,128,128]{2,1,0:T(8,128)(2,1)}, bf16[8,128,128]{2,1,0:T(8,128)(2,1)S(1)}, u32[]{:S(2)}) copy-start(bf16[8,128,128]{2,1,0:T(8,128)(2,1)S(1)} %collective-permute-done.refs_5_) | copy-start | bytes 786436
  96.2 23.0 %copy-start.22 = (bf16[8,128,128]{2,1,0:T(8,128)(2,1)}, bf16[8,128,128]{2,1,0:T(8,128)(2,1)S(1)}, u32[]{:S(2)}) copy-start(bf16[8,128,128]{2,1,0:T(8,128)(2,1)S(1)} %collective-permute-done.1.refs_6_) | copy-start | bytes 786436
  96.2 23.0 %copy-start.23 = (bf16[8,128,128]{2,1,0:T(8,128)(2,1)}, bf16[8,128,128]{2,1,0:T(8,128)(2,1)S(1)}, u32[]{:S(2)}) copy-start(bf16[8,128,128]{2,1,0:T(8,128)(2,1)S(1)} %collective-permute-done.2.refs_7_) | copy-start | bytes 786436
  96.3 11.3 %all-to-all-start.3 = ((bf16[8,128,128]{2,1,0:T(8,128)(2,1)}), bf16[8,128,128]{2,1,0:T(8,128)(2,1)S(1)}, u32[]{:S(2)}, u32[]{:S(2)}) async-start(bf16[8,128,128]{2,1,0:T(8,128)(2,1)} %get-tuple-element.188), calls=%async_computation.3 | async-start | bytes 524288 | tf_op jit(solution)/shard_map/all_to_all | solution.py:392
  100.4 18.8 %collective-permute-start.6 = (bf16[128,1024]{1,0:T(8,128)(2,1)}, bf16[128,1024]{1,0:T(8,128)(2,1)}, u32[]{:S(2)}, u32[]{:S(2)}) collective-permute-start(bf16[128,1024]{1,0:T(8,128)(2,1)} %get-tuple-element.210.refs_0_), channel_id=1, source_target_pairs={{0,2},{1,3},{2,0},{3,1},{4,6},{5,7},{6,4},{7,5},{8,10},{9,11},{10,... | collective-permute-start | bytes 786440 | tf_op jit(solution)/shard_map/ppermute | solution.py:445
  101.8 30.3 %collective-permute-start.10 = (bf16[128,1024]{1,0:T(8,128)(2,1)}, bf16[128,1024]{1,0:T(8,128)(2,1)}, u32[]{:S(2)}, u32[]{:S(2)}) collective-permute-start(bf16[128,1024]{1,0:T(8,128)(2,1)} %get-tuple-element.210.refs_0_), channel_id=1, source_target_pairs={{0,1},{1,0},{2,3},{3,2},{4,5},{5,4},{6,7},{7,6},{8,9},{9,8},{10,11... | collective-permute-start | bytes 786440 | tf_op jit(solution)/shard_map/ppermute | solution.py:445
  102.4 16.8 %collective-permute-start.7 = (bf16[128,1024]{1,0:T(8,128)(2,1)}, bf16[128,1024]{1,0:T(8,128)(2,1)S(1)}, u32[]{:S(2)}, u32[]{:S(2)}) collective-permute-start(bf16[128,1024]{1,0:T(8,128)(2,1)} %get-tuple-element.192), channel_id=1, source_target_pairs={{0,1},{1,0},{2,3},{3,2},{4,5},{5,4},{6,7},{7,6},{8,9},{9,8},{10,11... | collective-permute-start | bytes 786440 | tf_op jit(solution)/shard_map/ppermute | solution.py:445
  102.4 16.8 %collective-permute-start.8 = (bf16[128,1024]{1,0:T(8,128)(2,1)}, bf16[128,1024]{1,0:T(8,128)(2,1)S(1)}, u32[]{:S(2)}, u32[]{:S(2)}) collective-permute-start(bf16[128,1024]{1,0:T(8,128)(2,1)} %get-tuple-element.193), channel_id=1, source_target_pairs={{0,2},{1,3},{2,0},{3,1},{4,6},{5,7},{6,4},{7,5},{8,10},{9,11},{10,... | collective-permute-start | bytes 786440 | tf_op jit(solution)/shard_map/ppermute | solution.py:445
  102.6 17.3 %collective-permute-start.9 = (bf16[128,1024]{1,0:T(8,128)(2,1)}, bf16[128,1024]{1,0:T(8,128)(2,1)S(1)}, u32[]{:S(2)}, u32[]{:S(2)}) collective-permute-start(bf16[128,1024]{1,0:T(8,128)(2,1)} %get-tuple-element.194), channel_id=1, source_target_pairs={{0,3},{1,2},{2,1},{3,0},{4,7},{5,6},{6,5},{7,4},{8,11},{9,10},{10,... | collective-permute-start | bytes 786440 | tf_op jit(solution)/shard_map/ppermute | solution.py:445
  119.9 29.2 %all-to-all-start.4 = ((bf16[8,384,128]{2,1,0:T(8,128)(2,1)}), bf16[8,384,128]{2,1,0:T(8,128)(2,1)}, u32[]{:S(2)}, u32[]{:S(2)}) async-start(bf16[8,384,128]{2,1,0:T(8,128)(2,1)} %attend_backward.1), calls=%async_computation.4 | async-start | bytes 1572864 | tf_op jit(solution)/shard_map/all_to_all | solution.py:392
  125.3 8.4 %collective-permute-start.11 = (bf16[128,1024]{1,0:T(8,128)(2,1)}, bf16[128,1024]{1,0:T(8,128)(2,1)}, u32[]{:S(2)}, u32[]{:S(2)}) collective-permute-start(bf16[128,1024]{1,0:T(8,128)(2,1)} %collective-permute-done.6.refs_2_), channel_id=1, source_target_pairs={{0,1},{1,0},{2,3},{3,2},{4,5},{5,4},{6,7},{7,6},{8,9},{9,8},{10,11... | collective-permute-start | bytes 786440 | tf_op jit(solution)/shard_map/ppermute | solution.py:445
  125.6 8.1 %collective-permute-start.12 = (bf16[128,1280]{1,0:T(8,128)(2,1)}, bf16[128,1280]{1,0:T(8,128)(2,1)}, u32[]{:S(2)}, u32[]{:S(2)}) collective-permute-start(bf16[128,1280]{1,0:T(8,128)(2,1)} %get-tuple-element.217), channel_id=1, source_target_pairs={{0,1},{1,0},{2,3},{3,2},{4,5},{5,4},{6,7},{7,6},{8,9},{9,8},{10,11... | collective-permute-start | bytes 983048 | tf_op jit(solution)/shard_map/ppermute | solution.py:445
  125.8 9.3 %collective-permute-start.13 = (bf16[128,1280]{1,0:T(8,128)(2,1)}, bf16[128,1280]{1,0:T(8,128)(2,1)}, u32[]{:S(2)}, u32[]{:S(2)}) collective-permute-start(bf16[128,1280]{1,0:T(8,128)(2,1)} %get-tuple-element.218), channel_id=1, source_target_pairs={{0,2},{1,3},{2,0},{3,1},{4,6},{5,7},{6,4},{7,5},{8,10},{9,11},{10,... | collective-permute-start | bytes 983048 | tf_op jit(solution)/shard_map/ppermute | solution.py:445
  127.1 15.7 %collective-permute-start.14 = (bf16[128,1280]{1,0:T(8,128)(2,1)}, bf16[128,1280]{1,0:T(8,128)(2,1)}, u32[]{:S(2)}, u32[]{:S(2)}) collective-permute-start(bf16[128,1280]{1,0:T(8,128)(2,1)} %get-tuple-element.219), channel_id=1, source_target_pairs={{0,3},{1,2},{2,1},{3,0},{4,7},{5,6},{6,5},{7,4},{8,11},{9,10},{10,... | collective-permute-start | bytes 983048 | tf_op jit(solution)/shard_map/ppermute | solution.py:445
  132.1 30.1 %collective-permute-start.15 = (bf16[4,128,1024]{2,1,0:T(8,128)(2,1)}, bf16[4,128,1024]{2,1,0:T(8,128)(2,1)}, u32[]{:S(2)}, u32[]{:S(2)}) collective-permute-start(bf16[4,128,1024]{2,1,0:T(8,128)(2,1)} %get-tuple-element.226), channel_id=1, source_target_pairs={{0,4},{4,0},{8,12},{12,8},{16,20},{20,16},{24,28},{28,24},{1,5},{5... | collective-permute-start | bytes 3145736 | tf_op jit(solution)/shard_map/ppermute | solution.py:445
  147.7 26.9 %collective-permute-start.16 = (bf16[2,128,1280]{2,1,0:T(8,128)(2,1)}, bf16[2,128,1280]{2,1,0:T(8,128)(2,1)}, u32[]{:S(2)}, u32[]{:S(2)}) collective-permute-start(bf16[2,128,1280]{2,1,0:T(8,128)(2,1)} %get-tuple-element.235), channel_id=1, source_target_pairs={{0,4},{4,0},{8,12},{12,8},{16,20},{20,16},{24,28},{28,24},{1,5},{5... | collective-permute-start | bytes 1966088 | tf_op jit(solution)/shard_map/ppermute | solution.py:445
  157.7 18.4 %all-to-all-start.5 = ((bf16[4,128,1024]{2,1,0:T(8,128)(2,1)}), bf16[4,128,1024]{2,1,0:T(8,128)(2,1)}, u32[]{:S(2)}, u32[]{:S(2)}) async-start(bf16[4,128,1024]{2,1,0:T(8,128)(2,1)} %get-tuple-element.236), calls=%async_computation.5 | async-start | bytes 2097152 | tf_op jit(solution)/shard_map/all_to_all | solution.py:1044
  164.5 19.3 %collective-permute-start.19 = (bf16[2,128,1024]{2,1,0:T(8,128)(2,1)}, bf16[2,128,1024]{2,1,0:T(8,128)(2,1)}, u32[]{:S(2)}, u32[]{:S(2)}) collective-permute-start(bf16[2,128,1024]{2,1,0:T(8,128)(2,1)} %pair_sum.3), channel_id=1, source_target_pairs={{0,8},{4,12},{8,0},{12,4},{16,24},{20,28},{24,16},{28,20},{1,9},{5... | collective-permute-start | bytes 1572872 | tf_op jit(solution)/shard_map/ppermute | solution.py:445
  176.1 4.3 %collective-permute-start.17 = (bf16[2,832,256]{2,1,0:T(8,128)(2,1)}, bf16[2,832,256]{2,1,0:T(8,128)(2,1)}, u32[]{:S(2)}, u32[]{:S(2)}) collective-permute-start(bf16[2,832,256]{2,1,0:T(8,128)(2,1)} %get-tuple-element.238), channel_id=1, source_target_pairs={{0,1},{1,0},{2,3},{3,2},{4,5},{5,4},{6,7},{7,6},{8,9},{9,8},{10,11... | collective-permute-start | bytes 2555912 | tf_op jit(solution)/shard_map/ppermute | solution.py:445
  179.0 23.2 %collective-permute-start.21 = (bf16[2,128,1280]{2,1,0:T(8,128)(2,1)}, bf16[2,128,1280]{2,1,0:T(8,128)(2,1)}, u32[]{:S(2)}, u32[]{:S(2)}) collective-permute-start(bf16[2,128,1280]{2,1,0:T(8,128)(2,1)} %get-tuple-element.249), channel_id=1, source_target_pairs={{0,4},{4,0},{8,12},{12,8},{16,20},{20,16},{24,28},{28,24},{1,5},{5... | collective-permute-start | bytes 1966088 | tf_op jit(solution)/shard_map/ppermute | solution.py:445
  179.0 23.2 %collective-permute-start.22 = (bf16[2,128,1280]{2,1,0:T(8,128)(2,1)}, bf16[2,128,1280]{2,1,0:T(8,128)(2,1)}, u32[]{:S(2)}, u32[]{:S(2)}) collective-permute-start(bf16[2,128,1280]{2,1,0:T(8,128)(2,1)} %pair_sum.4), channel_id=1, source_target_pairs={{0,8},{4,12},{8,0},{12,4},{16,24},{20,28},{24,16},{28,20},{1,9},{5... | collective-permute-start | bytes 1966088 | tf_op jit(solution)/shard_map/ppermute | solution.py:445
  182.8 11.1 %collective-permute-start.18 = (bf16[832,256]{1,0:T(8,128)(2,1)}, bf16[832,256]{1,0:T(8,128)(2,1)}, u32[]{:S(2)}, u32[]{:S(2)}) collective-permute-start(bf16[832,256]{1,0:T(8,128)(2,1)} %get-tuple-element.240), channel_id=1, source_target_pairs={{0,2},{1,3},{2,0},{3,1},{4,6},{5,7},{6,4},{7,5},{8,10},{9,11},{10,... | collective-permute-start | bytes 1277960 | tf_op jit(solution)/shard_map/ppermute | solution.py:445
  186.3 23.6 %collective-permute-start.26 = (bf16[128,1024]{1,0:T(8,128)(2,1)}, bf16[128,1024]{1,0:T(8,128)(2,1)}, u32[]{:S(2)}, u32[]{:S(2)}) collective-permute-start(bf16[128,1024]{1,0:T(8,128)(2,1)} %get-tuple-element.259), channel_id=1, source_target_pairs={{0,16},{4,20},{8,24},{12,28},{16,0},{20,4},{24,8},{28,12},{1,17},{... | collective-permute-start | bytes 786440 | tf_op jit(solution)/shard_map/ppermute | solution.py:445
  195.9 6.2 %collective-permute-start.20 = (bf16[416,256]{1,0:T(8,128)(2,1)}, bf16[416,256]{1,0:T(8,128)(2,1)}, u32[]{:S(2)}, u32[]{:S(2)}) collective-permute-start(bf16[416,256]{1,0:T(8,128)(2,1)} %get-tuple-element.246), channel_id=1, source_target_pairs={{0,4},{4,0},{8,12},{12,8},{16,20},{20,16},{24,28},{28,24},{1,5},{5... | collective-permute-start | bytes 638984 | tf_op jit(solution)/shard_map/ppermute | solution.py:445
  201.9 30.6 %collective-permute-start.30 = (bf16[4,128,1024]{2,1,0:T(8,128)(2,1)}, bf16[4,128,1024]{2,1,0:T(8,128)(2,1)}, u32[]{:S(2)}, u32[]{:S(2)}) collective-permute-start(bf16[4,128,1024]{2,1,0:T(8,128)(2,1)} %get-tuple-element.267), channel_id=1, source_target_pairs={{0,4},{4,0},{8,12},{12,8},{16,20},{20,16},{24,28},{28,24},{1,5},{5... | collective-permute-start | bytes 3145736 | tf_op jit(solution)/shard_map/ppermute | solution.py:445
  203.9 7.2 %collective-permute-start.23 = (bf16[104,256]{1,0:T(8,128)(2,1)}, bf16[104,256]{1,0:T(8,128)(2,1)}, u32[]{:S(2)}, u32[]{:S(2)}) collective-permute-start(bf16[104,256]{1,0:T(8,128)(2,1)} %get-tuple-element.256), channel_id=1, source_target_pairs={{0,8},{4,12},{8,0},{12,4},{16,24},{20,28},{24,16},{28,20},{1,9},{5... | collective-permute-start | bytes 159752 | tf_op jit(solution)/shard_map/ppermute | solution.py:445
  204.0 7.1 %collective-permute-start.24 = (bf16[104,256]{1,0:T(8,128)(2,1)}, bf16[104,256]{1,0:T(8,128)(2,1)}, u32[]{:S(2)}, u32[]{:S(2)}) collective-permute-start(bf16[104,256]{1,0:T(8,128)(2,1)} %get-tuple-element.257), channel_id=1, source_target_pairs={{0,16},{4,20},{8,24},{12,28},{16,0},{20,4},{24,8},{28,12},{1,17},{... | collective-permute-start | bytes 159752 | tf_op jit(solution)/shard_map/ppermute | solution.py:445
  206.2 5.6 %collective-permute-start.25 = (bf16[104,256]{1,0:T(8,128)(2,1)}, bf16[104,256]{1,0:T(8,128)(2,1)}, u32[]{:S(2)}, u32[]{:S(2)}) collective-permute-start(bf16[104,256]{1,0:T(8,128)(2,1)} %get-tuple-element.258), channel_id=1, source_target_pairs={{0,24},{4,28},{8,16},{12,20},{16,8},{20,12},{24,0},{28,4},{1,25},{... | collective-permute-start | bytes 159752 | tf_op jit(solution)/shard_map/ppermute | solution.py:445
  209.9 22.5 %collective-permute-start.31 = (bf16[128,1280]{1,0:T(8,128)(2,1)}, bf16[128,1280]{1,0:T(8,128)(2,1)}, u32[]{:S(2)}, u32[]{:S(2)}) collective-permute-start(bf16[128,1280]{1,0:T(8,128)(2,1)} %get-tuple-element.268), channel_id=1, source_target_pairs={{0,16},{4,20},{8,24},{12,28},{16,0},{20,4},{24,8},{28,12},{1,17},{... | collective-permute-start | bytes 983048 | tf_op jit(solution)/shard_map/ppermute | solution.py:445
  213.4 5.4 %collective-permute-start.27 = (bf16[104,256]{1,0:T(8,128)(2,1)}, bf16[104,256]{1,0:T(8,128)(2,1)}, u32[]{:S(2)}, u32[]{:S(2)}) collective-permute-start(bf16[104,256]{1,0:T(8,128)(2,1)} %z_sum.1.refs_0_), channel_id=1, source_target_pairs={{0,8},{4,12},{8,0},{12,4},{16,24},{20,28},{24,16},{28,20},{1,9},{5... | collective-permute-start | bytes 159752 | tf_op jit(solution)/shard_map/ppermute | solution.py:445
  213.8 17.9 %collective-permute-start.28 = (bf16[104,256]{1,0:T(8,128)(2,1)}, bf16[104,256]{1,0:T(8,128)(2,1)}, u32[]{:S(2)}, u32[]{:S(2)}) collective-permute-start(bf16[104,256]{1,0:T(8,128)(2,1)} %z_sum.1.refs_0_), channel_id=1, source_target_pairs={{0,16},{4,20},{8,24},{12,28},{16,0},{20,4},{24,8},{28,12},{1,17},{... | collective-permute-start | bytes 159752 | tf_op jit(solution)/shard_map/ppermute | solution.py:445
  214.5 17.9 %collective-permute-start.29 = (bf16[104,256]{1,0:T(8,128)(2,1)}, bf16[104,256]{1,0:T(8,128)(2,1)}, u32[]{:S(2)}, u32[]{:S(2)}) collective-permute-start(bf16[104,256]{1,0:T(8,128)(2,1)} %z_sum.1.refs_0_), channel_id=1, source_target_pairs={{0,24},{4,28},{8,16},{12,20},{16,8},{20,12},{24,0},{28,4},{1,25},{... | collective-permute-start | bytes 159752 | tf_op jit(solution)/shard_map/ppermute | solution.py:445
  218.7 26.5 %collective-permute-start.33 = (bf16[128,1024]{1,0:T(8,128)(2,1)}, bf16[128,1024]{1,0:T(8,128)(2,1)}, u32[]{:S(2)}, u32[]{:S(2)}) collective-permute-start(bf16[128,1024]{1,0:T(8,128)(2,1)} %z_last_sum.3.refs_0_), channel_id=1, source_target_pairs={{0,2},{1,3},{2,0},{3,1},{4,6},{5,7},{6,4},{7,5},{8,10},{9,11},{10,... | collective-permute-start | bytes 786440 | tf_op jit(solution)/shard_map/ppermute | solution.py:445
  231.7 23.3 %collective-permute-start.36 = (bf16[128,1024]{1,0:T(8,128)(2,1)}, bf16[128,1024]{1,0:T(8,128)(2,1)}, u32[]{:S(2)}, u32[]{:S(2)}) collective-permute-start(bf16[128,1024]{1,0:T(8,128)(2,1)} %z_last_sum.3.refs_0_), channel_id=1, source_target_pairs={{0,1},{1,0},{2,3},{3,2},{4,5},{5,4},{6,7},{7,6},{8,9},{9,8},{10,11... | collective-permute-start | bytes 786440 | tf_op jit(solution)/shard_map/ppermute | solution.py:445
  234.7 16.9 %collective-permute-start.38 = (bf16[2,128,1024]{2,1,0:T(8,128)(2,1)}, bf16[2,128,1024]{2,1,0:T(8,128)(2,1)}, u32[]{:S(2)}, u32[]{:S(2)}) collective-permute-start(bf16[2,128,1024]{2,1,0:T(8,128)(2,1)} %pair_sum.5), channel_id=1, source_target_pairs={{0,8},{4,12},{8,0},{12,4},{16,24},{20,28},{24,16},{28,20},{1,9},{5... | collective-permute-start | bytes 1572872 | tf_op jit(solution)/shard_map/ppermute | solution.py:445
  237.0 10.8 %collective-permute-start.32 = (bf16[416,256]{1,0:T(8,128)(2,1)}, bf16[416,256]{1,0:T(8,128)(2,1)}, u32[]{:S(2)}, u32[]{:S(2)}) collective-permute-start(bf16[416,256]{1,0:T(8,128)(2,1)} %bitcast.84), channel_id=1, source_target_pairs={{0,4},{4,0},{8,12},{12,8},{16,20},{20,16},{24,28},{28,24},{1,5},{5... | collective-permute-start | bytes 638984 | tf_op jit(solution)/shard_map/ppermute | solution.py:445
  238.2 9.7 %all-to-all-start.6 = ((bf16[4,192,128]{2,1,0:T(8,128)(2,1)}), bf16[4,192,128]{2,1,0:T(8,128)(2,1)}, u32[]{:S(2)}, u32[]{:S(2)}) async-start(bf16[4,192,128]{2,1,0:T(8,128)(2,1)} %bitcast.30), calls=%async_computation.6 | async-start | bytes 393216 | tf_op jit(solution)/shard_map/all_to_all | solution.py:1108
  245.2 29.7 %collective-permute-start.44 = (bf16[128,1280]{1,0:T(8,128)(2,1)}, bf16[128,1280]{1,0:T(8,128)(2,1)}, u32[]{:S(2)}, u32[]{:S(2)}) collective-permute-start(bf16[128,1280]{1,0:T(8,128)(2,1)} %z_last_sum.5.refs_0_), channel_id=1, source_target_pairs={{0,1},{1,0},{2,3},{3,2},{4,5},{5,4},{6,7},{7,6},{8,9},{9,8},{10,11... | collective-permute-start | bytes 983048 | tf_op jit(solution)/shard_map/ppermute | solution.py:445
  245.2 9.8 %collective-permute-start.45 = (bf16[128,1280]{1,0:T(8,128)(2,1)}, bf16[128,1280]{1,0:T(8,128)(2,1)}, u32[]{:S(2)}, u32[]{:S(2)}) collective-permute-start(bf16[128,1280]{1,0:T(8,128)(2,1)} %z_last_sum.5.refs_0_), channel_id=1, source_target_pairs={{0,2},{1,3},{2,0},{3,1},{4,6},{5,7},{6,4},{7,5},{8,10},{9,11},{10,... | collective-permute-start | bytes 983048 | tf_op jit(solution)/shard_map/ppermute | solution.py:445
  251.3 12.7 %collective-permute-start.35 = (bf16[832,256]{1,0:T(8,128)(2,1)}, bf16[832,256]{1,0:T(8,128)(2,1)}, u32[]{:S(2)}, u32[]{:S(2)}) collective-permute-start(bf16[832,256]{1,0:T(8,128)(2,1)} %bitcast.33.m0), channel_id=1, source_target_pairs={{0,2},{1,3},{2,0},{3,1},{4,6},{5,7},{6,4},{7,5},{8,10},{9,11},{10,... | collective-permute-start | bytes 1277960 | tf_op jit(solution)/shard_map/ppermute | solution.py:445
  251.7 4.9 %collective-permute-start.37 = (bf16[128,1024]{1,0:T(8,128)(2,1)}, bf16[128,1024]{1,0:T(8,128)(2,1)}, u32[]{:S(2)}, u32[]{:S(2)}) collective-permute-start(bf16[128,1024]{1,0:T(8,128)(2,1)} %collective-permute-done.33.refs_2_), channel_id=1, source_target_pairs={{0,1},{1,0},{2,3},{3,2},{4,5},{5,4},{6,7},{7,6},{8,9},{9,8},{10,11... | collective-permute-start | bytes 786440 | tf_op jit(solution)/shard_map/ppermute | solution.py:445
  255.0 27.5 %collective-permute-start.34 = (bf16[832,256]{1,0:T(8,128)(2,1)}, bf16[832,256]{1,0:T(8,128)(2,1)}, u32[]{:S(2)}, u32[]{:S(2)}) collective-permute-start(bf16[832,256]{1,0:T(8,128)(2,1)} %bitcast.33.m0), channel_id=1, source_target_pairs={{0,1},{1,0},{2,3},{3,2},{4,5},{5,4},{6,7},{7,6},{8,9},{9,8},{10,11... | collective-permute-start | bytes 1277960 | tf_op jit(solution)/shard_map/ppermute | solution.py:445
  255.0 19.8 %collective-permute-start.46 = (bf16[128,1280]{1,0:T(8,128)(2,1)}, bf16[128,1280]{1,0:T(8,128)(2,1)}, u32[]{:S(2)}, u32[]{:S(2)}) collective-permute-start(bf16[128,1280]{1,0:T(8,128)(2,1)} %collective-permute-done.45.refs_2_), channel_id=1, source_target_pairs={{0,1},{1,0},{2,3},{3,2},{4,5},{5,4},{6,7},{7,6},{8,9},{9,8},{10,11... | collective-permute-start | bytes 983048 | tf_op jit(solution)/shard_map/ppermute | solution.py:445
  256.5 15.1 %collective-permute-start.40 = (bf16[128,1024]{1,0:T(8,128)(2,1)}, bf16[128,1024]{1,0:T(8,128)(2,1)}, u32[]{:S(2)}, u32[]{:S(2)}) collective-permute-start(bf16[128,1024]{1,0:T(8,128)(2,1)} %get-tuple-element.299), channel_id=1, source_target_pairs={{0,16},{4,20},{8,24},{12,28},{16,0},{20,4},{24,8},{28,12},{1,17},{... | collective-permute-start | bytes 786440 | tf_op jit(solution)/shard_map/ppermute | solution.py:445
  264.0 18.5 %collective-permute-start.39 = (bf16[832,256]{1,0:T(8,128)(2,1)}, bf16[832,256]{1,0:T(8,128)(2,1)}, u32[]{:S(2)}, u32[]{:S(2)}) collective-permute-start(bf16[832,256]{1,0:T(8,128)(2,1)} %collective-permute-done.35.m2), channel_id=1, source_target_pairs={{0,1},{1,0},{2,3},{3,2},{4,5},{5,4},{6,7},{7,6},{8,9},{9,8},{10,11... | collective-permute-start | bytes 1277960 | tf_op jit(solution)/shard_map/ppermute | solution.py:445
  273.4 7.8 %collective-permute-start.42 = (bf16[128,1024]{1,0:T(8,128)(2,1)}, bf16[128,1024]{1,0:T(8,128)(2,1)}, u32[]{:S(2)}, u32[]{:S(2)}) collective-permute-start(bf16[128,1024]{1,0:T(8,128)(2,1)} %z_last_sum.4.refs_0_), channel_id=1, source_target_pairs={{0,2},{1,3},{2,0},{3,1},{4,6},{5,7},{6,4},{7,5},{8,10},{9,11},{10,... | collective-permute-start | bytes 786440 | tf_op jit(solution)/shard_map/ppermute | solution.py:445
  277.7 10.9 %collective-permute-start.41 = (bf16[128,1024]{1,0:T(8,128)(2,1)}, bf16[128,1024]{1,0:T(8,128)(2,1)}, u32[]{:S(2)}, u32[]{:S(2)}) collective-permute-start(bf16[128,1024]{1,0:T(8,128)(2,1)} %z_last_sum.4.refs_0_), channel_id=1, source_target_pairs={{0,1},{1,0},{2,3},{3,2},{4,5},{5,4},{6,7},{7,6},{8,9},{9,8},{10,11... | collective-permute-start | bytes 786440 | tf_op jit(solution)/shard_map/ppermute | solution.py:445
  281.2 7.5 %collective-permute-start.43 = (bf16[128,1024]{1,0:T(8,128)(2,1)}, bf16[128,1024]{1,0:T(8,128)(2,1)}, u32[]{:S(2)}, u32[]{:S(2)}) collective-permute-start(bf16[128,1024]{1,0:T(8,128)(2,1)} %collective-permute-done.42.refs_2_), channel_id=1, source_target_pairs={{0,1},{1,0},{2,3},{3,2},{4,5},{5,4},{6,7},{7,6},{8,9},{9,8},{10,11... | collective-permute-start | bytes 786440 | tf_op jit(solution)/shard_map/ppermute | solution.py:445
  (18 other events, 70.8 us)
